TPU v7x, 32 devices: a whole 2x2x4 slice. The times are simulated.
32 devices in a mesh: seq: 4 (over z), row: 2 (over x), col: 4 (over y, core).
Axes of the slice: x: 2, y: 2, z: 4, core: 2. Of those that a mesh axis runs over, the one named last changes fastest.
Arguments:
- stream_in: float32 [2, 4096, 1536], P(None, 'seq', ('col', 'row')), may hold values from -6 to 6
- cotangent: float32 [2, 4096, 1536], P(None, 'seq', ('col', 'row')), may hold values from -6 to 6
- doc_lengths: int32 [2, 8], replicated, may hold values from 1 to 2048, 4096 in all within a row
- mixer_gain: float32 [1536], P(('col', 'row')), may hold values from 0.5 to 1.5
- input_weight: bfloat16 [1536, 2048], P('col', 'row'), may hold values from -0.15625 to 0.15625
- branch_weight: bfloat16 [1536, 2048], P('col', 'row'), may hold values from -0.15625 to 0.15625
- filter_taps: float32 [4, 2048], P(None, ('row', 'col')), may hold values from -3 to 3
- recall_gate: float32 [16, 128, 128], P('row'), may hold values from -0.5 to 0.5
- admit_gate: float32 [16, 128, 128], P('row'), may hold values from -0.5 to 0.5
- decay_param: float32 [2048], P(('row', 'col')), may hold values from 1 to 14
- output_weight: bfloat16 [2048, 1536], P('row', 'col'), may hold values from -0.25 to 0.25
- feed_gain: float32 [1536], P(('col', 'row')), may hold values from 0.5 to 1.5
- gate_weight: bfloat16 [1536, 4608], P('col', 'row'), may hold values from -0.15625 to 0.15625
- up_weight: bfloat16 [1536, 4608], P('col', 'row'), may hold values from -0.15625 to 0.15625
- down_weight: bfloat16 [4608, 1536], P('row', 'col'), may hold values from -0.1875 to 0.1875
Outputs:
- block_out: float32 [2, 4096, 1536], P(None, 'seq', ('col', 'row'))
- grad_stream: float32 [2, 4096, 1536], P(None, 'seq', ('col', 'row'))
- grad_mixer_gain: float32 [1536], P(('col', 'row'))
- grad_input_weight: float32 [1536, 2048], P('col', 'row')
- grad_branch_weight: float32 [1536, 2048], P('col', 'row')
- grad_filter_taps: float32 [4, 2048], P(None, ('row', 'col'))
- grad_recall_gate: float32 [16, 128, 128], P('row')
- grad_admit_gate: float32 [16, 128, 128], P('row')
- grad_decay_param: float32 [2048], P(('row', 'col'))
- grad_output_weight: float32 [2048, 1536], P('row', 'col')
- grad_feed_gain: float32 [1536], P(('col', 'row'))
- grad_gate_weight: float32 [1536, 4608], P('col', 'row')
- grad_up_weight: float32 [1536, 4608], P('col', 'row')
- grad_down_weight: float32 [4608, 1536], P('row', 'col')
All inputs are finite; a program needn't handle non-finite values.
Results may differ from a plain program's by a relative error of at most 0.014.
Values may be sent and summed in bfloat16 or wider, within the bound.
A program may use at most 256 MiB of HBM per device.

v0:
```python
import jax
import jax.numpy as jnp
from jax import lax
from jax.sharding import PartitionSpec as P

D = 1536
KW = 4


EPSILON = 1e-06
PRECISE = lax.Precision.HIGHEST
SUM_ROWS = (((0,), (0,)), ((), ()))
SUM_COLS = (((1,), (1,)), ((), ()))


def as_sent(value):
    return jax.tree.map(lambda a: a.astype(jnp.bfloat16) if a.dtype == jnp.float32 else a, value)


def passed_along(block, axis, distance):
    devices = range(lax.axis_size(axis))
    route = [(i - distance, i) for i in devices if i - distance in devices]
    return lax.ppermute(block, axis, route)


def entering_2(part, axis, combine, identity, reverse):
    count = lax.axis_size(axis)
    place = lax.axis_index(axis)
    ahead = count - 1 - place if reverse else place
    gathered = jax.tree.map(lambda a: lax.all_gather(a, axis), part)
    state = jax.tree.map(lambda a, e: jnp.zeros_like(a) + jnp.asarray(e, a.dtype), part, identity)

    def one(hop, state):
        source = count - 1 - hop if reverse else hop
        return combine(
            state, jax.tree.map(lambda a: lax.dynamic_index_in_dim(a, source, 0, False), gathered)
        )

    return lax.fori_loop(0, ahead, one, state)


def compose(first, second):
    return (first[0] * second[0], second[0] * first[1] + second[1])


def convolve(source, taps, offset, border):
    tokens = source.shape[0]
    extended = jnp.concatenate([border, source], axis=0)
    result = jnp.zeros_like(source)
    for lag_index in range(KW):
        anchor = KW - 1 - lag_index
        valid = (offset >= lag_index).astype(jnp.float32)[:, None]
        result = result + taps[lag_index] * extended[anchor : anchor + tokens] * valid
    return result


def slab_pre(conv_value, recall_value, admit_value):
    tokens = conv_value.shape[0]
    blocks = conv_value.reshape(tokens, recall_value.shape[0], recall_value.shape[1])
    recall_pre = jnp.einsum("thi,hij->thj", blocks, recall_value, precision=PRECISE).reshape(
        tokens, -1
    )
    admit_pre = jnp.einsum("thi,hij->thj", blocks, admit_value, precision=PRECISE).reshape(
        tokens, -1
    )
    return (recall_pre, admit_pre)


def own_terms(conv_value, recall_pre, admit_pre, decay_value, resume):
    recall = jax.nn.sigmoid(recall_pre)
    admit = jax.nn.sigmoid(admit_pre)
    log_decay = -8.0 * recall * jax.nn.softplus(-decay_value)
    decays = jnp.exp(log_decay) * resume[:, None]
    drives = jnp.sqrt(-jnp.expm1(2.0 * log_decay)) * admit * conv_value
    return (decays, drives)


def width_total(partial_value):
    return lax.psum(partial_value, ("row", "col"))


def gather_row(source):
    return lax.all_gather(source, "row", axis=1, tiled=True)


def gather_col(source):
    return jax.tree.map(
        lambda part, own: part.astype(own.dtype),
        lax.all_gather(as_sent(source), "col", axis=1, tiled=True),
        source,
    )


def scatter_col(source):
    return (
        lax.psum_scatter(source[0], "col", scatter_dimension=1, tiled=True),
        lax.psum_scatter(source[1], "col", scatter_dimension=1, tiled=True),
    )


def scatter_col_back(source):
    return lax.psum_scatter(source, "col", scatter_dimension=1, tiled=True)


def scatter_row(source):
    return lax.psum_scatter(source, "row", scatter_dimension=1, tiled=True)


def over_seq(grads):
    return (
        lax.psum(grads[0].astype(jnp.bfloat16), "seq").astype(jnp.float32),
        lax.psum(grads[1].astype(jnp.bfloat16), "seq").astype(jnp.float32),
        lax.psum(grads[2].astype(jnp.bfloat16), "seq").astype(jnp.float32),
        lax.psum(grads[3].astype(jnp.bfloat16), "seq").astype(jnp.float32),
        lax.psum(grads[4].astype(jnp.bfloat16), "seq").astype(jnp.float32),
        lax.psum(grads[5].astype(jnp.bfloat16), "seq").astype(jnp.float32),
        lax.psum(grads[6].astype(jnp.bfloat16), "seq").astype(jnp.float32),
        lax.psum(grads[7].astype(jnp.bfloat16), "seq").astype(jnp.float32),
        lax.psum(grads[8].astype(jnp.bfloat16), "seq").astype(jnp.float32),
        lax.psum(grads[9].astype(jnp.bfloat16), "seq").astype(jnp.float32),
        lax.psum(grads[10].astype(jnp.bfloat16), "seq").astype(jnp.float32),
        lax.psum(grads[11].astype(jnp.bfloat16), "seq").astype(jnp.float32),
    )


def normalize(source, scales):
    factor = lax.rsqrt(width_total(jnp.sum(source * source, axis=1)) / D + EPSILON)
    return (source * factor[:, None] * scales, factor)


def norm_back(source, scales, factor, grad_norm):
    weighted = scales * grad_norm
    summed = width_total(jnp.sum(weighted * source, axis=1))
    grad_source = (
        factor[:, None] * weighted - source * (factor * factor * factor * summed / D)[:, None]
    )
    grad_scales = jnp.sum(grad_norm * source * factor[:, None], axis=0)
    return (grad_source, grad_scales)


def doc_offset(lengths, anchor, tokens):
    starts = jnp.cumsum(lengths, dtype=jnp.int32) - lengths
    places = anchor + jnp.arange(tokens, dtype=jnp.int32)
    begins = jnp.max(jnp.where(starts[None, :] <= places[:, None], starts[None, :], 0), axis=1)
    return places - begins


def matmul_rows(left, right):
    return lax.dot_general(left, right, SUM_ROWS, preferred_element_type=jnp.float32)


def matmul_cols(left, right):
    return lax.dot_general(left, right, SUM_COLS, preferred_element_type=jnp.float32)


def local(
    stream_in,
    cotangent,
    doc_lengths,
    mixer_gain,
    input_weight,
    branch_weight,
    filter_taps,
    recall_gate,
    admit_gate,
    decay_param,
    output_weight,
    feed_gain,
    gate_weight,
    up_weight,
    down_weight,
):
    tokens = stream_in.shape[1]
    anchor = lax.axis_index("seq") * tokens
    channels = decay_param.shape[0]
    col_start = lax.axis_index("col") * channels
    params = (
        mixer_gain,
        input_weight,
        branch_weight,
        filter_taps,
        recall_gate,
        admit_gate,
        decay_param,
        output_weight,
        feed_gain,
        gate_weight,
        up_weight,
        down_weight,
    )
    totals = tuple((jnp.zeros(w.shape, jnp.float32) for w in params))
    identity = (jnp.ones_like(decay_param), jnp.zeros_like(decay_param))
    outputs = []
    grads_in = []
    for micro in range(stream_in.shape[0]):
        offset = doc_offset(doc_lengths[micro], anchor, tokens)
        resume = (offset > 0).astype(jnp.float32)
        source = stream_in[micro]
        normed, factor_one = normalize(source, mixer_gain)
        normed_low = normed.astype(jnp.bfloat16)
        normed_all = gather_row(normed_low)
        rec_in, branch = scatter_col(
            (
                jnp.dot(normed_all, input_weight, preferred_element_type=jnp.float32),
                jnp.dot(normed_all, branch_weight, preferred_element_type=jnp.float32),
            )
        )
        border = passed_along(rec_in[tokens - (KW - 1) :], "seq", 1)
        conv_out = convolve(rec_in, filter_taps, offset, border)
        conv_slab = lax.all_gather(conv_out, "col", axis=1, tiled=True)
        slab_values, slab_pull = jax.vjp(slab_pre, conv_slab, recall_gate, admit_gate)
        recall_pre = lax.dynamic_slice_in_dim(slab_values[0], col_start, channels, 1)
        admit_pre = lax.dynamic_slice_in_dim(slab_values[1], col_start, channels, 1)

        def local_gates(conv_value, recall_value, admit_value, decay_value):
            return own_terms(conv_value, recall_value, admit_value, decay_value, resume)

        (decays, drives), gates_pull = jax.vjp(
            local_gates, conv_out, recall_pre, admit_pre, decay_param
        )
        cum_decay, local_state = lax.associative_scan(compose, (decays, drives), axis=0)
        entering = entering_2((cum_decay[-1], local_state[-1]), "seq", compose, identity, False)[1]
        states = local_state + cum_decay * entering
        branch_act = jax.nn.gelu(branch)
        mixed_all = gather_col((states * branch_act).astype(jnp.bfloat16))
        middle = source + scatter_row(
            jnp.dot(mixed_all, output_weight, preferred_element_type=jnp.float32)
        )
        normed_two, factor_two = normalize(middle, feed_gain)
        normed_two_low = normed_two.astype(jnp.bfloat16)
        normed_two_all = gather_row(normed_two_low)
        gate_pre, up_pre = scatter_col(
            (
                jnp.dot(normed_two_all, gate_weight, preferred_element_type=jnp.float32),
                jnp.dot(normed_two_all, up_weight, preferred_element_type=jnp.float32),
            )
        )
        gate_act = jax.nn.gelu(gate_pre)
        hidden_all = gather_col((gate_act * up_pre).astype(jnp.bfloat16))
        outputs.append(
            middle
            + scatter_row(jnp.dot(hidden_all, down_weight, preferred_element_type=jnp.float32))
        )
        upstream = cotangent[micro]
        upstream_all = gather_row(upstream.astype(jnp.bfloat16))
        grad_down = matmul_rows(hidden_all, upstream_all)
        grad_hidden = scatter_col_back(matmul_cols(upstream_all, down_weight))
        gate_value, gelu_pull = jax.vjp(jax.nn.gelu, gate_pre)
        error_gate = gelu_pull(grad_hidden * up_pre)[0].astype(jnp.bfloat16)
        error_up = (grad_hidden * gate_act).astype(jnp.bfloat16)
        gate_err_all, up_err_all = gather_col((error_gate, error_up))
        grad_gate = matmul_rows(normed_two_all, gate_err_all)
        grad_up = matmul_rows(normed_two_all, up_err_all)
        grad_normed_two = scatter_row(
            matmul_cols(gate_err_all, gate_weight) + matmul_cols(up_err_all, up_weight)
        )
        back_middle, grad_feed = norm_back(middle, feed_gain, factor_two, grad_normed_two)
        grad_middle = upstream + back_middle
        rec_err_all = gather_row(grad_middle.astype(jnp.bfloat16))
        grad_output = matmul_rows(mixed_all, rec_err_all)
        grad_mixed = scatter_col_back(matmul_cols(rec_err_all, output_weight))
        branch_value, branch_pull = jax.vjp(jax.nn.gelu, branch)
        error_branch = branch_pull(grad_mixed * states)[0].astype(jnp.bfloat16)
        direct = grad_mixed * branch_act
        ahead = jnp.concatenate([decays[1:], jnp.ones_like(decays[:1])], axis=0)
        reach, partial_adj = lax.associative_scan(compose, (ahead, direct), axis=0, reverse=True)
        incoming = entering_2(
            (decays[0] * reach[0], decays[0] * partial_adj[0]), "seq", compose, identity, True
        )[1]
        adjoint = partial_adj + reach * incoming
        previous = jnp.concatenate([entering[None, :], states[:-1]], axis=0)
        conv_direct, grad_recall_pre, grad_admit_pre, grad_decay = gates_pull(
            (adjoint * previous, adjoint)
        )
        recall_all, admit_all = (
            lax.all_gather(grad_recall_pre.astype(jnp.bfloat16), "col", axis=1, tiled=True).astype(
                grad_recall_pre.dtype
            ),
            lax.all_gather(grad_admit_pre.astype(jnp.bfloat16), "col", axis=1, tiled=True).astype(
                grad_admit_pre.dtype
            ),
        )
        grad_slab, grad_recall, grad_admit = slab_pull((recall_all, admit_all))
        grad_conv_out = conv_direct + lax.dynamic_slice_in_dim(grad_slab, col_start, channels, 1)

        def local_conv(input_value, taps_value, border_value):
            return convolve(input_value, taps_value, offset, border_value)

        conv_value, conv_pull = jax.vjp(local_conv, rec_in, filter_taps, border)
        grad_rec_in, grad_taps, grad_border = conv_pull(grad_conv_out)
        from_next = passed_along(grad_border, "seq", -1)
        grad_rec_in = grad_rec_in + jnp.pad(from_next, ((tokens - (KW - 1), 0), (0, 0)))
        error_input = grad_rec_in.astype(jnp.bfloat16)
        in_err_all, branch_err_all = gather_col((error_input, error_branch))
        grad_input = matmul_rows(normed_all, in_err_all)
        grad_branch = matmul_rows(normed_all, branch_err_all)
        grad_normed = scatter_row(
            matmul_cols(in_err_all, input_weight) + matmul_cols(branch_err_all, branch_weight)
        )
        back_source, grad_mixer = norm_back(source, mixer_gain, factor_one, grad_normed)
        grads_in.append(grad_middle + back_source)
        local_grads = (
            grad_mixer,
            grad_input,
            grad_branch,
            grad_taps,
            grad_recall,
            grad_admit,
            grad_decay,
            grad_output,
            grad_feed,
            grad_gate,
            grad_up,
            grad_down,
        )
        local_grads = over_seq(local_grads)
        totals = tuple((acc + new for acc, new in zip(totals, local_grads)))
    return (jnp.stack(outputs), jnp.stack(grads_in)) + tuple(totals)


def solution(mesh):
    in_specs = (
        P(None, "seq", ("col", "row")),
        P(None, "seq", ("col", "row")),
        P(),
        P(("col", "row")),
        P("col", "row"),
        P("col", "row"),
        P(None, ("row", "col")),
        P("row", None, None),
        P("row", None, None),
        P(("row", "col")),
        P("row", "col"),
        P(("col", "row")),
        P("col", "row"),
        P("col", "row"),
        P("row", "col"),
    )
    out_specs = (
        P(None, "seq", ("col", "row")),
        P(None, "seq", ("col", "row")),
        P(("col", "row")),
        P("col", "row"),
        P("col", "row"),
        P(None, ("row", "col")),
        P("row", None, None),
        P("row", None, None),
        P(("row", "col")),
        P("row", "col"),
        P(("col", "row")),
        P("col", "row"),
        P("col", "row"),
        P("row", "col"),
    )
    return jax.shard_map(local, mesh=mesh, in_specs=in_specs, out_specs=out_specs, check_vma=False)
```

profile of v0, /device:TPU:0, one launch (start us, length us, event | category | flops | bytes accessed | tf_op | source)
XLA Modules:
  0.0 2798.5 jit_solution(11680751231451969564)
XLA Ops:
  8.9 15.4 all-reduce.185
  26.1 9.6 all_gather.113
  40.0 9.7 all_gather.106
  56.3 29.1 %reduce-scatter.33.cloned.1.call-done = f32[1024,256]{1,0:T(8,128)} async-done(((f32[1024,1024]{1,0:T(8,128)}), f32[1024,256]{1,0:T(8,128)}) %reduce-scatter.33.cloned.1.call-update) | async-done | bytes 1048592 | tf_op jit(solution)/shard_map/reduce_scatter | solution.py:96
  95.0 37.6 %reduce-scatter.21.cloned.1.call-done = f32[1024,256]{1,0:T(8,128)} async-done(((f32[1024,1024]{1,0:T(8,128)}), f32[1024,256]{1,0:T(8,128)}) %reduce-scatter.21.cloned.1.call-update) | async-done | bytes 1048592 | tf_op jit(solution)/shard_map/reduce_scatter | solution.py:96
  154.0 15.2 all-gather.33.cloned.1.call-done
  174.6 8.3 fusion.176
  188.2 17.6 all-gather.27.cloned.1.call-done
  211.1 8.4 fusion.168
  571.3 10.9 all-gather.2
  595.0 7.6 all-gather.3
  688.9 11.7 all-gather
  712.3 7.6 all-gather.1
  728.1 18.1 all-gather.29.cloned.1.call-done
  752.6 20.2 all_gather.120
  782.7 28.9 %reduce-scatter.25.cloned.1.call-done = f32[1024,192]{0,1:T(8,128)} async-done(((f32[1024,384]{0,1:T(8,128)}), f32[1024,192]{0,1:T(8,128)}) %reduce-scatter.25.cloned.1.call-update) | async-done | bytes 786448 | tf_op jit(solution)/shard_map/reduce_scatter | solution.py:106
  814.4 13.0 all-reduce.184
  828.7 10.6 all_gather.111
  839.4 6.8 fusion.172
  851.7 40.9 %reduce-scatter.45.cloned.1.call-done = f32[1024,576]{0,1:T(8,128)} async-done(((f32[1024,2304]{0,1:T(8,128)}), f32[1024,576]{0,1:T(8,128)}) %reduce-scatter.45.cloned.1.call-update) | async-done | bytes 2359312 | tf_op jit(solution)/shard_map/reduce_scatter | solution.py:102
  892.6 80.9 %reduce-scatter.29.cloned.1.call-done = f32[1024,576]{0,1:T(8,128)} async-done(((f32[1024,2304]{0,1:T(8,128)}), f32[1024,576]{0,1:T(8,128)}) %reduce-scatter.29.cloned.1.call-update) | async-done | bytes 2359312 | tf_op jit(solution)/shard_map/reduce_scatter | solution.py:97
  973.5 81.0 %reduce-scatter.27.cloned.1.call-done = f32[1024,576]{0,1:T(8,128)} async-done(((f32[1024,2304]{0,1:T(8,128)}), f32[1024,576]{0,1:T(8,128)}) %reduce-scatter.27.cloned.1.call-update) | async-done | bytes 2359312 | tf_op jit(solution)/shard_map/reduce_scatter | solution.py:96
  1054.5 5.7 multiply_convert_fusion.1
  1060.9 37.0 %all-gather.39.cloned.1.call-done = bf16[1024,2304]{0,1:T(8,128)(2,1)} async-done(((bf16[1024,576]{0,1:T(8,128)(2,1)}), bf16[1024,2304]{0,1:T(8,128)(2,1)}) %all-gather.39.cloned.1.call-update) | async-done | bytes 4718608 | tf_op jit(solution)/shard_map/all_gather | solution.py:89
  1103.3 34.0 %all-gather.41.cloned.1.call-done = bf16[1024,2304]{0,1:T(8,128)(2,1)} async-done(((bf16[1024,576]{0,1:T(8,128)(2,1)}), bf16[1024,2304]{0,1:T(8,128)(2,1)}) %all-gather.41.cloned.1.call-update) | async-done | bytes 4718608 | tf_op jit(solution)/shard_map/all_gather | solution.py:89
  1137.3 6.0 convolution_add_fusion.5
  1143.4 17.3 all_gather.130
  1166.8 7.0 reduce-scatter.47.cloned.1.call-done
  1175.8 11.7 all_gather.118
  1193.9 6.2 fusion.179
  1200.1 54.7 %reduce-scatter.53.cloned.1.call-done = f32[1024,576]{0,1:T(8,128)} async-done(((f32[1024,2304]{0,1:T(8,128)}), f32[1024,576]{0,1:T(8,128)}) %reduce-scatter.53.cloned.1.call-update) | async-done | bytes 2359312 | tf_op jit(solution)/shard_map/reduce_scatter | solution.py:102
  1254.9 81.1 %reduce-scatter.41.cloned.1.call-done = f32[1024,576]{0,1:T(8,128)} async-done(((f32[1024,2304]{0,1:T(8,128)}), f32[1024,576]{0,1:T(8,128)}) %reduce-scatter.41.cloned.1.call-update) | async-done | bytes 2359312 | tf_op jit(solution)/shard_map/reduce_scatter | solution.py:97
  1335.9 81.2 %reduce-scatter.39.cloned.1.call-done = f32[1024,576]{0,1:T(8,128)} async-done(((f32[1024,2304]{0,1:T(8,128)}), f32[1024,576]{0,1:T(8,128)}) %reduce-scatter.39.cloned.1.call-update) | async-done | bytes 2359312 | tf_op jit(solution)/shard_map/reduce_scatter | solution.py:96
  1425.5 34.9 %all-gather.51.cloned.1.call-done = bf16[1024,2304]{0,1:T(8,128)(2,1)} async-done(((bf16[1024,576]{0,1:T(8,128)(2,1)}), bf16[1024,2304]{0,1:T(8,128)(2,1)}) %all-gather.51.cloned.1.call-update) | async-done | bytes 4718608 | tf_op jit(solution)/shard_map/all_gather | solution.py:89
  1466.0 34.2 %all-gather.53.cloned.1.call-done = bf16[1024,2304]{0,1:T(8,128)(2,1)} async-done(((bf16[1024,576]{0,1:T(8,128)(2,1)}), bf16[1024,2304]{0,1:T(8,128)(2,1)}) %all-gather.53.cloned.1.call-update) | async-done | bytes 4718608 | tf_op jit(solution)/shard_map/all_gather | solution.py:89
  1500.2 6.5 convolution_add_fusion.4
  1506.7 33.2 %all-gather.31.cloned.1.call-done = bf16[1024,2304]{0,1:T(8,128)(2,1)} async-done(((bf16[1024,576]{0,1:T(8,128)(2,1)}), bf16[1024,2304]{0,1:T(8,128)(2,1)}) %all-gather.31.cloned.1.call-update) | async-done | bytes 4718608 | tf_op jit(solution)/shard_map/all_gather | solution.py:89
  1545.5 34.1 %all-gather.37.cloned.1.call-done = bf16[1024,2304]{0,1:T(8,128)(2,1)} async-done(((bf16[1024,576]{0,1:T(8,128)(2,1)}), bf16[1024,2304]{0,1:T(8,128)(2,1)}) %all-gather.37.cloned.1.call-update) | async-done | bytes 4718608 | tf_op jit(solution)/shard_map/all_gather | solution.py:89
  1585.2 23.3 reduce-scatter.55.cloned.1.call-done
  1609.8 13.1 all-reduce.183
  1623.0 14.5 reduce-scatter.31.cloned.1.call-done
  1637.5 29.0 %reduce-scatter.43.cloned.1.call-done = f32[1024,192]{0,1:T(8,128)} async-done(((f32[1024,384]{0,1:T(8,128)}), f32[1024,192]{0,1:T(8,128)}) %reduce-scatter.43.cloned.1.call-update) | async-done | bytes 786448 | tf_op jit(solution)/shard_map/reduce_scatter | solution.py:106
  1670.5 11.5 all_gather.133
  1686.3 10.6 all_gather.123
  1873.8 8.9 rev.18
  1887.8 10.9 all-gather.7
  1898.7 7.6 all-gather.6
  1906.4 9.0 rev.16
  1915.5 8.9 rev.17
  1924.3 9.5 all-gather.5
  1933.8 7.6 all-gather.4
  1941.7 6.3 multiply_reduce_fusion.1
  1954.5 18.9 all-gather.55.cloned.1.call-done
  1983.1 15.1 all-gather.43.cloned.1.call-done
  2007.5 15.7 all-gather.57.cloned.1.call-done
  2033.2 15.0 all-gather.45.cloned.1.call-done
  2082.6 6.5 convolution_convert_fusion.1
  2108.0 5.8 convolution_convert_fusion.3
  2113.8 6.4 convolution_convert_fusion
  2130.7 16.8 all-gather.59.cloned.1.call-done
  2180.7 24.5 reduce-scatter.59.cloned.1.call-done
  2207.1 11.9 all-reduce.186
  2219.0 12.8 all-reduce.182
  2236.8 539.2 %all-reduce.190.cloned.1.call-done = (bf16[384,1024]{1,0:T(8,128)(2,1)}, bf16[384,1024]{1,0:T(8,128)(2,1)}, bf16[384,1024]{1,0:T(8,128)(2,1)}, bf16[384,1024]{1,...) async-done(((bf16[384,1024]{1,0:T(8,128)(2,1)}, ...) | async-done | bytes 16384016 | tf_op jit(solution)/shard_map/psum | solution.py:112
  (1294 shorter events, 946.7 us)
Async XLA Ops:
  7.2 839.1 %copy-start = (bf16[384,2304]{1,0:T(8,128)(2,1)S(1)}, bf16[384,2304]{1,0:T(8,128)(2,1)}, u32[]{:S(2)}) copy-start(bf16[384,2304]{1,0:T(8,128)(2,1)} %param.36) | copy-start | bytes 5308420
  7.2 78.2 %reduce-scatter.33.cloned.1.call-start = ((), (), s32[]{:S(2)}) async-start(), calls=%async_computation.29 | async-start | bytes 5242880 | tf_op jit(solution)/shard_map/reduce_scatter | solution.py:96
  39.9 92.7 %reduce-scatter.21.cloned.1.call-start = ((), (), s32[]{:S(2)}) async-start(), calls=%async_computation.20 | async-start | bytes 5242880 | tf_op jit(solution)/shard_map/reduce_scatter | solution.py:96
  55.1 114.1 %all-gather.33.cloned.1.call-start = ((), (), s32[]{:S(2)}) async-start(), calls=%async_computation.30 | async-start | bytes 5242880 | tf_op jit(solution)/shard_map/all_gather | solution.py:210
  56.2 86.4 %copy-start.115 = (f32[1024]{0:T(1024)}, f32[1024]{0:T(1024)S(1)}, u32[]{:S(2)}) copy-start(f32[1024]{0:T(1024)S(1)} %get-tuple-element.601) | copy-start | bytes 12292
  56.2 86.4 %copy-start.117 = (f32[1024]{0:T(1024)}, f32[1024]{0:T(1024)S(1)}, u32[]{:S(2)}) copy-start(f32[1024]{0:T(1024)S(1)} %get-tuple-element.602) | copy-start | bytes 12292
  56.3 86.4 %copy-start.119 = (f32[1024]{0:T(1024)}, f32[1024]{0:T(1024)S(1)}, u32[]{:S(2)}) copy-start(f32[1024]{0:T(1024)S(1)} %get-tuple-element.603) | copy-start | bytes 12292
  56.3 86.4 %copy-start.121 = (f32[1024]{0:T(1024)}, f32[1024]{0:T(1024)S(1)}, u32[]{:S(2)}) copy-start(f32[1024]{0:T(1024)S(1)} %get-tuple-element.604) | copy-start | bytes 12292
  56.3 188.3 %copy-start.137 = (f32[1024]{0:T(1024)}, f32[1024]{0:T(1024)S(1)}, u32[]{:S(2)}) copy-start(f32[1024]{0:T(1024)S(1)} %get-tuple-element.605) | copy-start | bytes 12292
  86.1 4.7 collective-permute-start.1
  89.5 53.2 %copy-start.146 = (f32[1,256]{1,0:T(1,128)}, f32[1,256]{1,0:T(1,128)S(1)}, u32[]{:S(2)}) copy-start(f32[1,256]{1,0:T(1,128)S(1)} %get-tuple-element.597) | copy-start | bytes 3076
  89.5 53.2 %copy-start.148 = (f32[1,256]{1,0:T(1,128)}, f32[1,256]{1,0:T(1,128)S(1)}, u32[]{:S(2)}) copy-start(f32[1,256]{1,0:T(1,128)S(1)} %get-tuple-element.598) | copy-start | bytes 3076
  89.5 53.2 %copy-start.150 = (f32[1,256]{1,0:T(1,128)}, f32[1,256]{1,0:T(1,128)S(1)}, u32[]{:S(2)}) copy-start(f32[1,256]{1,0:T(1,128)S(1)} %get-tuple-element.599) | copy-start | bytes 3076
  89.5 53.2 %copy-start.152 = (f32[1,256]{1,0:T(1,128)}, f32[1,256]{1,0:T(1,128)S(1)}, u32[]{:S(2)}) copy-start(f32[1,256]{1,0:T(1,128)S(1)} %get-tuple-element.600) | copy-start | bytes 3076
  90.8 45.9 %copy-start.158 = (f32[3,256]{1,0:T(4,128)}, f32[3,256]{1,0:T(4,128)S(1)}, u32[]{:S(2)}) copy-start(f32[3,256]{1,0:T(4,128)S(1)} %collective-permute-done.1) | copy-start | bytes 9220
  94.9 110.8 %all-gather.27.cloned.1.call-start = ((), (), s32[]{:S(2)}) async-start(), calls=%async_computation.21 | async-start | bytes 5242880 | tf_op jit(solution)/shard_map/all_gather | solution.py:210
  133.3 4.7 collective-permute-start
  136.7 107.8 %copy-start.139 = (f32[1024]{0:T(1024)}, f32[1024]{0:T(1024)S(1)}, u32[]{:S(2)}) copy-start(f32[1024]{0:T(1024)S(1)} %get-tuple-element.588) | copy-start | bytes 12292
  142.8 494.3 %reduce-scatter.35.cloned.1.call-start = ((), (), s32[]{:S(2)}) async-start(), calls=%async_computation.31 | async-start | bytes 5242880 | tf_op jit(solution)/shard_map/reduce_scatter | solution.py:97
  147.9 572.0 %reduce-scatter.23.cloned.1.call-start = ((), (), s32[]{:S(2)}) async-start(), calls=%async_computation.22 | async-start | bytes 5242880 | tf_op jit(solution)/shard_map/reduce_scatter | solution.py:97
  152.8 571.4 %all-gather.35.cloned.1.call-start = ((), (), s32[]{:S(2)}) async-start(), calls=%async_computation.32 | async-start | bytes 2621440 | tf_op jit(solution)/shard_map/all_gather | solution.py:89
  154.0 90.6 %copy-start.141 = (f32[256]{0:T(256)}, f32[256]{0:T(256)S(1)}, u32[]{:S(2)}) copy-start(f32[256]{0:T(256)S(1)} %get-tuple-element.392) | copy-start | bytes 3076
  462.8 44.4 %copy-start.109 = (f32[31,256]{1,0:T(8,128)S(1)}, f32[31,256]{1,0:T(8,128)}, u32[]{:S(2)}) copy-start(f32[31,256]{1,0:T(8,128)} %get-tuple-element.520) | copy-start | bytes 95236
  641.3 105.0 %all-gather.29.cloned.1.call-start = ((), (), s32[]{:S(2)}) async-start(), calls=%async_computation.23 | async-start | bytes 2621440 | tf_op jit(solution)/shard_map/all_gather | solution.py:89
  724.0 58.6 %reduce-scatter.37.cloned.1.call-start = ((), (), s32[]{:S(2)}) async-start(), calls=%async_computation.33 | async-start | bytes 2359296 | tf_op jit(solution)/shard_map/reduce_scatter | solution.py:106
  728.1 83.5 %reduce-scatter.25.cloned.1.call-start = ((), (), s32[]{:S(2)}) async-start(), calls=%async_computation.24 | async-start | bytes 2359296 | tf_op jit(solution)/shard_map/reduce_scatter | solution.py:106
  750.2 142.4 %reduce-scatter.45.cloned.1.call-start = ((), (), s32[]{:S(2)}) async-start(), calls=%async_computation.38 | async-start | bytes 11796480 | tf_op jit(solution)/shard_map/reduce_scatter | solution.py:102
  778.7 48.6 %copy-start.162 = (f32[192]{0:T(256)S(1)}, f32[192]{0:T(256)}, u32[]{:S(2)}) copy-start(f32[192]{0:T(256)} %param.35) | copy-start | bytes 2308
  778.7 194.8 %reduce-scatter.29.cloned.1.call-start = ((), (), s32[]{:S(2)}) async-start(), calls=%async_computation.26 | async-start | bytes 11796480 | tf_op jit(solution)/shard_map/reduce_scatter | solution.py:97
  846.3 208.3 %reduce-scatter.27.cloned.1.call-start = ((), (), s32[]{:S(2)}) async-start(), calls=%async_computation.25 | async-start | bytes 11796480 | tf_op jit(solution)/shard_map/reduce_scatter | solution.py:96
  851.6 246.2 %all-gather.39.cloned.1.call-start = ((), (), s32[]{:S(2)}) async-start(), calls=%async_computation.39 | async-start | bytes 5898240 | tf_op jit(solution)/shard_map/all_gather | solution.py:89
  1060.2 77.1 %all-gather.41.cloned.1.call-start = ((), (), s32[]{:S(2)}) async-start(), calls=%async_computation.40 | async-start | bytes 5898240 | tf_op jit(solution)/shard_map/all_gather | solution.py:89
  1060.8 76.5 %copy-start.45 = (bf16[384,2304]{1,0:T(8,128)(2,1)S(1)}, bf16[384,2304]{1,0:T(8,128)(2,1)}, u32[]{:S(2)}) copy-start(bf16[384,2304]{1,0:T(8,128)(2,1)} %param.37) | copy-start | bytes 5308420
  1060.8 113.0 %reduce-scatter.47.cloned.1.call-start = ((), (), s32[]{:S(2)}) async-start(), calls=%async_computation.41 | async-start | bytes 2359296 | tf_op jit(solution)/shard_map/reduce_scatter | solution.py:106
  1143.3 111.5 %reduce-scatter.53.cloned.1.call-start = ((), (), s32[]{:S(2)}) async-start(), calls=%async_computation.48 | async-start | bytes 11796480 | tf_op jit(solution)/shard_map/reduce_scatter | solution.py:102
  1166.7 169.2 %reduce-scatter.41.cloned.1.call-start = ((), (), s32[]{:S(2)}) async-start(), calls=%async_computation.35 | async-start | bytes 11796480 | tf_op jit(solution)/shard_map/reduce_scatter | solution.py:97
  1193.8 223.4 %reduce-scatter.39.cloned.1.call-start = ((), (), s32[]{:S(2)}) async-start(), calls=%async_computation.34 | async-start | bytes 11796480 | tf_op jit(solution)/shard_map/reduce_scatter | solution.py:96
  1200.1 260.4 %all-gather.51.cloned.1.call-start = ((), (), s32[]{:S(2)}) async-start(), calls=%async_computation.49 | async-start | bytes 5898240 | tf_op jit(solution)/shard_map/all_gather | solution.py:89
  1422.9 77.3 %all-gather.53.cloned.1.call-start = ((), (), s32[]{:S(2)}) async-start(), calls=%async_computation.50 | async-start | bytes 5898240 | tf_op jit(solution)/shard_map/all_gather | solution.py:89
  1423.6 116.3 %all-gather.31.cloned.1.call-start = ((), (), s32[]{:S(2)}) async-start(), calls=%async_computation.27 | async-start | bytes 5898240 | tf_op jit(solution)/shard_map/all_gather | solution.py:89
  1424.3 155.3 %all-gather.37.cloned.1.call-start = ((), (), s32[]{:S(2)}) async-start(), calls=%async_computation.36 | async-start | bytes 5898240 | tf_op jit(solution)/shard_map/all_gather | solution.py:89
  1425.1 183.4 %reduce-scatter.55.cloned.1.call-start = ((), (), s32[]{:S(2)}) async-start(), calls=%async_computation.51 | async-start | bytes 2359296 | tf_op jit(solution)/shard_map/reduce_scatter | solution.py:106
  1465.9 74.0 %copy-start.36 = (bf16[2304,384]{1,0:T(8,128)(2,1)S(1)}, bf16[2304,384]{1,0:T(8,128)(2,1)}, u32[]{:S(2)}) copy-start(bf16[2304,384]{1,0:T(8,128)(2,1)} %param.38) | copy-start | bytes 5308420
  1506.7 130.8 %reduce-scatter.31.cloned.1.call-start = ((), (), s32[]{:S(2)}) async-start(), calls=%async_computation.28 | async-start | bytes 2359296 | tf_op jit(solution)/shard_map/reduce_scatter | solution.py:106
  1545.4 121.0 %reduce-scatter.43.cloned.1.call-start = ((), (), s32[]{:S(2)}) async-start(), calls=%async_computation.37 | async-start | bytes 2359296 | tf_op jit(solution)/shard_map/reduce_scatter | solution.py:106
  1585.1 81.3 %copy-start.60 = (f32[2,1024,192]{1,2,0:T(8,128)S(1)}, f32[2,1024,192]{1,2,0:T(8,128)}, u32[]{:S(2)}) copy-start(f32[2,1024,192]{1,2,0:T(8,128)} %param.25) | copy-start | bytes 4718596
  1585.1 164.0 %reduce-scatter.57.cloned.1.call-start = ((), (), s32[]{:S(2)}) async-start(), calls=%async_computation.52 | async-start | bytes 5242880 | tf_op jit(solution)/shard_map/reduce_scatter | solution.py:102
  1685.3 139.7 %reduce-scatter.49.cloned.1.call-start = ((), (), s32[]{:S(2)}) async-start(), calls=%async_computation.42 | async-start | bytes 5242880 | tf_op jit(solution)/shard_map/reduce_scatter | solution.py:102
  1700.2 273.2 %all-gather.55.cloned.1.call-start = ((), (), s32[]{:S(2)}) async-start(), calls=%async_computation.53 | async-start | bytes 2621440 | tf_op jit(solution)/shard_map/all_gather | solution.py:279
  1951.8 46.4 %all-gather.43.cloned.1.call-start = ((), (), s32[]{:S(2)}) async-start(), calls=%async_computation.43 | async-start | bytes 2621440 | tf_op jit(solution)/shard_map/all_gather | solution.py:279
  1952.4 70.8 %all-gather.57.cloned.1.call-start = ((), (), s32[]{:S(2)}) async-start(), calls=%async_computation.54 | async-start | bytes 2621440 | tf_op jit(solution)/shard_map/all_gather | solution.py:276
  1953.1 95.1 %all-gather.45.cloned.1.call-start = ((), (), s32[]{:S(2)}) async-start(), calls=%async_computation.44 | async-start | bytes 2621440 | tf_op jit(solution)/shard_map/all_gather | solution.py:276
  1953.9 135.2 %all-gather.49.cloned.1.call-start = ((), (), s32[]{:S(2)}) async-start(), calls=%async_computation.46 | async-start | bytes 2621440 | tf_op jit(solution)/shard_map/all_gather | solution.py:89
  1954.5 143.6 %all-gather.47.cloned.1.call-start = ((), (), s32[]{:S(2)}) async-start(), calls=%async_computation.45 | async-start | bytes 2621440 | tf_op jit(solution)/shard_map/all_gather | solution.py:89
  2068.0 5.5 collective-permute-start.2
  2074.4 52.5 %all-gather.61.cloned.1.call-start = ((), (), s32[]{:S(2)}) async-start(), calls=%async_computation.56 | async-start | bytes 2621440 | tf_op jit(solution)/shard_map/all_gather | solution.py:89
  2075.2 72.2 %all-gather.59.cloned.1.call-start = ((), (), s32[]{:S(2)}) async-start(), calls=%async_computation.55 | async-start | bytes 2621440 | tf_op jit(solution)/shard_map/all_gather | solution.py:89
  2076.1 5.5 collective-permute-start.3
  2082.5 98.2 %reduce-scatter.51.cloned.1.call-start = ((), (), s32[]{:S(2)}) async-start(), calls=%async_computation.47 | async-start | bytes 2359296 | tf_op jit(solution)/shard_map/reduce_scatter | solution.py:106
  2102.3 102.8 %reduce-scatter.59.cloned.1.call-start = ((), (), s32[]{:S(2)}) async-start(), calls=%async_computation.57 | async-start | bytes 2359296 | tf_op jit(solution)/shard_map/reduce_scatter | solution.py:106
  2151.6 624.4 %all-reduce.190.cloned.1.call-start = ((), (), s32[]{:S(2)}) async-start(), calls=%async_computation.58 | async-start | bytes 32768000 | tf_op jit(solution)/shard_map/psum | solution.py:112
  2180.6 51.3 %copy-start.155 = (f32[1024]{0:T(1024)S(1)}, f32[1024]{0:T(1024)}, u32[]{:S(2)}) copy-start(f32[1024]{0:T(1024)} %copy-done.154) | copy-start | bytes 12292
  2180.6 51.3 %copy-start.157 = (f32[1024]{0:T(1024)S(1)}, f32[1024]{0:T(1024)}, u32[]{:S(2)}) copy-start(f32[1024]{0:T(1024)} %copy-done.156) | copy-start | bytes 12292
  2180.7 51.2 %copy-start.67 = (f32[1024,192]{0,1:T(8,128)S(1)}, f32[1024,192]{0,1:T(8,128)}, u32[]{:S(2)}) copy-start(f32[1024,192]{0,1:T(8,128)} %reduce-scatter.51.cloned.1.call-done) | copy-start | bytes 2359300
  (174 other events, 1750.1 us)
Sparse Core Ops, SparseCore 0:
  40.0 45.2 reduce-scatter.32
  88.1 44.4 reduce-scatter.20
  134.7 34.4 all-gather.32
  171.2 34.4 all-gather.26
  208.1 44.5 reduce-scatter.34
  255.2 44.5 reduce-scatter.22
  641.4 23.9 all-gather.34
  724.2 22.0 all-gather.28
  749.1 33.5 reduce-scatter.36
  785.4 26.0 reduce-scatter.24
  814.2 78.4 reduce-scatter.44
  895.1 78.3 reduce-scatter.28
  976.1 78.3 reduce-scatter.26
  1060.3 37.4 all-gather.38
  1099.8 37.4 all-gather.40
  1143.4 30.3 reduce-scatter.46
  1176.4 78.4 reduce-scatter.52
  1257.5 78.4 reduce-scatter.40
  1338.7 78.4 reduce-scatter.38
  1423.0 37.4 all-gather.50
  1462.7 37.4 all-gather.52
  1502.4 37.4 all-gather.30
  1542.1 37.4 all-gather.36
  1582.4 26.0 reduce-scatter.54
  1611.3 26.1 reduce-scatter.30
  1640.3 26.1 reduce-scatter.42
  1685.4 44.5 reduce-scatter.56
  1732.7 44.5 reduce-scatter.48
  1951.9 21.4 all-gather.54
  1975.4 22.8 all-gather.42
  2000.4 22.8 all-gather.56
  2025.4 22.8 all-gather.44
  2050.2 22.8 all-gather.48
  2075.2 22.8 all-gather.46
  2099.7 22.8 all-gather.60
  2124.5 22.8 all-gather.58
  2150.1 26.0 reduce-scatter.50
  2179.1 26.0 reduce-scatter.58
  2210.7 565.3 all-reduce.189
where the time goes:
time: 2820 us; the launch traced here: 2800 us
  waiting for transfers between devices  1520 us (54%)
  local copies, waits for them, and re-layouts  543 us (19%)
  other arithmetic  246 us (9%)
  blocking collectives  241 us (9%)
  matrix products  220 us (8%)
    psum x1, waiting for transfers between devices, over_seq(): lax.psum(grads[1].astype(jnp.bfloat16), 'seq').astype(jnp.float32)  539 us
    all_gather x12, waiting for transfers between devices, gather_col(): lax.all_gather(as_sent(source), 'col', axis=1, tiled=True)  248 us
    reduce_scatter x4, waiting for transfers between devices, scatter_col(): lax.psum_scatter(source[0], 'col', scatter_dimension=1, tiled=True)  229 us
    slice x136, local copies, waits for them, and re-layouts, local(): lax.associative_scan(compose, (decays, drives), axis=0)  200 us
    reduce_scatter x4, waiting for transfers between devices, scatter_col(): lax.psum_scatter(source[1], 'col', scatter_dimension=1, tiled=True)  162 us
    reduce_scatter x8, waiting for transfers between devices, scatter_row(): return lax.psum_scatter(source, 'row', scatter_dimension=1, tiled=True)  131 us
    pad x72, local copies, waits for them, and re-layouts, local(): lax.associative_scan(compose, (decays, drives), axis=0)  110 us
    all_gather x8, blocking collectives, gather_row(): return lax.all_gather(source, 'row', axis=1, tiled=True)  101 us
  transfers between devices with their start and end apart: 43, of which 35 were waited for; matrix products, arithmetic and copies ran while one was open for 31% of the time, Pallas kernels for 0%

commit v1 on v0

--- a/solution.py
+++ b/solution.py
@@ -1,6 +1,10 @@
+import functools
+
 import jax
 import jax.numpy as jnp
 from jax import lax
+from jax.experimental import pallas as pl
+from jax.experimental.pallas import tpu as pltpu
 from jax.sharding import PartitionSpec as P
 
 D = 1536
@@ -318,6 +322,874 @@
     return (jnp.stack(outputs), jnp.stack(grads_in)) + tuple(totals)
 
 
+BF = jnp.bfloat16
+F32 = jnp.float32
+VMEM_LIMIT = 56 * 1024 * 1024
+ROW_BLOCK = 256
+GELU_A = 0.7978845608028654
+GELU_B = 0.044715
+
+
+def flip_row(a):
+    return lax.ppermute(a, "row", [(0, 1), (1, 0)])
+
+
+def flip_y(a):
+    return lax.ppermute(a, "col", [(i, i ^ 2) for i in range(4)])
+
+
+def flip_core(a):
+    return lax.ppermute(a, "col", [(i, i ^ 1) for i in range(4)])
+
+
+def shifted(a, distance):
+    return passed_along(a, "seq", distance)
+
+
+def cost(flops, moved, trans=0):
+    return pl.CostEstimate(flops=int(flops), bytes_accessed=int(moved), transcendentals=int(trans))
+
+
+def params():
+    return pltpu.CompilerParams(vmem_limit_bytes=VMEM_LIMIT, dimension_semantics=("arbitrary",))
+
+
+def nbytes(*arrays):
+    return sum(a.size * a.dtype.itemsize for a in arrays)
+
+
+def spread(halves):
+    first, second = halves
+    ax, ay = flip_row(first), flip_y(first)
+    bx, by = flip_row(second), flip_y(second)
+    return ((first, ax, ay, flip_y(ax)), (second, bx, by, flip_row(by)))
+
+
+def collect(halves):
+    (a0, a1, a2, a3), (b0, b1, b2, b3) = halves
+    a2 = (a2.astype(F32) + flip_row(a3).astype(F32)).astype(BF)
+    b1 = (b1.astype(F32) + flip_y(b3).astype(F32)).astype(BF)
+    return (
+        a0 + flip_row(a1).astype(F32) + flip_y(a2).astype(F32),
+        b0 + flip_row(b1).astype(F32) + flip_y(b2).astype(F32),
+    )
+
+
+def gelu_pair(v):
+    t = jnp.tanh(GELU_A * (v + GELU_B * v * v * v))
+    value = 0.5 * v * (1.0 + t)
+    slope = 0.5 * (1.0 + t) + 0.5 * v * (1.0 - t * t) * GELU_A * (1.0 + 3.0 * GELU_B * v * v)
+    return value, slope
+
+
+def minus_expm1(x):
+    series = 1.0 + x * (1.0 / 7.0)
+    for n in (6, 5, 4, 3, 2):
+        series = 1.0 + x * (1.0 / n) * series
+    return jnp.where(x > -0.3, -x * series, 1.0 - jnp.exp(x))
+
+
+def pair_up(left, right):
+    width = left.shape[1]
+    lane = lax.broadcasted_iota(jnp.int32, left.shape, 1)
+    low = lane < width // 2
+    return (
+        jnp.where(low, left, pltpu.roll(right, width // 2, 1)),
+        jnp.where(low, pltpu.roll(left, width // 2, 1), right),
+    )
+
+
+def dot_nn(a, b, precision=None):
+    return lax.dot_general(
+        a, b, (((1,), (0,)), ((), ())), precision=precision, preferred_element_type=F32
+    )
+
+
+def dot_nt(a, b, precision=None):
+    return lax.dot_general(
+        a, b, (((1,), (1,)), ((), ())), precision=precision, preferred_element_type=F32
+    )
+
+
+def dot_tn(a, b, precision=None):
+    return lax.dot_general(
+        a, b, (((0,), (0,)), ((), ())), precision=precision, preferred_element_type=F32
+    )
+
+
+def rows_spec(block, width, start=0):
+    return pl.BlockSpec((block, width), lambda i: (i + start, 0))
+
+
+def whole_spec(shape):
+    rank = len(shape)
+    return pl.BlockSpec(shape, lambda i: (0,) * rank, pipeline_mode=pl.Buffered(1))
+
+
+def head_spec(rows, width=128):
+    return pl.BlockSpec((rows, width), lambda h: (0, h))
+
+
+def sds(shape, dtype):
+    return jax.ShapeDtypeStruct(shape, dtype)
+
+
+def norm_uv_body(x0, x1, x2, x3, gain, w, keep, pass_on, u, v, scale):
+    parts = [r[...].astype(F32) for r in (x0, x1, x2, x3)]
+    width = parts[0].shape[1]
+    total = sum(jnp.sum(p * p, axis=1, keepdims=True) for p in parts)
+    s = lax.rsqrt(total / D + EPSILON)
+    scale[...] = s
+    normed = [p * s * gain[0:1, j * width : (j + 1) * width] for j, p in enumerate(parts)]
+    acc = None
+    for j, n in enumerate(normed):
+        term = dot_nn(n.astype(BF), w[j * width : (j + 1) * width, :])
+        acc = term if acc is None else acc + term
+    channels = u.shape[1]
+    u[...] = acc[:, :channels]
+    v[...] = acc[:, channels:]
+    for j in (0, 1):
+        k, p = pair_up(normed[2 * j], normed[2 * j + 1])
+        keep[:, j * width : (j + 1) * width] = k.astype(BF)
+        pass_on[:, j * width : (j + 1) * width] = p.astype(BF)
+
+
+def norm_uv(chunks, gain, w):
+    rows, width = chunks[0].shape
+    channels = w.shape[1] // 2
+    block = ROW_BLOCK
+    return pl.pallas_call(
+        norm_uv_body,
+        grid=(rows // block,),
+        in_specs=[rows_spec(block, width)] * 4 + [whole_spec(gain.shape), whole_spec(w.shape)],
+        out_specs=[rows_spec(block, 2 * width)] * 2
+        + [rows_spec(block, channels)] * 2
+        + [rows_spec(block, 1)],
+        out_shape=[sds((rows, 2 * width), BF)] * 2
+        + [sds((rows, channels), F32)] * 2
+        + [sds((rows, 1), F32)],
+        compiler_params=params(),
+        cost_estimate=cost(2 * rows * w.size, nbytes(w, *chunks) * 2),
+        name="norm_uv",
+    )(*chunks, gain, w)
+
+
+def chain(entries, count):
+    state = entries[(count - 1) * 8 + 1 : (count - 1) * 8 + 2, :]
+    for n in range(count - 2, -1, -1):
+        state = entries[n * 8 + 1 : n * 8 + 2, :] + entries[n * 8 : n * 8 + 1, :] * state
+    return state
+
+
+def recur_body(
+    ua, ub, border, off, taps, recall_w, admit_w, soft, conv, recall, admit, state, cum, ends, ext
+):
+    half = ua.shape[0]
+    rows = 2 * half
+    ext[0:8, :] = border[...]
+    ext[8 : 8 + half, :] = ua[...]
+    ext[8 + half : 8 + rows, :] = ub[...]
+    step = ROW_BLOCK
+    for r in range(0, rows, step):
+        o = off[8 + r : 8 + r + step, :]
+        total = taps[0:1, :] * ext[8 + r : 8 + r + step, :]
+        for k in range(1, KW):
+            term = taps[k : k + 1, :] * ext[8 + r - k : 8 + r - k + step, :]
+            total = total + jnp.where(o >= k, term, 0.0)
+        conv[r : r + step, :] = total
+        rec = jax.nn.sigmoid(dot_nn(total, recall_w[0], PRECISE))
+        adm = jax.nn.sigmoid(dot_nn(total, admit_w[0], PRECISE))
+        recall[r : r + step, :] = rec
+        admit[r : r + step, :] = adm
+        ell = -8.0 * rec * soft[0:1, :]
+        cum[r : r + step, :] = jnp.where(o > 0, jnp.exp(ell), 0.0)
+        state[r : r + step, :] = jnp.sqrt(minus_expm1(2.0 * ell)) * adm * total
+    seg = rows // 8
+
+    def one(i, carry):
+        h, p = carry
+        at = pl.ds(i, 8, stride=seg)
+        d = cum[at, :]
+        h = d * h + state[at, :]
+        p = d * p
+        state[at, :] = h
+        cum[at, :] = p
+        return h, p
+
+    zero = jnp.zeros((8, 128), F32)
+    h, p = lax.fori_loop(0, seg, one, (zero, zero + 1.0), unroll=8)
+    carry_h, carry_p = h[0:1, :], p[0:1, :]
+    for s in range(1, 8):
+        at = slice(s * seg, (s + 1) * seg)
+        c = cum[at, :]
+        state[at, :] = state[at, :] + c * carry_h
+        cum[at, :] = c * carry_p
+        carry_h = h[s : s + 1, :] + p[s : s + 1, :] * carry_h
+        carry_p = p[s : s + 1, :] * carry_p
+    ends[0:1, :] = carry_p
+    ends[1:2, :] = carry_h
+    ends[2:8, :] = jnp.zeros((6, 128), F32)
+
+
+def recur(ua, ub, border, off, taps, recall_w, admit_w, soft):
+    half, channels = ua.shape
+    rows = 2 * half
+    heads = channels // 128
+    gate = pl.BlockSpec((1, 128, 128), lambda h: (h, 0, 0))
+    full = sds((rows, channels), F32)
+    return pl.pallas_call(
+        recur_body,
+        grid=(heads,),
+        in_specs=[
+            head_spec(half),
+            head_spec(half),
+            head_spec(8),
+            whole_spec(off.shape),
+            head_spec(KW),
+            gate,
+            gate,
+            head_spec(1),
+        ],
+        out_specs=[head_spec(rows)] * 5 + [head_spec(8)],
+        out_shape=[full] * 5 + [sds((8, channels), F32)],
+        scratch_shapes=[pltpu.VMEM((rows + 8, 128), F32)],
+        compiler_params=params(),
+        cost_estimate=cost(rows * channels * 128 * 24, rows * channels * 4 * 6, rows * channels * 6),
+        name="recur",
+    )(ua, ub, border, off, taps, recall_w, admit_w, soft)
+
+
+def mix_body(count, local, cum, v, entries, w, states, mixed, q0, q1, q2, q3):
+    entering = chain(entries, count)
+    st = local[...] + cum[...] * entering
+    states[...] = st
+    act = gelu_pair(v[...])[0]
+    m = (st * act).astype(BF)
+    mixed[...] = m
+    width = q0.shape[1]
+    for j, q in enumerate((q0, q1, q2, q3)):
+        q[...] = dot_nn(m, w[:, j * width : (j + 1) * width]).astype(q.dtype)
+
+
+def mix(half_index, local, cum, v, entries, w):
+    rows, channels = v.shape
+    width = w.shape[1] // 4
+    block = ROW_BLOCK
+    start = half_index * (rows // block)
+    return pl.pallas_call(
+        functools.partial(mix_body, entries.shape[0] // 8),
+        grid=(rows // block,),
+        in_specs=[rows_spec(block, channels, start)] * 2
+        + [rows_spec(block, channels), whole_spec(entries.shape), whole_spec(w.shape)],
+        out_specs=[rows_spec(block, channels)] * 2 + [rows_spec(block, width)] * 4,
+        out_shape=[sds((rows, channels), F32), sds((rows, channels), BF), sds((rows, width), F32)]
+        + [sds((rows, width), BF)] * 3,
+        compiler_params=params(),
+        cost_estimate=cost(2 * rows * w.size, rows * channels * 18 + nbytes(w)),
+        name="mix",
+    )(local, cum, v, entries, w)
+
+
+def feed_body(*refs):
+    (x0, x1, x2, x3, e0, e1, e2, e3, gain, wgu, wd) = refs[:11]
+    (keep, pass_on, hid, eg, eu, ekeep, epass, scale, dots) = refs[11:20]
+    outs, backs = refs[20:24], refs[24:28]
+    parts = [r[...].astype(F32) for r in (x0, x1, x2, x3)]
+    width = parts[0].shape[1]
+    total = sum(jnp.sum(p * p, axis=1, keepdims=True) for p in parts)
+    s = lax.rsqrt(total / D + EPSILON)
+    scale[...] = s
+    normed = [p * s * gain[1:2, j * width : (j + 1) * width] for j, p in enumerate(parts)]
+    acc = None
+    for j, n in enumerate(normed):
+        term = dot_nn(n.astype(BF), wgu[j * width : (j + 1) * width, :])
+        acc = term if acc is None else acc + term
+    for j in (0, 1):
+        k, p = pair_up(normed[2 * j], normed[2 * j + 1])
+        keep[:, j * width : (j + 1) * width] = k.astype(BF)
+        pass_on[:, j * width : (j + 1) * width] = p.astype(BF)
+    errs = [r[...] for r in (e0, e1, e2, e3)]
+    wide = [e.astype(F32) for e in errs]
+    for j in (0, 1):
+        k, p = pair_up(wide[2 * j], wide[2 * j + 1])
+        ekeep[:, j * width : (j + 1) * width] = k.astype(BF)
+        epass[:, j * width : (j + 1) * width] = p.astype(BF)
+    units = hid.shape[1]
+    pre, up = acc[:, :units], acc[:, units:]
+    act, slope = gelu_pair(pre)
+    h = (act * up).astype(BF)
+    hid[...] = h
+    dh = None
+    for j, e in enumerate(errs):
+        term = dot_nt(e, wd[:, j * width : (j + 1) * width])
+        dh = term if dh is None else dh + term
+    g = (dh * up * slope).astype(BF)
+    b = (dh * act).astype(BF)
+    eg[...] = g
+    eu[...] = b
+    dots[...] = jnp.sum(g.astype(F32) * pre + b.astype(F32) * up, axis=1, keepdims=True)
+    for j, q in enumerate(backs):
+        q[...] = (
+            dot_nt(g, wgu[j * width : (j + 1) * width, :units])
+            + dot_nt(b, wgu[j * width : (j + 1) * width, units:])
+        ).astype(q.dtype)
+    for j, q in enumerate(outs):
+        q[...] = dot_nn(h, wd[:, j * width : (j + 1) * width]).astype(q.dtype)
+
+
+def feed(chunks, errs, gain, wgu, wd):
+    rows, width = chunks[0].shape
+    units = wd.shape[0]
+    block = ROW_BLOCK
+    quarters = [sds((rows, width), F32)] + [sds((rows, width), BF)] * 3
+    return pl.pallas_call(
+        feed_body,
+        grid=(rows // block,),
+        in_specs=[rows_spec(block, width)] * 8
+        + [whole_spec(gain.shape), whole_spec(wgu.shape), whole_spec(wd.shape)],
+        out_specs=[rows_spec(block, 2 * width)] * 2
+        + [rows_spec(block, units)] * 3
+        + [rows_spec(block, 2 * width)] * 2
+        + [rows_spec(block, 1)] * 2
+        + [rows_spec(block, width)] * 8,
+        out_shape=[sds((rows, 2 * width), BF)] * 2
+        + [sds((rows, units), BF)] * 3
+        + [sds((rows, 2 * width), BF)] * 2
+        + [sds((rows, 1), F32)] * 2
+        + quarters
+        + quarters,
+        compiler_params=params(),
+        cost_estimate=cost(
+            4 * rows * (wgu.size + wd.size), nbytes(wgu, wd) + rows * 30000, rows * units
+        ),
+        name="feed",
+    )(*chunks, *errs, gain, wgu, wd)
+
+
+def adjoint_body(*refs):
+    ea, eb = refs[0:4], refs[4:8]
+    (w, sa, sb, va, vb, recall, off, soft) = refs[8:16]
+    (part, reach, eva, evb, ends, keep, pass_on, ext) = refs[16:]
+    half = sa.shape[0]
+    rows = 2 * half
+    width = ea[0].shape[1]
+    step = ROW_BLOCK
+
+    @pl.when(pl.program_id(0) == 0)
+    def _():
+        for group, base in ((ea, 0), (eb, half)):
+            for j in (0, 1):
+                k, p = pair_up(group[2 * j][...].astype(F32), group[2 * j + 1][...].astype(F32))
+                at = (slice(base, base + half), slice(j * width, (j + 1) * width))
+                keep[at] = k.astype(BF)
+                pass_on[at] = p.astype(BF)
+
+    for r in range(0, rows, step):
+        o = off[8 + r : 8 + r + step, :]
+        ell = -8.0 * recall[r : r + step, :] * soft[0:1, :]
+        ext[r : r + step, :] = jnp.where(o > 0, jnp.exp(ell), 0.0)
+        group, states, branch, ev, base = (
+            (ea, sa, va, eva, r) if r < half else (eb, sb, vb, evb, r - half)
+        )
+        at = slice(base, base + step)
+        dm = None
+        for j in range(4):
+            term = dot_nt(group[j][at, :], w[:, j * width : (j + 1) * width])
+            dm = term if dm is None else dm + term
+        act, slope = gelu_pair(branch[at, :])
+        ev[at, :] = (dm * states[at, :] * slope).astype(BF)
+        part[r : r + step, :] = dm * act
+    ext[rows : rows + 8, :] = jnp.ones((8, 128), F32)
+    for r in range(0, rows, step):
+        reach[r : r + step, :] = ext[r + 1 : r + 1 + step, :]
+    seg = rows // 8
+
+    def one(n, carry):
+        h, p = carry
+        at = pl.ds(seg - 1 - n, 8, stride=seg)
+        d = reach[at, :]
+        h = d * h + part[at, :]
+        p = d * p
+        part[at, :] = h
+        reach[at, :] = p
+        return h, p
+
+    zero = jnp.zeros((8, 128), F32)
+    h, p = lax.fori_loop(0, seg, one, (zero, zero + 1.0), unroll=8)
+    carry_h, carry_p = h[7:8, :], p[7:8, :]
+    for s in range(6, -1, -1):
+        at = slice(s * seg, (s + 1) * seg)
+        c = reach[at, :]
+        part[at, :] = part[at, :] + c * carry_h
+        reach[at, :] = c * carry_p
+        carry_h = h[s : s + 1, :] + p[s : s + 1, :] * carry_h
+        carry_p = p[s : s + 1, :] * carry_p
+    first = ext[0:1, :]
+    ends[0:1, :] = first * carry_p
+    ends[1:2, :] = first * carry_h
+    ends[2:8, :] = jnp.zeros((6, 128), F32)
+
+
+def adjoint(errs, w, states, branch, recall, off, soft):
+    half, channels = states[0].shape
+    rows = 2 * half
+    width = errs[0][0].shape[1]
+    return pl.pallas_call(
+        adjoint_body,
+        grid=(channels // 128,),
+        in_specs=[whole_spec((half, width))] * 8
+        + [pl.BlockSpec((128, w.shape[1]), lambda h: (h, 0))]
+        + [head_spec(half)] * 4
+        + [head_spec(rows), whole_spec(off.shape), head_spec(1)],
+        out_specs=[head_spec(rows)] * 2
+        + [head_spec(half)] * 2
+        + [head_spec(8)]
+        + [whole_spec((rows, 2 * width))] * 2,
+        out_shape=[sds((rows, channels), F32)] * 2
+        + [sds((half, channels), BF)] * 2
+        + [sds((8, channels), F32)]
+        + [sds((rows, 2 * width), BF)] * 2,
+        scratch_shapes=[pltpu.VMEM((rows + 8, 128), F32)],
+        compiler_params=params(),
+        cost_estimate=cost(2 * rows * w.size, rows * channels * 20 + rows * D * 6, rows * channels * 3),
+        name="adjoint",
+    )(*errs[0], *errs[1], w, *states, *branch, recall, off, soft)
+
+
+def recur_back_body(count, *refs):
+    (part, reach, later, earlier, sa, sb, conv, recall, admit, off) = refs[:10]
+    (ua, ub, border, taps, recall_w, admit_w, soft) = refs[10:17]
+    (du, out_border, grad_recall, grad_admit, grad_small, st, uext, dc) = refs[17:]
+    half = sa.shape[0]
+    rows = 2 * half
+    step = ROW_BLOCK
+    st[0:8, :] = jnp.broadcast_to(chain(earlier, count), (8, 128))
+    st[8 : 8 + half, :] = sa[...]
+    st[8 + half : 8 + rows, :] = sb[...]
+    uext[0:8, :] = border[...]
+    uext[8 : 8 + half, :] = ua[...]
+    uext[8 + half : 8 + rows, :] = ub[...]
+    incoming = chain(later, count)
+    sp = soft[0:1, :]
+    dc[0:8, :] = jnp.zeros((8, 128), F32)
+    dc[8 + rows : 16 + rows, :] = jnp.zeros((8, 128), F32)
+    gr = ga = None
+    sums = [None] * (KW + 1)
+
+    def plus(total, term):
+        return term if total is None else total + term
+
+    for r in range(0, rows, step):
+        at = slice(r, r + step)
+        o = off[8 + r : 8 + r + step, :]
+        adj = part[at, :] + reach[at, :] * incoming
+        rec, adm, cv = recall[at, :], admit[at, :], conv[at, :]
+        ell = -8.0 * rec * sp
+        e = jnp.exp(ell)
+        m = jnp.sqrt(minus_expm1(2.0 * ell))
+        previous = jnp.where(o > 0, e * st[7 + r : 7 + r + step, :], 0.0)
+        ac = adj * cv
+        d_ell = adj * previous - ac * adm * (e * e) / m
+        d_rp = -8.0 * sp * d_ell * rec * (1.0 - rec)
+        d_ip = ac * m * adm * (1.0 - adm)
+        d_conv = (
+            adj * m * adm + dot_nt(d_rp, recall_w[0], PRECISE) + dot_nt(d_ip, admit_w[0], PRECISE)
+        )
+        dc[8 + r : 8 + r + step, :] = d_conv
+        gr = plus(gr, dot_tn(cv, d_rp, PRECISE))
+        ga = plus(ga, dot_tn(cv, d_ip, PRECISE))
+        for k in range(KW):
+            term = d_conv * uext[8 + r - k : 8 + r - k + step, :]
+            if k:
+                term = jnp.where(o >= k, term, 0.0)
+            sums[k] = plus(sums[k], jnp.sum(term, axis=0, keepdims=True))
+        sums[KW] = plus(sums[KW], jnp.sum(rec * d_ell, axis=0, keepdims=True))
+    grad_recall[0] = gr
+    grad_admit[0] = ga
+    for k in range(KW + 1):
+        grad_small[k : k + 1, :] = sums[k]
+    grad_small[KW + 1 : 8, :] = jnp.zeros((7 - KW, 128), F32)
+    for r in range(0, rows, step):
+        total = taps[0:1, :] * dc[8 + r : 8 + r + step, :]
+        for k in range(1, KW):
+            o = off[8 + r + k : 8 + r + k + step, :]
+            term = taps[k : k + 1, :] * dc[8 + r + k : 8 + r + k + step, :]
+            total = total + jnp.where(o >= k, term, 0.0)
+        du[r : r + step, :] = total
+    total = jnp.zeros((8, 128), F32)
+    for k in range(1, KW):
+        term = taps[k : k + 1, :] * dc[k : k + 8, :]
+        total = total + jnp.where(off[k : k + 8, :] >= k, term, 0.0)
+    out_border[...] = total
+
+
+def recur_back(part, reach, later, earlier, states, conv, recall, admit, off, u, border, taps, rw, aw, soft):
+    rows, channels = part.shape
+    half = rows // 2
+    heads = channels // 128
+    gate = pl.BlockSpec((1, 128, 128), lambda h: (h, 0, 0))
+    return pl.pallas_call(
+        functools.partial(recur_back_body, later.shape[0] // 8),
+        grid=(heads,),
+        in_specs=[
+            head_spec(rows),
+            head_spec(rows),
+            head_spec(later.shape[0]),
+            head_spec(earlier.shape[0]),
+            head_spec(half),
+            head_spec(half),
+            head_spec(rows),
+            head_spec(rows),
+            head_spec(rows),
+            whole_spec(off.shape),
+            head_spec(half),
+            head_spec(half),
+            head_spec(8),
+            head_spec(KW),
+            gate,
+            gate,
+            head_spec(1),
+        ],
+        out_specs=[head_spec(rows), head_spec(8), gate, gate, head_spec(8)],
+        out_shape=[
+            sds((rows, channels), F32),
+            sds((8, channels), F32),
+            sds((heads, 128, 128), F32),
+            sds((heads, 128, 128), F32),
+            sds((8, channels), F32),
+        ],
+        scratch_shapes=[
+            pltpu.VMEM((rows + 8, 128), F32),
+            pltpu.VMEM((rows + 8, 128), F32),
+            pltpu.VMEM((rows + 16, 128), F32),
+        ],
+        compiler_params=params(),
+        cost_estimate=cost(rows * channels * 128 * 48, rows * channels * 36, rows * channels * 4),
+        name="recur_back",
+    )(part, reach, later, earlier, *states, conv, recall, admit, off, *u, border, taps, rw, aw, soft)
+
+
+def enter_back_body(last, du, tail, ev, u, v, w, eu, dots, q0, q1, q2, q3):
+    d = du[...]
+    if last:
+        rows = d.shape[0]
+        extra = jnp.concatenate([jnp.zeros((rows - 8, d.shape[1]), F32), tail[...]], axis=0)
+        at_end = pl.program_id(0) == pl.num_programs(0) - 1
+        d = d + jnp.where(at_end, extra, 0.0)
+    e = d.astype(BF)
+    eu[...] = e
+    b = ev[...]
+    dots[...] = jnp.sum(e.astype(F32) * u[...] + b.astype(F32) * v[...], axis=1, keepdims=True)
+    channels = e.shape[1]
+    width = q0.shape[1]
+    for j, q in enumerate((q0, q1, q2, q3)):
+        q[...] = (
+            dot_nt(e, w[j * width : (j + 1) * width, :channels])
+            + dot_nt(b, w[j * width : (j + 1) * width, channels:])
+        ).astype(q.dtype)
+
+
+def enter_back(half_index, du, tail, ev, u, v, w):
+    rows, channels = u.shape
+    width = w.shape[0] // 4
+    block = ROW_BLOCK
+    start = half_index * (rows // block)
+    return pl.pallas_call(
+        functools.partial(enter_back_body, half_index == 1),
+        grid=(rows // block,),
+        in_specs=[rows_spec(block, channels, start), whole_spec(tail.shape)]
+        + [rows_spec(block, channels)] * 3
+        + [whole_spec(w.shape)],
+        out_specs=[rows_spec(block, channels), rows_spec(block, 1)] + [rows_spec(block, width)] * 4,
+        out_shape=[sds((rows, channels), BF), sds((rows, 1), F32), sds((rows, width), F32)]
+        + [sds((rows, width), BF)] * 3,
+        compiler_params=params(),
+        cost_estimate=cost(2 * rows * w.size, rows * channels * 16 + nbytes(w)),
+        name="enter_back",
+    )(du, tail, ev, u, v, w)
+
+
+def outer_body(la, lb, ra, rb, out):
+    out[...] = (dot_tn(la[...], ra[...]) + dot_tn(lb[...], rb[...])).astype(out.dtype)
+
+
+def outer(left, right):
+    rows, m = left[0].shape
+    n = right[0].shape[1]
+    block = 256 if m % 256 == 0 else 128
+    lhs = pl.BlockSpec((rows, block), lambda i: (0, i))
+    return pl.pallas_call(
+        outer_body,
+        grid=(m // block,),
+        in_specs=[lhs, lhs, whole_spec((rows, n)), whole_spec((rows, n))],
+        out_specs=rows_spec(block, n),
+        out_shape=sds((m, n), BF),
+        compiler_params=params(),
+        cost_estimate=cost(4 * rows * m * n, rows * (m + n) * 4 + m * n * 2),
+        name="outer",
+    )(*left, *right)
+
+
+def add_low(a, b):
+    return (a.astype(F32) + b.astype(F32)).astype(BF)
+
+
+def total_seq(g):
+    count = lax.axis_size("seq")
+    if count != 4:
+        return lax.psum(g, "seq")
+    place = lax.axis_index("seq")
+    g = add_low(g, lax.ppermute(g, "seq", [(0, 1), (3, 2)]))
+    g = add_low(g, lax.ppermute(g, "seq", [(1, 2), (2, 1)]))
+    back = lax.ppermute(g, "seq", [(1, 0), (2, 3)])
+    return jnp.where((place == 0) | (place == 3), back, g)
+
+
+def local_fast(
+    stream_in,
+    cotangent,
+    doc_lengths,
+    mixer_gain,
+    input_weight,
+    branch_weight,
+    filter_taps,
+    recall_gate,
+    admit_gate,
+    decay_param,
+    output_weight,
+    feed_gain,
+    gate_weight,
+    up_weight,
+    down_weight,
+):
+    tokens = stream_in.shape[1]
+    half = tokens // 2
+    count = lax.axis_size("seq")
+    part = stream_in.shape[2]
+    seq = lax.axis_index("seq")
+    row = lax.axis_index("row")
+    col = lax.axis_index("col")
+    y, core = col // 2, col % 2
+    lower = row == 0
+
+    def own_and_other(a, pick, axis):
+        size = a.shape[axis] // 2
+        return (
+            lax.dynamic_slice_in_dim(a, pick * size, size, axis),
+            lax.dynamic_slice_in_dim(a, (1 - pick) * size, size, axis),
+        )
+
+    def by_core(a):
+        own, other = own_and_other(a, core, 0)
+        return jnp.concatenate([own[0], flip_core(other)[0]], axis=1)
+
+    def in_halves(a):
+        return (a[:half], a[half:])
+
+    gains = jnp.stack([mixer_gain, feed_gain])
+    gains = jnp.concatenate([gains, flip_core(gains)], axis=1)
+    gains_x = flip_row(gains)
+    gains_y = flip_y(gains)
+    gains_all = jnp.concatenate([gains, gains_x, gains_y, flip_y(gains_x)], axis=1)
+
+    x = by_core(stream_in)
+    g = by_core(cotangent)
+
+    def four_blocks(w, axis):
+        own, other = own_and_other(w, y, axis)
+        far = flip_y(other)
+        return ((own, flip_core(own)), (far, flip_core(far)))
+
+    def rows_in_order(ws):
+        blocks = [four_blocks(w, 1) for w in ws]
+        pieces = []
+        for dy in (0, 1):
+            for dx in (0, 1):
+                for dc in (0, 1):
+                    start = part * (row ^ dx)
+                    pieces.append(
+                        jnp.concatenate(
+                            [lax.dynamic_slice_in_dim(b[dy][dc], start, part, 0) for b in blocks], axis=1
+                        )
+                    )
+        return jnp.concatenate(pieces, axis=0)
+
+    def cols_in_order(w):
+        blocks = four_blocks(w, 0)
+        chunks = []
+        for dy in (0, 1):
+            near, far = blocks[dy]
+            first = jnp.concatenate([near[:, :part], far[:, :part]], axis=1)
+            second = jnp.concatenate([near[:, part:], far[:, part:]], axis=1)
+            chunks += [jnp.where(lower, first, second), jnp.where(lower, second, first)]
+        return jnp.concatenate(chunks, axis=1)
+
+    w_in = rows_in_order((input_weight, branch_weight))
+    w_out = cols_in_order(output_weight)
+    w_gu = rows_in_order((gate_weight, up_weight))
+    w_down = cols_in_order(down_weight)
+
+    heads = recall_gate.shape[0] // 2
+    rw = lax.dynamic_slice_in_dim(recall_gate, y * heads, heads, 0)
+    aw = lax.dynamic_slice_in_dim(admit_gate, y * heads, heads, 0)
+    small = jnp.concatenate([filter_taps, decay_param[None], jnp.zeros((3,) + decay_param.shape, F32)])
+    sibling = flip_core(small)
+    small = jnp.where(
+        core == 0,
+        jnp.concatenate([small, sibling], axis=1),
+        jnp.concatenate([sibling, small], axis=1),
+    )
+    taps, decay = small[:KW], small[KW : KW + 1]
+    soft = jax.nn.softplus(-decay)
+
+    lengths = lax.dynamic_index_in_dim(doc_lengths, core, 0, False)
+    offset = doc_offset(lengths, seq * tokens, tokens)
+    edge = jnp.full((8,), -1, jnp.int32)
+    off = jnp.concatenate([edge, offset, edge])[:, None]
+
+    def neighbours(ends, sign):
+        return jnp.concatenate([shifted(ends, sign * n) for n in range(1, count)], axis=0)
+
+    ca, cb = spread(in_halves(x.astype(BF)))
+    nka, nsa, ua, va, s1a = norm_uv(ca, gains_all, w_in)
+    nkb, nsb, ub, vb, s1b = norm_uv(cb, gains_all, w_in)
+    border = shifted(ub[half - 8 :], 1)
+    conv, recall, admit, local_state, cum, ends = recur(ua, ub, border, off, taps, rw, aw, soft)
+    earlier = neighbours(ends, 1)
+    sa, ma, *qa = mix(0, local_state, cum, va, earlier, w_out)
+    sb, mb, *qb = mix(1, local_state, cum, vb, earlier, w_out)
+    mid = [r + h for r, h in zip(collect((qa, qb)), in_halves(x))]
+    da, db = spread([m.astype(BF) for m in mid])
+    fa, fb = spread(in_halves(g.astype(BF)))
+    feed_a = feed(da, fa, gains_all, w_gu, w_down)
+    feed_b = feed(db, fb, gains_all, w_gu, w_down)
+    out_chunk = jnp.concatenate(
+        [r + m for r, m in zip(collect((feed_a[9:13], feed_b[9:13])), mid)], axis=0
+    )
+
+    def summed(dots):
+        d = jnp.concatenate([a[:, 0] for a in dots])
+        d = d + flip_row(d)
+        d = d + flip_y(d)
+        return in_halves(d)
+
+    def norm_back_local(dn, dots, scales, source, gain):
+        grads, gain_grad = [], 0.0
+        for d, t, s, x_half in zip(dn, dots, scales, source):
+            grads.append(s * gain * d - x_half * (s * s * t[:, None] / D))
+            gain_grad = gain_grad + jnp.sum(d * x_half * s, axis=0)
+        return grads, gain_grad
+
+    dots2 = summed((feed_a[8], feed_b[8]))
+    dn2 = collect((feed_a[13:17], feed_b[13:17]))
+    back2, grad_feed = norm_back_local(dn2, dots2, (feed_a[7], feed_b[7]), mid, gains[1:2])
+    dx2 = [b + h for b, h in zip(back2, in_halves(g))]
+    ra, rb = spread([d.astype(BF) for d in dx2])
+
+    part_adj, reach, eva, evb, back_ends, erk, ers = adjoint(
+        (ra, rb), w_out, (sa, sb), (va, vb), recall, off, soft
+    )
+    later = neighbours(back_ends, -1)
+    du, out_border, grad_recall, grad_admit, grad_small = recur_back(
+        part_adj, reach, later, earlier, (sa, sb), conv, recall, admit, off, (ua, ub), border, taps, rw, aw, soft
+    )
+    tail = shifted(out_border, -1)
+    eua, dots_a, *ba = enter_back(0, du, tail, eva, ua, va, w_in)
+    eub, dots_b, *bb = enter_back(1, du, tail, evb, ub, vb, w_in)
+    dots1 = summed((dots_a, dots_b))
+    dn1 = collect((ba, bb))
+    back1, grad_mixer = norm_back_local(dn1, dots1, (s1a, s1b), in_halves(x), gains[0:1])
+    grad_chunk = jnp.concatenate([b + d for b, d in zip(back1, dx2)], axis=0)
+
+    def reduced(keep, send, axis):
+        both = add_low(keep, flip_core(send))
+        n = both.shape[axis] // 2
+        mine = lax.slice_in_dim(both, 0, n, axis=axis)
+        theirs = flip_y(lax.slice_in_dim(both, n, 2 * n, axis=axis))
+        return total_seq(mine), total_seq(theirs)
+
+    def rows_out(keep, send):
+        mine, theirs = reduced(keep, send, 0)
+        wide = jnp.where(
+            y == 0, jnp.concatenate([mine, theirs], axis=1), jnp.concatenate([theirs, mine], axis=1)
+        )
+        swapped = jnp.concatenate([wide[part:], wide[:part]], axis=0)
+        return jnp.where(lower, wide, swapped).astype(F32)
+
+    def cols_out(keep, send):
+        mine, theirs = reduced(keep, send, 1)
+        tall = jnp.where(
+            y == 0, jnp.concatenate([mine, theirs], axis=0), jnp.concatenate([theirs, mine], axis=0)
+        )
+        swapped = jnp.concatenate([tall[:, part:], tall[:, :part]], axis=1)
+        return jnp.where(lower, tall, swapped).astype(F32)
+
+    n2k, n2s = (feed_a[0], feed_b[0]), (feed_a[1], feed_b[1])
+    hid = (feed_a[2], feed_b[2])
+    eg, eu2 = (feed_a[3], feed_b[3]), (feed_a[4], feed_b[4])
+    eok, eos = (feed_a[5], feed_b[5]), (feed_a[6], feed_b[6])
+    grad_down = cols_out(outer(hid, eok), outer(hid, eos))
+    grad_gate = rows_out(outer(n2k, eg), outer(n2s, eg))
+    grad_up = rows_out(outer(n2k, eu2), outer(n2s, eu2))
+    grad_output = cols_out(
+        outer((ma, mb), in_halves(erk)), outer((ma, mb), in_halves(ers))
+    )
+    grad_input = rows_out(outer((nka, nkb), (eua, eub)), outer((nsa, nsb), (eua, eub)))
+    grad_branch = rows_out(outer((nka, nkb), (eva, evb)), outer((nsa, nsb), (eva, evb)))
+
+    width = recall_gate.shape[2] * heads
+    gain_rows = jnp.concatenate(
+        [grad_mixer[:part], grad_feed[:part], grad_mixer[part:], grad_feed[part:]]
+    )
+    channels = taps.shape[1]
+    lane = 128
+    pieces = [
+        grad_small[:KW].reshape(-1),
+        (grad_small[KW] * 8.0 * jax.nn.sigmoid(-decay[0])),
+        grad_recall.reshape(-1),
+        grad_admit.reshape(-1),
+    ]
+    flat = jnp.concatenate(pieces)
+    flat = flat + flip_core(flat)
+    mine_gain = gain_rows[: 2 * part] + flip_core(gain_rows[2 * part :])
+    flat = jnp.concatenate([flat, mine_gain])
+    flat = lax.psum(flat, "seq")
+    sizes = [KW * channels, channels, grad_recall.size, grad_admit.size, part, part]
+    cuts, at = [], 0
+    for s in sizes:
+        cuts.append(flat[at : at + s])
+        at += s
+    own = channels // 2
+    g_taps = lax.dynamic_slice_in_dim(cuts[0].reshape(KW, channels), core * own, own, 1)
+    g_decay = lax.dynamic_slice_in_dim(cuts[1], core * own, own, 0)
+    gates = jnp.stack([cuts[2].reshape(grad_recall.shape), cuts[3].reshape(grad_admit.shape)])
+    far = flip_y(gates)
+    gates = jnp.where(
+        y == 0, jnp.concatenate([gates, far], axis=1), jnp.concatenate([far, gates], axis=1)
+    )
+
+    def stacked(chunk):
+        own, other = chunk[:, :part], flip_core(chunk[:, part:])
+        return jnp.where(core == 0, jnp.stack([own, other]), jnp.stack([other, own]))
+
+    return (
+        stacked(out_chunk),
+        stacked(grad_chunk),
+        cuts[4],
+        grad_input,
+        grad_branch,
+        g_taps,
+        gates[0],
+        gates[1],
+        g_decay,
+        grad_output,
+        cuts[5],
+        grad_gate,
+        grad_up,
+        grad_down,
+    )
+
+
 def solution(mesh):
     in_specs = (
         P(None, "seq", ("col", "row")),
@@ -352,4 +1224,5 @@
         P("col", "row"),
         P("row", "col"),
     )
-    return jax.shard_map(local, mesh=mesh, in_specs=in_specs, out_specs=out_specs, check_vma=False)
+    plan = local_fast if mesh.shape["row"] == 2 and mesh.shape["col"] == 4 else local
+    return jax.shard_map(plan, mesh=mesh, in_specs=in_specs, out_specs=out_specs, check_vma=False)

time: 2820 us -> 989 us (0.35)
  waiting for transfers between devices: 1520 us -> 384 us
  local copies, waits for them, and re-layouts: 543 us -> 98.3 us
  blocking collectives: 241 us -> 0 us
  matrix products: 220 us -> 0 us
  Pallas kernels: 0 us -> 203 us
  starting transfers between devices: 12.1 us -> 169 us
  other arithmetic: 246 us -> 106 us
    reduce_scatter x20 -> x0, waiting for transfers between devices: 618 us -> none  [the longest x4 229 us: scatter_col(): lax.psum_scatter(source[0], 'col', scatter_dimension=1, tiled=True)]
    psum x1, waiting for transfers between devices: 539 us -> 0.01 us  [local_fast(): flat = lax.psum(flat, 'seq')]
    ppermute x0 -> x130, waiting for transfers between devices: none -> 377 us  [the longest x12 134 us: total_seq(): back = lax.ppermute(g, 'seq', [(1, 0), (2, 3)])]
    all_gather x18 -> x0, waiting for transfers between devices: 345 us -> none  [the longest x12 248 us: gather_col(): lax.all_gather(as_sent(source), 'col', axis=1, tiled=True)]
    slice x288 -> x35, local copies, waits for them, and re-layouts: 296 us -> 30.4 us  [the longest x8 9.67 us: cols_in_order(): first = jnp.concatenate([near[:, :part], far[:, :part]], axis=1)]
    dot_general x48 -> x0, matrix products: 220 us -> none  [the longest x12 56.1 us: matmul_cols(): lax.dot_general(left, right, SUM_COLS, preferred_element_type=jnp.float32)]
    pallas_call x0 -> x23, Pallas kernels: none -> 203 us  [the longest x12 63.7 us: outer(): pl.pallas_call(outer_body, grid=(m // block,), in_specs=[lhs, lhs, whole_...]
    all_gather x16 -> x0, blocking collectives: 175 us -> none  [the longest x8 101 us: gather_row(): return lax.all_gather(source, 'row', axis=1, tiled=True)]
  transfers between devices with their start and end apart: 43 -> 139, of which waited for: 35 -> 43; matrix products, arithmetic and copies ran while one was open for 31% -> 19% of each run, Pallas kernels for 0% -> 18%
where the time goes in v1:
time: 989 us; the launch traced here: 977 us
  waiting for transfers between devices  384 us (39%)
  Pallas kernels  203 us (21%)
  starting transfers between devices  169 us (17%)
  other arithmetic  106 us (11%)
  local copies, waits for them, and re-layouts  98.3 us (10%)
  between operations  16.7 us (2%)
    ppermute x12, waiting for transfers between devices, total_seq(): back = lax.ppermute(g, 'seq', [(1, 0), (2, 3)])  134 us
    ppermute x41, waiting for transfers between devices, flip_y(): return lax.ppermute(a, 'col', [(i, i ^ 2) for i in range(4)])  118 us
    ppermute x12, waiting for transfers between devices, total_seq(): g = add_low(g, lax.ppermute(g, 'seq', [(0, 1), (3, 2)]))  79.8 us
    pallas_call x12, Pallas kernels, outer(): pl.pallas_call(outer_body, grid=(m // block,), in_specs=[lhs, lhs, whole_...  63.7 us
    pallas_call x2, Pallas kernels, feed(): pl.pallas_call(feed_body, grid=(rows // block,), in_specs=[rows_spec(bloc...  52.2 us
    ppermute x12, starting transfers between devices, total_seq(): g = add_low(g, lax.ppermute(g, 'seq', [(0, 1), (3, 2)]))  49.1 us
    ppermute x27, waiting for transfers between devices, flip_row(): return lax.ppermute(a, 'row', [(0, 1), (1, 0)])  45.2 us
    ppermute x41, starting transfers between devices, flip_y(): return lax.ppermute(a, 'col', [(i, i ^ 2) for i in range(4)])  36.5 us
  transfers between devices with their start and end apart: 139, of which 43 were waited for; matrix products, arithmetic and copies ran while one was open for 19% of the time, Pallas kernels for 18%

profile of v1, /device:TPU:0, one launch (start us, length us, event | category | flops | bytes accessed | tf_op | source)
XLA Modules:
  0.0 976.8 jit_solution(7793346877972863250)
XLA Ops:
  63.4 4.8 collective-permute-done.10
  69.8 6.6 collective-permute-done.23
  99.8 41.5 %collective-permute-done.42 = bf16[1152,384]{1,0:T(8,128)(2,1)} collective-permute-done((bf16[1152,384]{1,0:T(8,128)(2,1)S(1)}, bf16[1152,384]{1,0:T(8,128)(2,1)}, u32[]{:S(2)}, u32[]{:S(2)}) %collective-permute-start.42) | collective-permute-done | bytes 884768 | tf_op jit(solution)/shard_map/ppermute | solution.py:338
  153.1 8.6 collective-permute-done.15.x2
  171.1 6.5 norm_uv.3
  181.8 6.4 norm_uv.2
  188.8 16.1 %recur.1 = (f32[1024,512]{1,0:T(8,128)}, f32[1024,512]{1,0:T(8,128)}, f32[1024,512]{1,0:T(8,128)}, f32[1024,512]{1,0:T(8,128)}, f32[1024,512]{1,0:T(8,128)}, /*index=5*/f32[8,512]{1,0:T(8,128)}) custom-call(f32[512,512]{1,0:T(8,128)} %get-tuple-element.100.ua.refs_10_.u, f32[512,512]{1,0:T(8,128)} %get-tuple-element.101.ub.refs_11_.u, f32[8,512]{1,0:T(8,128)} %copy-done.88, ...), custom_call_target="tpu_custom_call" | custom-call | flops 1610612736 | bytes 12582912 | tf_op jit(solution)/shard_map/recur/pallas_call | solution.py:540
  210.2 5.0 collective-permute-start.20
  216.6 4.5 collective-permute-start.21
  223.2 4.6 mix.2
  229.3 4.6 mix.3
  238.8 4.7 collective-permute-done.47
  251.0 3.8 collective-permute-done.49
  265.6 9.1 collective-permute-done.32.refs_5_
  283.5 16.2 %collective-permute-done.28.refs_1_ = bf16[512,384]{1,0:T(8,128)(2,1)} collective-permute-done((bf16[512,384]{1,0:T(8,128)(2,1)}, bf16[512,384]{1,0:T(8,128)(2,1)}, u32[]{:S(2)}, u32[]{:S(2)}) %collective-permute-start.28) | collective-permute-done | bytes 393248 | tf_op jit(solution)/shard_map/ppermute | solution.py:334
  304.5 26.2 %feed.3 = (bf16[512,768]{1,0:T(8,128)(2,1)}, bf16[512,768]{1,0:T(8,128)(2,1)}, bf16[512,1152]{1,0:T(8,128)(2,1)}, bf16[512,1152]{1,0:T(8,128)(2,1)}, bf16[512,11...) custom-call(bf16[512,384]{1,0:T(8,128)(2,1)} %copy-done.81, ...), custom_call_target="tpu_custom_call" | custom-call | flops 10871635968 | bytes 25976832 | tf_op jit(solution)/shard_map/feed/pallas_call | solution.py:645
  332.4 26.0 %feed.2 = (bf16[512,768]{1,0:T(8,128)(2,1)}, bf16[512,768]{1,0:T(8,128)(2,1)}, bf16[512,1152]{1,0:T(8,128)(2,1)}, bf16[512,1152]{1,0:T(8,128)(2,1)}, bf16[512,11...) custom-call(bf16[512,384]{1,0:T(8,128)(2,1)} %get-tuple-element.258., ...), custom_call_target="tpu_custom_call" | custom-call | flops 10871635968 | bytes 25976832 | tf_op jit(solution)/shard_map/feed/pallas_call | solution.py:645
  366.4 5.6 outer.19
  376.8 5.9 collective-permute-done.61
  395.3 8.0 collective-permute-done.62
  403.8 4.1 fusion.28
  409.9 8.0 collective-permute-done.46
  420.8 5.7 outer.18
  426.5 5.7 outer.21
  436.3 5.6 outer.20
  441.9 8.6 outer.23
  450.5 8.6 outer.22
  461.5 19.4 %adjoint.1 = (f32[1024,512]{1,0:T(8,128)}, f32[1024,512]{1,0:T(8,128)}, bf16[512,512]{1,0:T(8,128)(2,1)}, bf16[512,512]{1,0:T(8,128)(2,1)}, f32[8,512]{1,0:T(8,1...) custom-call(bf16[512,384]{1,0:T(8,128)(2,1)} %copy-done.39, bf16[512,384]{1,0:T(8,128)(2,1)} %collective-permute-done.65.refs_1_, ...), custom_call_target="tpu_custom_call" | custom-call | flops 1610612736 | bytes 19922944 | tf_op jit(solution)/shard_map/adjoint/pallas_call | solution.py:737
  484.8 4.2 outer.15
  489.0 4.3 outer.14
  503.3 17.0 %recur_back.1 = (f32[1024,512]{1,0:T(8,128)}, f32[8,512]{1,0:T(8,128)}, f32[4,128,128]{2,1,0:T(8,128)}, f32[4,128,128]{2,1,0:T(8,128)}, f32[8,512]{1,0:T(8,128)}) custom-call(f32[1024,512]{1,0:T(8,128)} %get-tuple-element.139.refs_0_, f32[1024,512]{1,0:T(8,128)} %get-tuple-element.140.refs_1_, f32[24,512]{1,0:T(8,128)} %pad_maximum_fusion.17.refs_2_, ...), custom_call_target="tpu_custom_call" | custom-call | flops 3221225472 | bytes 18874368 | tf_op jit(solution)/shard_map/recur_back/pallas_call | solution.py:831
  524.1 4.1 collective-permute-done.77.tail
  528.8 6.3 enter_back.3
  536.2 6.0 enter_back.2
  544.2 4.2 outer.13
  549.6 4.2 outer.12
  572.4 3.9 collective-permute-done.79
  586.7 5.0 collective-permute-start.115
  594.9 4.9 collective-permute-start.131
  599.8 9.2 collective-permute-done.80
  616.7 4.0 collective-permute-start.98
  623.0 14.5 %collective-permute-done.123 = bf16[384,1152]{1,0:T(8,128)(2,1)} collective-permute-done((bf16[384,1152]{1,0:T(8,128)(2,1)}, bf16[384,1152]{1,0:T(8,128)(2,1)}, u32[]{:S(2)}, u32[]{:S(2)}) %collective-permute-start.123) | collective-permute-done | bytes 884768 | tf_op jit(solution)/shard_map/ppermute | solution.py:942
  640.1 25.6 %collective-permute-done.131 = bf16[1152,384]{1,0:T(8,128)(2,1)} collective-permute-done((bf16[1152,384]{1,0:T(8,128)(2,1)}, bf16[1152,384]{1,0:T(8,128)(2,1)}, u32[]{:S(2)}, u32[]{:S(2)}) %collective-permute-start.131) | collective-permute-done | bytes 884768 | tf_op jit(solution)/shard_map/ppermute | solution.py:942
  665.8 4.5 collective-permute-start.107
  674.9 4.3 collective-permute-start.90
  679.3 3.9 collective-permute-done.107
  685.8 4.5 collective-permute-done.90
  690.3 5.3 collective-permute-start.102
  702.4 4.3 collective-permute-start.111
  717.8 7.5 collective-permute-start.94
  730.7 4.6 maximum_select_fusion
  751.6 10.8 %collective-permute-done.134 = bf16[1152,384]{1,0:T(8,128)(2,1)S(1)} collective-permute-done((bf16[1152,384]{1,0:T(8,128)(2,1)}, bf16[1152,384]{1,0:T(8,128)(2,1)S(1)}, u32[]{:S(2)}, u32[]{:S(2)}) %collective-permute-start.134) | collective-permute-done | bytes 884768 | tf_op jit(solution)/shard_map/ppermute | solution.py:338
  762.5 4.3 collective-permute-start.127
  770.6 16.5 %collective-permute-done.127 = bf16[384,1152]{1,0:T(8,128)(2,1)S(1)} collective-permute-done((bf16[384,1152]{1,0:T(8,128)(2,1)}, bf16[384,1152]{1,0:T(8,128)(2,1)S(1)}, u32[]{:S(2)}, u32[]{:S(2)}) %collective-permute-start.127) | collective-permute-done | bytes 884768 | tf_op jit(solution)/shard_map/ppermute | solution.py:942
  790.9 10.1 %collective-permute-done.135 = bf16[1152,384]{1,0:T(8,128)(2,1)S(1)} collective-permute-done((bf16[1152,384]{1,0:T(8,128)(2,1)S(1)}, bf16[1152,384]{1,0:T(8,128)(2,1)S(1)}, u32[]{:S(2)}, u32[]{:S(2)}) %collective-permute-start.135) | collective-permute-done | bytes 884768 | tf_op jit(solution)/shard_map/ppermute | solution.py:942
  807.2 7.5 collective-permute-done.109
  816.9 7.0 collective-permute-done.92
  825.2 28.2 %collective-permute-done.104 = bf16[384,512]{1,0:T(8,128)(2,1)S(1)} collective-permute-done((bf16[384,512]{1,0:T(8,128)(2,1)S(1)}, bf16[384,512]{1,0:T(8,128)(2,1)S(1)}, u32[]{:S(2)}, u32[]{:S(2)}) %collective-permute-start.104) | collective-permute-done | bytes 393248 | tf_op jit(solution)/shard_map/ppermute | solution.py:944
  856.4 19.7 %collective-permute-done.113 = bf16[512,384]{1,0:T(8,128)(2,1)S(1)} collective-permute-done((bf16[512,384]{1,0:T(8,128)(2,1)S(1)}, bf16[512,384]{1,0:T(8,128)(2,1)S(1)}, u32[]{:S(2)}, u32[]{:S(2)}) %collective-permute-start.113) | collective-permute-done | bytes 393248 | tf_op jit(solution)/shard_map/ppermute | solution.py:944
  879.5 6.7 collective-permute-done.96
  895.1 19.7 %collective-permute-done.133 = bf16[1152,384]{1,0:T(8,128)(2,1)S(1)} collective-permute-done((bf16[1152,384]{1,0:T(8,128)(2,1)S(1)}, bf16[1152,384]{1,0:T(8,128)(2,1)S(1)}, u32[]{:S(2)}, u32[]{:S(2)}) %collective-permute-start.133) | collective-permute-done | bytes 884768 | tf_op jit(solution)/shard_map/ppermute | solution.py:944
  914.9 18.9 %collective-permute-done.121 = bf16[384,1152]{1,0:T(8,128)(2,1)S(1)} collective-permute-done((bf16[384,1152]{1,0:T(8,128)(2,1)S(1)}, bf16[384,1152]{1,0:T(8,128)(2,1)S(1)}, u32[]{:S(2)}, u32[]{:S(2)}) %collective-permute-start.121) | collective-permute-done | bytes 884768 | tf_op jit(solution)/shard_map/ppermute | solution.py:944
  934.5 17.6 %collective-permute-done.129 = bf16[384,1152]{1,0:T(8,128)(2,1)S(1)} collective-permute-done((bf16[384,1152]{1,0:T(8,128)(2,1)S(1)}, bf16[384,1152]{1,0:T(8,128)(2,1)S(1)}, u32[]{:S(2)}, u32[]{:S(2)}) %collective-permute-start.129) | collective-permute-done | bytes 884768 | tf_op jit(solution)/shard_map/ppermute | solution.py:944
  952.8 8.8 collective-permute-done.137
  (698 shorter events, 347.5 us)
Async XLA Ops:
  7.2 689.3 %all-reduce.2.cloned.1.call-start = ((), (), s32[]{:S(2)}) async-start(), calls=%async_computation | async-start | bytes 1073152 | tf_op jit(solution)/shard_map/psum | solution.py:1156
  9.9 71.1 %collective-permute-start = (f32[1,1024,192]{1,2,0:T(8,128)}, f32[1,1024,192]{1,2,0:T(8,128)}, u32[]{:S(2)}, u32[]{:S(2)}) collective-permute-start(f32[1,1024,192]{1,2,0:T(8,128)} %get-tuple-element.309), channel_id=1, source_target_pairs={{0,1},{1,0},{2,3},{3,2},{4,5},{5,4},{6,7},{7,6},{8,9},{9,8},{10,11... | collective-permute-start | bytes 2359304 | tf_op jit(solution)/shard_map/ppermute | solution.py:342
  10.3 26.9 %collective-permute-start.4 = (f32[2,192]{1,0:T(2,128)S(1)}, f32[2,192]{1,0:T(2,128)S(1)}, u32[]{:S(2)}, u32[]{:S(2)}) collective-permute-start(f32[2,192]{1,0:T(2,128)S(1)} %pad_maximum_fusion.22), channel_id=1, source_target_pairs={{0,1},{1,0},{2,3},{3,2},{4,5},{5,4},{6,7},{7,6},{8,9},{9,8},{10,11... | collective-permute-start | bytes 4616 | tf_op jit(solution)/shard_map/ppermute | solution.py:342
  11.4 41.7 %collective-permute-start.9 = (bf16[384,512]{1,0:T(8,128)(2,1)}, bf16[384,512]{1,0:T(8,128)(2,1)}, u32[]{:S(2)}, u32[]{:S(2)}) collective-permute-start(bf16[384,512]{1,0:T(8,128)(2,1)} %get-tuple-element.357), channel_id=1, source_target_pairs={{0,1},{1,0},{2,3},{3,2},{4,5},{5,4},{6,7},{7,6},{8,9},{9,8},{10,11... | collective-permute-start | bytes 1179656 | tf_op jit(solution)/shard_map/ppermute | solution.py:342
  11.9 37.2 %collective-permute-start.18 = (f32[8,256]{1,0:T(8,128)S(1)}, f32[8,256]{1,0:T(8,128)S(1)}, u32[]{:S(2)}, u32[]{:S(2)}) collective-permute-start(f32[8,256]{1,0:T(8,128)S(1)} %pad_maximum_fusion.18), channel_id=1, source_target_pairs={{0,1},{1,0},{2,3},{3,2},{4,5},{5,4},{6,7},{7,6},{8,9},{9,8},{10,11... | collective-permute-start | bytes 24584 | tf_op jit(solution)/shard_map/ppermute | solution.py:342
  81.0 68.1 %collective-permute-start.38 = (bf16[384,1152]{1,0:T(8,128)(2,1)}, bf16[384,1152]{1,0:T(8,128)(2,1)}, u32[]{:S(2)}, u32[]{:S(2)}) collective-permute-start(bf16[384,1152]{1,0:T(8,128)(2,1)} %get-tuple-element.292), channel_id=1, source_target_pairs={{0,2},{1,3},{2,0},{3,1},{4,6},{5,7},{6,4},{7,5},{8,10},{9,11},{10,... | collective-permute-start | bytes 2654216 | tf_op jit(solution)/shard_map/ppermute | solution.py:338
  83.1 69.4 %collective-permute-start.37 = (bf16[384,1152]{1,0:T(8,128)(2,1)}, bf16[384,1152]{1,0:T(8,128)(2,1)}, u32[]{:S(2)}, u32[]{:S(2)}) collective-permute-start(bf16[384,1152]{1,0:T(8,128)(2,1)} %get-tuple-element.290), channel_id=1, source_target_pairs={{0,2},{1,3},{2,0},{3,1},{4,6},{5,7},{6,4},{7,5},{8,10},{9,11},{10,... | collective-permute-start | bytes 2654216 | tf_op jit(solution)/shard_map/ppermute | solution.py:338
  90.3 51.0 %collective-permute-start.42 = (bf16[1152,384]{1,0:T(8,128)(2,1)S(1)}, bf16[1152,384]{1,0:T(8,128)(2,1)}, u32[]{:S(2)}, u32[]{:S(2)}) collective-permute-start(bf16[1152,384]{1,0:T(8,128)(2,1)S(1)} %copy-done.53), channel_id=1, source_target_pairs={{0,2},{1,3},{2,0},{3,1},{4,6},{5,7},{6,4},{7,5},{8,10},{9,11},{10,... | collective-permute-start | bytes 2654216 | tf_op jit(solution)/shard_map/ppermute | solution.py:338
  95.9 47.6 %collective-permute-start.41 = (bf16[1152,384]{1,0:T(8,128)(2,1)S(1)}, bf16[1152,384]{1,0:T(8,128)(2,1)S(1)}, u32[]{:S(2)}, u32[]{:S(2)}) collective-permute-start(bf16[1152,384]{1,0:T(8,128)(2,1)S(1)} %copy-done.52), channel_id=1, source_target_pairs={{0,1},{1,0},{2,3},{3,2},{4,5},{5,4},{6,7},{7,6},{8,9},{9,8},{10,11... | collective-permute-start | bytes 2654216 | tf_op jit(solution)/shard_map/ppermute | solution.py:342
  97.2 68.0 %collective-permute-start.1 = (bf16[512,384]{1,0:T(8,128)(2,1)S(1)}, bf16[512,384]{1,0:T(8,128)(2,1)S(1)}, u32[]{:S(2)}, u32[]{:S(2)}) collective-permute-start(bf16[512,384]{1,0:T(8,128)(2,1)S(1)} %get-tuple-element.353.x0), channel_id=1, source_target_pairs={{0,4},{4,0},{1,5},{5,1},{2,6},{6,2},{3,7},{7,3},{8,12},{12,8},{9,1... | collective-permute-start | bytes 1179656 | tf_op jit(solution)/shard_map/ppermute | solution.py:334
  141.3 37.0 %collective-permute-start.2 = (bf16[512,384]{1,0:T(8,128)(2,1)S(1)}, bf16[512,384]{1,0:T(8,128)(2,1)S(1)}, u32[]{:S(2)}, u32[]{:S(2)}) collective-permute-start(bf16[512,384]{1,0:T(8,128)(2,1)S(1)} %get-tuple-element.353.x0), channel_id=1, source_target_pairs={{0,2},{1,3},{2,0},{3,1},{4,6},{5,7},{6,4},{7,5},{8,10},{9,11},{10,... | collective-permute-start | bytes 1179656 | tf_op jit(solution)/shard_map/ppermute | solution.py:338
  152.6 91.5 %collective-permute-start.54 = (bf16[512,384]{1,0:T(8,128)(2,1)}, bf16[512,384]{1,0:T(8,128)(2,1)}, u32[]{:S(2)}, u32[]{:S(2)}) collective-permute-start(bf16[512,384]{1,0:T(8,128)(2,1)} %get-tuple-element.347.refs_4_), channel_id=1, source_target_pairs={{0,2},{1,3},{2,0},{3,1},{4,6},{5,7},{6,4},{7,5},{8,10},{9,11},{10,... | collective-permute-start | bytes 1179656 | tf_op jit(solution)/shard_map/ppermute | solution.py:338
  166.7 78.9 %collective-permute-start.40 = (bf16[384,1152]{1,0:T(8,128)(2,1)}, bf16[384,1152]{1,0:T(8,128)(2,1)}, u32[]{:S(2)}, u32[]{:S(2)}) collective-permute-start(bf16[384,1152]{1,0:T(8,128)(2,1)} %collective-permute-done.38), channel_id=1, source_target_pairs={{0,1},{1,0},{2,3},{3,2},{4,5},{5,4},{6,7},{7,6},{8,9},{9,8},{10,11... | collective-permute-start | bytes 2654216 | tf_op jit(solution)/shard_map/ppermute | solution.py:342
  170.3 91.7 %collective-permute-start.39 = (bf16[384,1152]{1,0:T(8,128)(2,1)}, bf16[384,1152]{1,0:T(8,128)(2,1)}, u32[]{:S(2)}, u32[]{:S(2)}) collective-permute-start(bf16[384,1152]{1,0:T(8,128)(2,1)} %collective-permute-done.37), channel_id=1, source_target_pairs={{0,1},{1,0},{2,3},{3,2},{4,5},{5,4},{6,7},{7,6},{8,9},{9,8},{10,11... | collective-permute-start | bytes 2654216 | tf_op jit(solution)/shard_map/ppermute | solution.py:342
  178.3 55.6 %collective-permute-start.43 = (bf16[1152,384]{1,0:T(8,128)(2,1)}, bf16[1152,384]{1,0:T(8,128)(2,1)}, u32[]{:S(2)}, u32[]{:S(2)}) collective-permute-start(bf16[1152,384]{1,0:T(8,128)(2,1)} %collective-permute-done.42), channel_id=1, source_target_pairs={{0,1},{1,0},{2,3},{3,2},{4,5},{5,4},{6,7},{7,6},{8,9},{9,8},{10,11... | collective-permute-start | bytes 2654216 | tf_op jit(solution)/shard_map/ppermute | solution.py:342
  249.5 29.2 %collective-permute-start.53 = (bf16[512,384]{1,0:T(8,128)(2,1)}, bf16[512,384]{1,0:T(8,128)(2,1)S(1)}, u32[]{:S(2)}, u32[]{:S(2)}) collective-permute-start(bf16[512,384]{1,0:T(8,128)(2,1)} %get-tuple-element.347.refs_4_), channel_id=1, source_target_pairs={{0,4},{4,0},{1,5},{5,1},{2,6},{6,2},{3,7},{7,3},{8,12},{12,8},{9,1... | collective-permute-start | bytes 1179656 | tf_op jit(solution)/shard_map/ppermute | solution.py:334
  264.2 36.2 %collective-permute-start.50 = (bf16[512,384]{1,0:T(8,128)(2,1)S(1)}, bf16[512,384]{1,0:T(8,128)(2,1)S(1)}, u32[]{:S(2)}, u32[]{:S(2)}) collective-permute-start(bf16[512,384]{1,0:T(8,128)(2,1)S(1)} %get-tuple-element.272.refs_0_), channel_id=1, source_target_pairs={{0,4},{4,0},{1,5},{5,1},{2,6},{6,2},{3,7},{7,3},{8,12},{12,8},{9,1... | collective-permute-start | bytes 1179656 | tf_op jit(solution)/shard_map/ppermute | solution.py:334
  274.7 25.0 %collective-permute-start.28 = (bf16[512,384]{1,0:T(8,128)(2,1)}, bf16[512,384]{1,0:T(8,128)(2,1)}, u32[]{:S(2)}, u32[]{:S(2)}) collective-permute-start(bf16[512,384]{1,0:T(8,128)(2,1)} %get-tuple-element.258.refs_0_), channel_id=1, source_target_pairs={{0,4},{4,0},{1,5},{5,1},{2,6},{6,2},{3,7},{7,3},{8,12},{12,8},{9,1... | collective-permute-start | bytes 1179656 | tf_op jit(solution)/shard_map/ppermute | solution.py:334
  275.2 28.6 %collective-permute-start.52 = (bf16[512,384]{1,0:T(8,128)(2,1)S(1)}, bf16[512,384]{1,0:T(8,128)(2,1)S(1)}, u32[]{:S(2)}, u32[]{:S(2)}) collective-permute-start(bf16[512,384]{1,0:T(8,128)(2,1)S(1)} %collective-permute-done.51.refs_2_), channel_id=1, source_target_pairs={{0,4},{4,0},{1,5},{5,1},{2,6},{6,2},{3,7},{7,3},{8,12},{12,8},{9,1... | collective-permute-start | bytes 1179656 | tf_op jit(solution)/shard_map/ppermute | solution.py:334
  278.7 53.7 %collective-permute-start.33 = (bf16[512,384]{1,0:T(8,128)(2,1)S(1)}, bf16[512,384]{1,0:T(8,128)(2,1)}, u32[]{:S(2)}, u32[]{:S(2)}) collective-permute-start(bf16[512,384]{1,0:T(8,128)(2,1)S(1)} %copy-done.70), channel_id=1, source_target_pairs={{0,2},{1,3},{2,0},{3,1},{4,6},{5,7},{6,4},{7,5},{8,10},{9,11},{10,... | collective-permute-start | bytes 1179656 | tf_op jit(solution)/shard_map/ppermute | solution.py:338
  283.0 49.4 %collective-permute-start.34 = (bf16[512,384]{1,0:T(8,128)(2,1)}, bf16[512,384]{1,0:T(8,128)(2,1)}, u32[]{:S(2)}, u32[]{:S(2)}) collective-permute-start(bf16[512,384]{1,0:T(8,128)(2,1)} %collective-permute-done.32.refs_5_), channel_id=1, source_target_pairs={{0,2},{1,3},{2,0},{3,1},{4,6},{5,7},{6,4},{7,5},{8,10},{9,11},{10,... | collective-permute-start | bytes 1179656 | tf_op jit(solution)/shard_map/ppermute | solution.py:338
  299.7 32.7 %collective-permute-start.29 = (bf16[512,384]{1,0:T(8,128)(2,1)}, bf16[512,384]{1,0:T(8,128)(2,1)}, u32[]{:S(2)}, u32[]{:S(2)}) collective-permute-start(bf16[512,384]{1,0:T(8,128)(2,1)} %get-tuple-element.258.refs_0_), channel_id=1, source_target_pairs={{0,2},{1,3},{2,0},{3,1},{4,6},{5,7},{6,4},{7,5},{8,10},{9,11},{10,... | collective-permute-start | bytes 1179656 | tf_op jit(solution)/shard_map/ppermute | solution.py:338
  300.5 32.0 %collective-permute-start.30 = (bf16[512,384]{1,0:T(8,128)(2,1)}, bf16[512,384]{1,0:T(8,128)(2,1)}, u32[]{:S(2)}, u32[]{:S(2)}) collective-permute-start(bf16[512,384]{1,0:T(8,128)(2,1)} %collective-permute-done.28.refs_1_), channel_id=1, source_target_pairs={{0,2},{1,3},{2,0},{3,1},{4,6},{5,7},{6,4},{7,5},{8,10},{9,11},{10,... | collective-permute-start | bytes 1179656 | tf_op jit(solution)/shard_map/ppermute | solution.py:338
  361.9 25.5 %collective-permute-start.45 = (bf16[512,384]{1,0:T(8,128)(2,1)}, bf16[512,384]{1,0:T(8,128)(2,1)}, u32[]{:S(2)}, u32[]{:S(2)}) collective-permute-start(bf16[512,384]{1,0:T(8,128)(2,1)} %get-tuple-element.113), channel_id=1, source_target_pairs={{0,4},{4,0},{1,5},{5,1},{2,6},{6,2},{3,7},{7,3},{8,12},{12,8},{9,1... | collective-permute-start | bytes 1179656 | tf_op jit(solution)/shard_map/ppermute | solution.py:334
  362.3 26.8 %collective-permute-start.56 = (bf16[512,384]{1,0:T(8,128)(2,1)}, bf16[512,384]{1,0:T(8,128)(2,1)}, u32[]{:S(2)}, u32[]{:S(2)}) collective-permute-start(bf16[512,384]{1,0:T(8,128)(2,1)} %get-tuple-element.121), channel_id=1, source_target_pairs={{0,2},{1,3},{2,0},{3,1},{4,6},{5,7},{6,4},{7,5},{8,10},{9,11},{10,... | collective-permute-start | bytes 1179656 | tf_op jit(solution)/shard_map/ppermute | solution.py:338
  364.3 27.6 %collective-permute-start.60 = (bf16[512,384]{1,0:T(8,128)(2,1)}, bf16[512,384]{1,0:T(8,128)(2,1)}, u32[]{:S(2)}, u32[]{:S(2)}) collective-permute-start(bf16[512,384]{1,0:T(8,128)(2,1)} %get-tuple-element.126), channel_id=1, source_target_pairs={{0,4},{4,0},{1,5},{5,1},{2,6},{6,2},{3,7},{7,3},{8,12},{12,8},{9,1... | collective-permute-start | bytes 1179656 | tf_op jit(solution)/shard_map/ppermute | solution.py:334
  391.9 26.2 %collective-permute-start.58 = (bf16[512,384]{1,0:T(8,128)(2,1)}, bf16[512,384]{1,0:T(8,128)(2,1)S(1)}, u32[]{:S(2)}, u32[]{:S(2)}) collective-permute-start(bf16[512,384]{1,0:T(8,128)(2,1)} %get-tuple-element.122), channel_id=1, source_target_pairs={{0,2},{1,3},{2,0},{3,1},{4,6},{5,7},{6,4},{7,5},{8,10},{9,11},{10,... | collective-permute-start | bytes 1179656 | tf_op jit(solution)/shard_map/ppermute | solution.py:338
  407.9 26.3 %collective-permute-start.65 = (bf16[512,384]{1,0:T(8,128)(2,1)S(1)}, bf16[512,384]{1,0:T(8,128)(2,1)}, u32[]{:S(2)}, u32[]{:S(2)}) collective-permute-start(bf16[512,384]{1,0:T(8,128)(2,1)S(1)} %get-tuple-element.256.refs_0_), channel_id=1, source_target_pairs={{0,4},{4,0},{1,5},{5,1},{2,6},{6,2},{3,7},{7,3},{8,12},{12,8},{9,1... | collective-permute-start | bytes 1179656 | tf_op jit(solution)/shard_map/ppermute | solution.py:334
  409.5 25.5 %collective-permute-start.72 = (bf16[512,384]{1,0:T(8,128)(2,1)}, bf16[512,384]{1,0:T(8,128)(2,1)}, u32[]{:S(2)}, u32[]{:S(2)}) collective-permute-start(bf16[512,384]{1,0:T(8,128)(2,1)} %get-tuple-element.270.refs_4_), channel_id=1, source_target_pairs={{0,2},{1,3},{2,0},{3,1},{4,6},{5,7},{6,4},{7,5},{8,10},{9,11},{10,... | collective-permute-start | bytes 1179656 | tf_op jit(solution)/shard_map/ppermute | solution.py:338
  420.8 38.8 %collective-permute-start.59 = (f32[1024,192]{0,1:T(8,128)}, f32[1024,192]{0,1:T(8,128)S(1)}, u32[]{:S(2)}, u32[]{:S(2)}) collective-permute-start(f32[1024,192]{0,1:T(8,128)} %copy.70), channel_id=1, source_target_pairs={{0,1},{1,0},{2,3},{3,2},{4,5},{5,4},{6,7},{7,6},{8,9},{9,8},{10,11... | collective-permute-start | bytes 2359304 | tf_op jit(solution)/shard_map/ppermute | solution.py:342
  432.2 28.8 %collective-permute-start.66 = (bf16[512,384]{1,0:T(8,128)(2,1)S(1)}, bf16[512,384]{1,0:T(8,128)(2,1)}, u32[]{:S(2)}, u32[]{:S(2)}) collective-permute-start(bf16[512,384]{1,0:T(8,128)(2,1)S(1)} %get-tuple-element.256.refs_0_), channel_id=1, source_target_pairs={{0,2},{1,3},{2,0},{3,1},{4,6},{5,7},{6,4},{7,5},{8,10},{9,11},{10,... | collective-permute-start | bytes 1179656 | tf_op jit(solution)/shard_map/ppermute | solution.py:338
  433.1 28.3 %collective-permute-start.71 = (bf16[512,384]{1,0:T(8,128)(2,1)}, bf16[512,384]{1,0:T(8,128)(2,1)}, u32[]{:S(2)}, u32[]{:S(2)}) collective-permute-start(bf16[512,384]{1,0:T(8,128)(2,1)} %get-tuple-element.270.refs_4_), channel_id=1, source_target_pairs={{0,4},{4,0},{1,5},{5,1},{2,6},{6,2},{3,7},{7,3},{8,12},{12,8},{9,1... | collective-permute-start | bytes 1179656 | tf_op jit(solution)/shard_map/ppermute | solution.py:334
  434.2 27.2 %collective-permute-start.67 = (bf16[512,384]{1,0:T(8,128)(2,1)}, bf16[512,384]{1,0:T(8,128)(2,1)}, u32[]{:S(2)}, u32[]{:S(2)}) collective-permute-start(bf16[512,384]{1,0:T(8,128)(2,1)} %collective-permute-done.65.refs_1_), channel_id=1, source_target_pairs={{0,2},{1,3},{2,0},{3,1},{4,6},{5,7},{6,4},{7,5},{8,10},{9,11},{10,... | collective-permute-start | bytes 1179656 | tf_op jit(solution)/shard_map/ppermute | solution.py:338
  435.1 26.4 %collective-permute-start.73 = (bf16[512,384]{1,0:T(8,128)(2,1)}, bf16[512,384]{1,0:T(8,128)(2,1)}, u32[]{:S(2)}, u32[]{:S(2)}) collective-permute-start(bf16[512,384]{1,0:T(8,128)(2,1)} %collective-permute-done.72.refs_6_), channel_id=1, source_target_pairs={{0,4},{4,0},{1,5},{5,1},{2,6},{6,2},{3,7},{7,3},{8,12},{12,8},{9,1... | collective-permute-start | bytes 1179656 | tf_op jit(solution)/shard_map/ppermute | solution.py:334
  459.6 95.9 %collective-permute-start.114 = (bf16[768,1152]{1,0:T(8,128)(2,1)}, bf16[768,1152]{1,0:T(8,128)(2,1)}, u32[]{:S(2)}, u32[]{:S(2)}) collective-permute-start(bf16[768,1152]{1,0:T(8,128)(2,1)} %outer.19), channel_id=1, source_target_pairs={{0,1},{1,0},{2,3},{3,2},{4,5},{5,4},{6,7},{7,6},{8,9},{9,8},{10,11... | collective-permute-start | bytes 5308424 | tf_op jit(solution)/shard_map/ppermute | solution.py:342
  461.0 99.4 %collective-permute-start.122 = (bf16[768,1152]{1,0:T(8,128)(2,1)}, bf16[768,1152]{1,0:T(8,128)(2,1)}, u32[]{:S(2)}, u32[]{:S(2)}) collective-permute-start(bf16[768,1152]{1,0:T(8,128)(2,1)} %outer.21), channel_id=1, source_target_pairs={{0,1},{1,0},{2,3},{3,2},{4,5},{5,4},{6,7},{7,6},{8,9},{9,8},{10,11... | collective-permute-start | bytes 5308424 | tf_op jit(solution)/shard_map/ppermute | solution.py:342
  502.1 63.1 %collective-permute-start.130 = (bf16[1152,768]{1,0:T(8,128)(2,1)}, bf16[1152,768]{1,0:T(8,128)(2,1)}, u32[]{:S(2)}, u32[]{:S(2)}) collective-permute-start(bf16[1152,768]{1,0:T(8,128)(2,1)} %outer.23), channel_id=1, source_target_pairs={{0,1},{1,0},{2,3},{3,2},{4,5},{5,4},{6,7},{7,6},{8,9},{9,8},{10,11... | collective-permute-start | bytes 5308424 | tf_op jit(solution)/shard_map/ppermute | solution.py:342
  502.1 75.3 %collective-permute-start.97 = (bf16[768,512]{1,0:T(8,128)(2,1)}, bf16[768,512]{1,0:T(8,128)(2,1)}, u32[]{:S(2)}, u32[]{:S(2)}) collective-permute-start(bf16[768,512]{1,0:T(8,128)(2,1)} %outer.15), channel_id=1, source_target_pairs={{0,1},{1,0},{2,3},{3,2},{4,5},{5,4},{6,7},{7,6},{8,9},{9,8},{10,11... | collective-permute-start | bytes 2359304 | tf_op jit(solution)/shard_map/ppermute | solution.py:342
  553.8 27.2 %collective-permute-start.106 = (bf16[512,768]{1,0:T(8,128)(2,1)}, bf16[512,768]{1,0:T(8,128)(2,1)}, u32[]{:S(2)}, u32[]{:S(2)}) collective-permute-start(bf16[512,768]{1,0:T(8,128)(2,1)} %outer.17), channel_id=1, source_target_pairs={{0,1},{1,0},{2,3},{3,2},{4,5},{5,4},{6,7},{7,6},{8,9},{9,8},{10,11... | collective-permute-start | bytes 2359304 | tf_op jit(solution)/shard_map/ppermute | solution.py:342
  577.5 162.3 %collective-permute-start.118 = (bf16[384,1152]{1,0:T(8,128)(2,1)}, bf16[384,1152]{1,0:T(8,128)(2,1)}, u32[]{:S(2)}, u32[]{:S(2)}) collective-permute-start(bf16[384,1152]{1,0:T(8,128)(2,1)} %get-tuple-element.285), channel_id=1, source_target_pairs={{0,2},{1,3},{2,0},{3,1},{4,6},{5,7},{6,4},{7,5},{8,10},{9,11},{10,... | collective-permute-start | bytes 2654216 | tf_op jit(solution)/shard_map/ppermute | solution.py:338
  586.7 29.9 %collective-permute-start.115 = (bf16[384,1152]{1,0:T(8,128)(2,1)}, bf16[384,1152]{1,0:T(8,128)(2,1)}, u32[]{:S(2)}, u32[]{:S(2)}) collective-permute-start(bf16[384,1152]{1,0:T(8,128)(2,1)} %get-tuple-element.284), channel_id=1, source_target_pairs={{0,8},{24,16},{1,9},{25,17},{2,10},{26,18},{3,11},{27,19},{4,12},{... | collective-permute-start | bytes 2654216 | tf_op jit(solution)/shard_map/ppermute | solution.py:942
  591.7 45.8 %collective-permute-start.123 = (bf16[384,1152]{1,0:T(8,128)(2,1)}, bf16[384,1152]{1,0:T(8,128)(2,1)}, u32[]{:S(2)}, u32[]{:S(2)}) collective-permute-start(bf16[384,1152]{1,0:T(8,128)(2,1)} %get-tuple-element.280), channel_id=1, source_target_pairs={{0,8},{24,16},{1,9},{25,17},{2,10},{26,18},{3,11},{27,19},{4,12},{... | collective-permute-start | bytes 2654216 | tf_op jit(solution)/shard_map/ppermute | solution.py:942
  594.9 70.9 %collective-permute-start.131 = (bf16[1152,384]{1,0:T(8,128)(2,1)}, bf16[1152,384]{1,0:T(8,128)(2,1)}, u32[]{:S(2)}, u32[]{:S(2)}) collective-permute-start(bf16[1152,384]{1,0:T(8,128)(2,1)} %get-tuple-element.276), channel_id=1, source_target_pairs={{0,8},{24,16},{1,9},{25,17},{2,10},{26,18},{3,11},{27,19},{4,12},{... | collective-permute-start | bytes 2654216 | tf_op jit(solution)/shard_map/ppermute | solution.py:942
  614.9 69.3 %collective-permute-start.101 = (bf16[384,512]{1,0:T(8,128)(2,1)}, bf16[384,512]{1,0:T(8,128)(2,1)}, u32[]{:S(2)}, u32[]{:S(2)}) collective-permute-start(bf16[384,512]{1,0:T(8,128)(2,1)} %get-tuple-element.341), channel_id=1, source_target_pairs={{0,2},{1,3},{2,0},{3,1},{4,6},{5,7},{6,4},{7,5},{8,10},{9,11},{10,... | collective-permute-start | bytes 1179656 | tf_op jit(solution)/shard_map/ppermute | solution.py:338
  616.7 58.2 %collective-permute-start.98 = (bf16[384,512]{1,0:T(8,128)(2,1)}, bf16[384,512]{1,0:T(8,128)(2,1)S(1)}, u32[]{:S(2)}, u32[]{:S(2)}) collective-permute-start(bf16[384,512]{1,0:T(8,128)(2,1)} %get-tuple-element.340), channel_id=1, source_target_pairs={{0,8},{24,16},{1,9},{25,17},{2,10},{26,18},{3,11},{27,19},{4,12},{... | collective-permute-start | bytes 1179656 | tf_op jit(solution)/shard_map/ppermute | solution.py:942
  637.6 64.9 %collective-permute-start.110 = (bf16[512,384]{1,0:T(8,128)(2,1)}, bf16[512,384]{1,0:T(8,128)(2,1)}, u32[]{:S(2)}, u32[]{:S(2)}) collective-permute-start(bf16[512,384]{1,0:T(8,128)(2,1)} %get-tuple-element.337), channel_id=1, source_target_pairs={{0,2},{1,3},{2,0},{3,1},{4,6},{5,7},{6,4},{7,5},{8,10},{9,11},{10,... | collective-permute-start | bytes 1179656 | tf_op jit(solution)/shard_map/ppermute | solution.py:338
  683.2 33.0 %collective-permute-start.93 = (bf16[384,512]{1,0:T(8,128)(2,1)}, bf16[384,512]{1,0:T(8,128)(2,1)}, u32[]{:S(2)}, u32[]{:S(2)}) collective-permute-start(bf16[384,512]{1,0:T(8,128)(2,1)} %get-tuple-element.345), channel_id=1, source_target_pairs={{0,2},{1,3},{2,0},{3,1},{4,6},{5,7},{6,4},{7,5},{8,10},{9,11},{10,... | collective-permute-start | bytes 1179656 | tf_op jit(solution)/shard_map/ppermute | solution.py:338
  713.5 37.3 %collective-permute-start.126 = (bf16[384,1152]{1,0:T(8,128)(2,1)}, bf16[384,1152]{1,0:T(8,128)(2,1)}, u32[]{:S(2)}, u32[]{:S(2)}) collective-permute-start(bf16[384,1152]{1,0:T(8,128)(2,1)} %get-tuple-element.281), channel_id=1, source_target_pairs={{0,2},{1,3},{2,0},{3,1},{4,6},{5,7},{6,4},{7,5},{8,10},{9,11},{10,... | collective-permute-start | bytes 2654216 | tf_op jit(solution)/shard_map/ppermute | solution.py:338
  716.2 27.0 %collective-permute-start.91 = (bf16[384,512]{1,0:T(8,128)(2,1)}, bf16[384,512]{1,0:T(8,128)(2,1)}, u32[]{:S(2)}, u32[]{:S(2)}) collective-permute-start(bf16[384,512]{1,0:T(8,128)(2,1)} %add_convert_fusion.29), channel_id=1, source_target_pairs={{8,16},{16,8},{9,17},{17,9},{10,18},{18,10},{11,19},{19,11},{12,20... | collective-permute-start | bytes 1179656 | tf_op jit(solution)/shard_map/ppermute | solution.py:943
  740.7 26.1 %collective-permute-start.119 = (bf16[384,1152]{1,0:T(8,128)(2,1)}, bf16[384,1152]{1,0:T(8,128)(2,1)S(1)}, u32[]{:S(2)}, u32[]{:S(2)}) collective-permute-start(bf16[384,1152]{1,0:T(8,128)(2,1)} %collective-permute-done.118), channel_id=1, source_target_pairs={{0,8},{24,16},{1,9},{25,17},{2,10},{26,18},{3,11},{27,19},{4,12},{... | collective-permute-start | bytes 2654216 | tf_op jit(solution)/shard_map/ppermute | solution.py:942
  743.3 26.3 %collective-permute-start.116 = (bf16[384,1152]{1,0:T(8,128)(2,1)S(1)}, bf16[384,1152]{1,0:T(8,128)(2,1)S(1)}, u32[]{:S(2)}, u32[]{:S(2)}) collective-permute-start(bf16[384,1152]{1,0:T(8,128)(2,1)S(1)} %copy-done.20), channel_id=1, source_target_pairs={{8,16},{16,8},{9,17},{17,9},{10,18},{18,10},{11,19},{19,11},{12,20... | collective-permute-start | bytes 2654216 | tf_op jit(solution)/shard_map/ppermute | solution.py:943
  747.6 42.2 %collective-permute-start.124 = (bf16[384,1152]{1,0:T(8,128)(2,1)S(1)}, bf16[384,1152]{1,0:T(8,128)(2,1)S(1)}, u32[]{:S(2)}, u32[]{:S(2)}) collective-permute-start(bf16[384,1152]{1,0:T(8,128)(2,1)S(1)} %copy-done.19), channel_id=1, source_target_pairs={{8,16},{16,8},{9,17},{17,9},{10,18},{18,10},{11,19},{19,11},{12,20... | collective-permute-start | bytes 2654216 | tf_op jit(solution)/shard_map/ppermute | solution.py:943
  750.8 51.8 %collective-permute-start.132 = (bf16[1152,384]{1,0:T(8,128)(2,1)S(1)}, bf16[1152,384]{1,0:T(8,128)(2,1)S(1)}, u32[]{:S(2)}, u32[]{:S(2)}) collective-permute-start(bf16[1152,384]{1,0:T(8,128)(2,1)S(1)} %copy-done.18), channel_id=1, source_target_pairs={{8,16},{16,8},{9,17},{17,9},{10,18},{18,10},{11,19},{19,11},{12,20... | collective-permute-start | bytes 2654216 | tf_op jit(solution)/shard_map/ppermute | solution.py:943
  766.8 34.2 %collective-permute-start.135 = (bf16[1152,384]{1,0:T(8,128)(2,1)S(1)}, bf16[1152,384]{1,0:T(8,128)(2,1)S(1)}, u32[]{:S(2)}, u32[]{:S(2)}) collective-permute-start(bf16[1152,384]{1,0:T(8,128)(2,1)S(1)} %collective-permute-done.134), channel_id=1, source_target_pairs={{0,8},{24,16},{1,9},{25,17},{2,10},{26,18},{3,11},{27,19},{4,12},{... | collective-permute-start | bytes 2654216 | tf_op jit(solution)/shard_map/ppermute | solution.py:942
  769.6 34.0 %collective-permute-start.103 = (bf16[384,512]{1,0:T(8,128)(2,1)S(1)}, bf16[384,512]{1,0:T(8,128)(2,1)S(1)}, u32[]{:S(2)}, u32[]{:S(2)}) collective-permute-start(bf16[384,512]{1,0:T(8,128)(2,1)S(1)} %copy-done.44), channel_id=1, source_target_pairs={{8,16},{16,8},{9,17},{17,9},{10,18},{18,10},{11,19},{19,11},{12,20... | collective-permute-start | bytes 1179656 | tf_op jit(solution)/shard_map/ppermute | solution.py:943
  805.0 83.7 %collective-permute-start.120 = (bf16[384,1152]{1,0:T(8,128)(2,1)S(1)}, bf16[384,1152]{1,0:T(8,128)(2,1)S(1)}, u32[]{:S(2)}, u32[]{:S(2)}) collective-permute-start(bf16[384,1152]{1,0:T(8,128)(2,1)S(1)} %add_convert_fusion.12), channel_id=1, source_target_pairs={{8,16},{16,8},{9,17},{17,9},{10,18},{18,10},{11,19},{19,11},{12,20... | collective-permute-start | bytes 2654216 | tf_op jit(solution)/shard_map/ppermute | solution.py:943
  805.8 87.5 %collective-permute-start.117 = (bf16[384,1152]{1,0:T(8,128)(2,1)S(1)}, bf16[384,1152]{1,0:T(8,128)(2,1)S(1)}, u32[]{:S(2)}, u32[]{:S(2)}) collective-permute-start(bf16[384,1152]{1,0:T(8,128)(2,1)S(1)} %add_convert_fusion.13), channel_id=1, source_target_pairs={{8,0},{16,24},{9,1},{17,25},{10,2},{18,26},{11,3},{19,27},{12,4},{... | collective-permute-start | bytes 2654216 | tf_op jit(solution)/shard_map/ppermute | solution.py:944
  814.7 75.5 %collective-permute-start.128 = (bf16[384,1152]{1,0:T(8,128)(2,1)S(1)}, bf16[384,1152]{1,0:T(8,128)(2,1)S(1)}, u32[]{:S(2)}, u32[]{:S(2)}) collective-permute-start(bf16[384,1152]{1,0:T(8,128)(2,1)S(1)} %add_convert_fusion.8), channel_id=1, source_target_pairs={{8,16},{16,8},{9,17},{17,9},{10,18},{18,10},{11,19},{19,11},{12,20... | collective-permute-start | bytes 2654216 | tf_op jit(solution)/shard_map/ppermute | solution.py:943
  815.5 37.9 %collective-permute-start.104 = (bf16[384,512]{1,0:T(8,128)(2,1)S(1)}, bf16[384,512]{1,0:T(8,128)(2,1)S(1)}, u32[]{:S(2)}, u32[]{:S(2)}) collective-permute-start(bf16[384,512]{1,0:T(8,128)(2,1)S(1)} %add_convert_fusion.22), channel_id=1, source_target_pairs={{8,0},{16,24},{9,1},{17,25},{10,2},{18,26},{11,3},{19,27},{12,4},{... | collective-permute-start | bytes 1179656 | tf_op jit(solution)/shard_map/ppermute | solution.py:944
  823.9 71.1 %collective-permute-start.125 = (bf16[384,1152]{1,0:T(8,128)(2,1)S(1)}, bf16[384,1152]{1,0:T(8,128)(2,1)S(1)}, u32[]{:S(2)}, u32[]{:S(2)}) collective-permute-start(bf16[384,1152]{1,0:T(8,128)(2,1)S(1)} %add_convert_fusion.9), channel_id=1, source_target_pairs={{8,0},{16,24},{9,1},{17,25},{10,2},{18,26},{11,3},{19,27},{12,4},{... | collective-permute-start | bytes 2654216 | tf_op jit(solution)/shard_map/ppermute | solution.py:944
  888.7 26.2 %collective-permute-start.133 = (bf16[1152,384]{1,0:T(8,128)(2,1)S(1)}, bf16[1152,384]{1,0:T(8,128)(2,1)S(1)}, u32[]{:S(2)}, u32[]{:S(2)}) collective-permute-start(bf16[1152,384]{1,0:T(8,128)(2,1)S(1)} %add_convert_fusion.5), channel_id=1, source_target_pairs={{8,0},{16,24},{9,1},{17,25},{10,2},{18,26},{11,3},{19,27},{12,4},{... | collective-permute-start | bytes 2654216 | tf_op jit(solution)/shard_map/ppermute | solution.py:944
  890.2 43.6 %collective-permute-start.121 = (bf16[384,1152]{1,0:T(8,128)(2,1)S(1)}, bf16[384,1152]{1,0:T(8,128)(2,1)S(1)}, u32[]{:S(2)}, u32[]{:S(2)}) collective-permute-start(bf16[384,1152]{1,0:T(8,128)(2,1)S(1)} %add_convert_fusion.11), channel_id=1, source_target_pairs={{8,0},{16,24},{9,1},{17,25},{10,2},{18,26},{11,3},{19,27},{12,4},{... | collective-permute-start | bytes 2654216 | tf_op jit(solution)/shard_map/ppermute | solution.py:944
  891.7 60.4 %collective-permute-start.129 = (bf16[384,1152]{1,0:T(8,128)(2,1)S(1)}, bf16[384,1152]{1,0:T(8,128)(2,1)S(1)}, u32[]{:S(2)}, u32[]{:S(2)}) collective-permute-start(bf16[384,1152]{1,0:T(8,128)(2,1)S(1)} %add_convert_fusion.7), channel_id=1, source_target_pairs={{8,0},{16,24},{9,1},{17,25},{10,2},{18,26},{11,3},{19,27},{12,4},{... | collective-permute-start | bytes 2654216 | tf_op jit(solution)/shard_map/ppermute | solution.py:944
  893.3 68.3 %collective-permute-start.137 = (bf16[1152,384]{1,0:T(8,128)(2,1)S(1)}, bf16[1152,384]{1,0:T(8,128)(2,1)S(1)}, u32[]{:S(2)}, u32[]{:S(2)}) collective-permute-start(bf16[1152,384]{1,0:T(8,128)(2,1)S(1)} %add_convert_fusion.3), channel_id=1, source_target_pairs={{8,0},{16,24},{9,1},{17,25},{10,2},{18,26},{11,3},{19,27},{12,4},{... | collective-permute-start | bytes 2654216 | tf_op jit(solution)/shard_map/ppermute | solution.py:944
  (196 other events, 2339.3 us)
Sparse Core Ops, SparseCore 0:
  616.8 51.2 all-reduce.1

commit v2 on v1

--- a/solution.py
+++ b/solution.py
@@ -434,8 +434,144 @@
     return jax.ShapeDtypeStruct(shape, dtype)
 
 
-def norm_uv_body(x0, x1, x2, x3, gain, w, keep, pass_on, u, v, scale):
-    parts = [r[...].astype(F32) for r in (x0, x1, x2, x3)]
+MESH_ID = pl.DeviceIdType.MESH
+
+
+def neighbour_x():
+    return {"row": 1 - lax.axis_index("row")}
+
+
+def neighbour_y():
+    return {"col": lax.rem(lax.axis_index("col") + 2, 4)}
+
+
+def greet():
+    barrier = pltpu.get_barrier_semaphore()
+    for device in (neighbour_x(), neighbour_y()):
+        pl.semaphore_signal(barrier, inc=1, device_id=device, device_id_type=MESH_ID)
+    pl.semaphore_wait(barrier, 2)
+
+
+def message(src, dst, device, sems, n):
+    send, recv = sems
+    return pltpu.make_async_remote_copy(
+        src_ref=src,
+        dst_ref=dst,
+        send_sem=send.at[n],
+        recv_sem=recv.at[n],
+        device_id=device,
+        device_id_type=MESH_ID,
+    )
+
+
+def scatter_messages(q1, q2, q3, r3, rx, ry, sems, base):
+    half = q1.shape[0] // 2
+    a, b = pl.ds(0, half), pl.ds(half, half)
+    x, y = neighbour_x(), neighbour_y()
+    plan = ((q3, r3, a, x), (q3, r3, b, y), (q1, rx, a, x), (q2, ry, a, y), (q2, ry, b, y), (q1, rx, b, x))
+    return [
+        message(src.at[at, :], dst.at[at, :], dev, sems, base + n)
+        for n, (src, dst, at, dev) in enumerate(plan)
+    ]
+
+
+def gather_messages(own, gx, gy, gd, sems, base):
+    half = own.shape[0] // 2
+    a, b = pl.ds(0, half), pl.ds(half, half)
+    x, y = neighbour_x(), neighbour_y()
+    plan = ((own, gx, a, x), (own, gy, a, y), (own, gx, b, x), (own, gy, b, y), (gx, gd, a, y), (gy, gd, b, x))
+    return [
+        message(src.at[at, :], dst.at[at, :], dev, sems, base + n)
+        for n, (src, dst, at, dev) in enumerate(plan)
+    ]
+
+
+def add_into(dst, src, start, rows):
+    step = 128
+    for r in range(start, start + rows, step):
+        at = slice(r, r + step)
+        dst[at, :] = (dst[at, :].astype(F32) + src[at, :].astype(F32)).astype(dst.dtype)
+
+
+def load_rows(near, far, dst, sem):
+    part = near.shape[1] // 2
+    row = lax.axis_index("row")
+    copies = []
+    for dy in (0, 1):
+        for dx in (0, 1):
+            start = pl.multiple_of(part * (row + dx - 2 * row * dx), part)
+            for dc, src in enumerate((near, far)):
+                at = ((dy * 2 + dx) * 2 + dc) * part
+                copies.append(
+                    pltpu.make_async_copy(
+                        src.at[dy, pl.ds(start, part), :], dst.at[pl.ds(at, part), :], sem.at[len(copies)]
+                    )
+                )
+    for c in copies:
+        c.start()
+    return copies
+
+
+def comm_params(n):
+    return pltpu.CompilerParams(
+        vmem_limit_bytes=VMEM_LIMIT,
+        dimension_semantics=("arbitrary",),
+        collective_id=n,
+        has_side_effects=True,
+    )
+
+
+def any_spec():
+    return pl.BlockSpec(memory_space=pl.ANY)
+
+
+def held_spec(block, width, last):
+    return pl.BlockSpec((block, width), lambda i: (jnp.minimum(i, last), 0))
+
+
+def full_spec(shape):
+    rank = len(shape)
+    return pl.BlockSpec(shape, lambda i: (0,) * rank)
+
+
+def row_sums(values):
+    return dot_nt(jnp.ones((8, values.shape[1]), F32), values, PRECISE)
+
+
+def as_column(lanes, width):
+    first = (lax.broadcasted_iota(jnp.int32, (8, width), 0) == 0).astype(F32)
+    return dot_tn(lanes, first, PRECISE)
+
+
+def norm_uv_body(blocks, own, gain, near, far, n1, u, v, scale, w, gx, gy, gd, load, send, recv):
+    i = pl.program_id(0)
+    gather = gather_messages(own, gx, gy, gd, (send, recv), 0)
+
+    @pl.when(i == 0)
+    def _():
+        greet()
+        for n in range(4):
+            gather[n].start()
+        copies = load_rows(near, far, w, load)
+        gather[0].wait_recv()
+        gather[4].start()
+        gather[3].wait_recv()
+        gather[5].start()
+        for c in copies:
+            c.wait()
+        gather[1].wait_recv()
+        gather[4].wait_recv()
+
+    @pl.when(i == blocks // 2)
+    def _():
+        gather[2].wait_recv()
+        gather[5].wait_recv()
+        for m in gather:
+            m.wait_send()
+
+    block = u.shape[0]
+    at = pl.ds(pl.multiple_of(i * block, block), block)
+    parts = [r[at, :].astype(F32) for r in (own, gx, gy, gd)]
     width = parts[0].shape[1]
     total = sum(jnp.sum(p * p, axis=1, keepdims=True) for p in parts)
     s = lax.rsqrt(total / D + EPSILON)
@@ -450,28 +586,30 @@
     v[...] = acc[:, channels:]
     for j in (0, 1):
         k, p = pair_up(normed[2 * j], normed[2 * j + 1])
-        keep[:, j * width : (j + 1) * width] = k.astype(BF)
-        pass_on[:, j * width : (j + 1) * width] = p.astype(BF)
-
-
-def norm_uv(chunks, gain, w):
-    rows, width = chunks[0].shape
-    channels = w.shape[1] // 2
+        n1[:, j * width : (j + 1) * width] = k.astype(BF)
+        n1[:, (j + 2) * width : (j + 3) * width] = p.astype(BF)
+
+
+def norm_uv(own, gain, near, far):
+    rows, width = own.shape
+    w = pltpu.VMEM((4 * width, near.shape[2]), BF)
+    channels = near.shape[2] // 2
     block = ROW_BLOCK
+    blocks = rows // block
     return pl.pallas_call(
-        norm_uv_body,
-        grid=(rows // block,),
-        in_specs=[rows_spec(block, width)] * 4 + [whole_spec(gain.shape), whole_spec(w.shape)],
-        out_specs=[rows_spec(block, 2 * width)] * 2
-        + [rows_spec(block, channels)] * 2
-        + [rows_spec(block, 1)],
-        out_shape=[sds((rows, 2 * width), BF)] * 2
-        + [sds((rows, channels), F32)] * 2
-        + [sds((rows, 1), F32)],
-        compiler_params=params(),
-        cost_estimate=cost(2 * rows * w.size, nbytes(w, *chunks) * 2),
+        functools.partial(norm_uv_body, blocks),
+        grid=(blocks,),
+        in_specs=[whole_spec(own.shape), whole_spec(gain.shape), any_spec(), any_spec()],
+        out_specs=[rows_spec(block, 4 * width)] + [rows_spec(block, channels)] * 2 + [rows_spec(block, 1)],
+        out_shape=[sds((rows, 4 * width), BF)] + [sds((rows, channels), F32)] * 2 + [sds((rows, 1), F32)],
+        scratch_shapes=[w]
+        + [pltpu.VMEM((rows, width), BF)] * 3
+        + [pltpu.SemaphoreType.DMA((8,))]
+        + [pltpu.SemaphoreType.DMA((6,))] * 2,
+        compiler_params=comm_params(1),
+        cost_estimate=cost(60 * rows * near.size, nbytes(near, far)),
         name="norm_uv",
-    )(*chunks, gain, w)
+    )(own, gain, near, far)
 
 
 def chain(entries, count):
@@ -482,13 +620,27 @@
 
 
 def recur_body(
-    ua, ub, border, off, taps, recall_w, admit_w, soft, conv, recall, admit, state, cum, ends, ext
+    heads, u, border, off, taps, recall_w, admit_w, soft, own, conv, recall, admit, state, cum, ends, gx, gy, gd, ext, send, recv
 ):
-    half = ua.shape[0]
-    rows = 2 * half
+    rows = u.shape[0]
+    gather = gather_messages(own, gx, gy, gd, (send, recv), 0)
+    h = pl.program_id(0)
+
+    @pl.when(h == 0)
+    def _():
+        greet()
+        for n in range(4):
+            gather[n].start()
+
+    @pl.when(h == heads - 1)
+    def _():
+        gather[0].wait_recv()
+        gather[4].start()
+        gather[3].wait_recv()
+        gather[5].start()
+
     ext[0:8, :] = border[...]
-    ext[8 : 8 + half, :] = ua[...]
-    ext[8 + half : 8 + rows, :] = ub[...]
+    ext[8 : 8 + rows, :] = u[...]
     step = ROW_BLOCK
     for r in range(0, rows, step):
         o = off[8 + r : 8 + r + step, :]
@@ -530,171 +682,348 @@
     ends[1:2, :] = carry_h
     ends[2:8, :] = jnp.zeros((6, 128), F32)
 
-
-def recur(ua, ub, border, off, taps, recall_w, admit_w, soft):
-    half, channels = ua.shape
-    rows = 2 * half
+    @pl.when(pl.program_id(0) == heads - 1)
+    def _():
+        for n in (1, 2, 4, 5):
+            gather[n].wait_recv()
+        for m in gather:
+            m.wait_send()
+
+
+def recur(u, border, off, taps, recall_w, admit_w, soft, own):
+    rows, channels = u.shape
     heads = channels // 128
     gate = pl.BlockSpec((1, 128, 128), lambda h: (h, 0, 0))
     full = sds((rows, channels), F32)
     return pl.pallas_call(
-        recur_body,
+        functools.partial(recur_body, heads),
         grid=(heads,),
         in_specs=[
-            head_spec(half),
-            head_spec(half),
+            head_spec(rows),
             head_spec(8),
             whole_spec(off.shape),
             head_spec(KW),
             gate,
             gate,
             head_spec(1),
+            whole_spec(own.shape),
         ],
-        out_specs=[head_spec(rows)] * 5 + [head_spec(8)],
-        out_shape=[full] * 5 + [sds((8, channels), F32)],
-        scratch_shapes=[pltpu.VMEM((rows + 8, 128), F32)],
-        compiler_params=params(),
+        out_specs=[head_spec(rows)] * 5 + [head_spec(8)] + [any_spec()] * 3,
+        out_shape=[full] * 5 + [sds((8, channels), F32)] + [sds(own.shape, BF)] * 3,
+        scratch_shapes=[pltpu.VMEM((rows + 8, 128), F32)] + [pltpu.SemaphoreType.DMA((6,))] * 2,
+        compiler_params=comm_params(5),
         cost_estimate=cost(rows * channels * 128 * 24, rows * channels * 4 * 6, rows * channels * 6),
         name="recur",
-    )(ua, ub, border, off, taps, recall_w, admit_w, soft)
-
-
-def mix_body(count, local, cum, v, entries, w, states, mixed, q0, q1, q2, q3):
-    entering = chain(entries, count)
-    st = local[...] + cum[...] * entering
-    states[...] = st
-    act = gelu_pair(v[...])[0]
-    m = (st * act).astype(BF)
-    mixed[...] = m
-    width = q0.shape[1]
-    for j, q in enumerate((q0, q1, q2, q3)):
-        q[...] = dot_nn(m, w[:, j * width : (j + 1) * width]).astype(q.dtype)
-
-
-def mix(half_index, local, cum, v, entries, w):
+    )(u, border, off, taps, recall_w, admit_w, soft, own)
+
+
+def mix_body(
+    count, blocks, local, cum, v, x, entries, w, states, mixed, x2, own, gx, gy, gd, q0, q1, q2, q3, r3, rx, ry, send, recv
+):
+    i = pl.program_id(0)
+    sems = (send, recv)
+    scatter = scatter_messages(q1, q2, q3, r3, rx, ry, sems, 0)
+    gather = gather_messages(own, gx, gy, gd, sems, 6)
+    block = local.shape[0]
+    width = x.shape[1]
+    rows = x.shape[0]
+    half = rows // 2
+
+    @pl.when(i == 0)
+    def _():
+        greet()
+
+    @pl.when(i < blocks)
+    def _():
+        entering = chain(entries, count)
+        st = local[...] + cum[...] * entering
+        states[...] = st
+        m = (st * gelu_pair(v[...])[0]).astype(BF)
+        mixed[...] = m
+        at = pl.ds(pl.multiple_of(i * block, block), block)
+        for j, q in ((3, q3), (1, q1), (2, q2), (0, q0)):
+            q[at, :] = dot_nn(m, w[:, j * width : (j + 1) * width]).astype(q.dtype)
+
+    @pl.when(i == blocks // 2 - 1)
+    def _():
+        scatter[0].start()
+        scatter[2].start()
+
+    @pl.when(i == blocks - 1)
+    def _():
+        scatter[1].start()
+
+    @pl.when(i == blocks)
+    def _():
+        scatter[0].wait_recv()
+        add_into(q2, r3, 0, half)
+        scatter[3].start()
+        scatter[4].start()
+        scatter[1].wait_recv()
+        add_into(q1, r3, half, half)
+        scatter[5].start()
+        for base, first in ((0, 2), (half, 4)):
+            scatter[first].wait_recv()
+            scatter[first + 1].wait_recv()
+            for r in range(base, base + half, 128):
+                at = slice(r, r + 128)
+                total = x[at, :] + q0[at, :] + rx[at, :].astype(F32) + ry[at, :].astype(F32)
+                x2[at, :] = total
+                own[at, :] = total.astype(BF)
+            start = 0 if base == 0 else 2
+            gather[start].start()
+            gather[start + 1].start()
+        gather[0].wait_recv()
+        gather[4].start()
+        gather[3].wait_recv()
+        gather[5].start()
+        for n in (1, 2, 4, 5):
+            gather[n].wait_recv()
+        for m in scatter + gather:
+            m.wait_send()
+
+
+def mix(local, cum, v, x, entries, w):
     rows, channels = v.shape
     width = w.shape[1] // 4
     block = ROW_BLOCK
-    start = half_index * (rows // block)
+    blocks = rows // block
+    held = functools.partial(held_spec, block, last=blocks - 1)
+    chunk = pltpu.VMEM((rows, width), BF)
     return pl.pallas_call(
-        functools.partial(mix_body, entries.shape[0] // 8),
-        grid=(rows // block,),
-        in_specs=[rows_spec(block, channels, start)] * 2
-        + [rows_spec(block, channels), whole_spec(entries.shape), whole_spec(w.shape)],
-        out_specs=[rows_spec(block, channels)] * 2 + [rows_spec(block, width)] * 4,
+        functools.partial(mix_body, entries.shape[0] // 8, blocks),
+        grid=(blocks + 1,),
+        in_specs=[held(channels)] * 3
+        + [whole_spec(x.shape), whole_spec(entries.shape), whole_spec(w.shape)],
+        out_specs=[held(channels)] * 2 + [full_spec((rows, width))] * 2 + [any_spec()] * 3,
         out_shape=[sds((rows, channels), F32), sds((rows, channels), BF), sds((rows, width), F32)]
-        + [sds((rows, width), BF)] * 3,
-        compiler_params=params(),
-        cost_estimate=cost(2 * rows * w.size, rows * channels * 18 + nbytes(w)),
+        + [sds((rows, width), BF)] * 4,
+        scratch_shapes=[pltpu.VMEM((rows, width), F32)]
+        + [chunk] * 6
+        + [pltpu.SemaphoreType.DMA((12,))] * 2,
+        compiler_params=comm_params(2),
+        cost_estimate=cost(40 * rows * w.size, rows * channels * 18 + nbytes(w)),
         name="mix",
-    )(local, cum, v, entries, w)
-
-
-def feed_body(*refs):
-    (x0, x1, x2, x3, e0, e1, e2, e3, gain, wgu, wd) = refs[:11]
-    (keep, pass_on, hid, eg, eu, ekeep, epass, scale, dots) = refs[11:20]
-    outs, backs = refs[20:24], refs[24:28]
-    parts = [r[...].astype(F32) for r in (x0, x1, x2, x3)]
-    width = parts[0].shape[1]
-    total = sum(jnp.sum(p * p, axis=1, keepdims=True) for p in parts)
-    s = lax.rsqrt(total / D + EPSILON)
-    scale[...] = s
-    normed = [p * s * gain[1:2, j * width : (j + 1) * width] for j, p in enumerate(parts)]
-    acc = None
-    for j, n in enumerate(normed):
-        term = dot_nn(n.astype(BF), wgu[j * width : (j + 1) * width, :])
-        acc = term if acc is None else acc + term
-    for j in (0, 1):
-        k, p = pair_up(normed[2 * j], normed[2 * j + 1])
-        keep[:, j * width : (j + 1) * width] = k.astype(BF)
-        pass_on[:, j * width : (j + 1) * width] = p.astype(BF)
-    errs = [r[...] for r in (e0, e1, e2, e3)]
-    wide = [e.astype(F32) for e in errs]
-    for j in (0, 1):
-        k, p = pair_up(wide[2 * j], wide[2 * j + 1])
-        ekeep[:, j * width : (j + 1) * width] = k.astype(BF)
-        epass[:, j * width : (j + 1) * width] = p.astype(BF)
+    )(local, cum, v, x, entries, w)
+
+
+def feed_body(blocks, *refs):
+    (x0, x1, x2, x3, e0, e1, e2, e3, mid, cot, gain, near, far, wd) = refs[:14]
+    outs = refs[14:18]
+    (dx, own, gx, gy, gd, gain_grad, g_down, g_gu) = refs[18:26]
+    (wgu, load, n2, hid, ee, err, scale) = refs[26:33]
+    (q0, q1, q2, q3, r3, rx, ry, dots, dots_x, dots_y, send, recv) = refs[33:]
+    i = pl.program_id(0)
+    sems = (send, recv)
+    scatter = scatter_messages(q1, q2, q3, r3, rx, ry, sems, 0)
+    gather = gather_messages(own, gx, gy, gd, sems, 6)
+    small_x = message(dots, dots_x, neighbour_x(), sems, 12)
+    small_y = message(dots_x, dots_y, neighbour_y(), sems, 13)
+    block, width = x0.shape
+    rows = mid.shape[0]
+    half = rows // 2
     units = hid.shape[1]
-    pre, up = acc[:, :units], acc[:, units:]
-    act, slope = gelu_pair(pre)
-    h = (act * up).astype(BF)
-    hid[...] = h
-    dh = None
-    for j, e in enumerate(errs):
-        term = dot_nt(e, wd[:, j * width : (j + 1) * width])
-        dh = term if dh is None else dh + term
-    g = (dh * up * slope).astype(BF)
-    b = (dh * act).astype(BF)
-    eg[...] = g
-    eu[...] = b
-    dots[...] = jnp.sum(g.astype(F32) * pre + b.astype(F32) * up, axis=1, keepdims=True)
-    for j, q in enumerate(backs):
-        q[...] = (
-            dot_nt(g, wgu[j * width : (j + 1) * width, :units])
-            + dot_nt(b, wgu[j * width : (j + 1) * width, units:])
-        ).astype(q.dtype)
-    for j, q in enumerate(outs):
-        q[...] = dot_nn(h, wd[:, j * width : (j + 1) * width]).astype(q.dtype)
-
-
-def feed(chunks, errs, gain, wgu, wd):
+
+    @pl.when(i == 0)
+    def _():
+        copies = load_rows(near, far, wgu, load)
+        greet()
+        for c in copies:
+            c.wait()
+
+    @pl.when(i < blocks)
+    def _():
+        at = pl.ds(pl.multiple_of(i * block, block), block)
+        parts = [r[...].astype(F32) for r in (x0, x1, x2, x3)]
+        total = sum(jnp.sum(p * p, axis=1, keepdims=True) for p in parts)
+        s = lax.rsqrt(total / D + EPSILON)
+        scale[at, :] = s
+        normed = [p * s * gain[1:2, j * width : (j + 1) * width] for j, p in enumerate(parts)]
+        acc = None
+        for j, n in enumerate(normed):
+            term = dot_nn(n.astype(BF), wgu[j * width : (j + 1) * width, :])
+            acc = term if acc is None else acc + term
+        errs = [r[...] for r in (e0, e1, e2, e3)]
+        wide = [e.astype(F32) for e in errs]
+        for source, target in ((normed, n2), (wide, ee)):
+            for j in (0, 1):
+                k, p = pair_up(source[2 * j], source[2 * j + 1])
+                target[at, j * width : (j + 1) * width] = k.astype(BF)
+                target[at, (j + 2) * width : (j + 3) * width] = p.astype(BF)
+        pre, up = acc[:, :units], acc[:, units:]
+        act, slope = gelu_pair(pre)
+        h = (act * up).astype(BF)
+        hid[at, :] = h
+        dh = None
+        for j, e in enumerate(errs):
+            term = dot_nt(e, wd[:, j * width : (j + 1) * width])
+            dh = term if dh is None else dh + term
+        g = (dh * up * slope).astype(BF)
+        b = (dh * act).astype(BF)
+        err[at, :units] = g
+        err[at, units:] = b
+        dots[:, at] = row_sums(g.astype(F32) * pre + b.astype(F32) * up)
+        for j, q in ((3, q3), (1, q1), (2, q2), (0, q0)):
+            rows_w = slice(j * width, (j + 1) * width)
+            q[at, :] = (dot_nt(g, wgu[rows_w, :units]) + dot_nt(b, wgu[rows_w, units:])).astype(q.dtype)
+        for j, q in enumerate(outs):
+            q[...] = dot_nn(h, wd[:, j * width : (j + 1) * width]).astype(q.dtype)
+
+    @pl.when(i == blocks // 2 - 1)
+    def _():
+        scatter[0].start()
+        scatter[2].start()
+
+    @pl.when(i == blocks - 1)
+    def _():
+        scatter[1].start()
+        small_x.start()
+
+    @pl.when(i == blocks)
+    def _():
+        scatter[0].wait_recv()
+        add_into(q2, r3, 0, half)
+        scatter[3].start()
+        scatter[4].start()
+        small_x.wait_recv()
+        dots_x[...] = dots_x[...] + dots[...]
+        small_y.start()
+
+    @pl.when(i == blocks + 1)
+    def _():
+        scatter[1].wait_recv()
+        add_into(q1, r3, half, half)
+        scatter[5].start()
+
+    def finish(base, first, start):
+        scatter[first].wait_recv()
+        scatter[first + 1].wait_recv()
+        sum_grad = None
+        for r in range(base, base + half, 128):
+            at = slice(r, r + 128)
+            d = q0[at, :] + rx[at, :].astype(F32) + ry[at, :].astype(F32)
+            s, m = scale[at, :], mid[at, :]
+            t = as_column(dots_x[:, at] + dots_y[:, at], width)
+            new = cot[at, :] + s * own_gain * d - m * (s * s) * t * (1.0 / D)
+            dx[at, :] = new
+            own[at, :] = new.astype(BF)
+            term = jnp.sum(d * m * s, axis=0, keepdims=True)
+            sum_grad = term if sum_grad is None else sum_grad + term
+        gather[start].start()
+        gather[start + 1].start()
+        return sum_grad
+
+    own_gain = gain[1:2, :width]
+
+    @pl.when(i == blocks + 2)
+    def _():
+        small_y.wait_recv()
+        gain_grad[0:1, :] = finish(0, 2, 0)
+
+    @pl.when(i == blocks + 4)
+    def _():
+        gain_grad[0:1, :] = gain_grad[0:1, :] + finish(half, 4, 2)
+
+    @pl.when(i == blocks + 5)
+    def _():
+        gather[0].wait_recv()
+        gather[4].start()
+
+    @pl.when(i == blocks + 6)
+    def _():
+        gather[3].wait_recv()
+        gather[5].start()
+
+    tiles = units // width
+
+    @pl.when((i >= blocks) & (i < blocks + tiles))
+    def _():
+        at = pl.ds(pl.multiple_of((i - blocks) * width, width), width)
+        g_down[...] = dot_tn(hid[:, at], ee[...]).astype(BF)
+
+    @pl.when((i >= blocks + tiles) & (i < blocks + tiles + 4))
+    def _():
+        at = pl.ds(pl.multiple_of((i - blocks - tiles) * width, width), width)
+        g_gu[...] = dot_tn(n2[:, at], err[...]).astype(BF)
+
+    @pl.when(i == blocks + tiles + 4)
+    def _():
+        for n in (1, 2, 4, 5):
+            gather[n].wait_recv()
+        for m in scatter + gather + [small_x, small_y]:
+            m.wait_send()
+
+
+def feed(chunks, errs, mid, cot, gain, near, far, wd):
     rows, width = chunks[0].shape
     units = wd.shape[0]
     block = ROW_BLOCK
-    quarters = [sds((rows, width), F32)] + [sds((rows, width), BF)] * 3
+    blocks = rows // block
+    tiles = units // width
+    held = functools.partial(held_spec, block, last=blocks - 1)
+    chunk = pltpu.VMEM((rows, width), BF)
+    lanes = pltpu.VMEM((8, rows), F32)
+    down_spec = pl.BlockSpec((width, 4 * width), lambda i: (jnp.clip(i - blocks, 0, tiles - 1), 0))
+    gu_spec = pl.BlockSpec((width, 2 * units), lambda i: (jnp.clip(i - blocks - tiles, 0, 3), 0))
     return pl.pallas_call(
-        feed_body,
-        grid=(rows // block,),
-        in_specs=[rows_spec(block, width)] * 8
-        + [whole_spec(gain.shape), whole_spec(wgu.shape), whole_spec(wd.shape)],
-        out_specs=[rows_spec(block, 2 * width)] * 2
-        + [rows_spec(block, units)] * 3
-        + [rows_spec(block, 2 * width)] * 2
-        + [rows_spec(block, 1)] * 2
-        + [rows_spec(block, width)] * 8,
-        out_shape=[sds((rows, 2 * width), BF)] * 2
-        + [sds((rows, units), BF)] * 3
-        + [sds((rows, 2 * width), BF)] * 2
-        + [sds((rows, 1), F32)] * 2
-        + quarters
-        + quarters,
-        compiler_params=params(),
-        cost_estimate=cost(
-            4 * rows * (wgu.size + wd.size), nbytes(wgu, wd) + rows * 30000, rows * units
-        ),
+        functools.partial(feed_body, blocks),
+        grid=(blocks + tiles + 5,),
+        in_specs=[held(width)] * 8
+        + [whole_spec(mid.shape), whole_spec(cot.shape), whole_spec(gain.shape)]
+        + [any_spec(), any_spec(), whole_spec(wd.shape)],
+        out_specs=[held(width)] * 4
+        + [whole_spec((rows, width))] * 2
+        + [any_spec()] * 3
+        + [whole_spec((8, width)), down_spec, gu_spec],
+        out_shape=[sds((rows, width), F32)]
+        + [sds((rows, width), BF)] * 3
+        + [sds((rows, width), F32)]
+        + [sds((rows, width), BF)] * 4
+        + [sds((8, width), F32), sds((units, 4 * width), BF), sds((4 * width, 2 * units), BF)],
+        scratch_shapes=[
+            pltpu.VMEM((4 * width, 2 * units), BF),
+            pltpu.SemaphoreType.DMA((8,)),
+            pltpu.VMEM((rows, 4 * width), BF),
+            pltpu.VMEM((rows, units), BF),
+            pltpu.VMEM((rows, 4 * width), BF),
+            pltpu.VMEM((rows, 2 * units), BF),
+            pltpu.VMEM((rows, 1), F32),
+            pltpu.VMEM((rows, width), F32),
+        ]
+        + [chunk] * 6
+        + [lanes] * 3
+        + [pltpu.SemaphoreType.DMA((14,))] * 2,
+        compiler_params=comm_params(3),
+        cost_estimate=cost(48 * rows * wd.size, 3 * nbytes(wd) + rows * 30000, rows * units),
         name="feed",
-    )(*chunks, *errs, gain, wgu, wd)
+    )(*chunks, *errs, mid, cot, gain, near, far, wd)
 
 
 def adjoint_body(*refs):
-    ea, eb = refs[0:4], refs[4:8]
-    (w, sa, sb, va, vb, recall, off, soft) = refs[8:16]
-    (part, reach, eva, evb, ends, keep, pass_on, ext) = refs[16:]
-    half = sa.shape[0]
-    rows = 2 * half
-    width = ea[0].shape[1]
+    errs = refs[0:4]
+    (w, states, branch, recall, off, soft) = refs[4:10]
+    (part, reach, ev, ends, paired, ext) = refs[10:]
+    rows = states.shape[0]
+    width = errs[0].shape[1]
     step = ROW_BLOCK
 
     @pl.when(pl.program_id(0) == 0)
     def _():
-        for group, base in ((ea, 0), (eb, half)):
+        for r in range(0, rows, step):
+            at = slice(r, r + step)
             for j in (0, 1):
-                k, p = pair_up(group[2 * j][...].astype(F32), group[2 * j + 1][...].astype(F32))
-                at = (slice(base, base + half), slice(j * width, (j + 1) * width))
-                keep[at] = k.astype(BF)
-                pass_on[at] = p.astype(BF)
+                k, p = pair_up(errs[2 * j][at, :].astype(F32), errs[2 * j + 1][at, :].astype(F32))
+                paired[at, j * width : (j + 1) * width] = k.astype(BF)
+                paired[at, (j + 2) * width : (j + 3) * width] = p.astype(BF)
 
     for r in range(0, rows, step):
         o = off[8 + r : 8 + r + step, :]
         ell = -8.0 * recall[r : r + step, :] * soft[0:1, :]
         ext[r : r + step, :] = jnp.where(o > 0, jnp.exp(ell), 0.0)
-        group, states, branch, ev, base = (
-            (ea, sa, va, eva, r) if r < half else (eb, sb, vb, evb, r - half)
-        )
-        at = slice(base, base + step)
+        at = slice(r, r + step)
         dm = None
         for j in range(4):
-            term = dot_nt(group[j][at, :], w[:, j * width : (j + 1) * width])
+            term = dot_nt(errs[j][at, :], w[:, j * width : (j + 1) * width])
             dm = term if dm is None else dm + term
         act, slope = gelu_pair(branch[at, :])
         ev[at, :] = (dm * states[at, :] * slope).astype(BF)
@@ -731,44 +1060,35 @@
 
 
 def adjoint(errs, w, states, branch, recall, off, soft):
-    half, channels = states[0].shape
-    rows = 2 * half
-    width = errs[0][0].shape[1]
+    rows, channels = states.shape
+    width = errs[0].shape[1]
     return pl.pallas_call(
         adjoint_body,
         grid=(channels // 128,),
-        in_specs=[whole_spec((half, width))] * 8
+        in_specs=[whole_spec((rows, width))] * 4
         + [pl.BlockSpec((128, w.shape[1]), lambda h: (h, 0))]
-        + [head_spec(half)] * 4
-        + [head_spec(rows), whole_spec(off.shape), head_spec(1)],
-        out_specs=[head_spec(rows)] * 2
-        + [head_spec(half)] * 2
-        + [head_spec(8)]
-        + [whole_spec((rows, 2 * width))] * 2,
+        + [head_spec(rows)] * 3
+        + [whole_spec(off.shape), head_spec(1)],
+        out_specs=[head_spec(rows)] * 3 + [head_spec(8), whole_spec((rows, 4 * width))],
         out_shape=[sds((rows, channels), F32)] * 2
-        + [sds((half, channels), BF)] * 2
-        + [sds((8, channels), F32)]
-        + [sds((rows, 2 * width), BF)] * 2,
+        + [sds((rows, channels), BF), sds((8, channels), F32), sds((rows, 4 * width), BF)],
         scratch_shapes=[pltpu.VMEM((rows + 8, 128), F32)],
         compiler_params=params(),
         cost_estimate=cost(2 * rows * w.size, rows * channels * 20 + rows * D * 6, rows * channels * 3),
         name="adjoint",
-    )(*errs[0], *errs[1], w, *states, *branch, recall, off, soft)
+    )(*errs, w, states, branch, recall, off, soft)
 
 
 def recur_back_body(count, *refs):
-    (part, reach, later, earlier, sa, sb, conv, recall, admit, off) = refs[:10]
-    (ua, ub, border, taps, recall_w, admit_w, soft) = refs[10:17]
-    (du, out_border, grad_recall, grad_admit, grad_small, st, uext, dc) = refs[17:]
-    half = sa.shape[0]
-    rows = 2 * half
+    (part, reach, later, earlier, states, conv, recall, admit, off) = refs[:9]
+    (u, border, taps, recall_w, admit_w, soft) = refs[9:15]
+    (du, out_border, grad_recall, grad_admit, grad_small, st, uext, dc) = refs[15:]
+    rows = states.shape[0]
     step = ROW_BLOCK
     st[0:8, :] = jnp.broadcast_to(chain(earlier, count), (8, 128))
-    st[8 : 8 + half, :] = sa[...]
-    st[8 + half : 8 + rows, :] = sb[...]
+    st[8 : 8 + rows, :] = states[...]
     uext[0:8, :] = border[...]
-    uext[8 : 8 + half, :] = ua[...]
-    uext[8 + half : 8 + rows, :] = ub[...]
+    uext[8 : 8 + rows, :] = u[...]
     incoming = chain(later, count)
     sp = soft[0:1, :]
     dc[0:8, :] = jnp.zeros((8, 128), F32)
@@ -825,7 +1145,6 @@
 
 def recur_back(part, reach, later, earlier, states, conv, recall, admit, off, u, border, taps, rw, aw, soft):
     rows, channels = part.shape
-    half = rows // 2
     heads = channels // 128
     gate = pl.BlockSpec((1, 128, 128), lambda h: (h, 0, 0))
     return pl.pallas_call(
@@ -836,14 +1155,12 @@
             head_spec(rows),
             head_spec(later.shape[0]),
             head_spec(earlier.shape[0]),
-            head_spec(half),
-            head_spec(half),
+            head_spec(rows),
             head_spec(rows),
             head_spec(rows),
             head_spec(rows),
             whole_spec(off.shape),
-            head_spec(half),
-            head_spec(half),
+            head_spec(rows),
             head_spec(8),
             head_spec(KW),
             gate,
@@ -866,68 +1183,310 @@
         compiler_params=params(),
         cost_estimate=cost(rows * channels * 128 * 48, rows * channels * 36, rows * channels * 4),
         name="recur_back",
-    )(part, reach, later, earlier, *states, conv, recall, admit, off, *u, border, taps, rw, aw, soft)
-
-
-def enter_back_body(last, du, tail, ev, u, v, w, eu, dots, q0, q1, q2, q3):
-    d = du[...]
-    if last:
-        rows = d.shape[0]
-        extra = jnp.concatenate([jnp.zeros((rows - 8, d.shape[1]), F32), tail[...]], axis=0)
-        at_end = pl.program_id(0) == pl.num_programs(0) - 1
-        d = d + jnp.where(at_end, extra, 0.0)
-    e = d.astype(BF)
-    eu[...] = e
-    b = ev[...]
-    dots[...] = jnp.sum(e.astype(F32) * u[...] + b.astype(F32) * v[...], axis=1, keepdims=True)
-    channels = e.shape[1]
-    width = q0.shape[1]
-    for j, q in enumerate((q0, q1, q2, q3)):
-        q[...] = (
-            dot_nt(e, w[j * width : (j + 1) * width, :channels])
-            + dot_nt(b, w[j * width : (j + 1) * width, channels:])
-        ).astype(q.dtype)
-
-
-def enter_back(half_index, du, tail, ev, u, v, w):
+    )(part, reach, later, earlier, states, conv, recall, admit, off, u, border, taps, rw, aw, soft)
+
+
+def enter_back_body(blocks, *refs):
+    (du, tail, ev, u, v, near, far, scale, x, dx, gain) = refs[:11]
+    (eu, grad, gain_grad) = refs[11:14]
+    (w, load, q0, q1, q2, q3, r3, rx, ry, dots, dots_x, dots_y, send, recv) = refs[14:]
+    i = pl.program_id(0)
+    sems = (send, recv)
+    scatter = scatter_messages(q1, q2, q3, r3, rx, ry, sems, 0)
+    small_x = message(dots, dots_x, neighbour_x(), sems, 6)
+    small_y = message(dots_x, dots_y, neighbour_y(), sems, 7)
+    block, channels = du.shape
+    rows, width = x.shape
+    half = rows // 2
+
+    @pl.when(i == 0)
+    def _():
+        copies = load_rows(near, far, w, load)
+        greet()
+        for c in copies:
+            c.wait()
+
+    @pl.when(i < blocks)
+    def _():
+        at = pl.ds(pl.multiple_of(i * block, block), block)
+        d = du[...]
+        extra = jnp.concatenate([jnp.zeros((block - 8, channels), F32), tail[...]], axis=0)
+        d = d + jnp.where(i == blocks - 1, extra, 0.0)
+        e = d.astype(BF)
+        eu[...] = e
+        b = ev[...]
+        dots[:, at] = row_sums(e.astype(F32) * u[...] + b.astype(F32) * v[...])
+        for j, q in ((3, q3), (1, q1), (2, q2), (0, q0)):
+            rows_w = slice(j * width, (j + 1) * width)
+            q[at, :] = (dot_nt(e, w[rows_w, :channels]) + dot_nt(b, w[rows_w, channels:])).astype(q.dtype)
+
+    @pl.when(i == blocks // 2 - 1)
+    def _():
+        scatter[0].start()
+        scatter[2].start()
+
+    @pl.when(i == blocks - 1)
+    def _():
+        scatter[1].start()
+        small_x.start()
+
+    @pl.when(i == blocks)
+    def _():
+        scatter[0].wait_recv()
+        add_into(q2, r3, 0, half)
+        scatter[3].start()
+        scatter[4].start()
+        small_x.wait_recv()
+        dots_x[...] = dots_x[...] + dots[...]
+        small_y.start()
+        scatter[1].wait_recv()
+        add_into(q1, r3, half, half)
+        scatter[5].start()
+        small_y.wait_recv()
+        sum_grad = None
+        for base, first in ((0, 2), (half, 4)):
+            scatter[first].wait_recv()
+            scatter[first + 1].wait_recv()
+            for r in range(base, base + half, 128):
+                at = slice(r, r + 128)
+                d = q0[at, :] + rx[at, :].astype(F32) + ry[at, :].astype(F32)
+                s, m = scale[at, :], x[at, :]
+                t = as_column(dots_x[:, at] + dots_y[:, at], width)
+                grad[at, :] = dx[at, :] + s * gain[0:1, :width] * d - m * (s * s) * t * (1.0 / D)
+                term = jnp.sum(d * m * s, axis=0, keepdims=True)
+                sum_grad = term if sum_grad is None else sum_grad + term
+        gain_grad[0:1, :] = sum_grad
+        for m in scatter + [small_x, small_y]:
+            m.wait_send()
+
+
+def enter_back(du, tail, ev, u, v, near, far, scale, x, dx, gain):
     rows, channels = u.shape
-    width = w.shape[0] // 4
+    width = x.shape[1]
     block = ROW_BLOCK
-    start = half_index * (rows // block)
+    blocks = rows // block
+    held = functools.partial(held_spec, block, last=blocks - 1)
+    chunk = pltpu.VMEM((rows, width), BF)
+    lanes = pltpu.VMEM((8, rows), F32)
     return pl.pallas_call(
-        functools.partial(enter_back_body, half_index == 1),
-        grid=(rows // block,),
-        in_specs=[rows_spec(block, channels, start), whole_spec(tail.shape)]
-        + [rows_spec(block, channels)] * 3
-        + [whole_spec(w.shape)],
-        out_specs=[rows_spec(block, channels), rows_spec(block, 1)] + [rows_spec(block, width)] * 4,
-        out_shape=[sds((rows, channels), BF), sds((rows, 1), F32), sds((rows, width), F32)]
-        + [sds((rows, width), BF)] * 3,
-        compiler_params=params(),
-        cost_estimate=cost(2 * rows * w.size, rows * channels * 16 + nbytes(w)),
+        functools.partial(enter_back_body, blocks),
+        grid=(blocks + 1,),
+        in_specs=[held(channels), whole_spec(tail.shape)]
+        + [held(channels)] * 3
+        + [any_spec(), any_spec(), whole_spec(scale.shape), whole_spec(x.shape), whole_spec(dx.shape)]
+        + [whole_spec(gain.shape)],
+        out_specs=[held(channels), whole_spec((rows, width)), whole_spec((8, width))],
+        out_shape=[sds((rows, channels), BF), sds((rows, width), F32), sds((8, width), F32)],
+        scratch_shapes=[pltpu.VMEM((4 * width, 2 * channels), BF), pltpu.SemaphoreType.DMA((8,))]
+        + [pltpu.VMEM((rows, width), F32)]
+        + [chunk] * 6
+        + [lanes] * 3
+        + [pltpu.SemaphoreType.DMA((8,))] * 2,
+        compiler_params=comm_params(4),
+        cost_estimate=cost(40 * rows * near.size, rows * channels * 16 + nbytes(near, far)),
         name="enter_back",
-    )(du, tail, ev, u, v, w)
-
-
-def outer_body(la, lb, ra, rb, out):
-    out[...] = (dot_tn(la[...], ra[...]) + dot_tn(lb[...], rb[...])).astype(out.dtype)
-
-
-def outer(left, right):
-    rows, m = left[0].shape
-    n = right[0].shape[1]
-    block = 256 if m % 256 == 0 else 128
-    lhs = pl.BlockSpec((rows, block), lambda i: (0, i))
+    )(du, tail, ev, u, v, near, far, scale, x, dx, gain)
+
+
+def neighbour_core():
+    col = lax.axis_index("col")
+    return {"col": col + 1 - 2 * lax.rem(col, 2)}
+
+
+def neighbour_end():
+    seq = lax.axis_index("seq")
+    return {"seq": seq + 1 - 2 * lax.rem(seq, 2)}
+
+
+def neighbour_middle():
+    return {"seq": 3 - lax.axis_index("seq")}
+
+
+def plus_in(dst, src, rows, start=0):
+    step = 64
+    for r in range(start, start + rows, step):
+        at = slice(r, min(r + step, start + rows))
+        dst[at, :] = (dst[at, :].astype(F32) + src[at, :].astype(F32)).astype(dst.dtype)
+
+
+def tail_body(n1, eu, ev, mixed, er, small, mine_in, far_in, mine_out, far_out, small_out, *scratch):
+    (s_in, p_in, c_in, a_in, b_in, y_in, s_out, p_out, c_out, a_out, b_out, y_out) = scratch[:12]
+    (s_sm, c_sm, a_sm, b_sm, send, recv) = scratch[12:]
+    sems = (send, recv)
+    width = er.shape[1] // 4
+    half = width // 2
+    channels = eu.shape[1]
+    seq = lax.axis_index("seq")
+    middle = (seq == 1) | (seq == 2)
+    end = (seq == 0) | (seq == 3)
+    barrier = pltpu.get_barrier_semaphore()
+    for device in (neighbour_core(), neighbour_y(), neighbour_end(), neighbour_middle()):
+        pl.semaphore_signal(barrier, inc=1, device_id=device, device_id_type=MESH_ID)
+    pl.semaphore_wait(barrier, 4)
+
+    a, b = pl.ds(0, half), pl.ds(half, half)
+    c, d = pl.ds(2 * half, half), pl.ds(3 * half, half)
+    everything = pl.ds(0, s_sm.shape[0])
+    lanes_far, lanes_own = pl.ds(width, width), pl.ds(0, width)
+    group_in, group_out, group_sm = (s_in, a_in, b_in), (s_out, a_out, b_out), (s_sm, a_sm, b_sm)
+    views = [
+        [r.at[everything, :] for r in group_sm],
+        [r.at[:, lanes_far] for r in group_out],
+        [r.at[:, lanes_own] for r in group_out],
+        [r.at[c, :] for r in group_in],
+        [r.at[d, :] for r in group_in],
+        [r.at[a, :] for r in group_in],
+        [r.at[b, :] for r in group_in],
+    ]
+    count = len(views)
+    to_end = [message(s, z1, neighbour_end(), sems, n) for n, (s, z1, z2) in enumerate(views)]
+    to_middle = [message(s, z2, neighbour_middle(), sems, count + n) for n, (s, z1, z2) in enumerate(views)]
+    base = 2 * count
+    core_sm = message(small, c_sm, neighbour_core(), sems, base)
+    core_out = message(p_out, c_out, neighbour_core(), sems, base + 1)
+    core_in = [
+        message(p_in.at[at, :], c_in.at[at, :], neighbour_core(), sems, base + 2 + n)
+        for n, at in enumerate((c, d, a, b))
+    ]
+    y_out_m = message(s_out.at[:, lanes_far], y_out, neighbour_y(), sems, base + 6)
+    y_in_m = [
+        message(s_in.at[at, :], y_in.at[to, :], neighbour_y(), sems, base + 7 + n)
+        for n, (at, to) in enumerate(((c, a), (d, b)))
+    ]
+
+    core_sm.start()
+    g = dot_tn(mixed[...], er[...])
+    p_out[...] = g[:, 2 * width :].astype(BF)
+    core_out.start()
+    s_out[...] = g[:, : 2 * width].astype(BF)
+    s_sm[...] = small[...]
+
+    def tile(n, target, row):
+        at = slice(n * width, (n + 1) * width)
+        where = slice(row, row + width)
+        target[where, :channels] = dot_tn(n1[:, at], eu[...]).astype(BF)
+        target[where, channels:] = dot_tn(n1[:, at], ev[...]).astype(BF)
+
+    def begin(n):
+        @pl.when(end)
+        def _():
+            to_end[n].start()
+
+    def relay(n):
+        s, z1, z2 = views[n]
+
+        @pl.when(middle)
+        def _():
+            to_end[n].wait_recv()
+            plus_in(s, z1, s.shape[0])
+            to_middle[n].start()
+
+    def settle(n):
+        s, z1, z2 = views[n]
+
+        @pl.when(middle)
+        def _():
+            to_middle[n].wait_recv()
+            to_middle[n].wait_send()
+            plus_in(s, z2, s.shape[0])
+            to_end[n].start()
+
+    def finish(n):
+        s, z1, z2 = views[n]
+
+        @pl.when(end)
+        def _():
+            to_end[n].wait_recv()
+            to_end[n].wait_send()
+            step = 64
+            for r in range(0, s.shape[0], step):
+                at = slice(r, min(r + step, s.shape[0]))
+                s[at, :] = z1[at, :]
+
+        @pl.when(middle)
+        def _():
+            to_end[n].wait_send()
+
+    core_sm.wait_recv()
+    plus_in(s_sm, c_sm, s_sm.shape[0])
+    begin(0)
+    tile(3, p_in, width)
+    core_in[0].start()
+    core_in[1].start()
+    core_out.wait_recv()
+    plus_in(s_out, c_out, s_out.shape[0])
+    begin(1)
+    begin(2)
+    tile(1, s_in, width)
+    tile(2, p_in, 0)
+    core_in[2].start()
+    core_in[3].start()
+    core_in[0].wait_recv()
+    core_in[1].wait_recv()
+    plus_in(s_in, c_in, width, width)
+    begin(3)
+    begin(4)
+    tile(0, s_in, 0)
+    core_in[2].wait_recv()
+    core_in[3].wait_recv()
+    plus_in(s_in, c_in, width, 0)
+    begin(5)
+    begin(6)
+    relay(0)
+    relay(1)
+    settle(0)
+    relay(2)
+    settle(1)
+    finish(0)
+    finish(1)
+    y_out_m.start()
+    for n in range(3, count):
+        relay(n)
+        settle(n - 1)
+        if n < 5:
+            finish(n - 1)
+            if n == 4:
+                y_in_m[0].start()
+    settle(count - 1)
+    finish(4)
+    y_in_m[1].start()
+    finish(5)
+    finish(6)
+    small_out[...] = s_sm[...]
+    mine_in[...] = s_in[0:width, :]
+    mine_out[...] = s_out[:, 0:width]
+    y_out_m.wait_recv()
+    far_out[...] = y_out[...]
+    for m in y_in_m:
+        m.wait_recv()
+    far_in[...] = y_in[...]
+    for m in [core_sm, core_out, y_out_m] + core_in + y_in_m:
+        m.wait_send()
+
+
+def tail(n1, eu, ev, mixed, er, small):
+    rows, channels = eu.shape
+    width = er.shape[1] // 4
+    inner = mixed.shape[1]
+    big = pltpu.VMEM((2 * width, 2 * channels), BF)
+    tall = pltpu.VMEM((inner, 2 * width), BF)
+    tiny = pltpu.VMEM(small.shape, F32)
+    quarter_in, quarter_out = (width, 2 * channels), (inner, width)
     return pl.pallas_call(
-        outer_body,
-        grid=(m // block,),
-        in_specs=[lhs, lhs, whole_spec((rows, n)), whole_spec((rows, n))],
-        out_specs=rows_spec(block, n),
-        out_shape=sds((m, n), BF),
-        compiler_params=params(),
-        cost_estimate=cost(4 * rows * m * n, rows * (m + n) * 4 + m * n * 2),
-        name="outer",
-    )(*left, *right)
+        tail_body,
+        out_shape=[sds(quarter_in, BF)] * 2 + [sds(quarter_out, BF)] * 2 + [sds(small.shape, F32)],
+        scratch_shapes=[big] * 5
+        + [pltpu.VMEM(quarter_in, BF)]
+        + [tall] * 5
+        + [pltpu.VMEM(quarter_out, BF)]
+        + [tiny] * 4
+        + [pltpu.SemaphoreType.DMA((23,))] * 2,
+        compiler_params=pltpu.CompilerParams(
+            vmem_limit_bytes=VMEM_LIMIT, collective_id=6, has_side_effects=True
+        ),
+        cost_estimate=cost(20 * rows * n1.shape[1] * channels * 3, nbytes(n1, eu, ev, mixed, er)),
+        name="tail",
+    )(n1, eu, ev, mixed, er, small)
 
 
 def add_low(a, b):
@@ -995,39 +1554,69 @@
     x = by_core(stream_in)
     g = by_core(cotangent)
 
-    def four_blocks(w, axis):
-        own, other = own_and_other(w, y, axis)
-        far = flip_y(other)
-        return ((own, flip_core(own)), (far, flip_core(far)))
-
-    def rows_in_order(ws):
-        blocks = [four_blocks(w, 1) for w in ws]
-        pieces = []
-        for dy in (0, 1):
-            for dx in (0, 1):
-                for dc in (0, 1):
-                    start = part * (row ^ dx)
-                    pieces.append(
-                        jnp.concatenate(
-                            [lax.dynamic_slice_in_dim(b[dy][dc], start, part, 0) for b in blocks], axis=1
-                        )
-                    )
-        return jnp.concatenate(pieces, axis=0)
-
-    def cols_in_order(w):
-        blocks = four_blocks(w, 0)
+    def with_core(own, far):
+        near = jnp.stack([own, far])
+        return near, flip_core(near)
+
+    own_in, other_in = own_and_other(jnp.stack([input_weight, branch_weight]), y, 2)
+    far_in = flip_y(other_in)
+    near_in, sib_in = with_core(
+        jnp.concatenate([own_in[0], own_in[1]], axis=1), jnp.concatenate([far_in[0], far_in[1]], axis=1)
+    )
+
+    lanes = 2 * part
+    share = gate_weight.shape[0] // count
+    units = gate_weight.shape[1] // 2
+
+    def other_share(w, axis):
+        rows = w.shape[0] // (2 if axis == 0 else 1)
+        take = rows // count
+        start = seq * take + ((1 - y) * rows if axis == 0 else 0)
+        if axis == 0:
+            return lax.dynamic_slice(w, (start, 0), (take, w.shape[1]))
+        cols = w.shape[1] // 2
+        piece = lax.dynamic_slice(w, (start, (1 - y) * cols), (take, cols))
+        return jnp.concatenate([piece[:, n : n + lanes] for n in range(0, cols, lanes)], axis=0)
+
+    packed = jnp.concatenate(
+        [
+            other_share(gate_weight, 1),
+            other_share(up_weight, 1),
+            other_share(down_weight, 0),
+            other_share(output_weight, 0),
+        ],
+        axis=0,
+    )
+    packed = lax.all_gather(flip_y(packed), "seq", axis=0)
+
+    def late_weights(packed, gate_weight, up_weight, down_weight, output_weight):
+        def wide(at):
+            blocks = packed[:, at : at + share * (units // lanes)].reshape(count, units // lanes, share, lanes)
+            return blocks.transpose(0, 2, 1, 3).reshape(count * share, units)
+
+        step = share * (units // lanes)
+        far_gu = jnp.concatenate([wide(0), wide(step)], axis=1)
+        own_gu = jnp.concatenate(
+            [own_and_other(gate_weight, y, 1)[0], own_and_other(up_weight, y, 1)[0]], axis=1
+        )
+        near_gu, sib_gu = with_core(own_gu, far_gu)
+        d_rows = down_weight.shape[0] // 2
+        o_rows = output_weight.shape[0] // 2
+        at = 2 * step
+        far_d = packed[:, at : at + d_rows // count].reshape(d_rows, lanes)
+        at += d_rows // count
+        far_o = packed[:, at : at + o_rows // count].reshape(o_rows, lanes)
+        own_do = jnp.concatenate(
+            [own_and_other(output_weight, y, 0)[0], own_and_other(down_weight, y, 0)[0]], axis=0
+        )
+        near, sib = with_core(own_do, jnp.concatenate([far_o, far_d], axis=0))
         chunks = []
         for dy in (0, 1):
-            near, far = blocks[dy]
-            first = jnp.concatenate([near[:, :part], far[:, :part]], axis=1)
-            second = jnp.concatenate([near[:, part:], far[:, part:]], axis=1)
+            first = jnp.concatenate([near[dy][:, :part], sib[dy][:, :part]], axis=1)
+            second = jnp.concatenate([near[dy][:, part:], sib[dy][:, part:]], axis=1)
             chunks += [jnp.where(lower, first, second), jnp.where(lower, second, first)]
-        return jnp.concatenate(chunks, axis=1)
-
-    w_in = rows_in_order((input_weight, branch_weight))
-    w_out = cols_in_order(output_weight)
-    w_gu = rows_in_order((gate_weight, up_weight))
-    w_down = cols_in_order(down_weight)
+        both = jnp.concatenate(chunks, axis=1)
+        return near_gu, sib_gu, both[:o_rows], both[o_rows:]
 
     heads = recall_gate.shape[0] // 2
     rw = lax.dynamic_slice_in_dim(recall_gate, y * heads, heads, 0)
@@ -1050,116 +1639,83 @@
     def neighbours(ends, sign):
         return jnp.concatenate([shifted(ends, sign * n) for n in range(1, count)], axis=0)
 
-    ca, cb = spread(in_halves(x.astype(BF)))
-    nka, nsa, ua, va, s1a = norm_uv(ca, gains_all, w_in)
-    nkb, nsb, ub, vb, s1b = norm_uv(cb, gains_all, w_in)
-    border = shifted(ub[half - 8 :], 1)
-    conv, recall, admit, local_state, cum, ends = recur(ua, ub, border, off, taps, rw, aw, soft)
+    n1, u, v, s1 = norm_uv(x.astype(BF), gains_all, near_in, sib_in)
+    border = shifted(u[tokens - 8 :], 1)
+    g_low = g.astype(BF)
+    conv, recall, admit, local_state, cum, ends, *errs = recur(
+        u, border, off, taps, rw, aw, soft, g_low
+    )
+    late = lax.optimization_barrier(
+        (ends, packed, gate_weight, up_weight, down_weight, output_weight)
+    )
+    near_gu, sib_gu, w_out, w_down = late_weights(*late[1:])
     earlier = neighbours(ends, 1)
-    sa, ma, *qa = mix(0, local_state, cum, va, earlier, w_out)
-    sb, mb, *qb = mix(1, local_state, cum, vb, earlier, w_out)
-    mid = [r + h for r, h in zip(collect((qa, qb)), in_halves(x))]
-    da, db = spread([m.astype(BF) for m in mid])
-    fa, fb = spread(in_halves(g.astype(BF)))
-    feed_a = feed(da, fa, gains_all, w_gu, w_down)
-    feed_b = feed(db, fb, gains_all, w_gu, w_down)
-    out_chunk = jnp.concatenate(
-        [r + m for r, m in zip(collect((feed_a[9:13], feed_b[9:13])), mid)], axis=0
-    )
-
-    def summed(dots):
-        d = jnp.concatenate([a[:, 0] for a in dots])
-        d = d + flip_row(d)
-        d = d + flip_y(d)
-        return in_halves(d)
-
-    def norm_back_local(dn, dots, scales, source, gain):
-        grads, gain_grad = [], 0.0
-        for d, t, s, x_half in zip(dn, dots, scales, source):
-            grads.append(s * gain * d - x_half * (s * s * t[:, None] / D))
-            gain_grad = gain_grad + jnp.sum(d * x_half * s, axis=0)
-        return grads, gain_grad
-
-    dots2 = summed((feed_a[8], feed_b[8]))
-    dn2 = collect((feed_a[13:17], feed_b[13:17]))
-    back2, grad_feed = norm_back_local(dn2, dots2, (feed_a[7], feed_b[7]), mid, gains[1:2])
-    dx2 = [b + h for b, h in zip(back2, in_halves(g))]
-    ra, rb = spread([d.astype(BF) for d in dx2])
-
-    part_adj, reach, eva, evb, back_ends, erk, ers = adjoint(
-        (ra, rb), w_out, (sa, sb), (va, vb), recall, off, soft
-    )
+    states, mixed, mid, *mid_all = mix(local_state, cum, v, x, earlier, w_out)
+    p0, p1, p2, p3, dx2, *dx_all, grad_feed, g_down, g_gu = feed(
+        mid_all, [g_low] + errs, mid, g, gains_all, near_gu, sib_gu, w_down
+    )
+    outs = collect(tuple(zip(*(in_halves(p) for p in (p0, p1, p2, p3)))))
+    out_chunk = jnp.concatenate(outs, axis=0) + mid
+
+    part_adj, reach, ev, back_ends, er = adjoint(dx_all, w_out, states, v, recall, off, soft)
     later = neighbours(back_ends, -1)
     du, out_border, grad_recall, grad_admit, grad_small = recur_back(
-        part_adj, reach, later, earlier, (sa, sb), conv, recall, admit, off, (ua, ub), border, taps, rw, aw, soft
-    )
-    tail = shifted(out_border, -1)
-    eua, dots_a, *ba = enter_back(0, du, tail, eva, ua, va, w_in)
-    eub, dots_b, *bb = enter_back(1, du, tail, evb, ub, vb, w_in)
-    dots1 = summed((dots_a, dots_b))
-    dn1 = collect((ba, bb))
-    back1, grad_mixer = norm_back_local(dn1, dots1, (s1a, s1b), in_halves(x), gains[0:1])
-    grad_chunk = jnp.concatenate([b + d for b, d in zip(back1, dx2)], axis=0)
-
-    def reduced(keep, send, axis):
-        both = add_low(keep, flip_core(send))
-        n = both.shape[axis] // 2
-        mine = lax.slice_in_dim(both, 0, n, axis=axis)
-        theirs = flip_y(lax.slice_in_dim(both, n, 2 * n, axis=axis))
-        return total_seq(mine), total_seq(theirs)
-
-    def rows_out(keep, send):
-        mine, theirs = reduced(keep, send, 0)
+        part_adj, reach, later, earlier, states, conv, recall, admit, off, u, border, taps, rw, aw, soft
+    )
+    from_later = shifted(out_border, -1)
+    eu, grad_chunk, grad_mixer = enter_back(du, from_later, ev, u, v, near_in, sib_in, s1, x, dx2, gains_all)
+
+    def rows_out(mine, theirs):
         wide = jnp.where(
             y == 0, jnp.concatenate([mine, theirs], axis=1), jnp.concatenate([theirs, mine], axis=1)
         )
         swapped = jnp.concatenate([wide[part:], wide[:part]], axis=0)
         return jnp.where(lower, wide, swapped).astype(F32)
 
-    def cols_out(keep, send):
-        mine, theirs = reduced(keep, send, 1)
+    def cols_out(mine, theirs):
         tall = jnp.where(
             y == 0, jnp.concatenate([mine, theirs], axis=0), jnp.concatenate([theirs, mine], axis=0)
         )
         swapped = jnp.concatenate([tall[:, part:], tall[:, :part]], axis=1)
         return jnp.where(lower, tall, swapped).astype(F32)
 
-    n2k, n2s = (feed_a[0], feed_b[0]), (feed_a[1], feed_b[1])
-    hid = (feed_a[2], feed_b[2])
-    eg, eu2 = (feed_a[3], feed_b[3]), (feed_a[4], feed_b[4])
-    eok, eos = (feed_a[5], feed_b[5]), (feed_a[6], feed_b[6])
-    grad_down = cols_out(outer(hid, eok), outer(hid, eos))
-    grad_gate = rows_out(outer(n2k, eg), outer(n2s, eg))
-    grad_up = rows_out(outer(n2k, eu2), outer(n2s, eu2))
-    grad_output = cols_out(
-        outer((ma, mb), in_halves(erk)), outer((ma, mb), in_halves(ers))
-    )
-    grad_input = rows_out(outer((nka, nkb), (eua, eub)), outer((nsa, nsb), (eua, eub)))
-    grad_branch = rows_out(outer((nka, nkb), (eva, evb)), outer((nsa, nsb), (eva, evb)))
-
-    width = recall_gate.shape[2] * heads
-    gain_rows = jnp.concatenate(
-        [grad_mixer[:part], grad_feed[:part], grad_mixer[part:], grad_feed[part:]]
-    )
+    kept = 4 * part
     channels = taps.shape[1]
-    lane = 128
+    sum_down = add_low(g_down[:, :kept], flip_core(g_down[:, kept:]))
+    sum_gu = add_low(g_gu[:kept], flip_core(g_gu[kept:]))
+    mine_down, far_down = sum_down[:, :lanes], flip_y(sum_down[:, lanes:])
+    mine_gu, far_gu = sum_gu[:lanes], flip_y(sum_gu[lanes:])
+    mine_down, mine_gu = lax.psum((mine_down, mine_gu), "seq")
+    far_down, far_gu, _, _ = lax.optimization_barrier((far_down, far_gu, mine_down, mine_gu))
+    far_down, far_gu = lax.psum((far_down, far_gu), "seq")
+
+    own = channels // 2
     pieces = [
         grad_small[:KW].reshape(-1),
-        (grad_small[KW] * 8.0 * jax.nn.sigmoid(-decay[0])),
+        grad_small[KW] * 8.0 * jax.nn.sigmoid(-decay[0]),
         grad_recall.reshape(-1),
         grad_admit.reshape(-1),
     ]
+    gain_rows = jnp.stack([grad_mixer[0], grad_feed[0]])
+    gain_rows = jnp.where(
+        core == 0, gain_rows, jnp.concatenate([gain_rows[:, part:], gain_rows[:, :part]], axis=1)
+    )
+    pieces.append(gain_rows.reshape(-1))
+    sizes = [p.size for p in pieces]
     flat = jnp.concatenate(pieces)
-    flat = flat + flip_core(flat)
-    mine_gain = gain_rows[: 2 * part] + flip_core(gain_rows[2 * part :])
-    flat = jnp.concatenate([flat, mine_gain])
-    flat = lax.psum(flat, "seq")
-    sizes = [KW * channels, channels, grad_recall.size, grad_admit.size, part, part]
+    flat = jnp.pad(flat, (0, -flat.size % 8192)).reshape(-1, 128)
+    mine_in, far_in, mine_out, far_out, flat = tail(n1, eu, ev, mixed, er, flat)
+    flat = flat.reshape(-1)
     cuts, at = [], 0
     for s in sizes:
         cuts.append(flat[at : at + s])
         at += s
-    own = channels // 2
+    grad_down = cols_out(mine_down, far_down)
+    grad_gate = rows_out(mine_gu[:, :units], far_gu[:, :units])
+    grad_up = rows_out(mine_gu[:, units:], far_gu[:, units:])
+    grad_output = cols_out(mine_out, far_out)
+    grad_input = rows_out(mine_in[:, :channels], far_in[:, :channels])
+    grad_branch = rows_out(mine_in[:, channels:], far_in[:, channels:])
     g_taps = lax.dynamic_slice_in_dim(cuts[0].reshape(KW, channels), core * own, own, 1)
     g_decay = lax.dynamic_slice_in_dim(cuts[1], core * own, own, 0)
     gates = jnp.stack([cuts[2].reshape(grad_recall.shape), cuts[3].reshape(grad_admit.shape)])
@@ -1167,6 +1723,7 @@
     gates = jnp.where(
         y == 0, jnp.concatenate([gates, far], axis=1), jnp.concatenate([far, gates], axis=1)
     )
+    gain_grads = lax.dynamic_slice_in_dim(cuts[4].reshape(2, 2 * part), core * part, part, 1)
 
     def stacked(chunk):
         own, other = chunk[:, :part], flip_core(chunk[:, part:])
@@ -1175,7 +1732,7 @@
     return (
         stacked(out_chunk),
         stacked(grad_chunk),
-        cuts[4],
+        gain_grads[0],
         grad_input,
         grad_branch,
         g_taps,
@@ -1183,7 +1740,7 @@
         gates[1],
         g_decay,
         grad_output,
-        cuts[5],
+        gain_grads[1],
         grad_gate,
         grad_up,
         grad_down,
@@ -1224,5 +1781,5 @@
         P("col", "row"),
         P("row", "col"),
     )
-    plan = local_fast if mesh.shape["row"] == 2 and mesh.shape["col"] == 4 else local
+    plan = local_fast if dict(mesh.shape) == {"seq": 4, "row": 2, "col": 4} else local
     return jax.shard_map(plan, mesh=mesh, in_specs=in_specs, out_specs=out_specs, check_vma=False)

time: 989 us -> 794 us (0.80)
  Pallas kernels: 203 us -> 421 us
  waiting for transfers between devices: 384 us -> 184 us
  starting transfers between devices: 169 us -> 38.9 us
  other arithmetic: 106 us -> 50.6 us
  local copies, waits for them, and re-layouts: 98.3 us -> 76.7 us
    pallas_call x21 -> x6, Pallas kernels: 166 us -> 385 us  [the longest x1 107 us: feed(): pl.pallas_call(functools.partial(feed_body, blocks), grid=(blocks + tiles...]
    ppermute x36 -> x0, waiting for transfers between devices: 214 us -> none  [the longest x12 134 us: total_seq(): back = lax.ppermute(g, 'seq', [(1, 0), (2, 3)])]
    psum x1 -> x2, waiting for transfers between devices: 0.01 us -> 116 us  [the longest x1 81.3 us: local_fast(): far_down, far_gu = lax.psum((far_down, far_gu), 'seq')]
    ppermute x36 -> x0, starting transfers between devices: 75.4 us -> none  [the longest x12 49.1 us: total_seq(): g = add_low(g, lax.ppermute(g, 'seq', [(0, 1), (3, 2)]))]
    ppermute x41 -> x10, waiting for transfers between devices: 118 us -> 63.5 us  [flip_y(): return lax.ppermute(a, 'col', [(i, i ^ 2) for i in range(4)])]
    ppermute x27 -> x4, waiting for transfers between devices: 45.2 us -> 1.85 us  [flip_row(): return lax.ppermute(a, 'row', [(0, 1), (1, 0)])]
    dynamic_slice x21 -> x0, local copies, waits for them, and re-layouts: 30.6 us -> none  [the longest x16 22.6 us: rows_in_order(): lax.dynamic_slice_in_dim(b[dy][dc], start, part, 0)]
    ppermute x27 -> x4, starting transfers between devices: 31.2 us -> 5.03 us  [flip_row(): return lax.ppermute(a, 'row', [(0, 1), (1, 0)])]
  transfers between devices with their start and end apart: 139 -> 36, of which waited for: 43 -> 8; matrix products, arithmetic and copies ran while one was open for 19% -> 13% of each run, Pallas kernels for 18% -> 37%
where the time goes in v2:
time: 794 us; the launch traced here: 787 us
  Pallas kernels  421 us (53%)
  waiting for transfers between devices  184 us (23%)
  local copies, waits for them, and re-layouts  76.7 us (10%)
  other arithmetic  50.6 us (6%)
  starting transfers between devices  38.9 us (5%)
  between operations  15.1 us (2%)
    pallas_call x1, Pallas kernels, feed(): pl.pallas_call(functools.partial(feed_body, blocks), grid=(blocks + tiles...  107 us
    pallas_call x1, Pallas kernels, tail(): pl.pallas_call(tail_body, out_shape=[sds(quarter_in, BF)] * 2 + [sds(quar...  104 us
    psum x1, waiting for transfers between devices, local_fast(): far_down, far_gu = lax.psum((far_down, far_gu), 'seq')  81.3 us
    pallas_call x1, Pallas kernels, mix(): pl.pallas_call(functools.partial(mix_body, entries.shape[0] // 8, blocks)...  63.9 us
    ppermute x10, waiting for transfers between devices, flip_y(): return lax.ppermute(a, 'col', [(i, i ^ 2) for i in range(4)])  63.5 us
    pallas_call x1, Pallas kernels, enter_back(): pl.pallas_call(functools.partial(enter_back_body, blocks), grid=(blocks +...  41.3 us
    pallas_call x1, Pallas kernels, norm_uv(): pl.pallas_call(functools.partial(norm_uv_body, blocks), grid=(blocks,), i...  37.4 us
    psum x1, waiting for transfers between devices, local_fast(): mine_down, mine_gu = lax.psum((mine_down, mine_gu), 'seq')  34.4 us
  transfers between devices with their start and end apart: 36, of which 8 were waited for; matrix products, arithmetic and copies ran while one was open for 13% of the time, Pallas kernels for 37%

profile of v2, /device:TPU:0, one launch (start us, length us, event | category | flops | bytes accessed | tf_op | source)
XLA Modules:
  0.0 786.6 jit_solution(8050603712050947291)
XLA Ops:
  7.3 2.5 fusion.10
  9.8 3.0 collective-permute-start.5
  15.4 1.5 dynamic-slice_dynamic-update-slice_fusion.7
  17.0 1.5 dynamic-slice_dynamic-update-slice_fusion.6
  18.5 1.5 dynamic-slice_dynamic-update-slice_fusion.5
  20.0 1.5 dynamic-slice_dynamic-update-slice_fusion.4
  21.5 1.5 dynamic-slice_dynamic-update-slice_fusion.3
  23.1 1.5 dynamic-slice_dynamic-update-slice_fusion.2
  24.6 1.6 dynamic-slice_dynamic-update-slice_fusion
  26.2 1.5 dynamic-slice_dynamic-update-slice_fusion.1
  27.9 2.8 collective-permute-done.5
  33.6 1.7 collective-permute-start.2
  35.3 1.8 collective-permute-done.2
  37.2 2.5 collective-permute-start.3
  39.7 7.9 %collective-permute-done.3 = f32[2,384]{1,0:T(2,128)S(1)} collective-permute-done((f32[2,384]{1,0:T(2,128)S(1)}, f32[2,384]{1,0:T(2,128)S(1)}, u32[]{:S(2)}, u32[]{:S(2)}) %collective-permute-start.3) | collective-permute-done | bytes 3104 | tf_op jit(solution)/shard_map/ppermute | solution.py:338
  48.7 2.4 collective-permute-done.4
  55.8 2.4 copy.73
  58.2 1.5 copy.75
  59.7 3.0 fusion.19
  62.7 37.4 %norm_uv.1 = (bf16[1024,1536]{1,0:T(8,128)(2,1)}, f32[1024,512]{1,0:T(8,128)}, f32[1024,512]{1,0:T(8,128)}, f32[1024,1]{1,0:T(8,128)}) custom-call(bf16[1024,384]{1,0:T(8,128)(2,1)} %get-tuple-element.204.own, f32[2,1536]{1,0:T(2,128)} %concatenate.138.gain.refs_10_, bf16[2,384,1024]{2,1,0:T(8,128)(2,1)} %pad_maximum_fusion.9.near.refs_5_, ...), custom_call_target="tpu_custom_call" | custom-call | flops 48318382080 | bytes 3145728 | tf_op jit(solution)/shard_map/norm_uv/pallas_call | solution.py:599
  100.8 3.5 collective-permute-start.7
  104.3 1.7 fusion.18
  106.6 31.3 %recur.1 = (f32[1024,512]{1,0:T(8,128)}, f32[1024,512]{1,0:T(8,128)}, f32[1024,512]{1,0:T(8,128)}, f32[1024,512]{1,0:T(8,128)}, f32[1024,512]{1,0:T(8,128)}, /*i...) custom-call(f32[1024,512]{1,0:T(8,128)} %get-tuple-element.71.u.refs_9_.refs_3, ...), custom_call_target="tpu_custom_call" | custom-call | flops 1610612736 | bytes 12582912 | tf_op jit(solution)/shard_map/recur/pallas_call | solution.py:698
  137.9 3.8 collective-permute-start.10
  141.7 6.2 collective-permute-start.11
  147.9 1.5 collective-permute-start.12
  149.5 2.1 fusion.21
  163.6 1.9 pad_maximum_fusion.refs_13_
  165.5 63.9 %mix.1 = (f32[1024,512]{1,0:T(8,128)}, bf16[1024,512]{1,0:T(8,128)(2,1)}, f32[1024,384]{1,0:T(8,128)}, bf16[1024,384]{1,0:T(8,128)(2,1)}, bf16[1024,384]{1,0:T(8...) custom-call(f32[1024,512]{1,0:T(8,128)} %get-tuple-element.72.local, ...), custom_call_target="tpu_custom_call" | custom-call | flops 32212254720 | bytes 11010048 | tf_op jit(solution)/shard_map/mix/pallas_call | solution.py:793
  229.4 1.8 copy-done.39
  231.2 107.2 %feed.1 = (f32[1024,384]{1,0:T(8,128)}, bf16[1024,384]{1,0:T(8,128)(2,1)}, bf16[1024,384]{1,0:T(8,128)(2,1)}, bf16[1024,384]{1,0:T(8,128)(2,1)}, f32[1024,384]{1...) custom-call(bf16[1024,384]{1,0:T(8,128)(2,1)} %get-tuple-element.79., ...), custom_call_target="tpu_custom_call" | custom-call | flops 86973087744 | bytes 41336832 | tf_op jit(solution)/shard_map/feed/pallas_call | solution.py:968
  338.4 19.5 %adjoint.1 = (f32[1024,512]{1,0:T(8,128)}, f32[1024,512]{1,0:T(8,128)}, bf16[1024,512]{1,0:T(8,128)(2,1)}, f32[8,512]{1,0:T(8,128)}, bf16[1024,1536]{1,0:T(8,128)(2,1)}) custom-call(bf16[1024,384]{1,0:T(8,128)(2,1)} %get-tuple-element.93.refs_0_, bf16[1024,384]{1,0:T(8,128)(2,1)} %get-tuple-element.94.refs_1_, bf16[1024,384]{1,0:T(8,128)(2,1)} %get-tuple-element.95.refs_2_, ...), custom_call_target="tpu_custom_call" | custom-call | flops 1610612736 | bytes 19922944 | tf_op jit(solution)/shard_map/adjoint/pallas_call | solution.py:1065
  361.8 2.0 slice.329
  369.5 2.1 collective-permute-start.17
  372.2 17.0 %recur_back.1 = (f32[1024,512]{1,0:T(8,128)}, f32[8,512]{1,0:T(8,128)}, f32[4,128,128]{2,1,0:T(8,128)}, f32[4,128,128]{2,1,0:T(8,128)}, f32[8,512]{1,0:T(8,128)}) custom-call(f32[1024,512]{1,0:T(8,128)} %get-tuple-element.99.refs_0_, f32[1024,512]{1,0:T(8,128)} %get-tuple-element.100.refs_1_, f32[24,512]{1,0:T(8,128)} %pad_maximum_fusion.16.refs_2_, ...), custom_call_target="tpu_custom_call" | custom-call | flops 3221225472 | bytes 18874368 | tf_op jit(solution)/shard_map/recur_back/pallas_call | solution.py:1150
  393.9 2.5 collective-permute-done.26.refs_1_
  397.1 41.3 %enter_back.1 = (bf16[1024,512]{1,0:T(8,128)(2,1)}, f32[1024,384]{1,0:T(8,128)}, f32[8,384]{1,0:T(8,128)}) custom-call(f32[1024,512]{1,0:T(8,128)} %get-tuple-element.104.refs_0_, f32[8,512]{1,0:T(8,128)} %copy-done.40, bf16[1024,512]{1,0:T(8,128)(2,1)} %get-tuple-element.106.refs_2_.ev, f32[1024,512]{1,0:T(8,128)} %get-tuple-element.71.u.refs_9_.refs_3_, ...), custom_call_target="tpu_custom_call" | custom-call | flops 32212254720 | bytes 11534336 | tf_op jit(solution)/shard_map/enter_back/pallas_call | solution.py:1271
  440.1 103.9 %tail.1 = (bf16[384,1024]{1,0:T(8,128)(2,1)}, bf16[384,1024]{1,0:T(8,128)(2,1)}, bf16[512,384]{1,0:T(8,128)(2,1)}, bf16[512,384]{1,0:T(8,128)(2,1)}, f32[1088,128]{1,0:T(8,128)}) custom-call(bf16[1024,1536]{1,0:T(8,128)(2,1)} %get-tuple-element.110.n1, bf16[1024,512]{1,0:T(8,128)(2,1)} %get-tuple-element.111.eu, ...), custom_call_target="tpu_custom_call" | custom-call | flops 48318382080 | bytes 9437184 | tf_op jit(solution)/shard_map/tail/pallas_call | solution.py:1475
  544.1 2.0 fusion.32
  548.5 2.7 add_convert_fusion.1
  551.2 1.4 fusion.27
  552.6 3.0 add_convert_fusion
  555.6 2.0 fusion.20
  561.5 1.5 fusion.13
  564.0 1.4 fusion.12
  568.4 1.8 add_convert_fusion.2
  571.5 1.8 add_convert_fusion.3
  573.4 50.4 %collective-permute-done.31 = bf16[1152,384]{1,0:T(8,128)(2,1)} collective-permute-done((bf16[1152,384]{1,0:T(8,128)(2,1)}, bf16[1152,384]{1,0:T(8,128)(2,1)}, u32[]{:S(2)}, u32[]{:S(2)}) %collective-permute-start.31) | collective-permute-done | bytes 884768 | tf_op jit(solution)/shard_map/ppermute | solution.py:338
  626.7 34.4 %all-reduce.8.cloned.1.call-done = (bf16[1152,384]{1,0:T(8,128)(2,1)}, bf16[384,2304]{1,0:T(8,128)(2,1)}) async-done(((bf16[1152,384]{1,0:T(8,128)(2,1)}, bf16[384,2304]{1,0:T(8,128)(2,1)}), (bf16[1152,384]{1,0:T(8,128)(2,1)}, bf16[384,2304]{1,0:T(8,128)(2,1)})) %all-reduce.8.cloned.1.call-update) | async-done | bytes 2654224 | tf_op jit(solution)/shard_map/psum | solution.py:1688
  665.6 2.1 convert_add_fusion.1
  671.4 1.4 fusion.11
  672.8 1.4 maximum_select_fusion.8
  675.2 1.5 copy.84
  676.7 1.8 maximum_select_fusion.1
  678.5 1.7 copy.86
  680.2 1.5 copy.80
  681.6 1.8 maximum_select_fusion
  683.4 1.7 copy.85
  685.1 1.6 fusion.24
  686.8 81.3 %all-reduce.6.cloned.1.call-done = (bf16[384,2304]{1,0:T(8,128)(2,1)}, bf16[1152,384]{1,0:T(8,128)(2,1)}) async-done(((bf16[384,2304]{1,0:T(8,128)(2,1)}, bf16[1152,384]{1,0:T(8,128)(2,1)}), (bf16[384,2304]{1,0:T(8,128)(2,1)}, bf16[1152,384]{1,0:T(8,128)(2,1)})) %all-reduce.6.cloned.1.call-update) | async-done | bytes 2654224 | tf_op jit(solution)/shard_map/psum | solution.py:1690
  768.1 2.0 maximum_select_fusion.6
  772.8 2.6 fusion.2
  775.4 2.1 fusion.1
  777.5 2.1 fusion
  (246 shorter events, 68.0 us)
Async XLA Ops:
  7.2 5.5 copy-start.6
  7.2 142.3 %all-gather.3.cloned.1.call-start = ((), (), s32[]{:S(2)}) async-start(), calls=%async_computation | async-start | bytes 3809280 | tf_op jit(solution)/shard_map/all_gather | solution.py:1590
  9.7 4.0 copy-start.36
  9.8 4.0 copy-start.37
  9.8 20.9 %collective-permute-start.5 = (bf16[2,384,512]{2,1,0:T(8,128)(2,1)}, bf16[2,384,512]{2,1,0:T(8,128)(2,1)}, u32[]{:S(2)}, u32[]{:S(2)}) collective-permute-start(bf16[2,384,512]{2,1,0:T(8,128)(2,1)} %get-tuple-element.238), channel_id=1, source_target_pairs={{0,2},{1,3},{2,0},{3,1},{4,6},{5,7},{6,4},{7,5},{8,10},{9,11},{10,... | collective-permute-start | bytes 2359304 | tf_op jit(solution)/shard_map/ppermute | solution.py:338
  13.7 42.0 %collective-permute-start = (f32[1,1024,192]{1,2,0:T(8,128)}, f32[1,1024,192]{1,2,0:T(8,128)}, u32[]{:S(2)}, u32[]{:S(2)}) collective-permute-start(f32[1,1024,192]{1,2,0:T(8,128)} %get-tuple-element.240), channel_id=1, source_target_pairs={{0,1},{1,0},{2,3},{3,2},{4,5},{5,4},{6,7},{7,6},{8,9},{9,8},{10,11... | collective-permute-start | bytes 2359304 | tf_op jit(solution)/shard_map/ppermute | solution.py:342
  13.8 19.7 %collective-permute-start.1 = (f32[2,192]{1,0:T(2,128)S(1)}, f32[2,192]{1,0:T(2,128)S(1)}, u32[]{:S(2)}, u32[]{:S(2)}) collective-permute-start(f32[2,192]{1,0:T(2,128)S(1)} %pad_maximum_fusion.20), channel_id=1, source_target_pairs={{0,1},{1,0},{2,3},{3,2},{4,5},{5,4},{6,7},{7,6},{8,9},{9,8},{10,11... | collective-permute-start | bytes 4616 | tf_op jit(solution)/shard_map/ppermute | solution.py:342
  15.4 42.8 %collective-permute-start.9 = (f32[1,1024,192]{1,2,0:T(8,128)}, f32[1,1024,192]{1,2,0:T(8,128)}, u32[]{:S(2)}, u32[]{:S(2)}) collective-permute-start(f32[1,1024,192]{1,2,0:T(8,128)} %get-tuple-element.236), channel_id=1, source_target_pairs={{0,1},{1,0},{2,3},{3,2},{4,5},{5,4},{6,7},{7,6},{8,9},{9,8},{10,11... | collective-permute-start | bytes 2359304 | tf_op jit(solution)/shard_map/ppermute | solution.py:342
  27.8 28.0 %collective-permute-start.13 = (bf16[992,384]{1,0:T(8,128)(2,1)}, bf16[992,384]{1,0:T(8,128)(2,1)}, u32[]{:S(2)}, u32[]{:S(2)}) collective-permute-start(bf16[992,384]{1,0:T(8,128)(2,1)} %dynamic-slice_dynamic-update-slice_fusion.1), channel_id=1, source_target_pairs={{0,2},{1,3},{2,0},{3,1},{4,6},{5,7},{6,4},{7,5},{8,10},{9,11},{10,... | collective-permute-start | bytes 2285576 | tf_op jit(solution)/shard_map/ppermute | solution.py:338
  31.9 16.7 %copy-start.33 = (f32[4,256]{1,0:T(4,128)S(1)}, f32[4,256]{1,0:T(4,128)}, u32[]{:S(2)}) copy-start(f32[4,256]{1,0:T(4,128)} %param.21) | copy-start | bytes 12292
  31.9 16.7 %copy-start.35 = (f32[256]{0:T(256)S(1)}, f32[256]{0:T(256)}, u32[]{:S(2)}) copy-start(f32[256]{0:T(256)} %param.24) | copy-start | bytes 3076
  32.0 19.2 %copy-start.29 = (f32[8,128,128]{2,1,0:T(8,128)S(1)}, f32[8,128,128]{2,1,0:T(8,128)}, u32[]{:S(2)}) copy-start(f32[8,128,128]{2,1,0:T(8,128)} %param.23) | copy-start | bytes 1572868
  32.0 19.2 %copy-start.30 = (f32[8,128,128]{2,1,0:T(8,128)S(1)}, f32[8,128,128]{2,1,0:T(8,128)}, u32[]{:S(2)}) copy-start(f32[8,128,128]{2,1,0:T(8,128)} %param.22) | copy-start | bytes 1572868
  33.3 29.4 %collective-permute-start.6 = (bf16[2,384,1024]{2,1,0:T(8,128)(2,1)}, bf16[2,384,1024]{2,1,0:T(8,128)(2,1)}, u32[]{:S(2)}, u32[]{:S(2)}) collective-permute-start(bf16[2,384,1024]{2,1,0:T(8,128)(2,1)} %pad_maximum_fusion.9.near.refs_5_), channel_id=1, source_target_pairs={{0,1},{1,0},{2,3},{3,2},{4,5},{5,4},{6,7},{7,6},{8,9},{9,8},{10,11... | collective-permute-start | bytes 4718600 | tf_op jit(solution)/shard_map/ppermute | solution.py:342
  33.6 3.6 collective-permute-start.2
  37.2 10.4 %collective-permute-start.3 = (f32[2,384]{1,0:T(2,128)S(1)}, f32[2,384]{1,0:T(2,128)S(1)}, u32[]{:S(2)}, u32[]{:S(2)}) collective-permute-start(f32[2,384]{1,0:T(2,128)S(1)} %pad_maximum_fusion.19), channel_id=1, source_target_pairs={{0,2},{1,3},{2,0},{3,1},{4,6},{5,7},{6,4},{7,5},{8,10},{9,11},{10,... | collective-permute-start | bytes 9224 | tf_op jit(solution)/shard_map/ppermute | solution.py:338
  47.5 3.6 collective-permute-start.4
  51.1 3.4 collective-permute-start.8
  55.7 605.3 %all-reduce.8.cloned.1.call-start = ((), (), s32[]{:S(2)}) async-start(), calls=%async_computation.2 | async-start | bytes 5308416 | tf_op jit(solution)/shard_map/psum | solution.py:1688
  100.8 5.2 collective-permute-start.7
  137.9 15.6 %collective-permute-start.10 = (f32[8,512]{1,0:T(8,128)}, f32[8,512]{1,0:T(8,128)S(1)}, u32[]{:S(2)}, u32[]{:S(2)}) collective-permute-start(f32[8,512]{1,0:T(8,128)} %get-tuple-element.75), channel_id=1, source_target_pairs={{0,8},{8,16},{16,24},{1,9},{9,17},{17,25},{2,10},{10,18},{18,26},{... | collective-permute-start | bytes 49160 | tf_op jit(solution)/shard_map/ppermute | solution.py:27
  141.7 11.8 %collective-permute-start.11 = (f32[8,512]{1,0:T(8,128)}, f32[8,512]{1,0:T(8,128)S(1)}, u32[]{:S(2)}, u32[]{:S(2)}) collective-permute-start(f32[8,512]{1,0:T(8,128)} %get-tuple-element.75), channel_id=1, source_target_pairs={{0,16},{8,24},{1,17},{9,25},{2,18},{10,26},{3,19},{11,27},{4,20},{... | collective-permute-start | bytes 49160 | tf_op jit(solution)/shard_map/ppermute | solution.py:27
  147.9 5.6 collective-permute-start.12
  149.5 3.2 copy-start.28
  149.5 3.3 copy-start.21
  153.4 5.6 collective-permute-start.14
  157.3 72.1 %collective-permute-start.15 = (bf16[2,384,2304]{2,1,0:T(8,128)(2,1)S(1)}, bf16[2,384,2304]{2,1,0:T(8,128)(2,1)S(1)}, u32[]{:S(2)}, u32[]{:S(2)}) collective-permute-start(bf16[2,384,2304]{2,1,0:T(8,128)(2,1)S(1)} %pad_maximum_fusion.3.refs_11_), channel_id=1, source_target_pairs={{0,1},{1,0},{2,3},{3,2},{4,5},{5,4},{6,7},{7,6},{8,9},{9,8},{10,11... | collective-permute-start | bytes 10616840 | tf_op jit(solution)/shard_map/ppermute | solution.py:342
  229.4 1.8 copy-start.39
  338.4 23.4 %copy-start = (bf16[1536,2304]{1,0:T(8,128)(2,1)S(1)}, bf16[1536,2304]{1,0:T(8,128)(2,1)}, u32[]{:S(2)}) copy-start(bf16[1536,2304]{1,0:T(8,128)(2,1)} %get-tuple-element.124) | copy-start | bytes 21233668
  357.9 11.6 %collective-permute-start.23 = (f32[8,512]{1,0:T(8,128)}, f32[8,512]{1,0:T(8,128)S(1)}, u32[]{:S(2)}, u32[]{:S(2)}) collective-permute-start(f32[8,512]{1,0:T(8,128)} %get-tuple-element.101), channel_id=1, source_target_pairs={{8,0},{16,8},{24,16},{9,1},{17,9},{25,17},{10,2},{18,10},{26,18},{... | collective-permute-start | bytes 49160 | tf_op jit(solution)/shard_map/ppermute | solution.py:27
  359.2 10.3 %collective-permute-start.24 = (f32[8,512]{1,0:T(8,128)}, f32[8,512]{1,0:T(8,128)S(1)}, u32[]{:S(2)}, u32[]{:S(2)}) collective-permute-start(f32[8,512]{1,0:T(8,128)} %get-tuple-element.101), channel_id=1, source_target_pairs={{16,0},{24,8},{17,1},{25,9},{18,2},{26,10},{19,3},{27,11},{20,4},{... | collective-permute-start | bytes 49160 | tf_op jit(solution)/shard_map/ppermute | solution.py:27
  360.5 11.1 %collective-permute-start.25 = (f32[8,512]{1,0:T(8,128)}, f32[8,512]{1,0:T(8,128)S(1)}, u32[]{:S(2)}, u32[]{:S(2)}) collective-permute-start(f32[8,512]{1,0:T(8,128)} %get-tuple-element.101), channel_id=1, source_target_pairs={{24,0},{25,1},{26,2},{27,3},{28,4},{29,5},{30,6},{31,7}} | collective-permute-start | bytes 49160 | tf_op jit(solution)/shard_map/ppermute | solution.py:27
  361.8 3.3 copy-start.2
  363.8 188.8 %collective-permute-start.29 = (bf16[768,2304]{1,0:T(8,128)(2,1)}, bf16[768,2304]{1,0:T(8,128)(2,1)}, u32[]{:S(2)}, u32[]{:S(2)}) collective-permute-start(bf16[768,2304]{1,0:T(8,128)(2,1)} %slice.329), channel_id=1, source_target_pairs={{0,1},{1,0},{2,3},{3,2},{4,5},{5,4},{6,7},{7,6},{8,9},{9,8},{10,11... | collective-permute-start | bytes 10616840 | tf_op jit(solution)/shard_map/ppermute | solution.py:342
  365.1 2.8 copy-start.19
  365.2 3.5 copy-start.17
  365.2 182.9 %collective-permute-start.30 = (bf16[1152,768]{1,0:T(8,128)(2,1)S(1)}, bf16[1152,768]{1,0:T(8,128)(2,1)}, u32[]{:S(2)}, u32[]{:S(2)}) collective-permute-start(bf16[1152,768]{1,0:T(8,128)(2,1)S(1)} %slice.333), channel_id=1, source_target_pairs={{0,1},{1,0},{2,3},{3,2},{4,5},{5,4},{6,7},{7,6},{8,9},{9,8},{10,11... | collective-permute-start | bytes 5308424 | tf_op jit(solution)/shard_map/ppermute | solution.py:342
  369.5 198.1 %collective-permute-start.19 = (bf16[512,384]{1,0:T(8,128)(2,1)}, bf16[512,384]{1,0:T(8,128)(2,1)}, u32[]{:S(2)}, u32[]{:S(2)}) collective-permute-start(bf16[512,384]{1,0:T(8,128)(2,1)} %get-tuple-element.262), channel_id=1, source_target_pairs={{0,2},{1,3},{2,0},{3,1},{4,6},{5,7},{6,4},{7,5},{8,10},{9,11},{10,... | collective-permute-start | bytes 1179656 | tf_op jit(solution)/shard_map/ppermute | solution.py:338
  369.5 200.8 %collective-permute-start.17 = (bf16[512,384]{1,0:T(8,128)(2,1)}, bf16[512,384]{1,0:T(8,128)(2,1)}, u32[]{:S(2)}, u32[]{:S(2)}) collective-permute-start(bf16[512,384]{1,0:T(8,128)(2,1)} %get-tuple-element.261), channel_id=1, source_target_pairs={{0,4},{4,0},{1,5},{5,1},{2,6},{6,2},{3,7},{7,3},{8,12},{12,8},{9,1... | collective-permute-start | bytes 1179656 | tf_op jit(solution)/shard_map/ppermute | solution.py:334
  390.6 5.8 collective-permute-start.26
  396.5 268.4 %collective-permute-start.16 = (bf16[512,384]{1,0:T(8,128)(2,1)}, bf16[512,384]{1,0:T(8,128)(2,1)}, u32[]{:S(2)}, u32[]{:S(2)}) collective-permute-start(bf16[512,384]{1,0:T(8,128)(2,1)} %slice.291), channel_id=1, source_target_pairs={{0,4},{4,0},{1,5},{5,1},{2,6},{6,2},{3,7},{7,3},{8,12},{12,8},{9,1... | collective-permute-start | bytes 1179656 | tf_op jit(solution)/shard_map/ppermute | solution.py:334
  544.1 2.0 copy-start.16
  546.1 2.4 copy-start.3
  546.1 6.5 slice-start
  548.0 4.6 slice-start.1
  557.7 210.5 %all-reduce.6.cloned.1.call-start = ((), (), s32[]{:S(2)}) async-start(), calls=%async_computation.1 | async-start | bytes 5308416 | tf_op jit(solution)/shard_map/psum | solution.py:1690
  561.5 2.3 copy-start.9
  561.5 2.3 copy-start.10
  561.5 2.5 copy-start.12
  561.5 2.5 copy-start.13
  563.0 62.5 %collective-permute-start.32 = (bf16[384,2304]{1,0:T(8,128)(2,1)}, bf16[384,2304]{1,0:T(8,128)(2,1)}, u32[]{:S(2)}, u32[]{:S(2)}) collective-permute-start(bf16[384,2304]{1,0:T(8,128)(2,1)} %get-tuple-element.207), channel_id=1, source_target_pairs={{0,2},{1,3},{2,0},{3,1},{4,6},{5,7},{6,4},{7,5},{8,10},{9,11},{10,... | collective-permute-start | bytes 5308424 | tf_op jit(solution)/shard_map/ppermute | solution.py:338
  564.0 3.5 copy-start.24
  565.5 3.0 copy-start.20
  565.5 6.1 copy-start.18
  565.5 58.3 %collective-permute-start.31 = (bf16[1152,384]{1,0:T(8,128)(2,1)}, bf16[1152,384]{1,0:T(8,128)(2,1)}, u32[]{:S(2)}, u32[]{:S(2)}) collective-permute-start(bf16[1152,384]{1,0:T(8,128)(2,1)} %get-tuple-element.228), channel_id=1, source_target_pairs={{0,2},{1,3},{2,0},{3,1},{4,6},{5,7},{6,4},{7,5},{8,10},{9,11},{10,... | collective-permute-start | bytes 2654216 | tf_op jit(solution)/shard_map/ppermute | solution.py:338
  567.5 97.3 %collective-permute-start.21 = (bf16[512,384]{1,0:T(8,128)(2,1)}, bf16[512,384]{1,0:T(8,128)(2,1)}, u32[]{:S(2)}, u32[]{:S(2)}) collective-permute-start(bf16[512,384]{1,0:T(8,128)(2,1)} %slice.297), channel_id=1, source_target_pairs={{0,2},{1,3},{2,0},{3,1},{4,6},{5,7},{6,4},{7,5},{8,10},{9,11},{10,... | collective-permute-start | bytes 1179656 | tf_op jit(solution)/shard_map/ppermute | solution.py:338
  570.3 94.6 %collective-permute-start.20 = (bf16[512,384]{1,0:T(8,128)(2,1)}, bf16[512,384]{1,0:T(8,128)(2,1)}, u32[]{:S(2)}, u32[]{:S(2)}) collective-permute-start(bf16[512,384]{1,0:T(8,128)(2,1)} %add_convert_fusion.2), channel_id=1, source_target_pairs={{0,4},{4,0},{1,5},{5,1},{2,6},{6,2},{3,7},{7,3},{8,12},{12,8},{9,1... | collective-permute-start | bytes 1179656 | tf_op jit(solution)/shard_map/ppermute | solution.py:334
  623.8 41.1 %collective-permute-start.18 = (bf16[512,384]{1,0:T(8,128)(2,1)}, bf16[512,384]{1,0:T(8,128)(2,1)S(1)}, u32[]{:S(2)}, u32[]{:S(2)}) collective-permute-start(bf16[512,384]{1,0:T(8,128)(2,1)} %add_convert_fusion.3), channel_id=1, source_target_pairs={{0,2},{1,3},{2,0},{3,1},{4,6},{5,7},{6,4},{7,5},{8,10},{9,11},{10,... | collective-permute-start | bytes 1179656 | tf_op jit(solution)/shard_map/ppermute | solution.py:338
  625.5 47.4 %collective-permute-start.28 = (f32[2,4,128,128]{3,2,1,0:T(8,128)}, f32[2,4,128,128]{3,2,1,0:T(8,128)}, u32[]{:S(2)}, u32[]{:S(2)}) collective-permute-start(f32[2,4,128,128]{3,2,1,0:T(8,128)} %pad_maximum_fusion.15), channel_id=1, source_target_pairs={{0,2},{1,3},{2,0},{3,1},{4,6},{5,7},{6,4},{7,5},{8,10},{9,11},{10,... | collective-permute-start | bytes 1572872 | tf_op jit(solution)/shard_map/ppermute | solution.py:338
  664.9 10.3 %collective-permute-start.27 = (f32[1024,192]{0,1:T(8,128)}, f32[1024,192]{0,1:T(8,128)}, u32[]{:S(2)}, u32[]{:S(2)}) collective-permute-start(f32[1024,192]{0,1:T(8,128)} %copy.83), channel_id=1, source_target_pairs={{0,1},{1,0},{2,3},{3,2},{4,5},{5,4},{6,7},{7,6},{8,9},{9,8},{10,11... | collective-permute-start | bytes 2359304 | tf_op jit(solution)/shard_map/ppermute | solution.py:342
  665.6 2.4 copy-start.8
  669.6 1.8 copy-start.11
  670.8 9.4 %collective-permute-start.22 = (f32[1024,192]{0,1:T(8,128)}, f32[1024,192]{0,1:T(8,128)}, u32[]{:S(2)}, u32[]{:S(2)}) collective-permute-start(f32[1024,192]{0,1:T(8,128)} %copy.79), channel_id=1, source_target_pairs={{0,1},{1,0},{2,3},{3,2},{4,5},{5,4},{6,7},{7,6},{8,9},{9,8},{10,11... | collective-permute-start | bytes 2359304 | tf_op jit(solution)/shard_map/ppermute | solution.py:342
  685.1 83.0 %copy-start.14 = (bf16[1152,384]{1,0:T(8,128)(2,1)S(1)}, bf16[1152,384]{1,0:T(8,128)(2,1)}, u32[]{:S(2)}) copy-start(bf16[1152,384]{1,0:T(8,128)(2,1)} %get-tuple-element.200) | copy-start | bytes 2654212
  (15 other events, 17.4 us)
Sparse Core Ops, SparseCore 0:
  55.9 62.8 all-gather.2
  557.8 103.2 all-reduce.7
  663.5 104.5 all-reduce.5

commit v3 on v2

--- a/solution.py
+++ b/solution.py
@@ -324,7 +324,7 @@
 
 BF = jnp.bfloat16
 F32 = jnp.float32
-VMEM_LIMIT = 56 * 1024 * 1024
+VMEM_LIMIT = 60 * 1024 * 1024
 ROW_BLOCK = 256
 GELU_A = 0.7978845608028654
 GELU_B = 0.044715
@@ -462,6 +462,107 @@
         device_id=device,
         device_id_type=MESH_ID,
     )
+
+
+def neighbour_core():
+    col = lax.axis_index("col")
+    return {"col": col + 1 - 2 * lax.rem(col, 2)}
+
+
+def neighbour_end():
+    seq = lax.axis_index("seq")
+    return {"seq": seq + 1 - 2 * lax.rem(seq, 2)}
+
+
+def neighbour_middle():
+    return {"seq": 3 - lax.axis_index("seq")}
+
+
+def greet_all(devices):
+    barrier = pltpu.get_barrier_semaphore()
+    for device in devices:
+        pl.semaphore_signal(barrier, inc=1, device_id=device, device_id_type=MESH_ID)
+    pl.semaphore_wait(barrier, len(devices))
+
+
+def row_step(ref):
+    rows, lanes = ref.shape
+    step = 16
+    while step * 2 * lanes <= 32768 and rows % (step * 2) == 0:
+        step *= 2
+    return step
+
+
+def plus_in(dst, src):
+    step = row_step(dst)
+
+    def one(n, carry):
+        at = pl.ds(pl.multiple_of(n * step, step), step)
+        dst[at, :] = (dst[at, :].astype(F32) + src[at, :].astype(F32)).astype(dst.dtype)
+        return carry
+
+    lax.fori_loop(0, dst.shape[0] // step, one, 0)
+
+
+def put_in(dst, src):
+    step = row_step(dst)
+
+    def one(n, carry):
+        at = pl.ds(pl.multiple_of(n * step, step), step)
+        dst[at, :] = src[at, :].astype(dst.dtype)
+        return carry
+
+    lax.fori_loop(0, dst.shape[0] // step, one, 0)
+
+
+class SeqSum:
+    def __init__(self, pieces, sems, base):
+        self.pieces = pieces
+        count = len(pieces)
+        self.to_end = [message(s, a, neighbour_end(), sems, base + n) for n, (s, a, b) in enumerate(pieces)]
+        self.across = [
+            message(s, b, neighbour_middle(), sems, base + count + n) for n, (s, a, b) in enumerate(pieces)
+        ]
+        seq = lax.axis_index("seq")
+        self.middle = (seq == 1) | (seq == 2)
+        self.end = (seq == 0) | (seq == 3)
+
+    def begin(self, n):
+        @pl.when(self.end)
+        def _():
+            self.to_end[n].start()
+
+    def relay(self, n):
+        s, a, b = self.pieces[n]
+
+        @pl.when(self.middle)
+        def _():
+            self.to_end[n].wait_recv()
+            plus_in(s, a)
+            self.across[n].start()
+
+    def settle(self, n):
+        s, a, b = self.pieces[n]
+
+        @pl.when(self.middle)
+        def _():
+            self.across[n].wait_recv()
+            self.across[n].wait_send()
+            plus_in(s, b)
+            self.to_end[n].start()
+
+    def finish(self, n):
+        s, a, b = self.pieces[n]
+
+        @pl.when(self.end)
+        def _():
+            self.to_end[n].wait_recv()
+            self.to_end[n].wait_send()
+            put_in(s, a)
+
+        @pl.when(self.middle)
+        def _():
+            self.to_end[n].wait_send()
 
 
 def scatter_messages(q1, q2, q3, r3, rx, ry, sems, base):
@@ -810,9 +911,9 @@
 def feed_body(blocks, *refs):
     (x0, x1, x2, x3, e0, e1, e2, e3, mid, cot, gain, near, far, wd) = refs[:14]
     outs = refs[14:18]
-    (dx, own, gx, gy, gd, gain_grad, g_down, g_gu) = refs[18:26]
-    (wgu, load, n2, hid, ee, err, scale) = refs[26:33]
-    (q0, q1, q2, q3, r3, rx, ry, dots, dots_x, dots_y, send, recv) = refs[33:]
+    (dx, own, gx, gy, gd, gain_grad, s_down, s_gu) = refs[18:26]
+    (wgu, load, n2, hid, ee, err, scale, stage, c_down, c_gu) = refs[26:36]
+    (q0, q1, q2, q3, r3, rx, ry, dots, dots_x, dots_y, send, recv) = refs[36:]
     i = pl.program_id(0)
     sems = (send, recv)
     scatter = scatter_messages(q1, q2, q3, r3, rx, ry, sems, 0)
@@ -827,7 +928,7 @@
     @pl.when(i == 0)
     def _():
         copies = load_rows(near, far, wgu, load)
-        greet()
+        greet_all((neighbour_x(), neighbour_y(), neighbour_core()))
         for c in copies:
             c.wait()
 
@@ -935,19 +1036,58 @@
         gather[5].start()
 
     tiles = units // width
-
-    @pl.when((i >= blocks) & (i < blocks + tiles))
-    def _():
-        at = pl.ds(pl.multiple_of((i - blocks) * width, width), width)
-        g_down[...] = dot_tn(hid[:, at], ee[...]).astype(BF)
-
-    @pl.when((i >= blocks + tiles) & (i < blocks + tiles + 4))
-    def _():
-        at = pl.ds(pl.multiple_of((i - blocks - tiles) * width, width), width)
-        g_gu[...] = dot_tn(n2[:, at], err[...]).astype(BF)
+    to_core = [
+        message(stage, c_gu.at[pl.ds(n * width, width), :], neighbour_core(), sems, 14 + n) for n in (0, 1)
+    ] + [
+        message(
+            stage.at[:, pl.ds(n * 2 * width, 2 * width)],
+            c_down.at[pl.ds(n * width, width), :],
+            neighbour_core(),
+            sems,
+            16 + n,
+        )
+        for n in range(tiles)
+    ]
+
+    def gu_tile(n):
+        return dot_tn(n2[:, n * width : (n + 1) * width], err[...])
+
+    for n in (0, 1):
+
+        @pl.when(i == blocks + n)
+        def _():
+            g = gu_tile(2 + n).astype(BF)
+            if n:
+                to_core[0].wait_send()
+            stage[...] = g
+            to_core[n].start()
+
+    for n in range(tiles):
+
+        @pl.when(i == blocks + 2 + n)
+        def _():
+            at = slice(n * width, (n + 1) * width)
+            g = dot_tn(hid[:, at], ee[...])
+            if n == 0:
+                to_core[1].wait_send()
+            stage[:, n * 2 * width : (n + 1) * 2 * width] = g[:, 2 * width :].astype(BF)
+            to_core[2 + n].start()
+            s_down[at, :] = g[:, : 2 * width].astype(BF)
+
+    for n in (1, 0):
+
+        @pl.when(i == blocks + tiles + 3 - n)
+        def _():
+            to_core[n].wait_recv()
+            at = slice(n * width, (n + 1) * width)
+            s_gu[...] = (gu_tile(n) + c_gu[at, :].astype(F32)).astype(BF)
 
     @pl.when(i == blocks + tiles + 4)
     def _():
+        for n in range(tiles):
+            to_core[2 + n].wait_recv()
+            to_core[2 + n].wait_send()
+        plus_in(s_down, c_down)
         for n in (1, 2, 4, 5):
             gather[n].wait_recv()
         for m in scatter + gather + [small_x, small_y]:
@@ -963,8 +1103,7 @@
     held = functools.partial(held_spec, block, last=blocks - 1)
     chunk = pltpu.VMEM((rows, width), BF)
     lanes = pltpu.VMEM((8, rows), F32)
-    down_spec = pl.BlockSpec((width, 4 * width), lambda i: (jnp.clip(i - blocks, 0, tiles - 1), 0))
-    gu_spec = pl.BlockSpec((width, 2 * units), lambda i: (jnp.clip(i - blocks - tiles, 0, 3), 0))
+    gu_spec = pl.BlockSpec((width, 2 * units), lambda i: (jnp.where(i >= blocks + tiles + 3, 0, 1), 0))
     return pl.pallas_call(
         functools.partial(feed_body, blocks),
         grid=(blocks + tiles + 5,),
@@ -974,12 +1113,12 @@
         out_specs=[held(width)] * 4
         + [whole_spec((rows, width))] * 2
         + [any_spec()] * 3
-        + [whole_spec((8, width)), down_spec, gu_spec],
+        + [whole_spec((8, width)), whole_spec((units, 2 * width)), gu_spec],
         out_shape=[sds((rows, width), F32)]
         + [sds((rows, width), BF)] * 3
         + [sds((rows, width), F32)]
         + [sds((rows, width), BF)] * 4
-        + [sds((8, width), F32), sds((units, 4 * width), BF), sds((4 * width, 2 * units), BF)],
+        + [sds((8, width), F32), sds((units, 2 * width), BF), sds((2 * width, 2 * units), BF)],
         scratch_shapes=[
             pltpu.VMEM((4 * width, 2 * units), BF),
             pltpu.SemaphoreType.DMA((8,)),
@@ -988,27 +1127,122 @@
             pltpu.VMEM((rows, 4 * width), BF),
             pltpu.VMEM((rows, 2 * units), BF),
             pltpu.VMEM((rows, 1), F32),
+            pltpu.VMEM((width, 2 * units), BF),
+            pltpu.VMEM((units, 2 * width), BF),
+            pltpu.VMEM((2 * width, 2 * units), BF),
             pltpu.VMEM((rows, width), F32),
         ]
         + [chunk] * 6
         + [lanes] * 3
-        + [pltpu.SemaphoreType.DMA((14,))] * 2,
+        + [pltpu.SemaphoreType.DMA((16 + tiles,))] * 2,
         compiler_params=comm_params(3),
         cost_estimate=cost(48 * rows * wd.size, 3 * nbytes(wd) + rows * 30000, rows * units),
         name="feed",
     )(*chunks, *errs, mid, cot, gain, near, far, wd)
 
 
-def adjoint_body(*refs):
+def carried(entries, h, count):
+    state = entries[count - 1, h, 1:2, :]
+    for n in range(count - 2, -1, -1):
+        state = entries[n, h, 1:2, :] + entries[n, h, 0:1, :] * state
+    return state
+
+
+def back_body(heads, blocks, count, *refs):
     errs = refs[0:4]
-    (w, states, branch, recall, off, soft) = refs[4:10]
-    (part, reach, ev, ends, paired, ext) = refs[10:]
-    rows = states.shape[0]
-    width = errs[0].shape[1]
+    (w_out, states, branch, recall, conv, admit, u_head, off, soft) = refs[4:13]
+    (taps, recall_w, admit_w, border, earlier, u, v, near, far, scale, x, dx, gain) = refs[13:26]
+    (sum_gu, sum_down) = refs[26:28]
+    (ev, paired, eu, grad, gain_grad, grad_recall, grad_admit, grad_small) = refs[28:36]
+    (mine_gu, far_gu, mine_down, far_down) = refs[36:40]
+    (part, reach, ext, st, uext, dc, ends, later, edge, from_later, w, load) = refs[40:52]
+    (q0, q1, q2, q3, r3, rx, ry, dots, dots_x, dots_y) = refs[52:62]
+    (s_gu, a_gu, b_gu, s_dn, a_dn, b_dn, store, send, recv) = refs[62:]
+    i = pl.program_id(0)
+    sems = (send, recv)
+    seq = lax.axis_index("seq")
+    rows, width = x.shape
+    half = rows // 2
     step = ROW_BLOCK
-
-    @pl.when(pl.program_id(0) == 0)
-    def _():
+    seg = rows // 8
+    channels = heads * 128
+    block = step
+
+    scatter = scatter_messages(q1, q2, q3, r3, rx, ry, sems, 0)
+    small_x = message(dots, dots_x, neighbour_x(), sems, 6)
+    small_y = message(dots_x, dots_y, neighbour_y(), sems, 7)
+    hand_on = [message(ends, later.at[n - 1], {"seq": seq - n}, sems, 7 + n) for n in range(1, count + 1)]
+    base = 8 + count
+    hand_edge = message(edge, from_later, {"seq": seq - 1}, sems, base)
+    base += 1
+
+    rows_gu, rows_dn = width // 4, sum_down.shape[0] // 2
+    group_gu, group_dn = (s_gu, a_gu, b_gu), (s_dn, a_dn, b_dn)
+
+    def gu_at(n):
+        return pl.ds(n * rows_gu, rows_gu)
+
+    def dn_at(n):
+        return pl.ds(n * rows_dn, rows_dn)
+
+    places = [("gu", n) for n in (4, 5, 6, 7)] + [("far", n) for n in (0, 1)]
+    places += [("own", n) for n in (0, 1)] + [("gu", n) for n in (0, 1, 2, 3)]
+
+    def view(kind, n, ref):
+        if kind == "gu":
+            return ref.at[gu_at(n), :]
+        return ref.at[dn_at(n), pl.ds(width if kind == "far" else 0, width)]
+
+    pieces = [
+        [view(kind, n, r) for r in (group_gu if kind == "gu" else group_dn)] for kind, n in places
+    ]
+    total = SeqSum(pieces, sems, base)
+    base += 2 * len(pieces)
+    to_y, to_out = {}, {}
+    for p, (kind, n) in enumerate(places):
+        source = pieces[p][0]
+        if kind == "far":
+            to_y[p] = message(source, far_down.at[dn_at(n), :], neighbour_y(), sems, base + len(to_y))
+        elif kind == "own":
+            to_out[p] = pltpu.make_async_copy(source, mine_down.at[dn_at(n), :], store.at[len(to_out)])
+        elif n >= 4:
+            to_y[p] = message(source, far_gu.at[gu_at(n - 4), :], neighbour_y(), sems, base + len(to_y))
+        else:
+            to_out[p] = pltpu.make_async_copy(source, mine_gu.at[gu_at(n), :], store.at[len(to_out)])
+    loads = [
+        pltpu.make_async_copy(sum_gu, s_gu, load.at[8]),
+        pltpu.make_async_copy(sum_down, s_dn, load.at[9]),
+    ]
+
+    def tick(t):
+        if t + 2 < len(pieces):
+            total.begin(t + 2)
+        if t < len(pieces):
+            total.relay(t)
+        if 0 <= t - 1 < len(pieces):
+            total.settle(t - 1)
+        if 0 <= t - 2 < len(pieces):
+            total.finish(t - 2)
+            if t - 2 in to_y:
+                to_y[t - 2].start()
+            else:
+                to_out[t - 2].start()
+
+    @pl.when(i == 0)
+    def _():
+        for c in loads:
+            c.start()
+        copies = load_rows(near, far, w, load)
+        later[...] = jnp.zeros_like(later)
+        from_later[...] = jnp.zeros_like(from_later)
+        greet_all(
+            [neighbour_x(), neighbour_y()]
+            + [{"seq": lax.rem(seq + n, count + 1)} for n in range(1, count + 1)]
+        )
+        for c in loads + copies:
+            c.wait()
+        total.begin(0)
+        total.begin(1)
         for r in range(0, rows, step):
             at = slice(r, r + step)
             for j in (0, 1):
@@ -1016,297 +1250,337 @@
                 paired[at, j * width : (j + 1) * width] = k.astype(BF)
                 paired[at, (j + 2) * width : (j + 3) * width] = p.astype(BF)
 
-    for r in range(0, rows, step):
-        o = off[8 + r : 8 + r + step, :]
-        ell = -8.0 * recall[r : r + step, :] * soft[0:1, :]
-        ext[r : r + step, :] = jnp.where(o > 0, jnp.exp(ell), 0.0)
-        at = slice(r, r + step)
-        dm = None
-        for j in range(4):
-            term = dot_nt(errs[j][at, :], w[:, j * width : (j + 1) * width])
-            dm = term if dm is None else dm + term
-        act, slope = gelu_pair(branch[at, :])
-        ev[at, :] = (dm * states[at, :] * slope).astype(BF)
-        part[r : r + step, :] = dm * act
-    ext[rows : rows + 8, :] = jnp.ones((8, 128), F32)
-    for r in range(0, rows, step):
-        reach[r : r + step, :] = ext[r + 1 : r + 1 + step, :]
-    seg = rows // 8
-
-    def one(n, carry):
-        h, p = carry
-        at = pl.ds(seg - 1 - n, 8, stride=seg)
-        d = reach[at, :]
-        h = d * h + part[at, :]
-        p = d * p
-        part[at, :] = h
-        reach[at, :] = p
-        return h, p
-
-    zero = jnp.zeros((8, 128), F32)
-    h, p = lax.fori_loop(0, seg, one, (zero, zero + 1.0), unroll=8)
-    carry_h, carry_p = h[7:8, :], p[7:8, :]
-    for s in range(6, -1, -1):
-        at = slice(s * seg, (s + 1) * seg)
-        c = reach[at, :]
-        part[at, :] = part[at, :] + c * carry_h
-        reach[at, :] = c * carry_p
-        carry_h = h[s : s + 1, :] + p[s : s + 1, :] * carry_h
-        carry_p = p[s : s + 1, :] * carry_p
-    first = ext[0:1, :]
-    ends[0:1, :] = first * carry_p
-    ends[1:2, :] = first * carry_h
-    ends[2:8, :] = jnp.zeros((6, 128), F32)
-
-
-def adjoint(errs, w, states, branch, recall, off, soft):
-    rows, channels = states.shape
-    width = errs[0].shape[1]
-    return pl.pallas_call(
-        adjoint_body,
-        grid=(channels // 128,),
-        in_specs=[whole_spec((rows, width))] * 4
-        + [pl.BlockSpec((128, w.shape[1]), lambda h: (h, 0))]
-        + [head_spec(rows)] * 3
-        + [whole_spec(off.shape), head_spec(1)],
-        out_specs=[head_spec(rows)] * 3 + [head_spec(8), whole_spec((rows, 4 * width))],
-        out_shape=[sds((rows, channels), F32)] * 2
-        + [sds((rows, channels), BF), sds((8, channels), F32), sds((rows, 4 * width), BF)],
-        scratch_shapes=[pltpu.VMEM((rows + 8, 128), F32)],
-        compiler_params=params(),
-        cost_estimate=cost(2 * rows * w.size, rows * channels * 20 + rows * D * 6, rows * channels * 3),
-        name="adjoint",
-    )(*errs, w, states, branch, recall, off, soft)
-
-
-def recur_back_body(count, *refs):
-    (part, reach, later, earlier, states, conv, recall, admit, off) = refs[:9]
-    (u, border, taps, recall_w, admit_w, soft) = refs[9:15]
-    (du, out_border, grad_recall, grad_admit, grad_small, st, uext, dc) = refs[15:]
-    rows = states.shape[0]
-    step = ROW_BLOCK
-    st[0:8, :] = jnp.broadcast_to(chain(earlier, count), (8, 128))
-    st[8 : 8 + rows, :] = states[...]
-    uext[0:8, :] = border[...]
-    uext[8 : 8 + rows, :] = u[...]
-    incoming = chain(later, count)
-    sp = soft[0:1, :]
-    dc[0:8, :] = jnp.zeros((8, 128), F32)
-    dc[8 + rows : 16 + rows, :] = jnp.zeros((8, 128), F32)
-    gr = ga = None
-    sums = [None] * (KW + 1)
-
-    def plus(total, term):
-        return term if total is None else total + term
-
-    for r in range(0, rows, step):
-        at = slice(r, r + step)
-        o = off[8 + r : 8 + r + step, :]
-        adj = part[at, :] + reach[at, :] * incoming
-        rec, adm, cv = recall[at, :], admit[at, :], conv[at, :]
-        ell = -8.0 * rec * sp
-        e = jnp.exp(ell)
-        m = jnp.sqrt(minus_expm1(2.0 * ell))
-        previous = jnp.where(o > 0, e * st[7 + r : 7 + r + step, :], 0.0)
-        ac = adj * cv
-        d_ell = adj * previous - ac * adm * (e * e) / m
-        d_rp = -8.0 * sp * d_ell * rec * (1.0 - rec)
-        d_ip = ac * m * adm * (1.0 - adm)
-        d_conv = (
-            adj * m * adm + dot_nt(d_rp, recall_w[0], PRECISE) + dot_nt(d_ip, admit_w[0], PRECISE)
-        )
-        dc[8 + r : 8 + r + step, :] = d_conv
-        gr = plus(gr, dot_tn(cv, d_rp, PRECISE))
-        ga = plus(ga, dot_tn(cv, d_ip, PRECISE))
-        for k in range(KW):
-            term = d_conv * uext[8 + r - k : 8 + r - k + step, :]
-            if k:
-                term = jnp.where(o >= k, term, 0.0)
-            sums[k] = plus(sums[k], jnp.sum(term, axis=0, keepdims=True))
-        sums[KW] = plus(sums[KW], jnp.sum(rec * d_ell, axis=0, keepdims=True))
-    grad_recall[0] = gr
-    grad_admit[0] = ga
-    for k in range(KW + 1):
-        grad_small[k : k + 1, :] = sums[k]
-    grad_small[KW + 1 : 8, :] = jnp.zeros((7 - KW, 128), F32)
-    for r in range(0, rows, step):
-        total = taps[0:1, :] * dc[8 + r : 8 + r + step, :]
+    @pl.when(i < heads)
+    def _():
+        sp = soft[0:1, :]
+        part_h, reach_h = part.at[i], reach.at[i]
+        lane = pl.ds(pl.multiple_of(i * 128, 128), 128)
+        for r in range(0, rows, step):
+            at = slice(r, r + step)
+            o = off[8 + r : 8 + r + step, :]
+            ext[at, :] = jnp.where(o > 0, jnp.exp(-8.0 * recall[at, :] * sp), 0.0)
+            dm = None
+            for j in range(4):
+                term = dot_nt(errs[j][at, :], w_out[:, j * width : (j + 1) * width])
+                dm = term if dm is None else dm + term
+            act, slope = gelu_pair(branch[at, :])
+            ev[at, lane] = (dm * states[at, :] * slope).astype(BF)
+            part_h[at, :] = dm * act
+        ext[rows : rows + 8, :] = jnp.ones((8, 128), F32)
+        for r in range(0, rows, step):
+            reach_h[r : r + step, :] = ext[r + 1 : r + 1 + step, :]
+
+        def one(n, carry):
+            h, p = carry
+            at = pl.ds(seg - 1 - n, 8, stride=seg)
+            d = reach_h[at, :]
+            h = d * h + part_h[at, :]
+            p = d * p
+            part_h[at, :] = h
+            reach_h[at, :] = p
+            return h, p
+
+        zero = jnp.zeros((8, 128), F32)
+        h, p = lax.fori_loop(0, seg, one, (zero, zero + 1.0), unroll=8)
+        carry_h, carry_p = h[7:8, :], p[7:8, :]
+        for s in range(6, -1, -1):
+            at = slice(s * seg, (s + 1) * seg)
+            c = reach_h[at, :]
+            part_h[at, :] = part_h[at, :] + c * carry_h
+            reach_h[at, :] = c * carry_p
+            carry_h = h[s : s + 1, :] + p[s : s + 1, :] * carry_h
+            carry_p = p[s : s + 1, :] * carry_p
+        first = ext[0:1, :]
+        ends[i, 0:1, :] = first * carry_p
+        ends[i, 1:2, :] = first * carry_h
+        ends[i, 2:8, :] = jnp.zeros((6, 128), F32)
+
+    for n in range(1, count + 1):
+
+        @pl.when((i == heads - 1) & (seq >= n))
+        def _():
+            hand_on[n - 1].start()
+
+        @pl.when((i == heads) & (seq <= count - n))
+        def _():
+            hand_on[n - 1].wait_recv()
+
+    @pl.when((i >= heads) & (i < 2 * heads))
+    def _():
+        h = i - heads
+        part_h, reach_h = part.at[h], reach.at[h]
+        st[0:8, :] = jnp.broadcast_to(chain(earlier, count), (8, 128))
+        st[8 : 8 + rows, :] = states[...]
+        uext[0:8, :] = border[...]
+        uext[8 : 8 + rows, :] = u_head[...]
+        incoming = carried(later, h, count)
+        sp = soft[0:1, :]
+        dc[0:8, :] = jnp.zeros((8, 128), F32)
+        dc[8 + rows : 16 + rows, :] = jnp.zeros((8, 128), F32)
+        gr = ga = None
+        sums = [None] * (KW + 1)
+
+        def plus(total, term):
+            return term if total is None else total + term
+
+        for r in range(0, rows, step):
+            at = slice(r, r + step)
+            o = off[8 + r : 8 + r + step, :]
+            adj = part_h[at, :] + reach_h[at, :] * incoming
+            rec, adm, cv = recall[at, :], admit[at, :], conv[at, :]
+            ell = -8.0 * rec * sp
+            e = jnp.exp(ell)
+            m = jnp.sqrt(minus_expm1(2.0 * ell))
+            previous = jnp.where(o > 0, e * st[7 + r : 7 + r + step, :], 0.0)
+            ac = adj * cv
+            d_ell = adj * previous - ac * adm * (e * e) / m
+            d_rp = -8.0 * sp * d_ell * rec * (1.0 - rec)
+            d_ip = ac * m * adm * (1.0 - adm)
+            d_conv = (
+                adj * m * adm
+                + dot_nt(d_rp, recall_w[0], PRECISE)
+                + dot_nt(d_ip, admit_w[0], PRECISE)
+            )
+            dc[8 + r : 8 + r + step, :] = d_conv
+            gr = plus(gr, dot_tn(cv, d_rp, PRECISE))
+            ga = plus(ga, dot_tn(cv, d_ip, PRECISE))
+            for k in range(KW):
+                term = d_conv * uext[8 + r - k : 8 + r - k + step, :]
+                if k:
+                    term = jnp.where(o >= k, term, 0.0)
+                sums[k] = plus(sums[k], jnp.sum(term, axis=0, keepdims=True))
+            sums[KW] = plus(sums[KW], jnp.sum(rec * d_ell, axis=0, keepdims=True))
+        grad_recall[0] = gr
+        grad_admit[0] = ga
+        for k in range(KW + 1):
+            grad_small[k : k + 1, :] = sums[k]
+        grad_small[KW + 1 : 8, :] = jnp.zeros((7 - KW, 128), F32)
+        for r in range(0, rows, step):
+            du = taps[0:1, :] * dc[8 + r : 8 + r + step, :]
+            for k in range(1, KW):
+                o = off[8 + r + k : 8 + r + k + step, :]
+                term = taps[k : k + 1, :] * dc[8 + r + k : 8 + r + k + step, :]
+                du = du + jnp.where(o >= k, term, 0.0)
+            part_h[r : r + step, :] = du
+        over = jnp.zeros((8, 128), F32)
         for k in range(1, KW):
-            o = off[8 + r + k : 8 + r + k + step, :]
-            term = taps[k : k + 1, :] * dc[8 + r + k : 8 + r + k + step, :]
-            total = total + jnp.where(o >= k, term, 0.0)
-        du[r : r + step, :] = total
-    total = jnp.zeros((8, 128), F32)
-    for k in range(1, KW):
-        term = taps[k : k + 1, :] * dc[k : k + 8, :]
-        total = total + jnp.where(off[k : k + 8, :] >= k, term, 0.0)
-    out_border[...] = total
-
-
-def recur_back(part, reach, later, earlier, states, conv, recall, admit, off, u, border, taps, rw, aw, soft):
-    rows, channels = part.shape
-    heads = channels // 128
-    gate = pl.BlockSpec((1, 128, 128), lambda h: (h, 0, 0))
-    return pl.pallas_call(
-        functools.partial(recur_back_body, later.shape[0] // 8),
-        grid=(heads,),
-        in_specs=[
-            head_spec(rows),
-            head_spec(rows),
-            head_spec(later.shape[0]),
-            head_spec(earlier.shape[0]),
-            head_spec(rows),
-            head_spec(rows),
-            head_spec(rows),
-            head_spec(rows),
-            whole_spec(off.shape),
-            head_spec(rows),
-            head_spec(8),
-            head_spec(KW),
-            gate,
-            gate,
-            head_spec(1),
-        ],
-        out_specs=[head_spec(rows), head_spec(8), gate, gate, head_spec(8)],
-        out_shape=[
-            sds((rows, channels), F32),
-            sds((8, channels), F32),
-            sds((heads, 128, 128), F32),
-            sds((heads, 128, 128), F32),
-            sds((8, channels), F32),
-        ],
-        scratch_shapes=[
-            pltpu.VMEM((rows + 8, 128), F32),
-            pltpu.VMEM((rows + 8, 128), F32),
-            pltpu.VMEM((rows + 16, 128), F32),
-        ],
-        compiler_params=params(),
-        cost_estimate=cost(rows * channels * 128 * 48, rows * channels * 36, rows * channels * 4),
-        name="recur_back",
-    )(part, reach, later, earlier, states, conv, recall, admit, off, u, border, taps, rw, aw, soft)
-
-
-def enter_back_body(blocks, *refs):
-    (du, tail, ev, u, v, near, far, scale, x, dx, gain) = refs[:11]
-    (eu, grad, gain_grad) = refs[11:14]
-    (w, load, q0, q1, q2, q3, r3, rx, ry, dots, dots_x, dots_y, send, recv) = refs[14:]
-    i = pl.program_id(0)
-    sems = (send, recv)
-    scatter = scatter_messages(q1, q2, q3, r3, rx, ry, sems, 0)
-    small_x = message(dots, dots_x, neighbour_x(), sems, 6)
-    small_y = message(dots_x, dots_y, neighbour_y(), sems, 7)
-    block, channels = du.shape
-    rows, width = x.shape
-    half = rows // 2
-
-    @pl.when(i == 0)
-    def _():
-        copies = load_rows(near, far, w, load)
-        greet()
-        for c in copies:
-            c.wait()
-
-    @pl.when(i < blocks)
-    def _():
-        at = pl.ds(pl.multiple_of(i * block, block), block)
-        d = du[...]
-        extra = jnp.concatenate([jnp.zeros((block - 8, channels), F32), tail[...]], axis=0)
-        d = d + jnp.where(i == blocks - 1, extra, 0.0)
+            term = taps[k : k + 1, :] * dc[k : k + 8, :]
+            over = over + jnp.where(off[k : k + 8, :] >= k, term, 0.0)
+        edge[h] = over
+
+    @pl.when((i == 2 * heads - 1) & (seq >= 1))
+    def _():
+        hand_edge.start()
+
+    @pl.when((i == 2 * heads) & (seq < count))
+    def _():
+        hand_edge.wait_recv()
+
+    third = 2 * heads
+
+    @pl.when((i >= third) & (i < third + blocks))
+    def _():
+        at = pl.ds(pl.multiple_of((i - third) * block, block), block)
+        d = jnp.concatenate([part[h, at, :] for h in range(heads)], axis=1)
+        late = jnp.concatenate([from_later[h] for h in range(heads)], axis=1)
+        extra = jnp.concatenate([jnp.zeros((block - 8, channels), F32), late], axis=0)
+        d = d + jnp.where(i == third + blocks - 1, extra, 0.0)
         e = d.astype(BF)
         eu[...] = e
-        b = ev[...]
+        b = ev[at, :]
         dots[:, at] = row_sums(e.astype(F32) * u[...] + b.astype(F32) * v[...])
         for j, q in ((3, q3), (1, q1), (2, q2), (0, q0)):
             rows_w = slice(j * width, (j + 1) * width)
             q[at, :] = (dot_nt(e, w[rows_w, :channels]) + dot_nt(b, w[rows_w, channels:])).astype(q.dtype)
 
-    @pl.when(i == blocks // 2 - 1)
+    @pl.when(i == third + blocks // 2 - 1)
     def _():
         scatter[0].start()
         scatter[2].start()
 
-    @pl.when(i == blocks - 1)
+    @pl.when(i == third + blocks - 1)
     def _():
         scatter[1].start()
         small_x.start()
-
-    @pl.when(i == blocks)
-    def _():
         scatter[0].wait_recv()
         add_into(q2, r3, 0, half)
         scatter[3].start()
         scatter[4].start()
+
+    last = third + blocks
+
+    @pl.when(i == last)
+    def _():
         small_x.wait_recv()
         dots_x[...] = dots_x[...] + dots[...]
         small_y.start()
         scatter[1].wait_recv()
         add_into(q1, r3, half, half)
         scatter[5].start()
+
+    def finish(start, first):
+        scatter[first].wait_recv()
+        scatter[first + 1].wait_recv()
+        sum_grad = None
+        for r in range(start, start + half, 128):
+            at = slice(r, r + 128)
+            d = q0[at, :] + rx[at, :].astype(F32) + ry[at, :].astype(F32)
+            s, m = scale[at, :], x[at, :]
+            t = as_column(dots_x[:, at] + dots_y[:, at], width)
+            grad[at, :] = dx[at, :] + s * gain[0:1, :width] * d - m * (s * s) * t * (1.0 / D)
+            term = jnp.sum(d * m * s, axis=0, keepdims=True)
+            sum_grad = term if sum_grad is None else sum_grad + term
+        return sum_grad
+
+    for t in range(len(pieces) + 2):
+
+        @pl.when(i == t + 1)
+        def _():
+            tick(t)
+
+    @pl.when(i == last + 1)
+    def _():
         small_y.wait_recv()
-        sum_grad = None
-        for base, first in ((0, 2), (half, 4)):
-            scatter[first].wait_recv()
-            scatter[first + 1].wait_recv()
-            for r in range(base, base + half, 128):
-                at = slice(r, r + 128)
-                d = q0[at, :] + rx[at, :].astype(F32) + ry[at, :].astype(F32)
-                s, m = scale[at, :], x[at, :]
-                t = as_column(dots_x[:, at] + dots_y[:, at], width)
-                grad[at, :] = dx[at, :] + s * gain[0:1, :width] * d - m * (s * s) * t * (1.0 / D)
-                term = jnp.sum(d * m * s, axis=0, keepdims=True)
-                sum_grad = term if sum_grad is None else sum_grad + term
-        gain_grad[0:1, :] = sum_grad
-        for m in scatter + [small_x, small_y]:
+        gain_grad[0:1, :] = finish(0, 2)
+
+    @pl.when(i == last + 2)
+    def _():
+        gain_grad[0:1, :] = gain_grad[0:1, :] + finish(half, 4)
+        for n in range(1, count + 1):
+
+            @pl.when(seq >= n)
+            def _():
+                hand_on[n - 1].wait_send()
+
+        @pl.when(seq >= 1)
+        def _():
+            hand_edge.wait_send()
+
+        for m in to_y.values():
+            m.wait_recv()
+        for m in scatter + [small_x, small_y] + list(to_y.values()):
             m.wait_send()
-
-
-def enter_back(du, tail, ev, u, v, near, far, scale, x, dx, gain):
-    rows, channels = u.shape
+        for c in to_out.values():
+            c.wait()
+
+
+def back(errs, w_out, states, v, recall, conv, admit, u, off, soft, taps, rw, aw, border, earlier, near, far, scale, x, dx, gain, sum_gu, sum_down):
+    rows, channels = states.shape
     width = x.shape[1]
+    heads = channels // 128
     block = ROW_BLOCK
     blocks = rows // block
-    held = functools.partial(held_spec, block, last=blocks - 1)
+    count = earlier.shape[0] // 8
+    steps = 2 * heads + blocks + 3
+    assert steps >= 15
+
+    def both(i):
+        return jnp.where(i < heads, i, jnp.clip(i - heads, 0, heads - 1))
+
+    def second(i):
+        return jnp.clip(i - heads, 0, heads - 1)
+
+    def on(shape, pick, axis):
+        if axis == 0:
+            return pl.BlockSpec(shape, lambda i: (pick(i),) + (0,) * (len(shape) - 1))
+        return pl.BlockSpec(shape, lambda i: (0, pick(i)))
+
+    def third(i):
+        return jnp.clip(i - 2 * heads, 0, blocks - 1)
+
+    def first(i):
+        return jnp.minimum(i, heads - 1)
+
+    tall = (rows, 128)
+    gate = (1, 128, 128)
     chunk = pltpu.VMEM((rows, width), BF)
     lanes = pltpu.VMEM((8, rows), F32)
+    gu, dn = pltpu.VMEM(sum_gu.shape, BF), pltpu.VMEM(sum_down.shape, BF)
+    piece = pltpu.VMEM((heads, 8, 128), F32)
+    half_gu, half_dn = (sum_gu.shape[0] // 2, sum_gu.shape[1]), (sum_down.shape[0], width)
+    count_sems = 8 + count + 1 + 24 + 6
     return pl.pallas_call(
-        functools.partial(enter_back_body, blocks),
-        grid=(blocks + 1,),
-        in_specs=[held(channels), whole_spec(tail.shape)]
-        + [held(channels)] * 3
-        + [any_spec(), any_spec(), whole_spec(scale.shape), whole_spec(x.shape), whole_spec(dx.shape)]
-        + [whole_spec(gain.shape)],
-        out_specs=[held(channels), whole_spec((rows, width)), whole_spec((8, width))],
-        out_shape=[sds((rows, channels), BF), sds((rows, width), F32), sds((8, width), F32)],
-        scratch_shapes=[pltpu.VMEM((4 * width, 2 * channels), BF), pltpu.SemaphoreType.DMA((8,))]
-        + [pltpu.VMEM((rows, width), F32)]
+        functools.partial(back_body, heads, blocks, count),
+        grid=(steps,),
+        in_specs=[whole_spec((rows, width))] * 4
+        + [
+            on((128, 4 * width), first, 0),
+            on(tall, both, 1),
+            on(tall, first, 1),
+            on(tall, both, 1),
+            on(tall, second, 1),
+            on(tall, second, 1),
+            on(tall, second, 1),
+            whole_spec(off.shape),
+            on((1, 128), both, 1),
+            on((KW, 128), second, 1),
+            on(gate, second, 0),
+            on(gate, second, 0),
+            on((8, 128), second, 1),
+            on((8 * count, 128), second, 1),
+            on((block, channels), third, 0),
+            on((block, channels), third, 0),
+            any_spec(),
+            any_spec(),
+            whole_spec(scale.shape),
+            whole_spec(x.shape),
+            whole_spec(dx.shape),
+            whole_spec(gain.shape),
+            any_spec(),
+            any_spec(),
+        ],
+        out_specs=[
+            whole_spec((rows, channels)),
+            whole_spec((rows, 4 * width)),
+            on((block, channels), third, 0),
+            whole_spec((rows, width)),
+            whole_spec((8, width)),
+            on(gate, second, 0),
+            on(gate, second, 0),
+            on((8, 128), second, 1),
+        ]
+        + [any_spec()] * 4,
+        out_shape=[
+            sds((rows, channels), BF),
+            sds((rows, 4 * width), BF),
+            sds((rows, channels), BF),
+            sds((rows, width), F32),
+            sds((8, width), F32),
+            sds((heads, 128, 128), F32),
+            sds((heads, 128, 128), F32),
+            sds((8, channels), F32),
+            sds(half_gu, BF),
+            sds(half_gu, BF),
+            sds(half_dn, BF),
+            sds(half_dn, BF),
+        ],
+        scratch_shapes=[pltpu.VMEM((heads, rows, 128), F32)] * 2
+        + [
+            pltpu.VMEM((rows + 8, 128), F32),
+            pltpu.VMEM((rows + 8, 128), F32),
+            pltpu.VMEM((rows + 8, 128), F32),
+            pltpu.VMEM((rows + 16, 128), F32),
+            piece,
+            pltpu.VMEM((count, heads, 8, 128), F32),
+            piece,
+            piece,
+            pltpu.VMEM((4 * width, 2 * channels), BF),
+            pltpu.SemaphoreType.DMA((10,)),
+            pltpu.VMEM((rows, width), F32),
+        ]
         + [chunk] * 6
         + [lanes] * 3
-        + [pltpu.SemaphoreType.DMA((8,))] * 2,
+        + [gu] * 3
+        + [dn] * 3
+        + [pltpu.SemaphoreType.DMA((6,))]
+        + [pltpu.SemaphoreType.DMA((count_sems,))] * 2,
         compiler_params=comm_params(4),
-        cost_estimate=cost(40 * rows * near.size, rows * channels * 16 + nbytes(near, far)),
-        name="enter_back",
-    )(du, tail, ev, u, v, near, far, scale, x, dx, gain)
-
-
-def neighbour_core():
-    col = lax.axis_index("col")
-    return {"col": col + 1 - 2 * lax.rem(col, 2)}
-
-
-def neighbour_end():
-    seq = lax.axis_index("seq")
-    return {"seq": seq + 1 - 2 * lax.rem(seq, 2)}
-
-
-def neighbour_middle():
-    return {"seq": 3 - lax.axis_index("seq")}
-
-
-def plus_in(dst, src, rows, start=0):
-    step = 64
-    for r in range(start, start + rows, step):
-        at = slice(r, min(r + step, start + rows))
-        dst[at, :] = (dst[at, :].astype(F32) + src[at, :].astype(F32)).astype(dst.dtype)
+        cost_estimate=cost(4 * rows * near.size * 16, rows * channels * 60, rows * channels * 8),
+        name="back",
+    )(
+        *errs, w_out, states, v, recall, conv, admit, u, off, soft, taps, rw, aw, border, earlier,
+        u, v, near, far, scale, x, dx, gain, sum_gu, sum_down,
+    )
 
 
 def tail_body(n1, eu, ev, mixed, er, small, mine_in, far_in, mine_out, far_out, small_out, *scratch):
@@ -1316,31 +1590,20 @@
     width = er.shape[1] // 4
     half = width // 2
     channels = eu.shape[1]
-    seq = lax.axis_index("seq")
-    middle = (seq == 1) | (seq == 2)
-    end = (seq == 0) | (seq == 3)
-    barrier = pltpu.get_barrier_semaphore()
-    for device in (neighbour_core(), neighbour_y(), neighbour_end(), neighbour_middle()):
-        pl.semaphore_signal(barrier, inc=1, device_id=device, device_id_type=MESH_ID)
-    pl.semaphore_wait(barrier, 4)
-
-    a, b = pl.ds(0, half), pl.ds(half, half)
+    greet_all((neighbour_core(), neighbour_y(), neighbour_end(), neighbour_middle()))
+    half_rows = pl.ds(0, half)
+    a, b = half_rows, pl.ds(half, half)
     c, d = pl.ds(2 * half, half), pl.ds(3 * half, half)
-    everything = pl.ds(0, s_sm.shape[0])
+    inner = s_out.shape[0] // 2
+    up, low = pl.ds(0, inner), pl.ds(inner, inner)
     lanes_far, lanes_own = pl.ds(width, width), pl.ds(0, width)
-    group_in, group_out, group_sm = (s_in, a_in, b_in), (s_out, a_out, b_out), (s_sm, a_sm, b_sm)
-    views = [
-        [r.at[everything, :] for r in group_sm],
-        [r.at[:, lanes_far] for r in group_out],
-        [r.at[:, lanes_own] for r in group_out],
-        [r.at[c, :] for r in group_in],
-        [r.at[d, :] for r in group_in],
-        [r.at[a, :] for r in group_in],
-        [r.at[b, :] for r in group_in],
-    ]
-    count = len(views)
-    to_end = [message(s, z1, neighbour_end(), sems, n) for n, (s, z1, z2) in enumerate(views)]
-    to_middle = [message(s, z2, neighbour_middle(), sems, count + n) for n, (s, z1, z2) in enumerate(views)]
+    group_in, group_out = (s_in, a_in, b_in), (s_out, a_out, b_out)
+    pieces = [[s_sm, a_sm, b_sm]]
+    pieces += [[r.at[at, lanes_far] for r in group_out] for at in (up, low)]
+    pieces += [[r.at[at, lanes_own] for r in group_out] for at in (up, low)]
+    pieces += [[r.at[at, :] for r in group_in] for at in (c, d, a, b)]
+    count = len(pieces)
+    total = SeqSum(pieces, sems, 0)
     base = 2 * count
     core_sm = message(small, c_sm, neighbour_core(), sems, base)
     core_out = message(p_out, c_out, neighbour_core(), sems, base + 1)
@@ -1348,11 +1611,12 @@
         message(p_in.at[at, :], c_in.at[at, :], neighbour_core(), sems, base + 2 + n)
         for n, at in enumerate((c, d, a, b))
     ]
-    y_out_m = message(s_out.at[:, lanes_far], y_out, neighbour_y(), sems, base + 6)
-    y_in_m = [
-        message(s_in.at[at, :], y_in.at[to, :], neighbour_y(), sems, base + 7 + n)
-        for n, (at, to) in enumerate(((c, a), (d, b)))
-    ]
+    to_y = {
+        1: message(s_out.at[up, lanes_far], y_out.at[up, :], neighbour_y(), sems, base + 6),
+        2: message(s_out.at[low, lanes_far], y_out.at[low, :], neighbour_y(), sems, base + 7),
+        5: message(s_in.at[c, :], y_in.at[a, :], neighbour_y(), sems, base + 8),
+        6: message(s_in.at[d, :], y_in.at[b, :], neighbour_y(), sems, base + 9),
+    }
 
     core_sm.start()
     g = dot_tn(mixed[...], er[...])
@@ -1367,100 +1631,50 @@
         target[where, :channels] = dot_tn(n1[:, at], eu[...]).astype(BF)
         target[where, channels:] = dot_tn(n1[:, at], ev[...]).astype(BF)
 
-    def begin(n):
-        @pl.when(end)
-        def _():
-            to_end[n].start()
-
-    def relay(n):
-        s, z1, z2 = views[n]
-
-        @pl.when(middle)
-        def _():
-            to_end[n].wait_recv()
-            plus_in(s, z1, s.shape[0])
-            to_middle[n].start()
-
-    def settle(n):
-        s, z1, z2 = views[n]
-
-        @pl.when(middle)
-        def _():
-            to_middle[n].wait_recv()
-            to_middle[n].wait_send()
-            plus_in(s, z2, s.shape[0])
-            to_end[n].start()
-
-    def finish(n):
-        s, z1, z2 = views[n]
-
-        @pl.when(end)
-        def _():
-            to_end[n].wait_recv()
-            to_end[n].wait_send()
-            step = 64
-            for r in range(0, s.shape[0], step):
-                at = slice(r, min(r + step, s.shape[0]))
-                s[at, :] = z1[at, :]
-
-        @pl.when(middle)
-        def _():
-            to_end[n].wait_send()
-
     core_sm.wait_recv()
-    plus_in(s_sm, c_sm, s_sm.shape[0])
-    begin(0)
+    plus_in(s_sm, c_sm)
+    total.begin(0)
     tile(3, p_in, width)
     core_in[0].start()
     core_in[1].start()
     core_out.wait_recv()
-    plus_in(s_out, c_out, s_out.shape[0])
-    begin(1)
-    begin(2)
+    plus_in(s_out, c_out)
+    for n in range(1, 5):
+        total.begin(n)
     tile(1, s_in, width)
     tile(2, p_in, 0)
     core_in[2].start()
     core_in[3].start()
     core_in[0].wait_recv()
     core_in[1].wait_recv()
-    plus_in(s_in, c_in, width, width)
-    begin(3)
-    begin(4)
+    plus_in(s_in.at[pl.ds(width, width), :], c_in.at[pl.ds(width, width), :])
+    total.begin(5)
+    total.begin(6)
+    total.relay(0)
+    total.relay(1)
+    total.settle(0)
     tile(0, s_in, 0)
     core_in[2].wait_recv()
     core_in[3].wait_recv()
-    plus_in(s_in, c_in, width, 0)
-    begin(5)
-    begin(6)
-    relay(0)
-    relay(1)
-    settle(0)
-    relay(2)
-    settle(1)
-    finish(0)
-    finish(1)
-    y_out_m.start()
-    for n in range(3, count):
-        relay(n)
-        settle(n - 1)
-        if n < 5:
-            finish(n - 1)
-            if n == 4:
-                y_in_m[0].start()
-    settle(count - 1)
-    finish(4)
-    y_in_m[1].start()
-    finish(5)
-    finish(6)
-    small_out[...] = s_sm[...]
-    mine_in[...] = s_in[0:width, :]
-    mine_out[...] = s_out[:, 0:width]
-    y_out_m.wait_recv()
-    far_out[...] = y_out[...]
-    for m in y_in_m:
+    plus_in(s_in.at[pl.ds(0, width), :], c_in.at[pl.ds(0, width), :])
+    total.begin(7)
+    total.begin(8)
+    for n in range(2, count + 2):
+        if n < count:
+            total.relay(n)
+        if n - 1 < count:
+            total.settle(n - 1)
+        total.finish(n - 2)
+        if n - 2 in to_y:
+            to_y[n - 2].start()
+    put_in(small_out, s_sm)
+    put_in(mine_in, s_in.at[pl.ds(0, width), :])
+    put_in(mine_out, s_out.at[:, lanes_own])
+    for m in to_y.values():
         m.wait_recv()
-    far_in[...] = y_in[...]
-    for m in [core_sm, core_out, y_out_m] + core_in + y_in_m:
+    put_in(far_out, y_out)
+    put_in(far_in, y_in)
+    for m in [core_sm, core_out] + core_in + list(to_y.values()):
         m.wait_send()
 
 
@@ -1480,28 +1694,13 @@
         + [tall] * 5
         + [pltpu.VMEM(quarter_out, BF)]
         + [tiny] * 4
-        + [pltpu.SemaphoreType.DMA((23,))] * 2,
+        + [pltpu.SemaphoreType.DMA((28,))] * 2,
         compiler_params=pltpu.CompilerParams(
             vmem_limit_bytes=VMEM_LIMIT, collective_id=6, has_side_effects=True
         ),
         cost_estimate=cost(20 * rows * n1.shape[1] * channels * 3, nbytes(n1, eu, ev, mixed, er)),
         name="tail",
     )(n1, eu, ev, mixed, er, small)
-
-
-def add_low(a, b):
-    return (a.astype(F32) + b.astype(F32)).astype(BF)
-
-
-def total_seq(g):
-    count = lax.axis_size("seq")
-    if count != 4:
-        return lax.psum(g, "seq")
-    place = lax.axis_index("seq")
-    g = add_low(g, lax.ppermute(g, "seq", [(0, 1), (3, 2)]))
-    g = add_low(g, lax.ppermute(g, "seq", [(1, 2), (2, 1)]))
-    back = lax.ppermute(g, "seq", [(1, 0), (2, 3)])
-    return jnp.where((place == 0) | (place == 3), back, g)
 
 
 def local_fast(
@@ -1651,19 +1850,18 @@
     near_gu, sib_gu, w_out, w_down = late_weights(*late[1:])
     earlier = neighbours(ends, 1)
     states, mixed, mid, *mid_all = mix(local_state, cum, v, x, earlier, w_out)
-    p0, p1, p2, p3, dx2, *dx_all, grad_feed, g_down, g_gu = feed(
+    p0, p1, p2, p3, dx2, *dx_all, grad_feed, sum_down, sum_gu = feed(
         mid_all, [g_low] + errs, mid, g, gains_all, near_gu, sib_gu, w_down
     )
     outs = collect(tuple(zip(*(in_halves(p) for p in (p0, p1, p2, p3)))))
     out_chunk = jnp.concatenate(outs, axis=0) + mid
 
-    part_adj, reach, ev, back_ends, er = adjoint(dx_all, w_out, states, v, recall, off, soft)
-    later = neighbours(back_ends, -1)
-    du, out_border, grad_recall, grad_admit, grad_small = recur_back(
-        part_adj, reach, later, earlier, states, conv, recall, admit, off, u, border, taps, rw, aw, soft
-    )
-    from_later = shifted(out_border, -1)
-    eu, grad_chunk, grad_mixer = enter_back(du, from_later, ev, u, v, near_in, sib_in, s1, x, dx2, gains_all)
+    (
+        ev, er, eu, grad_chunk, grad_mixer, grad_recall, grad_admit, grad_small, mine_gu, far_gu, mine_down, far_down
+    ) = back(
+        dx_all, w_out, states, v, recall, conv, admit, u, off, soft, taps, rw, aw, border, earlier,
+        near_in, sib_in, s1, x, dx2, gains_all, sum_gu, sum_down,
+    )
 
     def rows_out(mine, theirs):
         wide = jnp.where(
@@ -1679,16 +1877,7 @@
         swapped = jnp.concatenate([tall[:, part:], tall[:, :part]], axis=1)
         return jnp.where(lower, tall, swapped).astype(F32)
 
-    kept = 4 * part
     channels = taps.shape[1]
-    sum_down = add_low(g_down[:, :kept], flip_core(g_down[:, kept:]))
-    sum_gu = add_low(g_gu[:kept], flip_core(g_gu[kept:]))
-    mine_down, far_down = sum_down[:, :lanes], flip_y(sum_down[:, lanes:])
-    mine_gu, far_gu = sum_gu[:lanes], flip_y(sum_gu[lanes:])
-    mine_down, mine_gu = lax.psum((mine_down, mine_gu), "seq")
-    far_down, far_gu, _, _ = lax.optimization_barrier((far_down, far_gu, mine_down, mine_gu))
-    far_down, far_gu = lax.psum((far_down, far_gu), "seq")
-
     own = channels // 2
     pieces = [
         grad_small[:KW].reshape(-1),

time: 794 us -> 678 us (0.85)
  waiting for transfers between devices: 184 us -> 23 us
  Pallas kernels: 421 us -> 490 us
  local copies, waits for them, and re-layouts: 76.7 us -> 65.8 us
    psum x2 -> x0, waiting for transfers between devices: 116 us -> none  [the longest x1 81.3 us: local_fast(): far_down, far_gu = lax.psum((far_down, far_gu), 'seq')]
    pallas_call x3 -> x1, Pallas kernels: 77.8 us -> 148 us  [back(): pl.pallas_call(functools.partial(back_body, heads, blocks, count), grid=(...]
    ppermute x10 -> x8, waiting for transfers between devices: 63.5 us -> 18 us  [flip_y(): return lax.ppermute(a, 'col', [(i, i ^ 2) for i in range(4)])]
    ppermute x8 -> x4, starting transfers between devices: 20.1 us -> 15.3 us  [passed_along(): return lax.ppermute(block, axis, route)]
    unnamed x105 -> x107, local copies, waits for them, and re-layouts: 28.3 us -> 24.8 us
  transfers between devices with their start and end apart: 36 -> 26, of which waited for: 8 -> 6; matrix products, arithmetic and copies ran while one was open for 13% -> 12% of each run, Pallas kernels for 37% -> 20%
where the time goes in v3:
time: 678 us; the launch traced here: 671 us
  Pallas kernels  490 us (72%)
  local copies, waits for them, and re-layouts  65.8 us (10%)
  other arithmetic  44.6 us (7%)
  starting transfers between devices  32.3 us (5%)
  waiting for transfers between devices  23 us (3%)
  between operations  15.2 us (2%)
    pallas_call x1, Pallas kernels, back(): pl.pallas_call(functools.partial(back_body, heads, blocks, count), grid=(...  148 us
    pallas_call x1, Pallas kernels, feed(): pl.pallas_call(functools.partial(feed_body, blocks), grid=(blocks + tiles...  107 us
    pallas_call x1, Pallas kernels, tail(): pl.pallas_call(tail_body, out_shape=[sds(quarter_in, BF)] * 2 + [sds(quar...  102 us
    pallas_call x1, Pallas kernels, mix(): pl.pallas_call(functools.partial(mix_body, entries.shape[0] // 8, blocks)...  63.9 us
    pallas_call x1, Pallas kernels, norm_uv(): pl.pallas_call(functools.partial(norm_uv_body, blocks), grid=(blocks,), i...  37.5 us
    pallas_call x1, Pallas kernels, recur(): pl.pallas_call(functools.partial(recur_body, heads), grid=(heads,), in_sp...  31.3 us
    unnamed x107, local copies, waits for them, and re-layouts  24.8 us
    ppermute x8, waiting for transfers between devices, flip_y(): return lax.ppermute(a, 'col', [(i, i ^ 2) for i in range(4)])  18 us
  transfers between devices with their start and end apart: 26, of which 6 were waited for; matrix products, arithmetic and copies ran while one was open for 12% of the time, Pallas kernels for 20%

profile of v3, /device:TPU:0, one launch (start us, length us, event | category | flops | bytes accessed | tf_op | source)
XLA Modules:
  0.0 670.7 jit_solution(10979870428868253676)
XLA Ops:
  7.3 2.5 fusion.10
  9.8 3.0 collective-permute-start.5
  15.4 1.5 dynamic-slice_dynamic-update-slice_fusion.7
  17.0 1.5 dynamic-slice_dynamic-update-slice_fusion.6
  18.5 1.5 dynamic-slice_dynamic-update-slice_fusion.5
  20.0 1.5 dynamic-slice_dynamic-update-slice_fusion.4
  21.5 1.5 dynamic-slice_dynamic-update-slice_fusion.3
  23.1 1.5 dynamic-slice_dynamic-update-slice_fusion.2
  24.6 1.6 dynamic-slice_dynamic-update-slice_fusion
  26.2 1.5 dynamic-slice_dynamic-update-slice_fusion.1
  27.9 2.8 collective-permute-done.5
  32.0 1.3 pad_maximum_fusion.9.near.refs_20_
  33.6 1.7 collective-permute-start.2
  35.3 1.8 collective-permute-done.2
  37.2 2.5 collective-permute-start.3
  39.7 7.9 %collective-permute-done.3 = f32[2,384]{1,0:T(2,128)S(1)} collective-permute-done((f32[2,384]{1,0:T(2,128)S(1)}, f32[2,384]{1,0:T(2,128)S(1)}, u32[]{:S(2)}, u32[]{:S(2)}) %collective-permute-start.3) | collective-permute-done | bytes 3104 | tf_op jit(solution)/shard_map/ppermute | solution.py:338
  48.7 2.4 collective-permute-done.4
  55.7 2.4 copy.70
  58.1 1.5 copy.72
  59.6 3.0 fusion.19
  62.6 37.5 %norm_uv.1 = (bf16[1024,1536]{1,0:T(8,128)(2,1)}, f32[1024,512]{1,0:T(8,128)}, f32[1024,512]{1,0:T(8,128)}, f32[1024,1]{1,0:T(8,128)}) custom-call(bf16[1024,384]{1,0:T(8,128)(2,1)} %get-tuple-element.194.own, f32[2,1536]{1,0:T(2,128)} %concatenate.135.gain.refs_10_.refs_25_, bf16[2,384,1024]{2,1,0:T(8,128)(2,1)} %pad_maximum_fusion.9.near.refs_20_, ...), custom_call_target="tpu_custom_call" | custom-call | flops 48318382080 | bytes 3145728 | tf_op jit(solution)/shard_map/norm_uv/pallas_call | solution.py:700
  100.8 3.5 collective-permute-start.7
  104.3 1.7 fusion.18
  106.6 31.3 %recur.1 = (f32[1024,512]{1,0:T(8,128)}, f32[1024,512]{1,0:T(8,128)}, f32[1024,512]{1,0:T(8,128)}, f32[1024,512]{1,0:T(8,128)}, f32[1024,512]{1,0:T(8,128)}, /*i...) custom-call(f32[1024,512]{1,0:T(8,128)} %get-tuple-element.68.u.refs_10_.refs_, ...), custom_call_target="tpu_custom_call" | custom-call | flops 1610612736 | bytes 12582912 | tf_op jit(solution)/shard_map/recur/pallas_call | solution.py:799
  137.9 3.8 collective-permute-start.10
  141.7 6.2 collective-permute-start.11
  147.9 1.8 collective-permute-start.12
  149.8 2.1 fusion.20
  162.6 1.3 pad_maximum_fusion.7.w.refs_4_
  163.9 1.9 pad_maximum_fusion.refs_13_
  165.8 63.9 %mix.1 = (f32[1024,512]{1,0:T(8,128)}, bf16[1024,512]{1,0:T(8,128)(2,1)}, f32[1024,384]{1,0:T(8,128)}, bf16[1024,384]{1,0:T(8,128)(2,1)}, bf16[1024,384]{1,0:T(8...) custom-call(f32[1024,512]{1,0:T(8,128)} %get-tuple-element.69.local, ...), custom_call_target="tpu_custom_call" | custom-call | flops 32212254720 | bytes 11010048 | tf_op jit(solution)/shard_map/mix/pallas_call | solution.py:894
  229.7 107.4 %feed.1 = (f32[1024,384]{1,0:T(8,128)}, bf16[1024,384]{1,0:T(8,128)(2,1)}, bf16[1024,384]{1,0:T(8,128)(2,1)}, bf16[1024,384]{1,0:T(8,128)(2,1)}, f32[1024,384]{1...) custom-call(bf16[1024,384]{1,0:T(8,128)(2,1)} %get-tuple-element.76., ...), custom_call_target="tpu_custom_call" | custom-call | flops 86973087744 | bytes 41336832 | tf_op jit(solution)/shard_map/feed/pallas_call | solution.py:1107
  337.0 147.6 %back.1 = (bf16[1024,512]{1,0:T(8,128)(2,1)}, bf16[1024,1536]{1,0:T(8,128)(2,1)}, bf16[1024,512]{1,0:T(8,128)(2,1)}, f32[1024,384]{1,0:T(8,128)}, f32[8,384]{1,0...) custom-call(bf16[1024,384]{1,0:T(8,128)(2,1)} %get-tuple-element.90., ...), custom_call_target="tpu_custom_call" | custom-call | flops 51539607552 | bytes 31457280 | tf_op jit(solution)/shard_map/back/pallas_call | solution.py:1502
  485.4 1.3 divide_multiply_fusion
  486.7 2.5 maximum_select_fusion.6
  489.2 1.9 fusion.21
  491.3 1.3 copy-done.17
  493.2 1.3 fusion.22
  494.9 1.5 fusion.25
  501.8 102.3 %tail.1 = (bf16[384,1024]{1,0:T(8,128)(2,1)}, bf16[384,1024]{1,0:T(8,128)(2,1)}, bf16[512,384]{1,0:T(8,128)(2,1)}, bf16[512,384]{1,0:T(8,128)(2,1)}, f32[1088,128]{1,0:T(8,128)}) custom-call(bf16[1024,1536]{1,0:T(8,128)(2,1)} %get-tuple-element.103.n1, bf16[1024,512]{1,0:T(8,128)(2,1)} %get-tuple-element.104.eu, bf16[1024,512]{1,0:T(8,128)(2,1)} %get-tuple-element.105.ev, ...), custom_call_target="tpu_custom_call" | custom-call | flops 48318382080 | bytes 9437184 | tf_op jit(solution)/shard_map/tail/pallas_call | solution.py:1689
  604.1 1.6 maximum_select_fusion.13
  610.8 1.7 slice_bitcast_fusion.3
  616.4 2.6 fusion.2
  619.0 2.2 fusion.1
  622.2 2.1 fusion
  624.3 1.5 fusion.13
  628.6 1.2 collective-permute-start.21
  631.0 1.2 add_convert_fusion
  632.3 1.2 collective-permute-start.20
  633.5 3.1 collective-permute-done.17
  636.6 1.2 add_convert_fusion.1
  639.4 1.4 fusion.12
  640.9 4.9 collective-permute-done.18
  645.7 1.4 convert_add_fusion.1
  647.4 1.3 slice_bitcast_fusion.2
  648.7 1.2 copy.76
  649.9 1.4 fusion.11
  651.3 1.3 maximum_select_fusion.8
  653.7 1.5 copy.80
  655.2 1.8 maximum_select_fusion.1
  657.0 1.7 copy.82
  658.7 1.5 copy.77
  660.2 1.8 maximum_select_fusion
  661.9 1.7 copy.81
  (216 shorter events, 45.9 us)
Async XLA Ops:
  7.2 5.5 copy-start.19
  7.2 142.6 %all-gather.3.cloned.1.call-start = ((), (), s32[]{:S(2)}) async-start(), calls=%async_computation | async-start | bytes 3809280 | tf_op jit(solution)/shard_map/all_gather | solution.py:1789
  9.7 4.0 copy-start.40
  9.8 4.0 copy-start.41
  9.8 20.9 %collective-permute-start.5 = (bf16[2,384,512]{2,1,0:T(8,128)(2,1)}, bf16[2,384,512]{2,1,0:T(8,128)(2,1)}, u32[]{:S(2)}, u32[]{:S(2)}) collective-permute-start(bf16[2,384,512]{2,1,0:T(8,128)(2,1)} %get-tuple-element.224), channel_id=1, source_target_pairs={{0,2},{1,3},{2,0},{3,1},{4,6},{5,7},{6,4},{7,5},{8,10},{9,11},{10,... | collective-permute-start | bytes 2359304 | tf_op jit(solution)/shard_map/ppermute | solution.py:338
  12.7 1.7 copy-start.20
  13.7 41.9 %collective-permute-start = (f32[1,1024,192]{1,2,0:T(8,128)}, f32[1,1024,192]{1,2,0:T(8,128)}, u32[]{:S(2)}, u32[]{:S(2)}) collective-permute-start(f32[1,1024,192]{1,2,0:T(8,128)} %get-tuple-element.226), channel_id=1, source_target_pairs={{0,1},{1,0},{2,3},{3,2},{4,5},{5,4},{6,7},{7,6},{8,9},{9,8},{10,11... | collective-permute-start | bytes 2359304 | tf_op jit(solution)/shard_map/ppermute | solution.py:342
  13.8 19.7 %collective-permute-start.1 = (f32[2,192]{1,0:T(2,128)S(1)}, f32[2,192]{1,0:T(2,128)S(1)}, u32[]{:S(2)}, u32[]{:S(2)}) collective-permute-start(f32[2,192]{1,0:T(2,128)S(1)} %pad_maximum_fusion.19), channel_id=1, source_target_pairs={{0,1},{1,0},{2,3},{3,2},{4,5},{5,4},{6,7},{7,6},{8,9},{9,8},{10,11... | collective-permute-start | bytes 4616 | tf_op jit(solution)/shard_map/ppermute | solution.py:342
  15.4 42.7 %collective-permute-start.9 = (f32[1,1024,192]{1,2,0:T(8,128)}, f32[1,1024,192]{1,2,0:T(8,128)}, u32[]{:S(2)}, u32[]{:S(2)}) collective-permute-start(f32[1,1024,192]{1,2,0:T(8,128)} %get-tuple-element.222), channel_id=1, source_target_pairs={{0,1},{1,0},{2,3},{3,2},{4,5},{5,4},{6,7},{7,6},{8,9},{9,8},{10,11... | collective-permute-start | bytes 2359304 | tf_op jit(solution)/shard_map/ppermute | solution.py:342
  27.8 27.9 %collective-permute-start.13 = (bf16[992,384]{1,0:T(8,128)(2,1)}, bf16[992,384]{1,0:T(8,128)(2,1)}, u32[]{:S(2)}, u32[]{:S(2)}) collective-permute-start(bf16[992,384]{1,0:T(8,128)(2,1)} %dynamic-slice_dynamic-update-slice_fusion.1), channel_id=1, source_target_pairs={{0,2},{1,3},{2,0},{3,1},{4,6},{5,7},{6,4},{7,5},{8,10},{9,11},{10,... | collective-permute-start | bytes 2285576 | tf_op jit(solution)/shard_map/ppermute | solution.py:338
  31.9 1.3 copy-start.42
  31.9 16.7 %copy-start.37 = (f32[4,256]{1,0:T(4,128)S(1)}, f32[4,256]{1,0:T(4,128)}, u32[]{:S(2)}) copy-start(f32[4,256]{1,0:T(4,128)} %param.21) | copy-start | bytes 12292
  31.9 16.7 %copy-start.39 = (f32[256]{0:T(256)S(1)}, f32[256]{0:T(256)}, u32[]{:S(2)}) copy-start(f32[256]{0:T(256)} %param.24) | copy-start | bytes 3076
  32.0 19.2 %copy-start.34 = (f32[8,128,128]{2,1,0:T(8,128)S(1)}, f32[8,128,128]{2,1,0:T(8,128)}, u32[]{:S(2)}) copy-start(f32[8,128,128]{2,1,0:T(8,128)} %param.23) | copy-start | bytes 1572868
  32.0 19.2 %copy-start.35 = (f32[8,128,128]{2,1,0:T(8,128)S(1)}, f32[8,128,128]{2,1,0:T(8,128)}, u32[]{:S(2)}) copy-start(f32[8,128,128]{2,1,0:T(8,128)} %param.22) | copy-start | bytes 1572868
  33.3 29.3 %collective-permute-start.6 = (bf16[2,384,1024]{2,1,0:T(8,128)(2,1)}, bf16[2,384,1024]{2,1,0:T(8,128)(2,1)}, u32[]{:S(2)}, u32[]{:S(2)}) collective-permute-start(bf16[2,384,1024]{2,1,0:T(8,128)(2,1)} %pad_maximum_fusion.9.near.refs_20_), channel_id=1, source_target_pairs={{0,1},{1,0},{2,3},{3,2},{4,5},{5,4},{6,7},{7,6},{8,9},{9,8},{10,11... | collective-permute-start | bytes 4718600 | tf_op jit(solution)/shard_map/ppermute | solution.py:342
  33.6 3.6 collective-permute-start.2
  37.2 10.4 %collective-permute-start.3 = (f32[2,384]{1,0:T(2,128)S(1)}, f32[2,384]{1,0:T(2,128)S(1)}, u32[]{:S(2)}, u32[]{:S(2)}) collective-permute-start(f32[2,384]{1,0:T(2,128)S(1)} %pad_maximum_fusion.18), channel_id=1, source_target_pairs={{0,2},{1,3},{2,0},{3,1},{4,6},{5,7},{6,4},{7,5},{8,10},{9,11},{10,... | collective-permute-start | bytes 9224 | tf_op jit(solution)/shard_map/ppermute | solution.py:338
  47.5 3.6 collective-permute-start.4
  51.1 3.3 collective-permute-start.8
  100.8 5.2 collective-permute-start.7
  137.9 15.9 %collective-permute-start.10 = (f32[8,512]{1,0:T(8,128)}, f32[8,512]{1,0:T(8,128)S(1)}, u32[]{:S(2)}, u32[]{:S(2)}) collective-permute-start(f32[8,512]{1,0:T(8,128)} %get-tuple-element.72), channel_id=1, source_target_pairs={{0,8},{8,16},{16,24},{1,9},{9,17},{17,25},{2,10},{10,18},{18,26},{... | collective-permute-start | bytes 49160 | tf_op jit(solution)/shard_map/ppermute | solution.py:27
  141.7 12.1 %collective-permute-start.11 = (f32[8,512]{1,0:T(8,128)}, f32[8,512]{1,0:T(8,128)S(1)}, u32[]{:S(2)}, u32[]{:S(2)}) collective-permute-start(f32[8,512]{1,0:T(8,128)} %get-tuple-element.72), channel_id=1, source_target_pairs={{0,16},{8,24},{1,17},{9,25},{2,18},{10,26},{3,19},{11,27},{4,20},{... | collective-permute-start | bytes 49160 | tf_op jit(solution)/shard_map/ppermute | solution.py:27
  147.9 5.9 collective-permute-start.12
  149.8 3.2 copy-start.33
  149.8 3.3 copy-start.29
  153.7 5.6 collective-permute-start.14
  154.6 1.5 copy-start.30
  155.3 1.6 copy-start.31
  157.5 1.8 copy-start.11
  157.5 72.1 %collective-permute-start.15 = (bf16[2,384,2304]{2,1,0:T(8,128)(2,1)S(1)}, bf16[2,384,2304]{2,1,0:T(8,128)(2,1)}, u32[]{:S(2)}, u32[]{:S(2)}) collective-permute-start(bf16[2,384,2304]{2,1,0:T(8,128)(2,1)S(1)} %pad_maximum_fusion.3.refs_11_), channel_id=1, source_target_pairs={{0,1},{1,0},{2,3},{3,2},{4,5},{5,4},{6,7},{7,6},{8,9},{9,8},{10,11... | collective-permute-start | bytes 10616840 | tf_op jit(solution)/shard_map/ppermute | solution.py:342
  489.2 1.9 copy-start.18
  491.1 1.5 copy-start.17
  494.9 1.8 copy-start
  604.1 1.9 copy-start.32
  605.7 2.9 copy-start.27
  606.0 2.7 copy-start.26
  606.1 1.5 copy-start.15
  607.6 43.8 %collective-permute-start.24 = (f32[2,4,128,128]{3,2,1,0:T(8,128)}, f32[2,4,128,128]{3,2,1,0:T(8,128)}, u32[]{:S(2)}, u32[]{:S(2)}) collective-permute-start(f32[2,4,128,128]{3,2,1,0:T(8,128)} %pad_maximum_fusion.15), channel_id=1, source_target_pairs={{0,2},{1,3},{2,0},{3,1},{4,6},{5,7},{6,4},{7,5},{8,10},{9,11},{10,... | collective-permute-start | bytes 1572872 | tf_op jit(solution)/shard_map/ppermute | solution.py:338
  608.8 2.1 copy-start.12
  610.8 1.7 copy-start.25
  610.8 3.6 copy-start.28
  612.5 3.8 copy-start.4
  612.5 3.8 copy-start.5
  613.5 17.6 %collective-permute-start.19 = (bf16[512,384]{1,0:T(8,128)(2,1)}, bf16[512,384]{1,0:T(8,128)(2,1)}, u32[]{:S(2)}, u32[]{:S(2)}) collective-permute-start(bf16[512,384]{1,0:T(8,128)(2,1)} %get-tuple-element.248), channel_id=1, source_target_pairs={{0,2},{1,3},{2,0},{3,1},{4,6},{5,7},{6,4},{7,5},{8,10},{9,11},{10,... | collective-permute-start | bytes 1179656 | tf_op jit(solution)/shard_map/ppermute | solution.py:338
  615.2 25.6 %collective-permute-start.16 = (bf16[512,384]{1,0:T(8,128)(2,1)}, bf16[512,384]{1,0:T(8,128)(2,1)}, u32[]{:S(2)}, u32[]{:S(2)}) collective-permute-start(bf16[512,384]{1,0:T(8,128)(2,1)} %slice.267), channel_id=1, source_target_pairs={{0,4},{4,0},{1,5},{5,1},{2,6},{6,2},{3,7},{7,3},{8,12},{12,8},{9,1... | collective-permute-start | bytes 1179656 | tf_op jit(solution)/shard_map/ppermute | solution.py:334
  616.4 2.6 copy-start.7
  616.4 2.6 copy-start.8
  619.0 2.2 copy-start.1
  619.0 2.7 copy-start.9
  619.0 3.2 copy-start.10
  626.1 10.6 %collective-permute-start.17 = (bf16[512,384]{1,0:T(8,128)(2,1)}, bf16[512,384]{1,0:T(8,128)(2,1)}, u32[]{:S(2)}, u32[]{:S(2)}) collective-permute-start(bf16[512,384]{1,0:T(8,128)(2,1)} %get-tuple-element.247), channel_id=1, source_target_pairs={{0,4},{4,0},{1,5},{5,1},{2,6},{6,2},{3,7},{7,3},{8,12},{12,8},{9,1... | collective-permute-start | bytes 1179656 | tf_op jit(solution)/shard_map/ppermute | solution.py:334
  627.4 12.0 %copy-start.3 = (bf16[384,1024]{1,0:T(8,128)(2,1)S(1)}, bf16[384,1024]{1,0:T(8,128)(2,1)}, u32[]{:S(2)}) copy-start(bf16[384,1024]{1,0:T(8,128)(2,1)} %copy-done.2) | copy-start | bytes 2359300
  627.4 12.0 %copy-start.23 = (bf16[192,1024]{1,0:T(8,128)(2,1)S(1)}, bf16[192,1024]{1,0:T(8,128)(2,1)}, u32[]{:S(2)}) copy-start(bf16[192,1024]{1,0:T(8,128)(2,1)} %get-tuple-element.239) | copy-start | bytes 1179652
  627.4 12.0 %copy-start.24 = (bf16[192,1024]{1,0:T(8,128)(2,1)S(1)}, bf16[192,1024]{1,0:T(8,128)(2,1)}, u32[]{:S(2)}) copy-start(bf16[192,1024]{1,0:T(8,128)(2,1)} %get-tuple-element.240) | copy-start | bytes 1179652
  628.6 12.2 %collective-permute-start.21 = (bf16[512,384]{1,0:T(8,128)(2,1)S(1)}, bf16[512,384]{1,0:T(8,128)(2,1)S(1)}, u32[]{:S(2)}, u32[]{:S(2)}) collective-permute-start(bf16[512,384]{1,0:T(8,128)(2,1)S(1)} %slice.273), channel_id=1, source_target_pairs={{0,2},{1,3},{2,0},{3,1},{4,6},{5,7},{6,4},{7,5},{8,10},{9,11},{10,... | collective-permute-start | bytes 1179656 | tf_op jit(solution)/shard_map/ppermute | solution.py:338
  632.3 8.6 %collective-permute-start.20 = (bf16[512,384]{1,0:T(8,128)(2,1)S(1)}, bf16[512,384]{1,0:T(8,128)(2,1)S(1)}, u32[]{:S(2)}, u32[]{:S(2)}) collective-permute-start(bf16[512,384]{1,0:T(8,128)(2,1)S(1)} %add_convert_fusion), channel_id=1, source_target_pairs={{0,4},{4,0},{1,5},{5,1},{2,6},{6,2},{3,7},{7,3},{8,12},{12,8},{9,1... | collective-permute-start | bytes 1179656 | tf_op jit(solution)/shard_map/ppermute | solution.py:334
  637.9 7.9 %copy-start.22 = (f32[1024,384]{1,0:T(8,128)S(1)}, f32[1024,384]{1,0:T(8,128)}, u32[]{:S(2)}) copy-start(f32[1024,384]{1,0:T(8,128)} %get-tuple-element.86) | copy-start | bytes 4718596
  637.9 7.8 %collective-permute-start.18 = (bf16[512,384]{1,0:T(8,128)(2,1)S(1)}, bf16[512,384]{1,0:T(8,128)(2,1)S(1)}, u32[]{:S(2)}, u32[]{:S(2)}) collective-permute-start(bf16[512,384]{1,0:T(8,128)(2,1)S(1)} %add_convert_fusion.1), channel_id=1, source_target_pairs={{0,2},{1,3},{2,0},{3,1},{4,6},{5,7},{6,4},{7,5},{8,10},{9,11},{10,... | collective-permute-start | bytes 1179656 | tf_op jit(solution)/shard_map/ppermute | solution.py:338
  640.8 12.9 %collective-permute-start.23 = (f32[1024,192]{0,1:T(8,128)S(1)}, f32[1024,192]{0,1:T(8,128)}, u32[]{:S(2)}, u32[]{:S(2)}) collective-permute-start(f32[1024,192]{0,1:T(8,128)S(1)} %copy.79), channel_id=1, source_target_pairs={{0,1},{1,0},{2,3},{3,2},{4,5},{5,4},{6,7},{7,6},{8,9},{9,8},{10,11... | collective-permute-start | bytes 2359304 | tf_op jit(solution)/shard_map/ppermute | solution.py:342
  645.7 1.5 copy-start.21
  649.9 1.4 copy-start.14
  649.9 1.4 copy-start.16
  649.9 8.8 %collective-permute-start.22 = (f32[1024,192]{0,1:T(8,128)}, f32[1024,192]{0,1:T(8,128)}, u32[]{:S(2)}, u32[]{:S(2)}) collective-permute-start(f32[1024,192]{0,1:T(8,128)} %copy.76), channel_id=1, source_target_pairs={{0,1},{1,0},{2,3},{3,2},{4,5},{5,4},{6,7},{7,6},{8,9},{9,8},{10,11... | collective-permute-start | bytes 2359304 | tf_op jit(solution)/shard_map/ppermute | solution.py:342
  (6 other events, 4.8 us)
Sparse Core Ops, SparseCore 0:
  55.8 62.8 all-gather.2

commit v4 on v3

--- a/solution.py
+++ b/solution.py
@@ -330,22 +330,6 @@
 GELU_B = 0.044715
 
 
-def flip_row(a):
-    return lax.ppermute(a, "row", [(0, 1), (1, 0)])
-
-
-def flip_y(a):
-    return lax.ppermute(a, "col", [(i, i ^ 2) for i in range(4)])
-
-
-def flip_core(a):
-    return lax.ppermute(a, "col", [(i, i ^ 1) for i in range(4)])
-
-
-def shifted(a, distance):
-    return passed_along(a, "seq", distance)
-
-
 def cost(flops, moved, trans=0):
     return pl.CostEstimate(flops=int(flops), bytes_accessed=int(moved), transcendentals=int(trans))
 
@@ -356,23 +340,6 @@
 
 def nbytes(*arrays):
     return sum(a.size * a.dtype.itemsize for a in arrays)
-
-
-def spread(halves):
-    first, second = halves
-    ax, ay = flip_row(first), flip_y(first)
-    bx, by = flip_row(second), flip_y(second)
-    return ((first, ax, ay, flip_y(ax)), (second, bx, by, flip_row(by)))
-
-
-def collect(halves):
-    (a0, a1, a2, a3), (b0, b1, b2, b3) = halves
-    a2 = (a2.astype(F32) + flip_row(a3).astype(F32)).astype(BF)
-    b1 = (b1.astype(F32) + flip_y(b3).astype(F32)).astype(BF)
-    return (
-        a0 + flip_row(a1).astype(F32) + flip_y(a2).astype(F32),
-        b0 + flip_row(b1).astype(F32) + flip_y(b2).astype(F32),
-    )
 
 
 def gelu_pair(v):
@@ -587,6 +554,17 @@
     ]
 
 
+def gather_messages_by_x(own, gx, gy, gd, sems, base):
+    half = own.shape[0] // 2
+    a, b = pl.ds(0, half), pl.ds(half, half)
+    x, y = neighbour_x(), neighbour_y()
+    plan = ((own, gx, a, x), (own, gy, a, y), (own, gx, b, x), (own, gy, b, y), (gy, gd, a, x), (gy, gd, b, x))
+    return [
+        message(src.at[at, :], dst.at[at, :], dev, sems, base + n)
+        for n, (src, dst, at, dev) in enumerate(plan)
+    ]
+
+
 def add_into(dst, src, start, rows):
     step = 128
     for r in range(start, start + rows, step):
@@ -594,22 +572,25 @@
         dst[at, :] = (dst[at, :].astype(F32) + src[at, :].astype(F32)).astype(dst.dtype)
 
 
-def load_rows(near, far, dst, sem):
-    part = near.shape[1] // 2
+def load_rows(gate_w, up_w, sib_own, far, sib_far, dst, sem):
+    width, lanes = far.shape
+    part, units = width // 2, lanes // 2
     row = lax.axis_index("row")
+    y = lax.div(lax.axis_index("col"), 2)
+    own = pl.ds(pl.multiple_of(y * units, units), units)
     copies = []
-    for dy in (0, 1):
-        for dx in (0, 1):
-            start = pl.multiple_of(part * (row + dx - 2 * row * dx), part)
-            for dc, src in enumerate((near, far)):
-                at = ((dy * 2 + dx) * 2 + dc) * part
-                copies.append(
-                    pltpu.make_async_copy(
-                        src.at[dy, pl.ds(start, part), :], dst.at[pl.ds(at, part), :], sem.at[len(copies)]
-                    )
-                )
-    for c in copies:
-        c.start()
+
+    def copy(src, dst):
+        copies.append(pltpu.make_async_copy(src, dst, sem.at[len(copies)]))
+        copies[-1].start()
+
+    for dx in (0, 1):
+        rows = pl.ds(pl.multiple_of(part * (row + dx - 2 * row * dx), part), part)
+        at = [pl.ds(((n // 2 * 2 + dx) * 2 + n % 2) * part, part) for n in range(4)]
+        copy(gate_w.at[rows, own], dst.at[at[0], pl.ds(0, units)])
+        copy(up_w.at[rows, own], dst.at[at[0], pl.ds(units, units)])
+        for n, src in enumerate((sib_own, far, sib_far)):
+            copy(src.at[rows, :], dst.at[at[n + 1], :])
     return copies
 
 
@@ -644,217 +625,363 @@
     return dot_tn(lanes, first, PRECISE)
 
 
-def norm_uv_body(blocks, own, gain, near, far, n1, u, v, scale, w, gx, gy, gd, load, send, recv):
+def chain(entries, count):
+    state = entries[count - 1, 0, 1:2, :]
+    for n in range(count - 2, -1, -1):
+        state = entries[n, 0, 1:2, :] + entries[n, 0, 0:1, :] * state
+    return state
+
+
+def carried(entries, h, count):
+    state = entries[count - 1, h, 1:2, :]
+    for n in range(count - 2, -1, -1):
+        state = entries[n, h, 1:2, :] + entries[n, h, 0:1, :] * state
+    return state
+
+
+class Messages:
+    def __init__(self, sems):
+        self.sems, self.used = sems, 0
+
+    def new(self, src, dst, device):
+        self.used += 1
+        return message(src, dst, device, self.sems, self.used - 1)
+
+    def block(self, maker, *refs):
+        made = maker(*refs, self.sems, self.used)
+        self.used += len(made)
+        return made
+
+
+FRONT_MESSAGES = 80
+
+
+def front_body(heads, blocks, count, *refs):
+    (stream, cot, in_w, br_w, out_w, gate_w, up_w, down_w) = refs[:8]
+    (gains_in, small_in, recall_gate, admit_gate, off) = refs[8:13]
+    (x, g, e_own, w_out, w_down, gains_out, small, s1, u, v, border_out, earlier_out, mid, own) = refs[13:27]
+    (n1, conv, recall, admit, states, mixed) = refs[27:33]
+    (ex, ey, ed, mx, my, md, far_gu, sib_own, sib_far, w_in_out) = refs[33:43]
+    (x_own, x_recv, g_own, g_recv, gains_recv, small_recv, own_low, gx, gy, gd) = refs[43:53]
+    (w_in, gains, border, earlier) = refs[53:57]
+    (wo, wd, local, cum, ext, ends, q0, q1, q2, q3, r3, rx, ry, load, send, recv) = refs[57:]
     i = pl.program_id(0)
-    gather = gather_messages(own, gx, gy, gd, (send, recv), 0)
+    seq, row, col = lax.axis_index("seq"), lax.axis_index("row"), lax.axis_index("col")
+    y = lax.div(col, 2)
+    core = lax.rem(col, 2)
+    rows, width = x.shape
+    part = width // 2
+    half = rows // 2
+    block = rows // blocks
+    channels = u.shape[1]
+    units = gate_w.shape[1] // 2
+    to_x, to_y, to_core = neighbour_x(), neighbour_y(), neighbour_core()
+    made = Messages((send, recv))
+    copies = []
+
+    def copy(src, dst):
+        copies.append(pltpu.make_async_copy(src, dst, load.at[len(copies)]))
+        return copies[-1]
+
+    swap = [
+        made.new(stream.at[1 - core], x_recv, to_core),
+        made.new(gains_in, gains_recv, to_core),
+        made.new(small_in, small_recv, to_core),
+    ]
+    swap_g = made.new(cot.at[1 - core], g_recv, to_core)
+    x_copy, g_copy = copy(stream.at[core], x_own), copy(cot.at[core], g_own)
+    gains_x = made.new(gains.at[:, pl.ds(0, width)], gains.at[:, pl.ds(width, width)], to_x)
+    gains_y = made.new(gains.at[:, pl.ds(0, width)], gains.at[:, pl.ds(2 * width, width)], to_y)
+    gains_d = made.new(gains.at[:, pl.ds(width, width)], gains.at[:, pl.ds(3 * width, width)], to_y)
+
+    def place(dy, dx, dc):
+        return pl.ds(pl.multiple_of(((dy * 2 + dx) * 2 + dc) * part, part), part)
+
+    own_cols = pl.ds(pl.multiple_of(y * channels, channels), channels)
+    other_cols = pl.ds(pl.multiple_of((1 - y) * channels, channels), channels)
+    in_own, in_far, in_core, in_pass = [], [], [], []
+    for n, w in enumerate((in_w, br_w)):
+        lanes = pl.ds(n * channels, channels)
+        for k in (0, 1):
+            source = pl.ds(k * part, part)
+            dx = row + k - 2 * row * k
+            in_far.append(made.new(w.at[source, other_cols], w_in.at[place(1, dx, 0), lanes], to_y))
+            in_own.append(copy(w.at[source, own_cols], w_in.at[place(0, dx, 0), lanes]))
+            in_core.append(made.new(w.at[source, own_cols], w_in.at[place(0, dx, 1), lanes], to_core))
+            in_pass.append(
+                made.new(w_in.at[place(1, dx, 0), lanes], w_in.at[place(1, dx, 1), lanes], to_core)
+            )
+
+    own_rows = pl.ds(pl.multiple_of(y * channels, channels), channels)
+    other_rows = pl.ds(pl.multiple_of((1 - y) * channels, channels), channels)
+    wo_own = copy(out_w.at[own_rows, :], wo.at[0, 0])
+    wo_far = made.new(out_w.at[other_rows, :], wo.at[1, 0], to_y)
+    wo_core = made.new(out_w.at[own_rows, :], wo.at[0, 1], to_core)
+    wo_pass = made.new(wo.at[1, 0], wo.at[1, 1], to_core)
+
+    share, share_d = gate_w.shape[0] // (count + 1), units // (count + 1)
+    own_units = pl.ds(pl.multiple_of(y * units, units), units)
+    other_units = pl.ds(pl.multiple_of((1 - y) * units, units), units)
+    at_seq = pl.ds(pl.multiple_of(seq * share, share), share)
+    at_seq_d = pl.ds(pl.multiple_of(seq * share_d, share_d), share_d)
+    far_d = wd.at[1, 0]
+    first_lanes, last_lanes = pl.ds(0, units), pl.ds(units, units)
+    from_d = pl.ds(pl.multiple_of((1 - y) * units + seq * share_d, share_d), share_d)
+    ff_far = [
+        made.new(down_w.at[from_d, :], far_d.at[at_seq_d, :], to_y),
+        made.new(gate_w.at[at_seq, other_units], far_gu.at[at_seq, first_lanes], to_y),
+        made.new(up_w.at[at_seq, other_units], far_gu.at[at_seq, last_lanes], to_y),
+    ]
+    others = [{"seq": lax.rem(seq + n, count + 1)} for n in range(1, count + 1)]
+    ff_share = [made.new(far_d.at[at_seq_d, :], far_d.at[at_seq_d, :], device) for device in others]
+    ff_share += [made.new(far_gu.at[at_seq, :], far_gu.at[at_seq, :], device) for device in others]
+    ff_core = [
+        made.new(gate_w.at[:, own_units], sib_own.at[:, first_lanes], to_core),
+        made.new(up_w.at[:, own_units], sib_own.at[:, last_lanes], to_core),
+        made.new(down_w.at[own_units, :], wd.at[0, 1], to_core),
+    ]
+    ff_pass = [made.new(far_gu, sib_far, to_core), made.new(far_d, wd.at[1, 1], to_core)]
+    wd_own = copy(down_w.at[own_units, :], wd.at[0, 0])
+    ahead = len(copies)
+    w_in_store = copy(w_in, w_in_out)
+
+    gather_n = made.block(gather_messages_by_x, own_low, gx, gy, gd)
+    gather_e = made.block(gather_messages_by_x, e_own, ex, ey, ed)
+    scatter = made.block(scatter_messages, q1, q2, q3, r3, rx, ry)
+    gather_m = made.block(gather_messages, own, mx, my, md)
+    edge = made.new(u.at[pl.ds(rows - 8, 8), :], border, {"seq": seq + 1})
+    hand_on = [made.new(ends, earlier.at[n - 1], {"seq": seq + n}) for n in range(1, count + 1)]
+
+    def put_together(left, right, full, low):
+        step = 128
+        for r in range(0, rows, step):
+            at = slice(r, r + step)
+            whole = jnp.concatenate([left[at, :], right[at, :]], axis=1)
+            full[at, :] = whole
+            low[at, :] = whole.astype(BF)
 
     @pl.when(i == 0)
     def _():
-        greet()
-        for n in range(4):
-            gather[n].start()
-        copies = load_rows(near, far, w, load)
-        gather[0].wait_recv()
-        gather[4].start()
-        gather[3].wait_recv()
-        gather[5].start()
-        for c in copies:
+        for c in copies[:ahead]:
+            c.start()
+        border[...] = jnp.zeros_like(border)
+        earlier[...] = jnp.zeros_like(earlier)
+        greet_all(
+            [to_x, to_y, to_core] + [{"seq": lax.rem(seq + n, count + 1)} for n in range(1, count + 1)]
+        )
+        for m in swap:
+            m.start()
+        for m in in_far:
+            m.start()
+        x_copy.wait()
+        swap[0].wait_recv()
+        put_together(x_own, x_recv, x, own_low)
+        for m in gather_n[:4]:
+            m.start()
+        for m in in_core:
+            m.start()
+        swap[1].wait_recv()
+        gains[:, 0:width] = jnp.concatenate([gains_in[...], gains_recv[...]], axis=1)
+        gains_x.start()
+        gains_y.start()
+        swap[2].wait_recv()
+        lane = small_in.shape[1]
+        small[:, pl.ds(pl.multiple_of(core * lane, lane), lane)] = small_in[...]
+        small[:, pl.ds(pl.multiple_of((1 - core) * lane, lane), lane)] = small_recv[...]
+        swap_g.start()
+        for m, n in zip(in_far, in_pass):
+            m.wait_recv()
+            n.start()
+        gains_x.wait_recv()
+        gains_d.start()
+        gather_n[1].wait_recv()
+        gather_n[4].start()
+        wo_core.start()
+        for m in ff_core:
+            m.start()
+        gather_n[3].wait_recv()
+        gather_n[5].start()
+        wo_far.start()
+        for m in ff_far:
+            m.start()
+        g_copy.wait()
+        swap_g.wait_recv()
+        put_together(g_own, g_recv, g, e_own)
+        for c in in_own:
             c.wait()
-        gather[1].wait_recv()
-        gather[4].wait_recv()
+        for m in in_core + in_pass:
+            m.wait_recv()
+        gains_y.wait_recv()
+        gains_d.wait_recv()
+        w_in_store.start()
+        gather_n[0].wait_recv()
+        gather_n[4].wait_recv()
+        for m in gather_e[:4]:
+            m.start()
 
     @pl.when(i == blocks // 2)
     def _():
-        gather[2].wait_recv()
-        gather[5].wait_recv()
-        for m in gather:
-            m.wait_send()
-
-    block = u.shape[0]
-    at = pl.ds(pl.multiple_of(i * block, block), block)
-    parts = [r[at, :].astype(F32) for r in (own, gx, gy, gd)]
-    width = parts[0].shape[1]
-    total = sum(jnp.sum(p * p, axis=1, keepdims=True) for p in parts)
-    s = lax.rsqrt(total / D + EPSILON)
-    scale[...] = s
-    normed = [p * s * gain[0:1, j * width : (j + 1) * width] for j, p in enumerate(parts)]
-    acc = None
-    for j, n in enumerate(normed):
-        term = dot_nn(n.astype(BF), w[j * width : (j + 1) * width, :])
-        acc = term if acc is None else acc + term
-    channels = u.shape[1]
-    u[...] = acc[:, :channels]
-    v[...] = acc[:, channels:]
-    for j in (0, 1):
-        k, p = pair_up(normed[2 * j], normed[2 * j + 1])
-        n1[:, j * width : (j + 1) * width] = k.astype(BF)
-        n1[:, (j + 2) * width : (j + 3) * width] = p.astype(BF)
-
-
-def norm_uv(own, gain, near, far):
-    rows, width = own.shape
-    w = pltpu.VMEM((4 * width, near.shape[2]), BF)
-    channels = near.shape[2] // 2
-    block = ROW_BLOCK
-    blocks = rows // block
-    return pl.pallas_call(
-        functools.partial(norm_uv_body, blocks),
-        grid=(blocks,),
-        in_specs=[whole_spec(own.shape), whole_spec(gain.shape), any_spec(), any_spec()],
-        out_specs=[rows_spec(block, 4 * width)] + [rows_spec(block, channels)] * 2 + [rows_spec(block, 1)],
-        out_shape=[sds((rows, 4 * width), BF)] + [sds((rows, channels), F32)] * 2 + [sds((rows, 1), F32)],
-        scratch_shapes=[w]
-        + [pltpu.VMEM((rows, width), BF)] * 3
-        + [pltpu.SemaphoreType.DMA((8,))]
-        + [pltpu.SemaphoreType.DMA((6,))] * 2,
-        compiler_params=comm_params(1),
-        cost_estimate=cost(60 * rows * near.size, nbytes(near, far)),
-        name="norm_uv",
-    )(own, gain, near, far)
-
-
-def chain(entries, count):
-    state = entries[(count - 1) * 8 + 1 : (count - 1) * 8 + 2, :]
-    for n in range(count - 2, -1, -1):
-        state = entries[n * 8 + 1 : n * 8 + 2, :] + entries[n * 8 : n * 8 + 1, :] * state
-    return state
-
-
-def recur_body(
-    heads, u, border, off, taps, recall_w, admit_w, soft, own, conv, recall, admit, state, cum, ends, gx, gy, gd, ext, send, recv
-):
-    rows = u.shape[0]
-    gather = gather_messages(own, gx, gy, gd, (send, recv), 0)
-    h = pl.program_id(0)
-
-    @pl.when(h == 0)
-    def _():
-        greet()
-        for n in range(4):
-            gather[n].start()
-
-    @pl.when(h == heads - 1)
-    def _():
-        gather[0].wait_recv()
-        gather[4].start()
-        gather[3].wait_recv()
-        gather[5].start()
-
-    ext[0:8, :] = border[...]
-    ext[8 : 8 + rows, :] = u[...]
-    step = ROW_BLOCK
-    for r in range(0, rows, step):
-        o = off[8 + r : 8 + r + step, :]
-        total = taps[0:1, :] * ext[8 + r : 8 + r + step, :]
-        for k in range(1, KW):
-            term = taps[k : k + 1, :] * ext[8 + r - k : 8 + r - k + step, :]
-            total = total + jnp.where(o >= k, term, 0.0)
-        conv[r : r + step, :] = total
-        rec = jax.nn.sigmoid(dot_nn(total, recall_w[0], PRECISE))
-        adm = jax.nn.sigmoid(dot_nn(total, admit_w[0], PRECISE))
-        recall[r : r + step, :] = rec
-        admit[r : r + step, :] = adm
-        ell = -8.0 * rec * soft[0:1, :]
-        cum[r : r + step, :] = jnp.where(o > 0, jnp.exp(ell), 0.0)
-        state[r : r + step, :] = jnp.sqrt(minus_expm1(2.0 * ell)) * adm * total
-    seg = rows // 8
-
-    def one(i, carry):
-        h, p = carry
-        at = pl.ds(i, 8, stride=seg)
-        d = cum[at, :]
-        h = d * h + state[at, :]
-        p = d * p
-        state[at, :] = h
-        cum[at, :] = p
-        return h, p
-
-    zero = jnp.zeros((8, 128), F32)
-    h, p = lax.fori_loop(0, seg, one, (zero, zero + 1.0), unroll=8)
-    carry_h, carry_p = h[0:1, :], p[0:1, :]
-    for s in range(1, 8):
-        at = slice(s * seg, (s + 1) * seg)
-        c = cum[at, :]
-        state[at, :] = state[at, :] + c * carry_h
-        cum[at, :] = c * carry_p
-        carry_h = h[s : s + 1, :] + p[s : s + 1, :] * carry_h
-        carry_p = p[s : s + 1, :] * carry_p
-    ends[0:1, :] = carry_p
-    ends[1:2, :] = carry_h
-    ends[2:8, :] = jnp.zeros((6, 128), F32)
-
-    @pl.when(pl.program_id(0) == heads - 1)
-    def _():
-        for n in (1, 2, 4, 5):
-            gather[n].wait_recv()
-        for m in gather:
-            m.wait_send()
-
-
-def recur(u, border, off, taps, recall_w, admit_w, soft, own):
-    rows, channels = u.shape
-    heads = channels // 128
-    gate = pl.BlockSpec((1, 128, 128), lambda h: (h, 0, 0))
-    full = sds((rows, channels), F32)
-    return pl.pallas_call(
-        functools.partial(recur_body, heads),
-        grid=(heads,),
-        in_specs=[
-            head_spec(rows),
-            head_spec(8),
-            whole_spec(off.shape),
-            head_spec(KW),
-            gate,
-            gate,
-            head_spec(1),
-            whole_spec(own.shape),
-        ],
-        out_specs=[head_spec(rows)] * 5 + [head_spec(8)] + [any_spec()] * 3,
-        out_shape=[full] * 5 + [sds((8, channels), F32)] + [sds(own.shape, BF)] * 3,
-        scratch_shapes=[pltpu.VMEM((rows + 8, 128), F32)] + [pltpu.SemaphoreType.DMA((6,))] * 2,
-        compiler_params=comm_params(5),
-        cost_estimate=cost(rows * channels * 128 * 24, rows * channels * 4 * 6, rows * channels * 6),
-        name="recur",
-    )(u, border, off, taps, recall_w, admit_w, soft, own)
-
-
-def mix_body(
-    count, blocks, local, cum, v, x, entries, w, states, mixed, x2, own, gx, gy, gd, q0, q1, q2, q3, r3, rx, ry, send, recv
-):
-    i = pl.program_id(0)
-    sems = (send, recv)
-    scatter = scatter_messages(q1, q2, q3, r3, rx, ry, sems, 0)
-    gather = gather_messages(own, gx, gy, gd, sems, 6)
-    block = local.shape[0]
-    width = x.shape[1]
-    rows = x.shape[0]
-    half = rows // 2
-
-    @pl.when(i == 0)
-    def _():
-        greet()
+        gather_n[2].wait_recv()
+        gather_n[5].wait_recv()
 
     @pl.when(i < blocks)
     def _():
-        entering = chain(entries, count)
-        st = local[...] + cum[...] * entering
+        at = pl.ds(pl.multiple_of(i * block, block), block)
+        parts = [r[at, :].astype(F32) for r in (own_low, gx, gy, gd)]
+        total = sum(jnp.sum(p * p, axis=1, keepdims=True) for p in parts)
+        s = lax.rsqrt(total / D + EPSILON)
+        s1[at, :] = s
+        normed = [p * s * gains[0:1, j * width : (j + 1) * width] for j, p in enumerate(parts)]
+        acc = None
+        for j, n in enumerate(normed):
+            term = dot_nn(n.astype(BF), w_in[j * width : (j + 1) * width, :])
+            acc = term if acc is None else acc + term
+        u[at, :] = acc[:, :channels]
+        v[at, :] = acc[:, channels:]
+        for j in (0, 1):
+            k, p = pair_up(normed[2 * j], normed[2 * j + 1])
+            n1[:, j * width : (j + 1) * width] = k.astype(BF)
+            n1[:, (j + 2) * width : (j + 3) * width] = p.astype(BF)
+
+    @pl.when((i == blocks - 1) & (seq < count))
+    def _():
+        edge.start()
+
+    @pl.when((i == blocks) & (seq > 0))
+    def _():
+        edge.wait_recv()
+
+    @pl.when(i == blocks - 1)
+    def _():
+        ff_far[0].wait_recv()
+        for m in ff_share[:count]:
+            m.start()
+
+    @pl.when((i >= blocks) & (i < blocks + heads))
+    def _():
+        h = i - blocks
+        lane = pl.ds(pl.multiple_of(h * 128, 128), 128)
+        state_h, cum_h = local.at[h], cum.at[h]
+        ext[0:8, :] = border[:, lane]
+        ext[8 : 8 + rows, :] = u[:, lane]
+        sp = small[KW : KW + 1, lane]
+        step = ROW_BLOCK
+        for r in range(0, rows, step):
+            o = off[8 + r : 8 + r + step, :]
+            total = small[0:1, lane] * ext[8 + r : 8 + r + step, :]
+            for k in range(1, KW):
+                term = small[k : k + 1, lane] * ext[8 + r - k : 8 + r - k + step, :]
+                total = total + jnp.where(o >= k, term, 0.0)
+            conv[r : r + step, :] = total
+            rec = jax.nn.sigmoid(dot_nn(total, recall_gate[y * heads + h], PRECISE))
+            adm = jax.nn.sigmoid(dot_nn(total, admit_gate[y * heads + h], PRECISE))
+            recall[r : r + step, :] = rec
+            admit[r : r + step, :] = adm
+            ell = -8.0 * rec * sp
+            cum_h[r : r + step, :] = jnp.where(o > 0, jnp.exp(ell), 0.0)
+            state_h[r : r + step, :] = jnp.sqrt(minus_expm1(2.0 * ell)) * adm * total
+        seg = rows // 8
+
+        def one(n, carry):
+            h, p = carry
+            at = pl.ds(n, 8, stride=seg)
+            d = cum_h[at, :]
+            h = d * h + state_h[at, :]
+            p = d * p
+            state_h[at, :] = h
+            cum_h[at, :] = p
+            return h, p
+
+        zero = jnp.zeros((8, 128), F32)
+        last, product = lax.fori_loop(0, seg, one, (zero, zero + 1.0), unroll=8)
+        carry_h, carry_p = last[0:1, :], product[0:1, :]
+        for s in range(1, 8):
+            at = slice(s * seg, (s + 1) * seg)
+            c = cum_h[at, :]
+            state_h[at, :] = state_h[at, :] + c * carry_h
+            cum_h[at, :] = c * carry_p
+            carry_h = last[s : s + 1, :] + product[s : s + 1, :] * carry_h
+            carry_p = product[s : s + 1, :] * carry_p
+        ends[h, 0:1, :] = carry_p
+        ends[h, 1:2, :] = carry_h
+        ends[h, 2:8, :] = jnp.zeros((6, 128), F32)
+
+    @pl.when(i == blocks + 1)
+    def _():
+        gather_e[1].wait_recv()
+        gather_e[4].start()
+        wo_far.wait_recv()
+        wo_pass.start()
+
+    @pl.when(i == blocks + 2)
+    def _():
+        gather_e[3].wait_recv()
+        gather_e[5].start()
+
+    def columns_in_order(pieces, out):
+        size = out.shape[0]
+        step = 128
+        lower = row == 0
+
+        def one(n, carry):
+            at = pl.ds(pl.multiple_of(n * step, step), step)
+            for dy in (0, 1):
+                first, second = pair_up(pieces[dy, 0, at, :].astype(F32), pieces[dy, 1, at, :].astype(F32))
+                near, far = jnp.where(lower, first, second), jnp.where(lower, second, first)
+                out[at, 2 * dy * width : (2 * dy + 1) * width] = near.astype(BF)
+                out[at, (2 * dy + 1) * width : (2 * dy + 2) * width] = far.astype(BF)
+            return carry
+
+        lax.fori_loop(0, size // step, one, 0)
+
+    @pl.when(i == blocks + heads - 1)
+    def _():
+        wo_own.wait()
+        wo_core.wait_recv()
+        wo_pass.wait_recv()
+        columns_in_order(wo, w_out)
+
+    for n in range(1, count + 1):
+
+        @pl.when((i == blocks + heads - 1) & (seq <= count - n))
+        def _():
+            hand_on[n - 1].start()
+
+        @pl.when((i == blocks + heads) & (seq >= n))
+        def _():
+            hand_on[n - 1].wait_recv()
+
+    @pl.when(i == blocks + heads)
+    def _():
+        for m in ff_far[1:]:
+            m.wait_recv()
+        for m in ff_share[count:]:
+            m.start()
+
+    third = blocks + heads
+
+    @pl.when((i >= third) & (i < third + blocks))
+    def _():
+        at = pl.ds(pl.multiple_of((i - third) * block, block), block)
+        st = jnp.concatenate(
+            [local[h, at, :] + cum[h, at, :] * carried(earlier, h, count) for h in range(heads)], axis=1
+        )
         states[...] = st
-        m = (st * gelu_pair(v[...])[0]).astype(BF)
+        m = (st * gelu_pair(v[at, :])[0]).astype(BF)
         mixed[...] = m
-        at = pl.ds(pl.multiple_of(i * block, block), block)
         for j, q in ((3, q3), (1, q1), (2, q2), (0, q0)):
-            q[at, :] = dot_nn(m, w[:, j * width : (j + 1) * width]).astype(q.dtype)
-
-    @pl.when(i == blocks // 2 - 1)
+            q[at, :] = dot_nn(m, w_out[:, j * width : (j + 1) * width]).astype(q.dtype)
+
+    @pl.when(i == third + blocks // 2 - 1)
     def _():
         scatter[0].start()
         scatter[2].start()
 
-    @pl.when(i == blocks - 1)
+    @pl.when(i == third + blocks - 1)
     def _():
         scatter[1].start()
 
-    @pl.when(i == blocks)
+    @pl.when(i == third + blocks)
     def _():
         scatter[0].wait_recv()
         add_into(q2, r3, 0, half)
@@ -863,57 +990,137 @@
         scatter[1].wait_recv()
         add_into(q1, r3, half, half)
         scatter[5].start()
+        gains_out[...] = gains[...]
+        border_out[...] = border[...]
+        earlier_out[...] = earlier[...]
+        w_in_store.wait()
+        for m in ff_share:
+            m.wait_recv()
+        for m in ff_pass:
+            m.start()
         for base, first in ((0, 2), (half, 4)):
             scatter[first].wait_recv()
             scatter[first + 1].wait_recv()
             for r in range(base, base + half, 128):
                 at = slice(r, r + 128)
                 total = x[at, :] + q0[at, :] + rx[at, :].astype(F32) + ry[at, :].astype(F32)
-                x2[at, :] = total
+                mid[at, :] = total
                 own[at, :] = total.astype(BF)
             start = 0 if base == 0 else 2
-            gather[start].start()
-            gather[start + 1].start()
-        gather[0].wait_recv()
-        gather[4].start()
-        gather[3].wait_recv()
-        gather[5].start()
+            gather_m[start].start()
+            gather_m[start + 1].start()
+        wd_own.wait()
+        for m in ff_core + ff_pass:
+            m.wait_recv()
+        columns_in_order(wd, w_down)
+        gather_m[0].wait_recv()
+        gather_m[4].start()
+        gather_m[3].wait_recv()
+        gather_m[5].start()
         for n in (1, 2, 4, 5):
-            gather[n].wait_recv()
-        for m in scatter + gather:
+            gather_m[n].wait_recv()
+        for n in (0, 2, 4, 5):
+            gather_e[n].wait_recv()
+        sent = swap + [swap_g, gains_x, gains_y, gains_d] + in_far + in_core + in_pass
+        sent += [wo_far, wo_core, wo_pass] + ff_far + ff_share + ff_core + ff_pass
+        for m in sent + gather_n + gather_e + scatter + gather_m:
             m.wait_send()
 
-
-def mix(local, cum, v, x, entries, w):
-    rows, channels = v.shape
-    width = w.shape[1] // 4
+        @pl.when(seq < count)
+        def _():
+            edge.wait_send()
+
+        for n in range(1, count + 1):
+
+            @pl.when(seq <= count - n)
+            def _():
+                hand_on[n - 1].wait_send()
+
+
+def front(stream, cot, in_w, br_w, out_w, gate_w, up_w, down_w, gains, small, recall_gate, admit_gate, off, count):
+    rows, part = stream.shape[1:]
+    width = 2 * part
+    channels = in_w.shape[1] // 2
+    units = gate_w.shape[1] // 2
+    heads = channels // 128
     block = ROW_BLOCK
     blocks = rows // block
-    held = functools.partial(held_spec, block, last=blocks - 1)
-    chunk = pltpu.VMEM((rows, width), BF)
+
+    def norm_at(i):
+        return (jnp.minimum(i, blocks - 1), 0)
+
+    def head_at(i):
+        return (0, jnp.clip(i - blocks, 0, heads - 1))
+
+    def mix_at(i):
+        return (jnp.clip(i - blocks - heads, 0, blocks - 1), 0)
+
+    chunk_low, chunk = sds((rows, width), BF), sds((rows, width), F32)
+    wide = sds((rows, channels), F32)
+    held = [
+        chunk,
+        chunk,
+        chunk_low,
+        sds((channels, 4 * width), BF),
+        sds((units, 4 * width), BF),
+        sds((8, 4 * width), F32),
+        sds((8, channels), F32),
+        sds((rows, 1), F32),
+        wide,
+        wide,
+        sds((8, channels), F32),
+        sds((count, heads, 8, 128), F32),
+        chunk,
+        chunk_low,
+    ]
+    blocked = [sds((rows, 4 * width), BF), wide, wide, wide, wide, sds((rows, channels), BF)]
+    away = [chunk_low] * 6 + [sds((width, 2 * units), BF)] * 3 + [sds((4 * width, 2 * channels), BF)]
+    piece = pltpu.VMEM((rows, width), BF)
+    side = pltpu.VMEM((rows, part), F32)
+    tall = pl.BlockSpec((rows, 128), head_at)
     return pl.pallas_call(
-        functools.partial(mix_body, entries.shape[0] // 8, blocks),
-        grid=(blocks + 1,),
-        in_specs=[held(channels)] * 3
-        + [whole_spec(x.shape), whole_spec(entries.shape), whole_spec(w.shape)],
-        out_specs=[held(channels)] * 2 + [full_spec((rows, width))] * 2 + [any_spec()] * 3,
-        out_shape=[sds((rows, channels), F32), sds((rows, channels), BF), sds((rows, width), F32)]
-        + [sds((rows, width), BF)] * 4,
-        scratch_shapes=[pltpu.VMEM((rows, width), F32)]
-        + [chunk] * 6
-        + [pltpu.SemaphoreType.DMA((12,))] * 2,
-        compiler_params=comm_params(2),
-        cost_estimate=cost(40 * rows * w.size, rows * channels * 18 + nbytes(w)),
-        name="mix",
-    )(local, cum, v, x, entries, w)
+        functools.partial(front_body, heads, blocks, count),
+        grid=(2 * blocks + heads + 1,),
+        in_specs=[any_spec()] * 8
+        + [whole_spec(a.shape) for a in (gains, small, recall_gate, admit_gate, off)],
+        out_specs=[whole_spec(s.shape) for s in held]
+        + [pl.BlockSpec((block, 4 * width), norm_at)]
+        + [tall] * 3
+        + [pl.BlockSpec((block, channels), mix_at)] * 2
+        + [any_spec()] * 10,
+        out_shape=held + blocked + away,
+        scratch_shapes=[side] * 4
+        + [pltpu.VMEM(gains.shape, F32), pltpu.VMEM(small.shape, F32)]
+        + [piece] * 4
+        + [
+            pltpu.VMEM((4 * width, 2 * channels), BF),
+            pltpu.VMEM((8, 4 * width), F32),
+            pltpu.VMEM((8, channels), F32),
+            pltpu.VMEM((count, heads, 8, 128), F32),
+            pltpu.VMEM((2, 2, channels, width), BF),
+            pltpu.VMEM((2, 2, units, width), BF),
+            pltpu.VMEM((heads, rows, 128), F32),
+            pltpu.VMEM((heads, rows, 128), F32),
+            pltpu.VMEM((rows + 8, 128), F32),
+            pltpu.VMEM((heads, 8, 128), F32),
+            pltpu.VMEM((rows, width), F32),
+        ]
+        + [piece] * 6
+        + [pltpu.SemaphoreType.DMA((9,))]
+        + [pltpu.SemaphoreType.DMA((FRONT_MESSAGES,))] * 2,
+        compiler_params=comm_params(1),
+        cost_estimate=cost(200 * rows * in_w.size, rows * 40000),
+        name="front",
+    )(stream, cot, in_w, br_w, out_w, gate_w, up_w, down_w, gains, small, recall_gate, admit_gate, off)
 
 
 def feed_body(blocks, *refs):
-    (x0, x1, x2, x3, e0, e1, e2, e3, mid, cot, gain, near, far, wd) = refs[:14]
-    outs = refs[14:18]
-    (dx, own, gx, gy, gd, gain_grad, s_down, s_gu) = refs[18:26]
-    (wgu, load, n2, hid, ee, err, scale, stage, c_down, c_gu) = refs[26:36]
-    (q0, q1, q2, q3, r3, rx, ry, dots, dots_x, dots_y, send, recv) = refs[36:]
+    (x0, x1, x2, x3, e0, e1, e2, e3, mid, cot, gain, wd) = refs[:12]
+    weights = refs[12:17]
+    outs = refs[17:21]
+    (dx, own, gx, gy, gd, gain_grad, s_down, s_gu) = refs[21:29]
+    (wgu, load, n2, hid, ee, err, scale, stage, c_down, c_gu) = refs[29:39]
+    (q0, q1, q2, q3, r3, rx, ry, dots, dots_x, dots_y, send, recv) = refs[39:]
     i = pl.program_id(0)
     sems = (send, recv)
     scatter = scatter_messages(q1, q2, q3, r3, rx, ry, sems, 0)
@@ -927,7 +1134,7 @@
 
     @pl.when(i == 0)
     def _():
-        copies = load_rows(near, far, wgu, load)
+        copies = load_rows(*weights, wgu, load)
         greet_all((neighbour_x(), neighbour_y(), neighbour_core()))
         for c in copies:
             c.wait()
@@ -1094,7 +1301,7 @@
             m.wait_send()
 
 
-def feed(chunks, errs, mid, cot, gain, near, far, wd):
+def feed(chunks, errs, mid, cot, gain, wd, weights):
     rows, width = chunks[0].shape
     units = wd.shape[0]
     block = ROW_BLOCK
@@ -1109,7 +1316,8 @@
         grid=(blocks + tiles + 5,),
         in_specs=[held(width)] * 8
         + [whole_spec(mid.shape), whole_spec(cot.shape), whole_spec(gain.shape)]
-        + [any_spec(), any_spec(), whole_spec(wd.shape)],
+        + [whole_spec(wd.shape)]
+        + [any_spec()] * 5,
         out_specs=[held(width)] * 4
         + [whole_spec((rows, width))] * 2
         + [any_spec()] * 3
@@ -1121,7 +1329,7 @@
         + [sds((8, width), F32), sds((units, 2 * width), BF), sds((2 * width, 2 * units), BF)],
         scratch_shapes=[
             pltpu.VMEM((4 * width, 2 * units), BF),
-            pltpu.SemaphoreType.DMA((8,)),
+            pltpu.SemaphoreType.DMA((10,)),
             pltpu.VMEM((rows, 4 * width), BF),
             pltpu.VMEM((rows, units), BF),
             pltpu.VMEM((rows, 4 * width), BF),
@@ -1138,26 +1346,19 @@
         compiler_params=comm_params(3),
         cost_estimate=cost(48 * rows * wd.size, 3 * nbytes(wd) + rows * 30000, rows * units),
         name="feed",
-    )(*chunks, *errs, mid, cot, gain, near, far, wd)
-
-
-def carried(entries, h, count):
-    state = entries[count - 1, h, 1:2, :]
-    for n in range(count - 2, -1, -1):
-        state = entries[n, h, 1:2, :] + entries[n, h, 0:1, :] * state
-    return state
+    )(*chunks, *errs, mid, cot, gain, wd, *weights)
 
 
 def back_body(heads, blocks, count, *refs):
     errs = refs[0:4]
     (w_out, states, branch, recall, conv, admit, u_head, off, soft) = refs[4:13]
-    (taps, recall_w, admit_w, border, earlier, u, v, near, far, scale, x, dx, gain) = refs[13:26]
-    (sum_gu, sum_down) = refs[26:28]
-    (ev, paired, eu, grad, gain_grad, grad_recall, grad_admit, grad_small) = refs[28:36]
-    (mine_gu, far_gu, mine_down, far_down) = refs[36:40]
-    (part, reach, ext, st, uext, dc, ends, later, edge, from_later, w, load) = refs[40:52]
-    (q0, q1, q2, q3, r3, rx, ry, dots, dots_x, dots_y) = refs[52:62]
-    (s_gu, a_gu, b_gu, s_dn, a_dn, b_dn, store, send, recv) = refs[62:]
+    (taps, recall_w, admit_w, border, earlier, u, v, w, scale, x, dx, gain) = refs[13:25]
+    (sum_gu, sum_down) = refs[25:27]
+    (ev, paired, eu, grad, gain_grad, grad_recall, grad_admit, grad_small) = refs[27:35]
+    (mine_gu, far_gu, mine_down, far_down) = refs[35:39]
+    (part, reach, ext, st, uext, dc, ends, later, edge, from_later, load) = refs[39:50]
+    (q0, q1, q2, q3, r3, rx, ry, dots, dots_x, dots_y) = refs[50:60]
+    (s_gu, a_gu, b_gu, s_dn, a_dn, b_dn, store, send, recv) = refs[60:]
     i = pl.program_id(0)
     sems = (send, recv)
     seq = lax.axis_index("seq")
@@ -1210,8 +1411,8 @@
         else:
             to_out[p] = pltpu.make_async_copy(source, mine_gu.at[gu_at(n), :], store.at[len(to_out)])
     loads = [
-        pltpu.make_async_copy(sum_gu, s_gu, load.at[8]),
-        pltpu.make_async_copy(sum_down, s_dn, load.at[9]),
+        pltpu.make_async_copy(sum_gu, s_gu, load.at[0]),
+        pltpu.make_async_copy(sum_down, s_dn, load.at[1]),
     ]
 
     def tick(t):
@@ -1232,14 +1433,13 @@
     def _():
         for c in loads:
             c.start()
-        copies = load_rows(near, far, w, load)
         later[...] = jnp.zeros_like(later)
         from_later[...] = jnp.zeros_like(from_later)
         greet_all(
             [neighbour_x(), neighbour_y()]
             + [{"seq": lax.rem(seq + n, count + 1)} for n in range(1, count + 1)]
         )
-        for c in loads + copies:
+        for c in loads:
             c.wait()
         total.begin(0)
         total.begin(1)
@@ -1464,13 +1664,13 @@
             c.wait()
 
 
-def back(errs, w_out, states, v, recall, conv, admit, u, off, soft, taps, rw, aw, border, earlier, near, far, scale, x, dx, gain, sum_gu, sum_down):
+def back(errs, w_out, states, v, recall, conv, admit, u, off, soft, taps, rw, aw, border, earlier, w, scale, x, dx, gain, sum_gu, sum_down):
     rows, channels = states.shape
     width = x.shape[1]
     heads = channels // 128
     block = ROW_BLOCK
     blocks = rows // block
-    count = earlier.shape[0] // 8
+    count = earlier.shape[0]
     steps = 2 * heads + blocks + 3
     assert steps >= 15
 
@@ -1493,6 +1693,7 @@
 
     tall = (rows, 128)
     gate = (1, 128, 128)
+    own_gate = on(gate, second, 0)
     chunk = pltpu.VMEM((rows, width), BF)
     lanes = pltpu.VMEM((8, rows), F32)
     gu, dn = pltpu.VMEM(sum_gu.shape, BF), pltpu.VMEM(sum_down.shape, BF)
@@ -1514,14 +1715,13 @@
             whole_spec(off.shape),
             on((1, 128), both, 1),
             on((KW, 128), second, 1),
-            on(gate, second, 0),
-            on(gate, second, 0),
+            own_gate,
+            own_gate,
             on((8, 128), second, 1),
-            on((8 * count, 128), second, 1),
+            pl.BlockSpec((count, 1, 8, 128), lambda i: (0, second(i), 0, 0)),
             on((block, channels), third, 0),
             on((block, channels), third, 0),
-            any_spec(),
-            any_spec(),
+            whole_spec(w.shape),
             whole_spec(scale.shape),
             whole_spec(x.shape),
             whole_spec(dx.shape),
@@ -1564,8 +1764,7 @@
             pltpu.VMEM((count, heads, 8, 128), F32),
             piece,
             piece,
-            pltpu.VMEM((4 * width, 2 * channels), BF),
-            pltpu.SemaphoreType.DMA((10,)),
+            pltpu.SemaphoreType.DMA((2,)),
             pltpu.VMEM((rows, width), F32),
         ]
         + [chunk] * 6
@@ -1575,132 +1774,325 @@
         + [pltpu.SemaphoreType.DMA((6,))]
         + [pltpu.SemaphoreType.DMA((count_sems,))] * 2,
         compiler_params=comm_params(4),
-        cost_estimate=cost(4 * rows * near.size * 16, rows * channels * 60, rows * channels * 8),
+        cost_estimate=cost(64 * rows * w.size, rows * channels * 60, rows * channels * 8),
         name="back",
     )(
         *errs, w_out, states, v, recall, conv, admit, u, off, soft, taps, rw, aw, border, earlier,
-        u, v, near, far, scale, x, dx, gain, sum_gu, sum_down,
+        u, v, w, scale, x, dx, gain, sum_gu, sum_down,
     )
 
 
-def tail_body(n1, eu, ev, mixed, er, small, mine_in, far_in, mine_out, far_out, small_out, *scratch):
-    (s_in, p_in, c_in, a_in, b_in, y_in, s_out, p_out, c_out, a_out, b_out, y_out) = scratch[:12]
-    (s_sm, c_sm, a_sm, b_sm, send, recv) = scratch[12:]
-    sems = (send, recv)
-    width = er.shape[1] // 4
+TAIL_MESSAGES = 48
+
+
+def tail_body(*refs):
+    (mixed, er, n1, eu, ev, grad_recall, grad_admit, grad_small, grad_mixer, grad_feed) = refs[:10]
+    (p0, p1, p2, p3, mid, grad_chunk) = refs[10:16]
+    (mine_in, far_in, mine_out, far_out, gates, tiny_out, out, grad) = refs[16:24]
+    (n1_v, eu_v, ev_v, s_in, p_in, c_in, a_in, b_in, y_in, s_out, p_out, c_out, a_out, b_out, y_out) = refs[24:39]
+    (s_gt, p_gt, c_gt, a_gt, b_gt, y_gt, s_ty, p_ty, c_ty, a_ty, b_ty) = refs[39:50]
+    (q1, q2, q3, r3, rx, ry, own_a, other_a, own_b, other_b, load, send, recv) = refs[50:]
+    made = Messages((send, recv))
+    col = lax.axis_index("col")
+    y, core = lax.div(col, 2), lax.rem(col, 2)
+    to_core, to_y = neighbour_core(), neighbour_y()
+    rows, width = p0.shape
+    part = width // 2
+    half_tokens = rows // 2
+    channels = eu.shape[1]
+    heads = grad_recall.shape[0]
+    copies = []
+
+    def copy(src, dst):
+        copies.append(pltpu.make_async_copy(src, dst, load.at[len(copies)]))
+        return copies[-1]
+
+    outs_in = [copy(p3, q3), copy(p1, q1), copy(p2, q2)]
+    late = [copy(n1, n1_v), copy(eu, eu_v), copy(ev, ev_v)]
+    scatter = made.block(scatter_messages, q1, q2, q3, r3, rx, ry)
     half = width // 2
-    channels = eu.shape[1]
-    greet_all((neighbour_core(), neighbour_y(), neighbour_end(), neighbour_middle()))
-    half_rows = pl.ds(0, half)
-    a, b = half_rows, pl.ds(half, half)
+    a, b = pl.ds(0, half), pl.ds(half, half)
     c, d = pl.ds(2 * half, half), pl.ds(3 * half, half)
     inner = s_out.shape[0] // 2
     up, low = pl.ds(0, inner), pl.ds(inner, inner)
     lanes_far, lanes_own = pl.ds(width, width), pl.ds(0, width)
     group_in, group_out = (s_in, a_in, b_in), (s_out, a_out, b_out)
-    pieces = [[s_sm, a_sm, b_sm]]
+    pieces = [[s_ty, a_ty, b_ty], [s_gt, a_gt, b_gt]]
     pieces += [[r.at[at, lanes_far] for r in group_out] for at in (up, low)]
     pieces += [[r.at[at, lanes_own] for r in group_out] for at in (up, low)]
     pieces += [[r.at[at, :] for r in group_in] for at in (c, d, a, b)]
     count = len(pieces)
-    total = SeqSum(pieces, sems, 0)
-    base = 2 * count
-    core_sm = message(small, c_sm, neighbour_core(), sems, base)
-    core_out = message(p_out, c_out, neighbour_core(), sems, base + 1)
-    core_in = [
-        message(p_in.at[at, :], c_in.at[at, :], neighbour_core(), sems, base + 2 + n)
-        for n, at in enumerate((c, d, a, b))
-    ]
-    to_y = {
-        1: message(s_out.at[up, lanes_far], y_out.at[up, :], neighbour_y(), sems, base + 6),
-        2: message(s_out.at[low, lanes_far], y_out.at[low, :], neighbour_y(), sems, base + 7),
-        5: message(s_in.at[c, :], y_in.at[a, :], neighbour_y(), sems, base + 8),
-        6: message(s_in.at[d, :], y_in.at[b, :], neighbour_y(), sems, base + 9),
+    total = SeqSum(pieces, (send, recv), made.used)
+    made.used += 2 * count
+    core_ty, core_gt = made.new(p_ty, c_ty, to_core), made.new(p_gt, c_gt, to_core)
+    core_out = made.new(p_out, c_out, to_core)
+    core_in = [made.new(p_in.at[at, :], c_in.at[at, :], to_core) for at in (c, d, a, b)]
+    over_y = {
+        1: made.new(s_gt, y_gt, to_y),
+        2: made.new(s_out.at[up, lanes_far], y_out.at[up, :], to_y),
+        3: made.new(s_out.at[low, lanes_far], y_out.at[low, :], to_y),
+        6: made.new(s_in.at[c, :], y_in.at[a, :], to_y),
+        7: made.new(s_in.at[d, :], y_in.at[b, :], to_y),
     }
-
-    core_sm.start()
+    send_out, send_grad = made.new(other_a, out.at[core], to_core), made.new(other_b, grad.at[core], to_core)
+    keep_out, keep_grad = copy(own_a, out.at[core]), copy(own_b, grad.at[core])
+
+    for m in outs_in + late:
+        m.start()
+    greet_all((neighbour_x(), to_y, to_core, neighbour_end(), neighbour_middle()))
+
+    for n, source in enumerate((grad_recall, grad_admit)):
+        for h in range(heads):
+            at = slice((n * heads + h) * 128, (n * heads + h + 1) * 128)
+            p_gt[at, :] = source[h].astype(BF)
+    core_gt.start()
+    p_ty[...] = jnp.zeros_like(p_ty)
+    p_ty[0:8, :] = grad_small[...]
+    for n, source in enumerate((grad_mixer, grad_feed)):
+        g = jnp.broadcast_to(source[0:1, :], (8, width))
+        g = jnp.where(core == 0, g, pltpu.roll(g, part, 1))
+        p_ty[8 + n : 9 + n, 0:width] = g[0:1, :]
+    core_ty.start()
+    for m in outs_in:
+        m.wait()
+    scatter[0].start()
+    scatter[1].start()
+    scatter[2].start()
     g = dot_tn(mixed[...], er[...])
     p_out[...] = g[:, 2 * width :].astype(BF)
     core_out.start()
     s_out[...] = g[:, : 2 * width].astype(BF)
-    s_sm[...] = small[...]
+    core_ty.wait_recv()
+    s_ty[...] = p_ty[...] + c_ty[...]
+    total.begin(0)
+    core_gt.wait_recv()
+    put_in(s_gt, p_gt)
+    plus_in(s_gt, c_gt)
+    total.begin(1)
 
     def tile(n, target, row):
         at = slice(n * width, (n + 1) * width)
         where = slice(row, row + width)
-        target[where, :channels] = dot_tn(n1[:, at], eu[...]).astype(BF)
-        target[where, channels:] = dot_tn(n1[:, at], ev[...]).astype(BF)
-
-    core_sm.wait_recv()
-    plus_in(s_sm, c_sm)
-    total.begin(0)
+        target[where, :channels] = dot_tn(n1_v[:, at], eu_v[...]).astype(BF)
+        target[where, channels:] = dot_tn(n1_v[:, at], ev_v[...]).astype(BF)
+
+    core_out.wait_recv()
+    plus_in(s_out, c_out)
+    for n in range(2, 6):
+        total.begin(n)
+    for m in late:
+        m.wait()
     tile(3, p_in, width)
     core_in[0].start()
     core_in[1].start()
-    core_out.wait_recv()
-    plus_in(s_out, c_out)
-    for n in range(1, 5):
-        total.begin(n)
     tile(1, s_in, width)
+    total.relay(0)
+    total.relay(1)
+    total.settle(0)
+    core_in[0].wait_recv()
+    core_in[1].wait_recv()
+    plus_in(s_in.at[pl.ds(width, width), :], c_in.at[pl.ds(width, width), :])
+    total.begin(6)
+    total.begin(7)
+    total.relay(2)
+    total.settle(1)
+    total.finish(0)
     tile(2, p_in, 0)
     core_in[2].start()
     core_in[3].start()
-    core_in[0].wait_recv()
-    core_in[1].wait_recv()
-    plus_in(s_in.at[pl.ds(width, width), :], c_in.at[pl.ds(width, width), :])
-    total.begin(5)
-    total.begin(6)
-    total.relay(0)
-    total.relay(1)
-    total.settle(0)
+    total.relay(3)
+    total.settle(2)
+    total.finish(1)
+    over_y[1].start()
     tile(0, s_in, 0)
     core_in[2].wait_recv()
     core_in[3].wait_recv()
     plus_in(s_in.at[pl.ds(0, width), :], c_in.at[pl.ds(0, width), :])
-    total.begin(7)
     total.begin(8)
-    for n in range(2, count + 2):
+    total.begin(9)
+
+    def chunk_out(value, own, other, at):
+        own[at, :] = value[:, :part]
+        other[at, :] = pltpu.roll(value, part, 1)[:, :part]
+
+    def finish_out(start, first):
+        scatter[first].wait_recv()
+        scatter[first + 1].wait_recv()
+        for r in range(start, start + half_tokens, 128):
+            at = slice(r, r + 128)
+            value = p0[at, :] + rx[at, :].astype(F32) + ry[at, :].astype(F32) + mid[at, :]
+            chunk_out(value, own_a, other_a, at)
+
+    for n in range(4, count + 2):
         if n < count:
             total.relay(n)
         if n - 1 < count:
             total.settle(n - 1)
         total.finish(n - 2)
-        if n - 2 in to_y:
-            to_y[n - 2].start()
-    put_in(small_out, s_sm)
+        if n - 2 in over_y:
+            over_y[n - 2].start()
+        if n == 4:
+            scatter[0].wait_recv()
+            add_into(q2, r3, 0, half_tokens)
+            scatter[3].start()
+            scatter[4].start()
+        if n == 5:
+            scatter[1].wait_recv()
+            add_into(q1, r3, half_tokens, half_tokens)
+            scatter[5].start()
+            for r in range(0, rows, 128):
+                at = slice(r, r + 128)
+                chunk_out(grad_chunk[at, :], own_b, other_b, at)
+            send_grad.start()
+            keep_grad.start()
+        if n == 8:
+            finish_out(0, 2)
+        if n == 9:
+            finish_out(half_tokens, 4)
+            send_out.start()
+            keep_out.start()
+    put_in(tiny_out, s_ty)
     put_in(mine_in, s_in.at[pl.ds(0, width), :])
     put_in(mine_out, s_out.at[:, lanes_own])
-    for m in to_y.values():
-        m.wait_recv()
+    over_y[1].wait_recv()
+    for n in (0, 1):
+        for h in range(heads):
+            at = slice((n * heads + h) * 128, (n * heads + h + 1) * 128)
+            gates[n, y * heads + h] = s_gt[at, :].astype(F32)
+            gates[n, (1 - y) * heads + h] = y_gt[at, :].astype(F32)
+    for n in (2, 3, 6, 7):
+        over_y[n].wait_recv()
     put_in(far_out, y_out)
     put_in(far_in, y_in)
-    for m in [core_sm, core_out] + core_in + list(to_y.values()):
+    for m in (send_out, send_grad):
+        m.wait_recv()
+    for m in [core_ty, core_gt, core_out, send_out, send_grad] + core_in + list(over_y.values()) + scatter:
         m.wait_send()
-
-
-def tail(n1, eu, ev, mixed, er, small):
+    keep_out.wait()
+    keep_grad.wait()
+
+
+def tail(mixed, er, n1, eu, ev, grad_recall, grad_admit, grad_small, grad_mixer, grad_feed, parts, mid, grad_chunk):
     rows, channels = eu.shape
-    width = er.shape[1] // 4
+    width = mid.shape[1]
+    part = width // 2
+    heads = grad_recall.shape[0]
     inner = mixed.shape[1]
     big = pltpu.VMEM((2 * width, 2 * channels), BF)
     tall = pltpu.VMEM((inner, 2 * width), BF)
-    tiny = pltpu.VMEM(small.shape, F32)
+    gate = pltpu.VMEM((2 * heads * 128, 128), BF)
+    tiny = pltpu.VMEM((16, channels), F32)
+    piece = pltpu.VMEM((rows, width), BF)
+    side = pltpu.VMEM((rows, part), F32)
     quarter_in, quarter_out = (width, 2 * channels), (inner, width)
+    final = sds((2, rows, part), F32)
     return pl.pallas_call(
         tail_body,
-        out_shape=[sds(quarter_in, BF)] * 2 + [sds(quarter_out, BF)] * 2 + [sds(small.shape, F32)],
-        scratch_shapes=[big] * 5
+        in_specs=[pl.BlockSpec(memory_space=pltpu.VMEM)] * 2
+        + [any_spec()] * 3
+        + [pl.BlockSpec(memory_space=pltpu.VMEM)] * 6
+        + [any_spec()] * 3
+        + [pl.BlockSpec(memory_space=pltpu.VMEM)] * 2,
+        out_specs=[pl.BlockSpec(memory_space=pltpu.VMEM)] * 6 + [any_spec()] * 2,
+        out_shape=[sds(quarter_in, BF)] * 2
+        + [sds(quarter_out, BF)] * 2
+        + [sds((2, 2 * heads, 128, 128), F32), sds((16, channels), F32), final, final],
+        scratch_shapes=[
+            pltpu.VMEM((rows, 4 * width), BF),
+            pltpu.VMEM((rows, channels), BF),
+            pltpu.VMEM((rows, channels), BF),
+        ]
+        + [big] * 5
         + [pltpu.VMEM(quarter_in, BF)]
         + [tall] * 5
         + [pltpu.VMEM(quarter_out, BF)]
-        + [tiny] * 4
-        + [pltpu.SemaphoreType.DMA((28,))] * 2,
+        + [gate] * 6
+        + [tiny] * 5
+        + [piece] * 6
+        + [side] * 4
+        + [pltpu.SemaphoreType.DMA((8,))]
+        + [pltpu.SemaphoreType.DMA((TAIL_MESSAGES,))] * 2,
         compiler_params=pltpu.CompilerParams(
             vmem_limit_bytes=VMEM_LIMIT, collective_id=6, has_side_effects=True
         ),
-        cost_estimate=cost(20 * rows * n1.shape[1] * channels * 3, nbytes(n1, eu, ev, mixed, er)),
+        cost_estimate=cost(60 * rows * width * channels * 4, nbytes(n1, eu, ev, mixed, er)),
         name="tail",
-    )(n1, eu, ev, mixed, er, small)
+    )(mixed, er, n1, eu, ev, grad_recall, grad_admit, grad_small, grad_mixer, grad_feed, *parts, mid, grad_chunk)
+
+
+def arrange_body(place, mine_gu, far_gu, mine_dn, far_dn, mine_in, far_in, mine_out, far_out, *outs):
+    gate, up, down, inp, branch, out = outs
+    row, y = place[0], place[1]
+    first = pl.program_id(0) == 0
+
+    def side_by_side(mine, far, left, right):
+        lanes = left.shape[1] // 2
+        for target, at in ((left, 0), (right, mine.shape[1] // 2)):
+            m = mine[:, at : at + lanes].astype(F32)
+            t = far[:, at : at + lanes].astype(F32)
+            target[:, :lanes] = jnp.where(y == 0, m, t)
+            target[:, lanes:] = jnp.where(y == 0, t, m)
+
+    def stack_up(mine, far, target):
+        value = jnp.where(first, mine[...].astype(F32), far[...].astype(F32))
+        target[...] = jnp.where(row == 0, value, pltpu.roll(value, value.shape[1] // 2, 1))
+
+    side_by_side(mine_gu, far_gu, gate, up)
+    side_by_side(mine_in, far_in, inp, branch)
+    stack_up(mine_dn, far_dn, down)
+    stack_up(mine_out, far_out, out)
+
+
+def arrange(place, mine_gu, far_gu, mine_dn, far_dn, mine_in, far_in, mine_out, far_out):
+    width, units = mine_dn.shape[1], mine_dn.shape[0]
+    inner = mine_out.shape[0]
+    lanes_gu, lanes_in = mine_gu.shape[1], mine_in.shape[1]
+    quarter = width // 4
+
+    def rows_in(i, j, place):
+        return (2 * i + j, 0)
+
+    def rows_to(i, j, place):
+        return (2 * (i + place[0] - 2 * i * place[0]) + j, 0)
+
+    def near(i, j, place):
+        return (jnp.where(i == 0, j, 1), 0)
+
+    def far(i, j, place):
+        return (jnp.where(i == 0, 0, j), 0)
+
+    def stack_to(i, j, place):
+        return (2 * (i + place[1] - 2 * i * place[1]) + j, 0)
+
+    def spec(rows, lanes, at):
+        return pl.BlockSpec((rows, lanes), at)
+
+    shapes = [(width, lanes_gu)] * 2 + [(2 * units, width)] + [(width, lanes_in)] * 2 + [(2 * inner, width)]
+    return pl.pallas_call(
+        arrange_body,
+        grid_spec=pltpu.PrefetchScalarGridSpec(
+            num_scalar_prefetch=1,
+            grid=(2, 2),
+            in_specs=[
+                spec(quarter, lanes_gu, rows_in),
+                spec(quarter, lanes_gu, rows_in),
+                spec(units // 2, width, near),
+                spec(units // 2, width, far),
+                spec(quarter, lanes_in, rows_in),
+                spec(quarter, lanes_in, rows_in),
+                spec(inner // 2, width, near),
+                spec(inner // 2, width, far),
+            ],
+            out_specs=[spec(quarter, lanes_gu, rows_to)] * 2
+            + [spec(units // 2, width, stack_to)]
+            + [spec(quarter, lanes_in, rows_to)] * 2
+            + [spec(inner // 2, width, stack_to)],
+        ),
+        out_shape=[sds(s, F32) for s in shapes],
+        compiler_params=pltpu.CompilerParams(vmem_limit_bytes=VMEM_LIMIT),
+        cost_estimate=cost(1000000, 24000000),
+        name="arrange",
+    )(place, mine_gu, far_gu, mine_dn, far_dn, mine_in, far_in, mine_out, far_out)
 
 
 def local_fast(
@@ -1721,213 +2113,66 @@
     down_weight,
 ):
     tokens = stream_in.shape[1]
-    half = tokens // 2
     count = lax.axis_size("seq")
     part = stream_in.shape[2]
     seq = lax.axis_index("seq")
     row = lax.axis_index("row")
     col = lax.axis_index("col")
     y, core = col // 2, col % 2
-    lower = row == 0
-
-    def own_and_other(a, pick, axis):
-        size = a.shape[axis] // 2
-        return (
-            lax.dynamic_slice_in_dim(a, pick * size, size, axis),
-            lax.dynamic_slice_in_dim(a, (1 - pick) * size, size, axis),
-        )
-
-    def by_core(a):
-        own, other = own_and_other(a, core, 0)
-        return jnp.concatenate([own[0], flip_core(other)[0]], axis=1)
-
-    def in_halves(a):
-        return (a[:half], a[half:])
-
-    gains = jnp.stack([mixer_gain, feed_gain])
-    gains = jnp.concatenate([gains, flip_core(gains)], axis=1)
-    gains_x = flip_row(gains)
-    gains_y = flip_y(gains)
-    gains_all = jnp.concatenate([gains, gains_x, gains_y, flip_y(gains_x)], axis=1)
-
-    x = by_core(stream_in)
-    g = by_core(cotangent)
-
-    def with_core(own, far):
-        near = jnp.stack([own, far])
-        return near, flip_core(near)
-
-    own_in, other_in = own_and_other(jnp.stack([input_weight, branch_weight]), y, 2)
-    far_in = flip_y(other_in)
-    near_in, sib_in = with_core(
-        jnp.concatenate([own_in[0], own_in[1]], axis=1), jnp.concatenate([far_in[0], far_in[1]], axis=1)
-    )
-
-    lanes = 2 * part
-    share = gate_weight.shape[0] // count
-    units = gate_weight.shape[1] // 2
-
-    def other_share(w, axis):
-        rows = w.shape[0] // (2 if axis == 0 else 1)
-        take = rows // count
-        start = seq * take + ((1 - y) * rows if axis == 0 else 0)
-        if axis == 0:
-            return lax.dynamic_slice(w, (start, 0), (take, w.shape[1]))
-        cols = w.shape[1] // 2
-        piece = lax.dynamic_slice(w, (start, (1 - y) * cols), (take, cols))
-        return jnp.concatenate([piece[:, n : n + lanes] for n in range(0, cols, lanes)], axis=0)
-
-    packed = jnp.concatenate(
-        [
-            other_share(gate_weight, 1),
-            other_share(up_weight, 1),
-            other_share(down_weight, 0),
-            other_share(output_weight, 0),
-        ],
-        axis=0,
-    )
-    packed = lax.all_gather(flip_y(packed), "seq", axis=0)
-
-    def late_weights(packed, gate_weight, up_weight, down_weight, output_weight):
-        def wide(at):
-            blocks = packed[:, at : at + share * (units // lanes)].reshape(count, units // lanes, share, lanes)
-            return blocks.transpose(0, 2, 1, 3).reshape(count * share, units)
-
-        step = share * (units // lanes)
-        far_gu = jnp.concatenate([wide(0), wide(step)], axis=1)
-        own_gu = jnp.concatenate(
-            [own_and_other(gate_weight, y, 1)[0], own_and_other(up_weight, y, 1)[0]], axis=1
-        )
-        near_gu, sib_gu = with_core(own_gu, far_gu)
-        d_rows = down_weight.shape[0] // 2
-        o_rows = output_weight.shape[0] // 2
-        at = 2 * step
-        far_d = packed[:, at : at + d_rows // count].reshape(d_rows, lanes)
-        at += d_rows // count
-        far_o = packed[:, at : at + o_rows // count].reshape(o_rows, lanes)
-        own_do = jnp.concatenate(
-            [own_and_other(output_weight, y, 0)[0], own_and_other(down_weight, y, 0)[0]], axis=0
-        )
-        near, sib = with_core(own_do, jnp.concatenate([far_o, far_d], axis=0))
-        chunks = []
-        for dy in (0, 1):
-            first = jnp.concatenate([near[dy][:, :part], sib[dy][:, :part]], axis=1)
-            second = jnp.concatenate([near[dy][:, part:], sib[dy][:, part:]], axis=1)
-            chunks += [jnp.where(lower, first, second), jnp.where(lower, second, first)]
-        both = jnp.concatenate(chunks, axis=1)
-        return near_gu, sib_gu, both[:o_rows], both[o_rows:]
-
     heads = recall_gate.shape[0] // 2
     rw = lax.dynamic_slice_in_dim(recall_gate, y * heads, heads, 0)
     aw = lax.dynamic_slice_in_dim(admit_gate, y * heads, heads, 0)
-    small = jnp.concatenate([filter_taps, decay_param[None], jnp.zeros((3,) + decay_param.shape, F32)])
-    sibling = flip_core(small)
-    small = jnp.where(
-        core == 0,
-        jnp.concatenate([small, sibling], axis=1),
-        jnp.concatenate([sibling, small], axis=1),
+    soft_own = jax.nn.softplus(-decay_param)[None]
+    small = jnp.concatenate(
+        [filter_taps, soft_own, decay_param[None], jnp.zeros((2,) + decay_param.shape, F32)]
     )
-    taps, decay = small[:KW], small[KW : KW + 1]
-    soft = jax.nn.softplus(-decay)
+    gains = jnp.concatenate([mixer_gain[None], feed_gain[None], jnp.zeros((6, part), F32)])
 
     lengths = lax.dynamic_index_in_dim(doc_lengths, core, 0, False)
     offset = doc_offset(lengths, seq * tokens, tokens)
     edge = jnp.full((8,), -1, jnp.int32)
     off = jnp.concatenate([edge, offset, edge])[:, None]
 
-    def neighbours(ends, sign):
-        return jnp.concatenate([shifted(ends, sign * n) for n in range(1, count)], axis=0)
-
-    n1, u, v, s1 = norm_uv(x.astype(BF), gains_all, near_in, sib_in)
-    border = shifted(u[tokens - 8 :], 1)
-    g_low = g.astype(BF)
-    conv, recall, admit, local_state, cum, ends, *errs = recur(
-        u, border, off, taps, rw, aw, soft, g_low
+    (
+        x, g, g_low, w_out, w_down, gains_all, small, s1, u, v, border, earlier, mid, mid_low,
+        n1, conv, recall, admit, states, mixed, ex, ey, ed, mx, my, md, far_w, sib_own, sib_far, w_in,
+    ) = front(
+        stream_in, cotangent, input_weight, branch_weight, output_weight, gate_weight, up_weight, down_weight,
+        gains, small, recall_gate, admit_gate, off, count - 1,
     )
-    late = lax.optimization_barrier(
-        (ends, packed, gate_weight, up_weight, down_weight, output_weight)
+    taps, soft, decay = small[:KW], small[KW : KW + 1], small[KW + 1 : KW + 2]
+    p0, p1, p2, p3, dx2, *dx_all, grad_feed, sum_down, sum_gu = feed(
+        (mid_low, mx, my, md), (g_low, ex, ey, ed), mid, g, gains_all, w_down,
+        (gate_weight, up_weight, sib_own, far_w, sib_far),
     )
-    near_gu, sib_gu, w_out, w_down = late_weights(*late[1:])
-    earlier = neighbours(ends, 1)
-    states, mixed, mid, *mid_all = mix(local_state, cum, v, x, earlier, w_out)
-    p0, p1, p2, p3, dx2, *dx_all, grad_feed, sum_down, sum_gu = feed(
-        mid_all, [g_low] + errs, mid, g, gains_all, near_gu, sib_gu, w_down
-    )
-    outs = collect(tuple(zip(*(in_halves(p) for p in (p0, p1, p2, p3)))))
-    out_chunk = jnp.concatenate(outs, axis=0) + mid
-
     (
         ev, er, eu, grad_chunk, grad_mixer, grad_recall, grad_admit, grad_small, mine_gu, far_gu, mine_down, far_down
     ) = back(
         dx_all, w_out, states, v, recall, conv, admit, u, off, soft, taps, rw, aw, border, earlier,
-        near_in, sib_in, s1, x, dx2, gains_all, sum_gu, sum_down,
+        w_in, s1, x, dx2, gains_all, sum_gu, sum_down,
     )
 
-    def rows_out(mine, theirs):
-        wide = jnp.where(
-            y == 0, jnp.concatenate([mine, theirs], axis=1), jnp.concatenate([theirs, mine], axis=1)
-        )
-        swapped = jnp.concatenate([wide[part:], wide[:part]], axis=0)
-        return jnp.where(lower, wide, swapped).astype(F32)
-
-    def cols_out(mine, theirs):
-        tall = jnp.where(
-            y == 0, jnp.concatenate([mine, theirs], axis=0), jnp.concatenate([theirs, mine], axis=0)
-        )
-        swapped = jnp.concatenate([tall[:, part:], tall[:, :part]], axis=1)
-        return jnp.where(lower, tall, swapped).astype(F32)
-
-    channels = taps.shape[1]
-    own = channels // 2
-    pieces = [
-        grad_small[:KW].reshape(-1),
-        grad_small[KW] * 8.0 * jax.nn.sigmoid(-decay[0]),
-        grad_recall.reshape(-1),
-        grad_admit.reshape(-1),
-    ]
-    gain_rows = jnp.stack([grad_mixer[0], grad_feed[0]])
-    gain_rows = jnp.where(
-        core == 0, gain_rows, jnp.concatenate([gain_rows[:, part:], gain_rows[:, :part]], axis=1)
+    mine_in, far_in, mine_out, far_out, gates, tiny, out, grad = tail(
+        mixed, er, n1, eu, ev, grad_recall, grad_admit, grad_small, grad_mixer, grad_feed,
+        (p0, p1, p2, p3), mid, grad_chunk,
     )
-    pieces.append(gain_rows.reshape(-1))
-    sizes = [p.size for p in pieces]
-    flat = jnp.concatenate(pieces)
-    flat = jnp.pad(flat, (0, -flat.size % 8192)).reshape(-1, 128)
-    mine_in, far_in, mine_out, far_out, flat = tail(n1, eu, ev, mixed, er, flat)
-    flat = flat.reshape(-1)
-    cuts, at = [], 0
-    for s in sizes:
-        cuts.append(flat[at : at + s])
-        at += s
-    grad_down = cols_out(mine_down, far_down)
-    grad_gate = rows_out(mine_gu[:, :units], far_gu[:, :units])
-    grad_up = rows_out(mine_gu[:, units:], far_gu[:, units:])
-    grad_output = cols_out(mine_out, far_out)
-    grad_input = rows_out(mine_in[:, :channels], far_in[:, :channels])
-    grad_branch = rows_out(mine_in[:, channels:], far_in[:, channels:])
-    g_taps = lax.dynamic_slice_in_dim(cuts[0].reshape(KW, channels), core * own, own, 1)
-    g_decay = lax.dynamic_slice_in_dim(cuts[1], core * own, own, 0)
-    gates = jnp.stack([cuts[2].reshape(grad_recall.shape), cuts[3].reshape(grad_admit.shape)])
-    far = flip_y(gates)
-    gates = jnp.where(
-        y == 0, jnp.concatenate([gates, far], axis=1), jnp.concatenate([far, gates], axis=1)
+    place = jnp.stack([row, y]).astype(jnp.int32)
+    grad_gate, grad_up, grad_down, grad_input, grad_branch, grad_output = arrange(
+        place, mine_gu, far_gu, mine_down, far_down, mine_in, far_in, mine_out, far_out
     )
-    gain_grads = lax.dynamic_slice_in_dim(cuts[4].reshape(2, 2 * part), core * part, part, 1)
-
-    def stacked(chunk):
-        own, other = chunk[:, :part], flip_core(chunk[:, part:])
-        return jnp.where(core == 0, jnp.stack([own, other]), jnp.stack([other, own]))
-
+    own = taps.shape[1] // 2
+    mine = lax.dynamic_slice_in_dim(tiny[:8], core * own, own, 1)
+    gain_grads = lax.dynamic_slice_in_dim(tiny[8:10, : 2 * part], core * part, part, 1)
     return (
-        stacked(out_chunk),
-        stacked(grad_chunk),
+        out,
+        grad,
         gain_grads[0],
         grad_input,
         grad_branch,
-        g_taps,
+        mine[:KW],
         gates[0],
         gates[1],
-        g_decay,
+        mine[KW] * 8.0 * jax.nn.sigmoid(-decay_param),
         grad_output,
         gain_grads[1],
         grad_gate,

time: 678 us -> 554 us (0.82)
  local copies, waits for them, and re-layouts: 65.8 us -> 15.5 us
  other arithmetic: 44.6 us -> 3.56 us
  Pallas kernels: 490 us -> 528 us
  starting transfers between devices: 32.3 us -> 0 us
  waiting for transfers between devices: 23 us -> 0 us
  between operations: 15.2 us -> 1.04 us
    ppermute x25 -> x0, starting transfers between devices: 32.2 us -> none  [the longest x4 15.3 us: passed_along(): return lax.ppermute(block, axis, route)]
    ppermute x25 -> x0, waiting for transfers between devices: 23 us -> none  [the longest x8 18 us: flip_y(): return lax.ppermute(a, 'col', [(i, i ^ 2) for i in range(4)])]
    pallas_call x4 -> x3, Pallas kernels: 235 us -> 254 us  [the longest x1 156 us: front(): pl.pallas_call(functools.partial(front_body, heads, blocks, count), grid=...]
    convert_element_type x10 -> x0, other arithmetic: 18.3 us -> none  [the longest x4 7.13 us: rows_out(): return jnp.where(lower, wide, swapped).astype(F32)]
    slice x27 -> x5, local copies, waits for them, and re-layouts: 17.5 us -> 1.78 us  [the longest x2 1.18 us: local_fast(): taps, soft, decay = (small[:KW], small[KW:KW + 1], small[KW + 1:KW + 2])]
    unnamed x107 -> x28, local copies, waits for them, and re-layouts: 24.8 us -> 9.33 us
    select_n x14 -> x1, other arithmetic: 13.2 us -> 0.01 us  [local_fast(): soft_own = jax.nn.softplus(-decay_param)[None]]
    pallas_call x1, Pallas kernels: 107 us -> 118 us  [feed(): pl.pallas_call(functools.partial(feed_body, blocks), grid=(blocks + tiles...]
  transfers between devices with their start and end apart: 26 -> 0, of which waited for: 6 -> 0; matrix products, arithmetic and copies ran while one was open for 12% -> 0% of each run, Pallas kernels for 20% -> 0%
where the time goes in v4:
time: 554 us; the launch traced here: 548 us
  Pallas kernels  528 us (95%)
  local copies, waits for them, and re-layouts  15.5 us (3%)
    pallas_call x1, Pallas kernels, back(): pl.pallas_call(functools.partial(back_body, heads, blocks, count), grid=(...  156 us
    pallas_call x1, Pallas kernels, front(): pl.pallas_call(functools.partial(front_body, heads, blocks, count), grid=...  156 us
    pallas_call x1, Pallas kernels, feed(): pl.pallas_call(functools.partial(feed_body, blocks), grid=(blocks + tiles...  118 us
    pallas_call x1, Pallas kernels, tail(): pl.pallas_call(tail_body, in_specs=[pl.BlockSpec(memory_space=pltpu.VMEM)...  88.1 us

profile of v4, /device:TPU:0, one launch (start us, length us, event | category | flops | bytes accessed | tf_op | source)
XLA Modules:
  0.0 547.7 jit_solution(7247436009972988147)
XLA Ops:
  0.7 0.7 constant_dynamic-slice_fusion.4
  1.4 0.2 reduce-window_clone.1
  1.5 0.7 subtract_bitcast_fusion
  2.2 0.1 select_reduce_fusion
  2.3 0.1 concatenate.11
  2.4 1.0 broadcast_in_dim.42.refs_12_.refs_11_
  3.4 0.0 copy-start.1
  3.4 2.9 copy.39.refs_0_
  6.3 0.0 copy-done.1
  6.3 0.0 copy-start.6
  6.3 0.0 copy-start.9
  6.3 0.0 copy-start.10
  6.4 0.0 copy-start.11
  6.4 1.8 copy.40.refs_1_
  8.2 0.0 copy-done.6
  8.2 0.1 pad.5.clone
  8.3 0.0 copy-done.9
  8.3 0.7 maximum_maximum_fusion.1.refs_9_
  8.9 0.1 pad.8.clone
  9.0 0.0 copy-done.10
  9.0 0.0 copy-done.11
  9.0 0.7 maximum_maximum_fusion.refs_8_
  9.7 155.5 %front.1 = (f32[1024,384]{1,0:T(8,128)}, f32[1024,384]{1,0:T(8,128)}, bf16[1024,384]{1,0:T(8,128)(2,1)}, bf16[512,1536]{1,0:T(8,128)(2,1)}, bf16[1152,1536]{1,0:...) custom-call(f32[2,1024,192]{2,1,0:T(8,128)} %copy.39.refs_0_, ...), custom_call_target="tpu_custom_call" | custom-call | flops 80530636800 | bytes 40960000 | tf_op jit(solution)/shard_map/front/pallas_call | solution.py:1081
  165.2 0.0 copy-start.8
  165.2 0.0 copy-start.3
  165.2 0.0 copy-start.4
  165.2 118.2 %feed.1 = (f32[1024,384]{1,0:T(8,128)}, bf16[1024,384]{1,0:T(8,128)(2,1)}, bf16[1024,384]{1,0:T(8,128)(2,1)}, bf16[1024,384]{1,0:T(8,128)(2,1)}, f32[1024,384]{1...) custom-call(bf16[1024,384]{1,0:T(8,128)(2,1)} %get-tuple-element.83., ...), custom_call_target="tpu_custom_call" | custom-call | flops 86973087744 | bytes 41336832 | tf_op jit(solution)/shard_map/feed/pallas_call | solution.py:1314
  283.5 0.0 copy-done.8
  283.5 0.6 slice.31.refs_13_
  284.1 0.6 slice.30.refs_12_
  284.7 0.0 copy-done.3
  284.7 0.0 copy-done.4
  284.7 0.8 constant_dynamic-slice_fusion.2
  285.5 155.8 %back.1 = (bf16[1024,512]{1,0:T(8,128)(2,1)}, bf16[1024,1536]{1,0:T(8,128)(2,1)}, bf16[1024,512]{1,0:T(8,128)(2,1)}, f32[1024,384]{1,0:T(8,128)}, f32[8,384]{1,0...) custom-call(bf16[1024,384]{1,0:T(8,128)(2,1)} %get-tuple-element.98., ...), custom_call_target="tpu_custom_call" | custom-call | flops 103079215104 | bytes 31457280 | tf_op jit(solution)/shard_map/back/pallas_call | solution.py:1703
  441.3 88.1 %tail.1 = (bf16[384,1024]{1,0:T(8,128)(2,1)}, bf16[384,1024]{1,0:T(8,128)(2,1)}, bf16[512,384]{1,0:T(8,128)(2,1)}, bf16[512,384]{1,0:T(8,128)(2,1)}, f32[2,8,128...) custom-call(bf16[1024,512]{1,0:T(8,128)(2,1)} %get-tuple-element.82.refs_0_, ...), custom_call_target="tpu_custom_call" | custom-call | flops 48318382080 | bytes 9437184 | tf_op jit(solution)/shard_map/tail/pallas_call | solution.py:1989
  529.5 0.6 pad_add_fusion.place
  530.0 9.9 %arrange.1 = (f32[384,2304]{1,0:T(8,128)}, f32[384,2304]{1,0:T(8,128)}, f32[2304,384]{1,0:T(8,128)}, f32[384,1024]{1,0:T(8,128)}, f32[384,1024]{1,0:T(8,128)}, /*index=5*/f32[1024,384]{1,0:T(8,128)}) custom-call(s32[2]{0:T(128)} %pad_add_fusion.place, bf16[384,2304]{1,0:T(8,128)(2,1)} %get-tuple-element.135.mine_gu, ...), custom_call_target="tpu_custom_call" | custom-call | flops 1000000 | bytes 24000000 | tf_op jit(solution)/shard_map/arrange/pallas_call | solution.py:2071
  539.9 0.0 copy-start
  539.9 2.9 copy.43
  542.9 0.0 copy-done
  542.9 0.0 copy-start.2
  542.9 1.7 copy.44
  544.5 0.0 copy-start.5
  544.5 0.0 copy-start.7
  544.5 0.0 copy-done.2
  544.5 1.0 slice_bitcast_fusion
  545.6 0.0 copy-done.5
  545.6 0.6 constant_dynamic-slice_fusion
  546.2 0.1 dynamic-slice_multiply_fusion
  546.3 0.0 copy-done.7
  546.3 0.6 divide_multiply_fusion
  546.9 0.6 fusion.1
  (8 shorter events, 0.0 us)
Async XLA Ops:
  3.4 2.9 copy-start.1
  6.3 1.8 copy-start.6
  6.3 1.9 copy-start.9
  6.3 2.7 copy-start.10
  6.4 2.7 copy-start.11
  165.2 118.3 %copy-start.8 = (f32[8,512]{1,0:T(8,128)S(1)}, f32[8,512]{1,0:T(8,128)}, u32[]{:S(2)}) copy-start(f32[8,512]{1,0:T(8,128)} %get-tuple-element.109) | copy-start | bytes 49156
  165.2 119.5 %copy-start.3 = (f32[8,128,128]{2,1,0:T(8,128)S(1)}, f32[8,128,128]{2,1,0:T(8,128)}, u32[]{:S(2)}) copy-start(f32[8,128,128]{2,1,0:T(8,128)} %refs_10_.1) | copy-start | bytes 1572868
  165.2 119.5 %copy-start.4 = (f32[8,128,128]{2,1,0:T(8,128)S(1)}, f32[8,128,128]{2,1,0:T(8,128)}, u32[]{:S(2)}) copy-start(f32[8,128,128]{2,1,0:T(8,128)} %refs_11_.1) | copy-start | bytes 1572868
  539.9 2.9 copy-start
  542.9 1.7 copy-start.2
  544.5 1.0 copy-start.5
  544.5 1.7 copy-start.7

commit v5 on v4

--- a/solution.py
+++ b/solution.py
@@ -324,7 +324,7 @@
 
 BF = jnp.bfloat16
 F32 = jnp.float32
-VMEM_LIMIT = 60 * 1024 * 1024
+VMEM_LIMIT = 62 * 1024 * 1024
 ROW_BLOCK = 256
 GELU_A = 0.7978845608028654
 GELU_B = 0.044715
@@ -466,6 +466,17 @@
     def one(n, carry):
         at = pl.ds(pl.multiple_of(n * step, step), step)
         dst[at, :] = (dst[at, :].astype(F32) + src[at, :].astype(F32)).astype(dst.dtype)
+        return carry
+
+    lax.fori_loop(0, dst.shape[0] // step, one, 0)
+
+
+def put_sum(dst, left, right):
+    step = row_step(dst)
+
+    def one(n, carry):
+        at = pl.ds(pl.multiple_of(n * step, step), step)
+        dst[at, :] = (left[at, :].astype(F32) + right[at, :].astype(F32)).astype(dst.dtype)
         return carry
 
     lax.fori_loop(0, dst.shape[0] // step, one, 0)
@@ -566,10 +577,7 @@
 
 
 def add_into(dst, src, start, rows):
-    step = 128
-    for r in range(start, start + rows, step):
-        at = slice(r, r + step)
-        dst[at, :] = (dst[at, :].astype(F32) + src[at, :].astype(F32)).astype(dst.dtype)
+    plus_in(dst.at[pl.ds(start, rows), :], src.at[pl.ds(start, rows), :])
 
 
 def load_rows(gate_w, up_w, sib_own, far, sib_far, dst, sem):
@@ -617,12 +625,34 @@
 
 
 def row_sums(values):
-    return dot_nt(jnp.ones((8, values.shape[1]), F32), values, PRECISE)
+    folded = values[:, :128]
+    for n in range(128, values.shape[1], 128):
+        folded = folded + values[:, n : n + 128]
+    return dot_nt(jnp.ones((8, 128), F32), folded, PRECISE)
 
 
 def as_column(lanes, width):
-    first = (lax.broadcasted_iota(jnp.int32, (8, width), 0) == 0).astype(F32)
-    return dot_tn(lanes, first, PRECISE)
+    first = (lax.broadcasted_iota(jnp.int32, (8, 128), 0) == 0).astype(F32)
+    column = dot_tn(lanes, first, PRECISE)
+    return jnp.concatenate([column] * (width // 128), axis=1)
+
+
+def norm_back_rows(start, rows, own_sum, low_x, low_y, dots_x, dots_y, scale, source, gain, base, out, low):
+    width = source.shape[1]
+    step = 128
+
+    def one(n, sum_grad):
+        at = pl.ds(pl.multiple_of(start + n * step, step), step)
+        d = own_sum[at, :] + low_x[at, :].astype(F32) + low_y[at, :].astype(F32)
+        s, m = scale[at, :], source[at, :]
+        t = as_column(dots_x[:, at] + dots_y[:, at], width)
+        new = base[at, :] + s * gain * d - m * (s * s) * t * (1.0 / D)
+        out[at, :] = new
+        if low is not None:
+            low[at, :] = new.astype(BF)
+        return sum_grad + jnp.sum(d * m * s, axis=0, keepdims=True)
+
+    return lax.fori_loop(0, rows // step, one, jnp.zeros((1, width), F32))
 
 
 def chain(entries, count):
@@ -661,10 +691,10 @@
     (gains_in, small_in, recall_gate, admit_gate, off) = refs[8:13]
     (x, g, e_own, w_out, w_down, gains_out, small, s1, u, v, border_out, earlier_out, mid, own) = refs[13:27]
     (n1, conv, recall, admit, states, mixed) = refs[27:33]
-    (ex, ey, ed, mx, my, md, far_gu, sib_own, sib_far, w_in_out) = refs[33:43]
-    (x_own, x_recv, g_own, g_recv, gains_recv, small_recv, own_low, gx, gy, gd) = refs[43:53]
-    (w_in, gains, border, earlier) = refs[53:57]
-    (wo, wd, local, cum, ext, ends, q0, q1, q2, q3, r3, rx, ry, load, send, recv) = refs[57:]
+    (mx, my, md, far_gu, sib_own, sib_far, w_in_out) = refs[33:40]
+    (x_own, x_recv, g_own, g_recv, gains_recv, small_recv, own_low, gx, gy, gd) = refs[40:50]
+    (w_in, gains, border, earlier) = refs[50:54]
+    (wo, wd, local, cum, ext, ends, q0, q1, q2, q3, r3, rx, ry, load, send, recv) = refs[54:]
     i = pl.program_id(0)
     seq, row, col = lax.axis_index("seq"), lax.axis_index("row"), lax.axis_index("col")
     y = lax.div(col, 2)
@@ -746,7 +776,6 @@
     w_in_store = copy(w_in, w_in_out)
 
     gather_n = made.block(gather_messages_by_x, own_low, gx, gy, gd)
-    gather_e = made.block(gather_messages_by_x, e_own, ex, ey, ed)
     scatter = made.block(scatter_messages, q1, q2, q3, r3, rx, ry)
     gather_m = made.block(gather_messages, own, mx, my, md)
     edge = made.new(u.at[pl.ds(rows - 8, 8), :], border, {"seq": seq + 1})
@@ -754,11 +783,15 @@
 
     def put_together(left, right, full, low):
         step = 128
-        for r in range(0, rows, step):
-            at = slice(r, r + step)
+
+        def one(n, carry):
+            at = pl.ds(pl.multiple_of(n * step, step), step)
             whole = jnp.concatenate([left[at, :], right[at, :]], axis=1)
             full[at, :] = whole
             low[at, :] = whole.astype(BF)
+            return carry
+
+        lax.fori_loop(0, rows // step, one, 0)
 
     @pl.when(i == 0)
     def _():
@@ -770,8 +803,6 @@
             [to_x, to_y, to_core] + [{"seq": lax.rem(seq + n, count + 1)} for n in range(1, count + 1)]
         )
         for m in swap:
-            m.start()
-        for m in in_far:
             m.start()
         x_copy.wait()
         swap[0].wait_recv()
@@ -789,9 +820,6 @@
         small[:, pl.ds(pl.multiple_of(core * lane, lane), lane)] = small_in[...]
         small[:, pl.ds(pl.multiple_of((1 - core) * lane, lane), lane)] = small_recv[...]
         swap_g.start()
-        for m, n in zip(in_far, in_pass):
-            m.wait_recv()
-            n.start()
         gains_x.wait_recv()
         gains_d.start()
         gather_n[1].wait_recv()
@@ -801,12 +829,14 @@
             m.start()
         gather_n[3].wait_recv()
         gather_n[5].start()
+        for m in in_far:
+            m.start()
+        for m, n in zip(in_far, in_pass):
+            m.wait_recv()
+            n.start()
         wo_far.start()
         for m in ff_far:
             m.start()
-        g_copy.wait()
-        swap_g.wait_recv()
-        put_together(g_own, g_recv, g, e_own)
         for c in in_own:
             c.wait()
         for m in in_core + in_pass:
@@ -816,8 +846,12 @@
         w_in_store.start()
         gather_n[0].wait_recv()
         gather_n[4].wait_recv()
-        for m in gather_e[:4]:
-            m.start()
+
+    @pl.when(i == 1)
+    def _():
+        g_copy.wait()
+        swap_g.wait_recv()
+        put_together(g_own, g_recv, g, e_own)
 
     @pl.when(i == blocks // 2)
     def _():
@@ -908,15 +942,8 @@
 
     @pl.when(i == blocks + 1)
     def _():
-        gather_e[1].wait_recv()
-        gather_e[4].start()
         wo_far.wait_recv()
         wo_pass.start()
-
-    @pl.when(i == blocks + 2)
-    def _():
-        gather_e[3].wait_recv()
-        gather_e[5].start()
 
     def columns_in_order(pieces, out):
         size = out.shape[0]
@@ -1001,11 +1028,15 @@
         for base, first in ((0, 2), (half, 4)):
             scatter[first].wait_recv()
             scatter[first + 1].wait_recv()
-            for r in range(base, base + half, 128):
-                at = slice(r, r + 128)
+
+            def one(n, carry):
+                at = pl.ds(pl.multiple_of(base + n * 128, 128), 128)
                 total = x[at, :] + q0[at, :] + rx[at, :].astype(F32) + ry[at, :].astype(F32)
                 mid[at, :] = total
                 own[at, :] = total.astype(BF)
+                return carry
+
+            lax.fori_loop(0, half // 128, one, 0)
             start = 0 if base == 0 else 2
             gather_m[start].start()
             gather_m[start + 1].start()
@@ -1019,11 +1050,9 @@
         gather_m[5].start()
         for n in (1, 2, 4, 5):
             gather_m[n].wait_recv()
-        for n in (0, 2, 4, 5):
-            gather_e[n].wait_recv()
         sent = swap + [swap_g, gains_x, gains_y, gains_d] + in_far + in_core + in_pass
         sent += [wo_far, wo_core, wo_pass] + ff_far + ff_share + ff_core + ff_pass
-        for m in sent + gather_n + gather_e + scatter + gather_m:
+        for m in sent + gather_n + scatter + gather_m:
             m.wait_send()
 
         @pl.when(seq < count)
@@ -1074,7 +1103,7 @@
         chunk_low,
     ]
     blocked = [sds((rows, 4 * width), BF), wide, wide, wide, wide, sds((rows, channels), BF)]
-    away = [chunk_low] * 6 + [sds((width, 2 * units), BF)] * 3 + [sds((4 * width, 2 * channels), BF)]
+    away = [chunk_low] * 3 + [sds((width, 2 * units), BF)] * 3 + [sds((4 * width, 2 * channels), BF)]
     piece = pltpu.VMEM((rows, width), BF)
     side = pltpu.VMEM((rows, part), F32)
     tall = pl.BlockSpec((rows, 128), head_at)
@@ -1087,7 +1116,7 @@
         + [pl.BlockSpec((block, 4 * width), norm_at)]
         + [tall] * 3
         + [pl.BlockSpec((block, channels), mix_at)] * 2
-        + [any_spec()] * 10,
+        + [any_spec()] * 7,
         out_shape=held + blocked + away,
         scratch_shapes=[side] * 4
         + [pltpu.VMEM(gains.shape, F32), pltpu.VMEM(small.shape, F32)]
@@ -1114,30 +1143,68 @@
     )(stream, cot, in_w, br_w, out_w, gate_w, up_w, down_w, gains, small, recall_gate, admit_gate, off)
 
 
+FEED_MESSAGES = 64
+FEED_CUTS = 4
+
+
 def feed_body(blocks, *refs):
-    (x0, x1, x2, x3, e0, e1, e2, e3, mid, cot, gain, wd) = refs[:12]
-    weights = refs[12:17]
-    outs = refs[17:21]
-    (dx, own, gx, gy, gd, gain_grad, s_down, s_gu) = refs[21:29]
-    (wgu, load, n2, hid, ee, err, scale, stage, c_down, c_gu) = refs[29:39]
-    (q0, q1, q2, q3, r3, rx, ry, dots, dots_x, dots_y, send, recv) = refs[39:]
+    (x0, x1, x2, x3, e_own, mid, cot, gain, wd_in) = refs[:9]
+    weights = refs[9:14]
+    outs = refs[14:18]
+    (dx, own, gx, gy, gd, gain_grad, s_down, s_gu) = refs[18:26]
+    (wgu, wd, ex, ey, ed, load, n2, hid, ee, err, scale, stage, c_down, c_gu, a_down, b_down) = refs[26:42]
+    (a_gu, b_gu, free, q0, q1, q2, q3, r3, rx, ry, dots, dots_x, dots_y, send, recv) = refs[42:]
     i = pl.program_id(0)
-    sems = (send, recv)
-    scatter = scatter_messages(q1, q2, q3, r3, rx, ry, sems, 0)
-    gather = gather_messages(own, gx, gy, gd, sems, 6)
-    small_x = message(dots, dots_x, neighbour_x(), sems, 12)
-    small_y = message(dots_x, dots_y, neighbour_y(), sems, 13)
+    made = Messages((send, recv))
     block, width = x0.shape
     rows = mid.shape[0]
     half = rows // 2
     units = hid.shape[1]
+    tiles = units // width
+    scatter = made.block(scatter_messages, q1, q2, q3, r3, rx, ry)
+    gather = made.block(gather_messages, own, gx, gy, gd)
+    halves = (pl.ds(0, half), pl.ds(half, half))
+    small_x = [made.new(dots.at[:, at], dots_x.at[:, at], neighbour_x()) for at in halves]
+    small_y = [made.new(dots_x.at[:, at], dots_y.at[:, at], neighbour_y()) for at in halves]
+    gu_core = [made.new(stage, c_gu, neighbour_core()) for n in (0, 1)]
+    down_core = [
+        made.new(
+            stage.at[:, pl.ds(n * 2 * width, 2 * width)], c_down.at[pl.ds(n * width, width), :], neighbour_core()
+        )
+        for n in range(tiles)
+    ]
+    part_d = units // 2
+    pieces = [
+        [r.at[pl.ds(n * part_d, part_d), pl.ds(lane, width)] for r in (s_down, a_down, b_down)]
+        for lane in (width, 0)
+        for n in range(2)
+    ]
+    cut = 2 * width // 8
+    for n in range(FEED_CUTS // 2):
+        at = pl.ds(n * cut, cut)
+        pieces.append([s_gu.at[pl.ds(width + n * cut, cut), :], a_gu.at[at, :], b_gu.at[at, :]])
+    total = SeqSum(pieces, (send, recv), made.used)
+    made.used += 2 * len(pieces)
+
+    gather_e = made.block(gather_messages, e_own, ex, ey, ed)
+    load_d = pltpu.make_async_copy(wd_in, wd, load.at[10])
+    load_cot = pltpu.make_async_copy(cot, dx, load.at[11])
+    second = blocks + tiles
+    third = second + blocks
 
     @pl.when(i == 0)
     def _():
         copies = load_rows(*weights, wgu, load)
-        greet_all((neighbour_x(), neighbour_y(), neighbour_core()))
+        load_d.start()
+        load_cot.start()
+        greet_all(
+            (neighbour_x(), neighbour_y(), neighbour_core(), neighbour_end(), neighbour_middle())
+        )
+        for m in gather_e[:4]:
+            m.start()
         for c in copies:
             c.wait()
+        load_d.wait()
 
     @pl.when(i < blocks)
     def _():
@@ -1151,20 +1218,53 @@
         for j, n in enumerate(normed):
             term = dot_nn(n.astype(BF), wgu[j * width : (j + 1) * width, :])
             acc = term if acc is None else acc + term
-        errs = [r[...] for r in (e0, e1, e2, e3)]
-        wide = [e.astype(F32) for e in errs]
-        for source, target in ((normed, n2), (wide, ee)):
+        for j in (0, 1):
+            k, p = pair_up(normed[2 * j], normed[2 * j + 1])
+            n2[at, j * width : (j + 1) * width] = k.astype(BF)
+            n2[at, (j + 2) * width : (j + 3) * width] = p.astype(BF)
+        pre, up = acc[:, :units], acc[:, units:]
+        err[at, :units] = pre.astype(BF)
+        err[at, units:] = up.astype(BF)
+        h = (gelu_pair(pre)[0] * up).astype(BF)
+        hid[at, :] = h
+        for j, q in enumerate(outs):
+            q[...] = dot_nn(h, wd[:, j * width : (j + 1) * width]).astype(q.dtype)
+
+    @pl.when(i == blocks - 2)
+    def _():
+        gather_e[0].wait_recv()
+        gather_e[4].start()
+
+    @pl.when(i == blocks - 1)
+    def _():
+        gather_e[3].wait_recv()
+        gather_e[5].start()
+
+    @pl.when(i == blocks)
+    def _():
+        for n in (1, 2, 4, 5):
+            gather_e[n].wait_recv()
+        step = 128
+
+        def one(n, carry):
+            at = pl.ds(pl.multiple_of(n * step, step), step)
+            wide = [r[at, :].astype(F32) for r in (e_own, ex, ey, ed)]
             for j in (0, 1):
-                k, p = pair_up(source[2 * j], source[2 * j + 1])
-                target[at, j * width : (j + 1) * width] = k.astype(BF)
-                target[at, (j + 2) * width : (j + 3) * width] = p.astype(BF)
-        pre, up = acc[:, :units], acc[:, units:]
+                k, p = pair_up(wide[2 * j], wide[2 * j + 1])
+                ee[at, j * width : (j + 1) * width] = k.astype(BF)
+                ee[at, (j + 2) * width : (j + 3) * width] = p.astype(BF)
+            return carry
+
+        lax.fori_loop(0, rows // step, one, 0)
+
+    @pl.when((i >= second) & (i < third))
+    def _():
+        at = pl.ds(pl.multiple_of((i - second) * block, block), block)
+        pre, up = err[at, :units].astype(F32), err[at, units:].astype(F32)
         act, slope = gelu_pair(pre)
-        h = (act * up).astype(BF)
-        hid[at, :] = h
         dh = None
-        for j, e in enumerate(errs):
-            term = dot_nt(e, wd[:, j * width : (j + 1) * width])
+        for j, r in enumerate((e_own, ex, ey, ed)):
+            term = dot_nt(r[at, :], wd[:, j * width : (j + 1) * width])
             dh = term if dh is None else dh + term
         g = (dh * up * slope).astype(BF)
         b = (dh * act).astype(BF)
@@ -1174,134 +1274,146 @@
         for j, q in ((3, q3), (1, q1), (2, q2), (0, q0)):
             rows_w = slice(j * width, (j + 1) * width)
             q[at, :] = (dot_nt(g, wgu[rows_w, :units]) + dot_nt(b, wgu[rows_w, units:])).astype(q.dtype)
-        for j, q in enumerate(outs):
-            q[...] = dot_nn(h, wd[:, j * width : (j + 1) * width]).astype(q.dtype)
-
-    @pl.when(i == blocks // 2 - 1)
+
+    def hand_dots(n):
+        small_x[n].wait_recv()
+        dots_x[:, halves[n]] = dots_x[:, halves[n]] + dots[:, halves[n]]
+        small_y[n].start()
+
+    own_gain = gain[1:2, :width]
+
+    def finish(start, first):
+        scatter[first].wait_recv()
+        scatter[first + 1].wait_recv()
+        return norm_back_rows(
+            start, half, q0, rx, ry, dots_x, dots_y, scale, mid, own_gain, dx, dx, own
+        )
+
+    @pl.when(i == second + blocks // 2 - 1)
     def _():
         scatter[0].start()
         scatter[2].start()
-
-    @pl.when(i == blocks - 1)
-    def _():
-        scatter[1].start()
-        small_x.start()
-
-    @pl.when(i == blocks)
+        small_x[0].start()
+
+    @pl.when(i == third - 2)
     def _():
         scatter[0].wait_recv()
         add_into(q2, r3, 0, half)
         scatter[3].start()
+        hand_dots(0)
+
+    @pl.when(i == third - 1)
+    def _():
+        scatter[1].start()
+        small_x[1].start()
         scatter[4].start()
-        small_x.wait_recv()
-        dots_x[...] = dots_x[...] + dots[...]
-        small_y.start()
-
-    @pl.when(i == blocks + 1)
+        load_cot.wait()
+        small_y[0].wait_recv()
+        gain_grad[0:1, :] = finish(0, 2)
+        gather[0].start()
+        gather[1].start()
+
+    @pl.when((i >= blocks) & (i < blocks + tiles))
+    def _():
+        k = i - blocks
+        at = pl.ds(pl.multiple_of(k * width, width), width)
+        g = dot_tn(hid[:, at], ee[...])
+        stage[:, pl.ds(pl.multiple_of(k * 2 * width, 2 * width), 2 * width)] = g[:, 2 * width :].astype(BF)
+        s_down[at, :] = g[:, : 2 * width].astype(BF)
+
+    for n in range(tiles):
+
+        @pl.when(i == blocks + n)
+        def _():
+            down_core[n].start()
+
+    @pl.when(i == second)
+    def _():
+        for n in range(tiles):
+            down_core[n].wait_recv()
+            down_core[n].wait_send()
+        plus_in(s_down, c_down)
+        for n in range(3):
+            total.begin(n)
+
+    for n in (0, 1):
+
+        @pl.when(i == third + 1 + 2 * n)
+        def _():
+            gu_core[n].wait_send()
+
+    @pl.when((i >= third) & (i < third + 4))
+    def _():
+        k = i - third
+        n = jnp.where(k < 2, 3 - 2 * k, 6 - 2 * k)
+        at = pl.ds(pl.multiple_of(n * width, width), width)
+        stage[...] = dot_tn(n2[:, at], err[...]).astype(BF)
+
+    for n in (0, 1):
+
+        @pl.when(i == third + 2 * n)
+        def _():
+            if n:
+                pl.semaphore_wait(free, 1)
+            gu_core[n].start()
+
+        @pl.when(i == third + 2 * n + 1)
+        def _():
+            gu_core[n].wait_recv()
+            target = s_gu.at[pl.ds((1 - n) * width, width), :]
+            put_sum(target, stage, c_gu)
+            if not n:
+                pl.semaphore_signal(free, inc=1, device_id=neighbour_core(), device_id_type=MESH_ID)
+
+    @pl.when(i == third + 1)
+    def _():
+        for n in range(4, len(pieces)):
+            total.begin(n)
+
+    ticks = [second + 1, second + 3] + [third + 1 + n for n in range(len(pieces))]
+    for t, where in enumerate(ticks):
+
+        @pl.when(i == where)
+        def _():
+            if t + 3 < 4:
+                total.begin(t + 3)
+            if t < len(pieces):
+                total.relay(t)
+            if 0 <= t - 1 < len(pieces):
+                total.settle(t - 1)
+            if t >= 2:
+                total.finish(t - 2)
+
+    @pl.when(i == third)
     def _():
         scatter[1].wait_recv()
         add_into(q1, r3, half, half)
         scatter[5].start()
-
-    def finish(base, first, start):
-        scatter[first].wait_recv()
-        scatter[first + 1].wait_recv()
-        sum_grad = None
-        for r in range(base, base + half, 128):
-            at = slice(r, r + 128)
-            d = q0[at, :] + rx[at, :].astype(F32) + ry[at, :].astype(F32)
-            s, m = scale[at, :], mid[at, :]
-            t = as_column(dots_x[:, at] + dots_y[:, at], width)
-            new = cot[at, :] + s * own_gain * d - m * (s * s) * t * (1.0 / D)
-            dx[at, :] = new
-            own[at, :] = new.astype(BF)
-            term = jnp.sum(d * m * s, axis=0, keepdims=True)
-            sum_grad = term if sum_grad is None else sum_grad + term
-        gather[start].start()
-        gather[start + 1].start()
-        return sum_grad
-
-    own_gain = gain[1:2, :width]
-
-    @pl.when(i == blocks + 2)
-    def _():
-        small_y.wait_recv()
-        gain_grad[0:1, :] = finish(0, 2, 0)
-
-    @pl.when(i == blocks + 4)
-    def _():
-        gain_grad[0:1, :] = gain_grad[0:1, :] + finish(half, 4, 2)
-
-    @pl.when(i == blocks + 5)
-    def _():
+        hand_dots(1)
+
+    @pl.when(i == third + 2)
+    def _():
+        small_y[1].wait_recv()
+        gain_grad[0:1, :] = gain_grad[0:1, :] + finish(half, 4)
+        gather[2].start()
+        gather[3].start()
         gather[0].wait_recv()
         gather[4].start()
 
-    @pl.when(i == blocks + 6)
+    @pl.when(i == third + 4)
     def _():
         gather[3].wait_recv()
         gather[5].start()
 
-    tiles = units // width
-    to_core = [
-        message(stage, c_gu.at[pl.ds(n * width, width), :], neighbour_core(), sems, 14 + n) for n in (0, 1)
-    ] + [
-        message(
-            stage.at[:, pl.ds(n * 2 * width, 2 * width)],
-            c_down.at[pl.ds(n * width, width), :],
-            neighbour_core(),
-            sems,
-            16 + n,
-        )
-        for n in range(tiles)
-    ]
-
-    def gu_tile(n):
-        return dot_tn(n2[:, n * width : (n + 1) * width], err[...])
-
-    for n in (0, 1):
-
-        @pl.when(i == blocks + n)
-        def _():
-            g = gu_tile(2 + n).astype(BF)
-            if n:
-                to_core[0].wait_send()
-            stage[...] = g
-            to_core[n].start()
-
-    for n in range(tiles):
-
-        @pl.when(i == blocks + 2 + n)
-        def _():
-            at = slice(n * width, (n + 1) * width)
-            g = dot_tn(hid[:, at], ee[...])
-            if n == 0:
-                to_core[1].wait_send()
-            stage[:, n * 2 * width : (n + 1) * 2 * width] = g[:, 2 * width :].astype(BF)
-            to_core[2 + n].start()
-            s_down[at, :] = g[:, : 2 * width].astype(BF)
-
-    for n in (1, 0):
-
-        @pl.when(i == blocks + tiles + 3 - n)
-        def _():
-            to_core[n].wait_recv()
-            at = slice(n * width, (n + 1) * width)
-            s_gu[...] = (gu_tile(n) + c_gu[at, :].astype(F32)).astype(BF)
-
-    @pl.when(i == blocks + tiles + 4)
-    def _():
-        for n in range(tiles):
-            to_core[2 + n].wait_recv()
-            to_core[2 + n].wait_send()
-        plus_in(s_down, c_down)
+    @pl.when(i == third + 2 + len(pieces))
+    def _():
         for n in (1, 2, 4, 5):
             gather[n].wait_recv()
-        for m in scatter + gather + [small_x, small_y]:
+        for m in scatter + gather + gather_e + small_x + small_y:
             m.wait_send()
 
 
-def feed(chunks, errs, mid, cot, gain, wd, weights):
+def feed(chunks, err_own, mid, cot, gain, wd, weights):
     rows, width = chunks[0].shape
     units = wd.shape[0]
     block = ROW_BLOCK
@@ -1310,18 +1422,17 @@
     held = functools.partial(held_spec, block, last=blocks - 1)
     chunk = pltpu.VMEM((rows, width), BF)
     lanes = pltpu.VMEM((8, rows), F32)
-    gu_spec = pl.BlockSpec((width, 2 * units), lambda i: (jnp.where(i >= blocks + tiles + 3, 0, 1), 0))
+    landing = pltpu.VMEM((units, 2 * width), BF)
     return pl.pallas_call(
         functools.partial(feed_body, blocks),
-        grid=(blocks + tiles + 5,),
-        in_specs=[held(width)] * 8
-        + [whole_spec(mid.shape), whole_spec(cot.shape), whole_spec(gain.shape)]
-        + [whole_spec(wd.shape)]
-        + [any_spec()] * 5,
+        grid=(2 * blocks + tiles + 7 + FEED_CUTS // 2,),
+        in_specs=[held(width)] * 4
+        + [whole_spec(err_own.shape), whole_spec(mid.shape), any_spec(), whole_spec(gain.shape)]
+        + [any_spec()] * 6,
         out_specs=[held(width)] * 4
         + [whole_spec((rows, width))] * 2
         + [any_spec()] * 3
-        + [whole_spec((8, width)), whole_spec((units, 2 * width)), gu_spec],
+        + [whole_spec((8, width)), whole_spec((units, 2 * width)), whole_spec((2 * width, 2 * units))],
         out_shape=[sds((rows, width), F32)]
         + [sds((rows, width), BF)] * 3
         + [sds((rows, width), F32)]
@@ -1329,36 +1440,46 @@
         + [sds((8, width), F32), sds((units, 2 * width), BF), sds((2 * width, 2 * units), BF)],
         scratch_shapes=[
             pltpu.VMEM((4 * width, 2 * units), BF),
-            pltpu.SemaphoreType.DMA((10,)),
+            pltpu.VMEM(wd.shape, BF),
+            chunk,
+            chunk,
+            chunk,
+            pltpu.SemaphoreType.DMA((12,)),
             pltpu.VMEM((rows, 4 * width), BF),
             pltpu.VMEM((rows, units), BF),
             pltpu.VMEM((rows, 4 * width), BF),
             pltpu.VMEM((rows, 2 * units), BF),
             pltpu.VMEM((rows, 1), F32),
             pltpu.VMEM((width, 2 * units), BF),
-            pltpu.VMEM((units, 2 * width), BF),
-            pltpu.VMEM((2 * width, 2 * units), BF),
+            landing,
+            pltpu.VMEM((width, 2 * units), BF),
+            landing,
+            landing,
+            pltpu.VMEM((FEED_CUTS * width // 8, 2 * units), BF),
+            pltpu.VMEM((FEED_CUTS * width // 8, 2 * units), BF),
+            pltpu.SemaphoreType.REGULAR,
             pltpu.VMEM((rows, width), F32),
         ]
         + [chunk] * 6
         + [lanes] * 3
-        + [pltpu.SemaphoreType.DMA((16 + tiles,))] * 2,
+        + [pltpu.SemaphoreType.DMA((FEED_MESSAGES,))] * 2,
         compiler_params=comm_params(3),
         cost_estimate=cost(48 * rows * wd.size, 3 * nbytes(wd) + rows * 30000, rows * units),
         name="feed",
-    )(*chunks, *errs, mid, cot, gain, wd, *weights)
+    )(*chunks, err_own, mid, cot, gain, wd, *weights)
 
 
 def back_body(heads, blocks, count, *refs):
     errs = refs[0:4]
     (w_out, states, branch, recall, conv, admit, u_head, off, soft) = refs[4:13]
-    (taps, recall_w, admit_w, border, earlier, u, v, w, scale, x, dx, gain) = refs[13:25]
-    (sum_gu, sum_down) = refs[25:27]
-    (ev, paired, eu, grad, gain_grad, grad_recall, grad_admit, grad_small) = refs[27:35]
-    (mine_gu, far_gu, mine_down, far_down) = refs[35:39]
-    (part, reach, ext, st, uext, dc, ends, later, edge, from_later, load) = refs[39:50]
-    (q0, q1, q2, q3, r3, rx, ry, dots, dots_x, dots_y) = refs[50:60]
-    (s_gu, a_gu, b_gu, s_dn, a_dn, b_dn, store, send, recv) = refs[60:]
+    (taps, recall_w, admit_w, border, earlier, u, v, w_hbm, scale, x_hbm, dx_hbm, gain) = refs[13:25]
+    (sum_gu, sum_down, mixed) = refs[25:28]
+    (ev, eu, grad, gain_grad, grad_small) = refs[28:33]
+    (mine_gu, far_gu, far_down, mine_out, far_out, gates) = refs[33:39]
+    (w, x, dx, paired, part, reach, ext, st, uext, dc, ends, later, edge, from_later, load) = refs[39:54]
+    (q0, q1, q2, q3, r3, rx, ry, dots, dots_x, dots_y) = refs[54:64]
+    (s_gu, a_gu, b_gu, s_out, p_out, c_out, a_out, b_out) = refs[64:72]
+    (s_gt, p_gt, c_gt, a_gt, b_gt, store, send, recv) = refs[72:]
     i = pl.program_id(0)
     sems = (send, recv)
     seq = lax.axis_index("seq")
@@ -1377,78 +1498,116 @@
     hand_edge = message(edge, from_later, {"seq": seq - 1}, sems, base)
     base += 1
 
-    rows_gu, rows_dn = width // 4, sum_down.shape[0] // 2
-    group_gu, group_dn = (s_gu, a_gu, b_gu), (s_dn, a_dn, b_dn)
-
-    def gu_at(n):
-        return pl.ds(n * rows_gu, rows_gu)
-
-    def dn_at(n):
-        return pl.ds(n * rows_dn, rows_dn)
-
-    places = [("gu", n) for n in (4, 5, 6, 7)] + [("far", n) for n in (0, 1)]
-    places += [("own", n) for n in (0, 1)] + [("gu", n) for n in (0, 1, 2, 3)]
-
-    def view(kind, n, ref):
-        if kind == "gu":
-            return ref.at[gu_at(n), :]
-        return ref.at[dn_at(n), pl.ds(width if kind == "far" else 0, width)]
-
-    pieces = [
-        [view(kind, n, r) for r in (group_gu if kind == "gu" else group_dn)] for kind, n in places
+    cut, rows_out = width // 8, channels
+    y = lax.div(lax.axis_index("col"), 2)
+    to_side, to_core = neighbour_y(), neighbour_core()
+    size = heads * 128
+    pieces, to_y, to_out, stores = [], {}, {}, []
+
+    def store_copy(src, dst):
+        stores.append(pltpu.make_async_copy(src, dst, store.at[len(stores)]))
+        return stores[-1]
+
+    made = Messages(sems)
+    made.used = base
+    done = FEED_CUTS * cut
+    early_y = [
+        made.new(sum_down.at[:, pl.ds(width, width)], far_down, to_side),
+        made.new(sum_gu.at[pl.ds(width, done), :], far_gu.at[pl.ds(0, done), :], to_side),
     ]
-    total = SeqSum(pieces, sems, base)
-    base += 2 * len(pieces)
-    to_y, to_out = {}, {}
-    for p, (kind, n) in enumerate(places):
-        source = pieces[p][0]
-        if kind == "far":
-            to_y[p] = message(source, far_down.at[dn_at(n), :], neighbour_y(), sems, base + len(to_y))
-        elif kind == "own":
-            to_out[p] = pltpu.make_async_copy(source, mine_down.at[dn_at(n), :], store.at[len(to_out)])
-        elif n >= 4:
-            to_y[p] = message(source, far_gu.at[gu_at(n - 4), :], neighbour_y(), sems, base + len(to_y))
+    for start, rows_gu in ((12, 1), (13, 2), (15, 1), (0, 2), (2, 2), (4, 2), (6, 2)):
+        p = len(pieces)
+        at = pl.ds(start * cut, rows_gu * cut)
+        pieces.append([r.at[at, :] for r in (s_gu, a_gu, b_gu)])
+        if start >= 8:
+            target = far_gu.at[pl.ds((start - 8) * cut, rows_gu * cut), :]
+            to_y[p] = [made.new(pieces[p][0], target, to_side)]
         else:
-            to_out[p] = pltpu.make_async_copy(source, mine_gu.at[gu_at(n), :], store.at[len(to_out)])
+            to_out[p] = [store_copy(pieces[p][0], mine_gu.at[at, :])]
+    for lane in (width, 0):
+        for n in (0,):
+            p = len(pieces)
+            at = pl.ds(n * rows_out, rows_out)
+            pieces.append([r.at[at, pl.ds(lane, width)] for r in (s_out, a_out, b_out)])
+            if lane:
+                to_y[p] = [made.new(pieces[p][0], far_out.at[at, :], to_side)]
+            else:
+                to_out[p] = [store_copy(pieces[p][0], mine_out.at[at, :])]
+    p = len(pieces)
+    pieces.append([s_gt, a_gt, b_gt])
+    to_y[p], to_out[p] = [], []
+    for n in (0, 1):
+        source = s_gt.at[pl.ds(n * size, size), :]
+        target = gates.at[pl.ds(pl.multiple_of((2 * n + y) * size, size), size), :]
+        to_y[p].append(made.new(source, target, to_side))
+        to_out[p].append(store_copy(source, target))
+    total = SeqSum(pieces, sems, made.used)
+    made.used += 2 * len(pieces)
+    core_out, core_gt = made.new(p_out, c_out, to_core), made.new(p_gt, c_gt, to_core)
+    load_gu = pltpu.make_async_copy(sum_gu, s_gu, load.at[0])
     loads = [
-        pltpu.make_async_copy(sum_gu, s_gu, load.at[0]),
-        pltpu.make_async_copy(sum_down, s_dn, load.at[1]),
+        pltpu.make_async_copy(source, target, load.at[n + 1])
+        for n, (source, target) in enumerate(((w_hbm, w), (x_hbm, x), (dx_hbm, dx)))
     ]
 
     def tick(t):
-        if t + 2 < len(pieces):
-            total.begin(t + 2)
+        if t + 3 < len(pieces):
+            total.begin(t + 3)
         if t < len(pieces):
             total.relay(t)
         if 0 <= t - 1 < len(pieces):
             total.settle(t - 1)
         if 0 <= t - 2 < len(pieces):
             total.finish(t - 2)
-            if t - 2 in to_y:
-                to_y[t - 2].start()
-            else:
-                to_out[t - 2].start()
+            for m in to_y.get(t - 2, []) + to_out.get(t - 2, []):
+                m.start()
 
     @pl.when(i == 0)
     def _():
-        for c in loads:
-            c.start()
+        load_gu.start()
         later[...] = jnp.zeros_like(later)
         from_later[...] = jnp.zeros_like(from_later)
         greet_all(
-            [neighbour_x(), neighbour_y()]
+            [neighbour_x(), neighbour_y(), neighbour_core()]
             + [{"seq": lax.rem(seq + n, count + 1)} for n in range(1, count + 1)]
         )
+        load_gu.wait()
+        for n in range(3):
+            total.begin(n)
         for c in loads:
-            c.wait()
-        total.begin(0)
-        total.begin(1)
+            c.start()
+        for m in early_y:
+            m.start()
         for r in range(0, rows, step):
             at = slice(r, r + step)
             for j in (0, 1):
                 k, p = pair_up(errs[2 * j][at, :].astype(F32), errs[2 * j + 1][at, :].astype(F32))
                 paired[at, j * width : (j + 1) * width] = k.astype(BF)
                 paired[at, (j + 2) * width : (j + 3) * width] = p.astype(BF)
+
+    @pl.when(i == 3)
+    def _():
+        core_out.wait_recv()
+        plus_in(s_out, c_out)
+
+    @pl.when(i == 2 * heads + 1)
+    def _():
+        core_gt.wait_recv()
+        put_in(s_gt, p_gt)
+        plus_in(s_gt, c_gt)
+
+    for t in range(len(pieces) + 2):
+
+        @pl.when(i == (2 * t + 2 if t <= heads else t + heads + 3))
+        def _():
+            tick(t)
+
+    @pl.when(i == 1)
+    def _():
+        g = dot_tn(mixed[...], paired[...])
+        p_out[...] = g[:, 2 * width :].astype(BF)
+        core_out.start()
+        s_out[...] = g[:, : 2 * width].astype(BF)
 
     @pl.when(i < heads)
     def _():
@@ -1550,8 +1709,8 @@
                     term = jnp.where(o >= k, term, 0.0)
                 sums[k] = plus(sums[k], jnp.sum(term, axis=0, keepdims=True))
             sums[KW] = plus(sums[KW], jnp.sum(rec * d_ell, axis=0, keepdims=True))
-        grad_recall[0] = gr
-        grad_admit[0] = ga
+        for n, value in enumerate((gr, ga)):
+            p_gt[pl.ds(pl.multiple_of(n * size + h * 128, 128), 128), :] = value.astype(BF)
         for k in range(KW + 1):
             grad_small[k : k + 1, :] = sums[k]
         grad_small[KW + 1 : 8, :] = jnp.zeros((7 - KW, 128), F32)
@@ -1572,11 +1731,21 @@
     def _():
         hand_edge.start()
 
+    @pl.when(i == 2 * heads - 1)
+    def _():
+        core_gt.start()
+
+
     @pl.when((i == 2 * heads) & (seq < count))
     def _():
         hand_edge.wait_recv()
 
     third = 2 * heads
+
+    @pl.when(i == third)
+    def _():
+        for c in loads:
+            c.wait()
 
     @pl.when((i >= third) & (i < third + blocks))
     def _():
@@ -1621,22 +1790,9 @@
     def finish(start, first):
         scatter[first].wait_recv()
         scatter[first + 1].wait_recv()
-        sum_grad = None
-        for r in range(start, start + half, 128):
-            at = slice(r, r + 128)
-            d = q0[at, :] + rx[at, :].astype(F32) + ry[at, :].astype(F32)
-            s, m = scale[at, :], x[at, :]
-            t = as_column(dots_x[:, at] + dots_y[:, at], width)
-            grad[at, :] = dx[at, :] + s * gain[0:1, :width] * d - m * (s * s) * t * (1.0 / D)
-            term = jnp.sum(d * m * s, axis=0, keepdims=True)
-            sum_grad = term if sum_grad is None else sum_grad + term
-        return sum_grad
-
-    for t in range(len(pieces) + 2):
-
-        @pl.when(i == t + 1)
-        def _():
-            tick(t)
+        return norm_back_rows(
+            start, half, q0, rx, ry, dots_x, dots_y, scale, x, gain[0:1, :width], dx, grad, None
+        )
 
     @pl.when(i == last + 1)
     def _():
@@ -1656,23 +1812,26 @@
         def _():
             hand_edge.wait_send()
 
-        for m in to_y.values():
+
+    @pl.when(i == pl.num_programs(0) - 1)
+    def _():
+        sent_y = [m for group in to_y.values() for m in group] + early_y
+        for m in sent_y:
             m.wait_recv()
-        for m in scatter + [small_x, small_y] + list(to_y.values()):
+        for m in scatter + [small_x, small_y, core_out, core_gt] + sent_y:
             m.wait_send()
-        for c in to_out.values():
+        for c in stores:
             c.wait()
 
 
-def back(errs, w_out, states, v, recall, conv, admit, u, off, soft, taps, rw, aw, border, earlier, w, scale, x, dx, gain, sum_gu, sum_down):
+def back(errs, w_out, states, v, recall, conv, admit, u, off, soft, taps, rw, aw, border, earlier, w, scale, x, dx, gain, sum_gu, sum_down, mixed):
     rows, channels = states.shape
     width = x.shape[1]
     heads = channels // 128
     block = ROW_BLOCK
     blocks = rows // block
     count = earlier.shape[0]
-    steps = 2 * heads + blocks + 3
-    assert steps >= 15
+    steps = 2 * heads + blocks + 8
 
     def both(i):
         return jnp.where(i < heads, i, jnp.clip(i - heads, 0, heads - 1))
@@ -1696,10 +1855,12 @@
     own_gate = on(gate, second, 0)
     chunk = pltpu.VMEM((rows, width), BF)
     lanes = pltpu.VMEM((8, rows), F32)
-    gu, dn = pltpu.VMEM(sum_gu.shape, BF), pltpu.VMEM(sum_down.shape, BF)
+    gu = pltpu.VMEM(sum_gu.shape, BF)
+    pair, gate_sum = pltpu.VMEM((channels, 2 * width), BF), pltpu.VMEM((2 * channels, 128), BF)
     piece = pltpu.VMEM((heads, 8, 128), F32)
     half_gu, half_dn = (sum_gu.shape[0] // 2, sum_gu.shape[1]), (sum_down.shape[0], width)
-    count_sems = 8 + count + 1 + 24 + 6
+    half_out = (channels, width)
+    count_sems = 88
     return pl.pallas_call(
         functools.partial(back_body, heads, blocks, count),
         grid=(steps,),
@@ -1721,40 +1882,43 @@
             pl.BlockSpec((count, 1, 8, 128), lambda i: (0, second(i), 0, 0)),
             on((block, channels), third, 0),
             on((block, channels), third, 0),
-            whole_spec(w.shape),
+            any_spec(),
             whole_spec(scale.shape),
-            whole_spec(x.shape),
-            whole_spec(dx.shape),
+            any_spec(),
+            any_spec(),
             whole_spec(gain.shape),
             any_spec(),
             any_spec(),
+            whole_spec(mixed.shape),
         ],
         out_specs=[
             whole_spec((rows, channels)),
-            whole_spec((rows, 4 * width)),
             on((block, channels), third, 0),
             whole_spec((rows, width)),
             whole_spec((8, width)),
-            on(gate, second, 0),
-            on(gate, second, 0),
             on((8, 128), second, 1),
         ]
-        + [any_spec()] * 4,
+        + [any_spec()] * 6,
         out_shape=[
             sds((rows, channels), BF),
-            sds((rows, 4 * width), BF),
             sds((rows, channels), BF),
             sds((rows, width), F32),
             sds((8, width), F32),
-            sds((heads, 128, 128), F32),
-            sds((heads, 128, 128), F32),
             sds((8, channels), F32),
             sds(half_gu, BF),
             sds(half_gu, BF),
             sds(half_dn, BF),
-            sds(half_dn, BF),
+            sds(half_out, BF),
+            sds(half_out, BF),
+            sds((4 * channels, 128), BF),
         ],
-        scratch_shapes=[pltpu.VMEM((heads, rows, 128), F32)] * 2
+        scratch_shapes=[
+            pltpu.VMEM(w.shape, BF),
+            pltpu.VMEM((rows, width), F32),
+            pltpu.VMEM((rows, width), F32),
+            pltpu.VMEM((rows, 4 * width), BF),
+        ]
+        + [pltpu.VMEM((heads, rows, 128), F32)] * 2
         + [
             pltpu.VMEM((rows + 8, 128), F32),
             pltpu.VMEM((rows + 8, 128), F32),
@@ -1764,21 +1928,22 @@
             pltpu.VMEM((count, heads, 8, 128), F32),
             piece,
             piece,
-            pltpu.SemaphoreType.DMA((2,)),
+            pltpu.SemaphoreType.DMA((4,)),
             pltpu.VMEM((rows, width), F32),
         ]
         + [chunk] * 6
         + [lanes] * 3
         + [gu] * 3
-        + [dn] * 3
-        + [pltpu.SemaphoreType.DMA((6,))]
+        + [pair] * 5
+        + [gate_sum] * 5
+        + [pltpu.SemaphoreType.DMA((12,))]
         + [pltpu.SemaphoreType.DMA((count_sems,))] * 2,
         compiler_params=comm_params(4),
         cost_estimate=cost(64 * rows * w.size, rows * channels * 60, rows * channels * 8),
         name="back",
     )(
         *errs, w_out, states, v, recall, conv, admit, u, off, soft, taps, rw, aw, border, earlier,
-        u, v, w, scale, x, dx, gain, sum_gu, sum_down,
+        u, v, w, scale, x, dx, gain, sum_gu, sum_down, mixed,
     )
 
 
@@ -1786,21 +1951,19 @@
 
 
 def tail_body(*refs):
-    (mixed, er, n1, eu, ev, grad_recall, grad_admit, grad_small, grad_mixer, grad_feed) = refs[:10]
-    (p0, p1, p2, p3, mid, grad_chunk) = refs[10:16]
-    (mine_in, far_in, mine_out, far_out, gates, tiny_out, out, grad) = refs[16:24]
-    (n1_v, eu_v, ev_v, s_in, p_in, c_in, a_in, b_in, y_in, s_out, p_out, c_out, a_out, b_out, y_out) = refs[24:39]
-    (s_gt, p_gt, c_gt, a_gt, b_gt, y_gt, s_ty, p_ty, c_ty, a_ty, b_ty) = refs[39:50]
-    (q1, q2, q3, r3, rx, ry, own_a, other_a, own_b, other_b, load, send, recv) = refs[50:]
+    (n1, eu, ev, grad_small, grad_mixer, grad_feed) = refs[:6]
+    (p0, p1, p2, p3, mid, grad_chunk) = refs[6:12]
+    (mine_in, far_in, tiny_out, out, grad) = refs[12:17]
+    (s_in, p_in, c_in, a_in, b_in, s_ty, p_ty, c_ty, a_ty, b_ty) = refs[17:27]
+    (q0, md, gc, q1, q2, q3, r3, rx, ry, own_a, other_a, own_b, other_b, load, send, recv) = refs[27:]
     made = Messages((send, recv))
     col = lax.axis_index("col")
-    y, core = lax.div(col, 2), lax.rem(col, 2)
+    core = lax.rem(col, 2)
     to_core, to_y = neighbour_core(), neighbour_y()
     rows, width = p0.shape
     part = width // 2
     half_tokens = rows // 2
     channels = eu.shape[1]
-    heads = grad_recall.shape[0]
     copies = []
 
     def copy(src, dst):
@@ -1808,44 +1971,27 @@
         return copies[-1]
 
     outs_in = [copy(p3, q3), copy(p1, q1), copy(p2, q2)]
-    late = [copy(n1, n1_v), copy(eu, eu_v), copy(ev, ev_v)]
+    late = [copy(p0, q0), copy(mid, md), copy(grad_chunk, gc)]
     scatter = made.block(scatter_messages, q1, q2, q3, r3, rx, ry)
-    half = width // 2
-    a, b = pl.ds(0, half), pl.ds(half, half)
-    c, d = pl.ds(2 * half, half), pl.ds(3 * half, half)
-    inner = s_out.shape[0] // 2
-    up, low = pl.ds(0, inner), pl.ds(inner, inner)
-    lanes_far, lanes_own = pl.ds(width, width), pl.ds(0, width)
-    group_in, group_out = (s_in, a_in, b_in), (s_out, a_out, b_out)
-    pieces = [[s_ty, a_ty, b_ty], [s_gt, a_gt, b_gt]]
-    pieces += [[r.at[at, lanes_far] for r in group_out] for at in (up, low)]
-    pieces += [[r.at[at, lanes_own] for r in group_out] for at in (up, low)]
-    pieces += [[r.at[at, :] for r in group_in] for at in (c, d, a, b)]
+    cut = width // 4
+    order = [pl.ds(n * cut, cut) for n in (4, 5, 6, 7, 0, 1, 2, 3)]
+    pieces = [[s_ty, a_ty, b_ty]] + [[r.at[at, :] for r in (s_in, a_in, b_in)] for at in order]
     count = len(pieces)
     total = SeqSum(pieces, (send, recv), made.used)
     made.used += 2 * count
-    core_ty, core_gt = made.new(p_ty, c_ty, to_core), made.new(p_gt, c_gt, to_core)
-    core_out = made.new(p_out, c_out, to_core)
-    core_in = [made.new(p_in.at[at, :], c_in.at[at, :], to_core) for at in (c, d, a, b)]
+    core_ty = made.new(p_ty, c_ty, to_core)
+    far_rows, own_rows = pl.ds(width, width), pl.ds(0, width)
+    core_in = [made.new(p_in.at[at, :], c_in.at[at, :], to_core) for at in (far_rows, own_rows)]
     over_y = {
-        1: made.new(s_gt, y_gt, to_y),
-        2: made.new(s_out.at[up, lanes_far], y_out.at[up, :], to_y),
-        3: made.new(s_out.at[low, lanes_far], y_out.at[low, :], to_y),
-        6: made.new(s_in.at[c, :], y_in.at[a, :], to_y),
-        7: made.new(s_in.at[d, :], y_in.at[b, :], to_y),
+        n + 1: made.new(s_in.at[order[n], :], far_in.at[pl.ds(n * cut, cut), :], to_y) for n in range(4)
     }
     send_out, send_grad = made.new(other_a, out.at[core], to_core), made.new(other_b, grad.at[core], to_core)
     keep_out, keep_grad = copy(own_a, out.at[core]), copy(own_b, grad.at[core])
-
-    for m in outs_in + late:
+    keep_in = {n + 1: copy(s_in.at[order[n], :], mine_in.at[pl.ds((n - 4) * cut, cut), :]) for n in range(4, 8)}
+
+    for m in outs_in:
         m.start()
     greet_all((neighbour_x(), to_y, to_core, neighbour_end(), neighbour_middle()))
-
-    for n, source in enumerate((grad_recall, grad_admit)):
-        for h in range(heads):
-            at = slice((n * heads + h) * 128, (n * heads + h + 1) * 128)
-            p_gt[at, :] = source[h].astype(BF)
-    core_gt.start()
     p_ty[...] = jnp.zeros_like(p_ty)
     p_ty[0:8, :] = grad_small[...]
     for n, source in enumerate((grad_mixer, grad_feed)):
@@ -1853,77 +1999,71 @@
         g = jnp.where(core == 0, g, pltpu.roll(g, part, 1))
         p_ty[8 + n : 9 + n, 0:width] = g[0:1, :]
     core_ty.start()
+
+    def tile(n, target, row):
+        sub = width // 3
+
+        def one(k, carry):
+            at = pl.ds(pl.multiple_of(n * width + k * sub, sub), sub)
+            where = pl.ds(pl.multiple_of(row + k * sub, sub), sub)
+            left = n1[:, at]
+            target[where, :channels] = dot_tn(left, eu[...]).astype(BF)
+            target[where, channels:] = dot_tn(left, ev[...]).astype(BF)
+            return carry
+
+        lax.fori_loop(0, 3, one, 0)
+
+    def gather_core(n, at):
+        core_in[n].wait_recv()
+        plus_in(s_in.at[at, :], c_in.at[at, :])
+
+    tile(3, p_in, width)
+    core_in[0].start()
     for m in outs_in:
         m.wait()
-    scatter[0].start()
-    scatter[1].start()
-    scatter[2].start()
-    g = dot_tn(mixed[...], er[...])
-    p_out[...] = g[:, 2 * width :].astype(BF)
-    core_out.start()
-    s_out[...] = g[:, : 2 * width].astype(BF)
+    for m in late:
+        m.start()
+    for m in scatter[:3]:
+        m.start()
+    tile(1, s_in, width)
     core_ty.wait_recv()
     s_ty[...] = p_ty[...] + c_ty[...]
     total.begin(0)
-    core_gt.wait_recv()
-    put_in(s_gt, p_gt)
-    plus_in(s_gt, c_gt)
-    total.begin(1)
-
-    def tile(n, target, row):
-        at = slice(n * width, (n + 1) * width)
-        where = slice(row, row + width)
-        target[where, :channels] = dot_tn(n1_v[:, at], eu_v[...]).astype(BF)
-        target[where, channels:] = dot_tn(n1_v[:, at], ev_v[...]).astype(BF)
-
-    core_out.wait_recv()
-    plus_in(s_out, c_out)
-    for n in range(2, 6):
+    gather_core(0, far_rows)
+    for n in range(1, 5):
         total.begin(n)
-    for m in late:
-        m.wait()
-    tile(3, p_in, width)
-    core_in[0].start()
+    tile(2, p_in, 0)
     core_in[1].start()
-    tile(1, s_in, width)
     total.relay(0)
     total.relay(1)
     total.settle(0)
-    core_in[0].wait_recv()
-    core_in[1].wait_recv()
-    plus_in(s_in.at[pl.ds(width, width), :], c_in.at[pl.ds(width, width), :])
-    total.begin(6)
-    total.begin(7)
-    total.relay(2)
-    total.settle(1)
-    total.finish(0)
-    tile(2, p_in, 0)
-    core_in[2].start()
-    core_in[3].start()
-    total.relay(3)
-    total.settle(2)
-    total.finish(1)
-    over_y[1].start()
     tile(0, s_in, 0)
-    core_in[2].wait_recv()
-    core_in[3].wait_recv()
-    plus_in(s_in.at[pl.ds(0, width), :], c_in.at[pl.ds(0, width), :])
-    total.begin(8)
-    total.begin(9)
+    gather_core(1, own_rows)
+    for n in range(5, count):
+        total.begin(n)
 
     def chunk_out(value, own, other, at):
         own[at, :] = value[:, :part]
         other[at, :] = pltpu.roll(value, part, 1)[:, :part]
 
+    def in_steps(start, size, body):
+        def one(n, carry):
+            body(pl.ds(pl.multiple_of(start + n * 128, 128), 128))
+            return carry
+
+        lax.fori_loop(0, size // 128, one, 0)
+
     def finish_out(start, first):
         scatter[first].wait_recv()
         scatter[first + 1].wait_recv()
-        for r in range(start, start + half_tokens, 128):
-            at = slice(r, r + 128)
-            value = p0[at, :] + rx[at, :].astype(F32) + ry[at, :].astype(F32) + mid[at, :]
+
+        def body(at):
+            value = q0[at, :] + rx[at, :].astype(F32) + ry[at, :].astype(F32) + md[at, :]
             chunk_out(value, own_a, other_a, at)
 
-    for n in range(4, count + 2):
+        in_steps(start, half_tokens, body)
+
+    for n in range(2, count + 2):
         if n < count:
             total.relay(n)
         if n - 1 < count:
@@ -1931,93 +2071,67 @@
         total.finish(n - 2)
         if n - 2 in over_y:
             over_y[n - 2].start()
-        if n == 4:
+        if n - 2 in keep_in:
+            keep_in[n - 2].start()
+        if n == 2:
             scatter[0].wait_recv()
             add_into(q2, r3, 0, half_tokens)
             scatter[3].start()
             scatter[4].start()
-        if n == 5:
+        if n == 3:
             scatter[1].wait_recv()
             add_into(q1, r3, half_tokens, half_tokens)
             scatter[5].start()
-            for r in range(0, rows, 128):
-                at = slice(r, r + 128)
-                chunk_out(grad_chunk[at, :], own_b, other_b, at)
+            for m in late:
+                m.wait()
+            in_steps(0, rows, lambda at: chunk_out(gc[at, :], own_b, other_b, at))
             send_grad.start()
             keep_grad.start()
+        if n == 7:
+            finish_out(0, 2)
         if n == 8:
-            finish_out(0, 2)
-        if n == 9:
             finish_out(half_tokens, 4)
             send_out.start()
             keep_out.start()
     put_in(tiny_out, s_ty)
-    put_in(mine_in, s_in.at[pl.ds(0, width), :])
-    put_in(mine_out, s_out.at[:, lanes_own])
-    over_y[1].wait_recv()
-    for n in (0, 1):
-        for h in range(heads):
-            at = slice((n * heads + h) * 128, (n * heads + h + 1) * 128)
-            gates[n, y * heads + h] = s_gt[at, :].astype(F32)
-            gates[n, (1 - y) * heads + h] = y_gt[at, :].astype(F32)
-    for n in (2, 3, 6, 7):
-        over_y[n].wait_recv()
-    put_in(far_out, y_out)
-    put_in(far_in, y_in)
-    for m in (send_out, send_grad):
+    received = list(over_y.values()) + [send_out, send_grad]
+    for m in received:
         m.wait_recv()
-    for m in [core_ty, core_gt, core_out, send_out, send_grad] + core_in + list(over_y.values()) + scatter:
+    for m in [core_ty] + core_in + received + scatter:
         m.wait_send()
-    keep_out.wait()
-    keep_grad.wait()
-
-
-def tail(mixed, er, n1, eu, ev, grad_recall, grad_admit, grad_small, grad_mixer, grad_feed, parts, mid, grad_chunk):
+    for c in [keep_out, keep_grad] + list(keep_in.values()):
+        c.wait()
+
+
+def tail(n1, eu, ev, grad_small, grad_mixer, grad_feed, parts, mid, grad_chunk):
     rows, channels = eu.shape
     width = mid.shape[1]
     part = width // 2
-    heads = grad_recall.shape[0]
-    inner = mixed.shape[1]
     big = pltpu.VMEM((2 * width, 2 * channels), BF)
-    tall = pltpu.VMEM((inner, 2 * width), BF)
-    gate = pltpu.VMEM((2 * heads * 128, 128), BF)
     tiny = pltpu.VMEM((16, channels), F32)
     piece = pltpu.VMEM((rows, width), BF)
+    full = pltpu.VMEM((rows, width), F32)
     side = pltpu.VMEM((rows, part), F32)
-    quarter_in, quarter_out = (width, 2 * channels), (inner, width)
+    quarter_in = (width, 2 * channels)
     final = sds((2, rows, part), F32)
     return pl.pallas_call(
         tail_body,
-        in_specs=[pl.BlockSpec(memory_space=pltpu.VMEM)] * 2
-        + [any_spec()] * 3
-        + [pl.BlockSpec(memory_space=pltpu.VMEM)] * 6
-        + [any_spec()] * 3
-        + [pl.BlockSpec(memory_space=pltpu.VMEM)] * 2,
-        out_specs=[pl.BlockSpec(memory_space=pltpu.VMEM)] * 6 + [any_spec()] * 2,
-        out_shape=[sds(quarter_in, BF)] * 2
-        + [sds(quarter_out, BF)] * 2
-        + [sds((2, 2 * heads, 128, 128), F32), sds((16, channels), F32), final, final],
-        scratch_shapes=[
-            pltpu.VMEM((rows, 4 * width), BF),
-            pltpu.VMEM((rows, channels), BF),
-            pltpu.VMEM((rows, channels), BF),
-        ]
-        + [big] * 5
-        + [pltpu.VMEM(quarter_in, BF)]
-        + [tall] * 5
-        + [pltpu.VMEM(quarter_out, BF)]
-        + [gate] * 6
+        in_specs=[pl.BlockSpec(memory_space=pltpu.VMEM)] * 6 + [any_spec()] * 6,
+        out_specs=[any_spec()] * 2 + [pl.BlockSpec(memory_space=pltpu.VMEM)] + [any_spec()] * 2,
+        out_shape=[sds(quarter_in, BF)] * 2 + [sds((16, channels), F32), final, final],
+        scratch_shapes=[big] * 5
         + [tiny] * 5
+        + [full] * 3
         + [piece] * 6
         + [side] * 4
-        + [pltpu.SemaphoreType.DMA((8,))]
+        + [pltpu.SemaphoreType.DMA((12,))]
         + [pltpu.SemaphoreType.DMA((TAIL_MESSAGES,))] * 2,
         compiler_params=pltpu.CompilerParams(
             vmem_limit_bytes=VMEM_LIMIT, collective_id=6, has_side_effects=True
         ),
-        cost_estimate=cost(60 * rows * width * channels * 4, nbytes(n1, eu, ev, mixed, er)),
+        cost_estimate=cost(60 * rows * width * channels * 4, nbytes(n1, eu, ev)),
         name="tail",
-    )(mixed, er, n1, eu, ev, grad_recall, grad_admit, grad_small, grad_mixer, grad_feed, *parts, mid, grad_chunk)
+    )(n1, eu, ev, grad_small, grad_mixer, grad_feed, *parts, mid, grad_chunk)
 
 
 def arrange_body(place, mine_gu, far_gu, mine_dn, far_dn, mine_in, far_in, mine_out, far_out, *outs):
@@ -2044,7 +2158,7 @@
 
 
 def arrange(place, mine_gu, far_gu, mine_dn, far_dn, mine_in, far_in, mine_out, far_out):
-    width, units = mine_dn.shape[1], mine_dn.shape[0]
+    width, units = far_dn.shape[1], far_dn.shape[0]
     inner = mine_out.shape[0]
     lanes_gu, lanes_in = mine_gu.shape[1], mine_in.shape[1]
     quarter = width // 4
@@ -2135,31 +2249,30 @@
 
     (
         x, g, g_low, w_out, w_down, gains_all, small, s1, u, v, border, earlier, mid, mid_low,
-        n1, conv, recall, admit, states, mixed, ex, ey, ed, mx, my, md, far_w, sib_own, sib_far, w_in,
+        n1, conv, recall, admit, states, mixed, mx, my, md, far_w, sib_own, sib_far, w_in,
     ) = front(
         stream_in, cotangent, input_weight, branch_weight, output_weight, gate_weight, up_weight, down_weight,
         gains, small, recall_gate, admit_gate, off, count - 1,
     )
     taps, soft, decay = small[:KW], small[KW : KW + 1], small[KW + 1 : KW + 2]
     p0, p1, p2, p3, dx2, *dx_all, grad_feed, sum_down, sum_gu = feed(
-        (mid_low, mx, my, md), (g_low, ex, ey, ed), mid, g, gains_all, w_down,
+        (mid_low, mx, my, md), g_low, mid, g, gains_all, w_down,
         (gate_weight, up_weight, sib_own, far_w, sib_far),
     )
     (
-        ev, er, eu, grad_chunk, grad_mixer, grad_recall, grad_admit, grad_small, mine_gu, far_gu, mine_down, far_down
+        ev, eu, grad_chunk, grad_mixer, grad_small, mine_gu, far_gu, far_down, mine_out, far_out, gates
     ) = back(
         dx_all, w_out, states, v, recall, conv, admit, u, off, soft, taps, rw, aw, border, earlier,
-        w_in, s1, x, dx2, gains_all, sum_gu, sum_down,
+        w_in, s1, x, dx2, gains_all, sum_gu, sum_down, mixed,
     )
-
-    mine_in, far_in, mine_out, far_out, gates, tiny, out, grad = tail(
-        mixed, er, n1, eu, ev, grad_recall, grad_admit, grad_small, grad_mixer, grad_feed,
-        (p0, p1, p2, p3), mid, grad_chunk,
+    mine_in, far_in, tiny, out, grad = tail(
+        n1, eu, ev, grad_small, grad_mixer, grad_feed, (p0, p1, p2, p3), mid, grad_chunk
     )
     place = jnp.stack([row, y]).astype(jnp.int32)
     grad_gate, grad_up, grad_down, grad_input, grad_branch, grad_output = arrange(
-        place, mine_gu, far_gu, mine_down, far_down, mine_in, far_in, mine_out, far_out
+        place, mine_gu, far_gu, sum_down, far_down, mine_in, far_in, mine_out, far_out
     )
+    gates = gates.astype(F32).reshape((2,) + recall_gate.shape)
     own = taps.shape[1] // 2
     mine = lax.dynamic_slice_in_dim(tiny[:8], core * own, own, 1)
     gain_grads = lax.dynamic_slice_in_dim(tiny[8:10, : 2 * part], core * part, part, 1)

time: 554 us -> 520 us (0.939); the launches traced: 548 us -> 520 us
  Pallas kernels: 528 us -> 500 us
    pallas_call x1, Pallas kernels: 118 us -> 148 us  [feed(): pl.pallas_call(functools.partial(feed_body, blocks), grid=(2 * blocks + t...]
    pallas_call x1, Pallas kernels: 88.1 us -> 59.5 us  [tail(): pl.pallas_call(tail_body, in_specs=[pl.BlockSpec(memory_space=pltpu.VMEM)...]
    pallas_call x1, Pallas kernels: 156 us -> 134 us  [back(): pl.pallas_call(functools.partial(back_body, heads, blocks, count), grid=(...]
    pallas_call x1, Pallas kernels: 156 us -> 149 us  [front(): pl.pallas_call(functools.partial(front_body, heads, blocks, count), grid=...]
where the time goes in v5:
time: 520 us
  Pallas kernels  500 us (96%)
  local copies, waits for them, and re-layouts  15.6 us (3%)
    pallas_call x1, Pallas kernels, front(): pl.pallas_call(functools.partial(front_body, heads, blocks, count), grid=...  149 us
    pallas_call x1, Pallas kernels, feed(): pl.pallas_call(functools.partial(feed_body, blocks), grid=(2 * blocks + t...  148 us
    pallas_call x1, Pallas kernels, back(): pl.pallas_call(functools.partial(back_body, heads, blocks, count), grid=(...  134 us
    pallas_call x1, Pallas kernels, tail(): pl.pallas_call(tail_body, in_specs=[pl.BlockSpec(memory_space=pltpu.VMEM)...  59.5 us

profile of v5, /device:TPU:0, one launch (start us, length us, event | category | flops | bytes accessed | tf_op | source)
XLA Modules:
  0.0 519.6 jit_solution(13219138795224510097)
XLA Ops:
  0.7 0.7 constant_dynamic-slice_fusion.4
  1.4 0.2 reduce-window_clone.1
  1.5 0.7 subtract_bitcast_fusion
  2.2 0.1 select_reduce_fusion
  2.3 0.1 concatenate.11
  2.4 1.0 broadcast_in_dim.42.refs_12_.refs_11_
  3.4 0.0 copy-start.2
  3.4 2.9 copy.39.refs_0_
  6.3 0.0 copy-done.2
  6.3 0.0 copy-start.6
  6.3 0.0 copy-start.9
  6.3 0.0 copy-start.10
  6.4 0.0 copy-start.11
  6.4 1.8 copy.40.refs_1_
  8.2 0.0 copy-done.6
  8.2 0.1 pad.5.clone
  8.3 0.0 copy-done.9
  8.3 0.7 maximum_maximum_fusion.1.refs_9_
  8.9 0.1 pad.8.clone
  9.0 0.0 copy-done.10
  9.0 0.0 copy-done.11
  9.0 0.7 maximum_maximum_fusion.refs_8_
  9.7 148.8 %front.1 = (f32[1024,384]{1,0:T(8,128)}, f32[1024,384]{1,0:T(8,128)}, bf16[1024,384]{1,0:T(8,128)(2,1)}, bf16[512,1536]{1,0:T(8,128)(2,1)}, bf16[1152,1536]{1,0:...) custom-call(f32[2,1024,192]{2,1,0:T(8,128)} %copy.39.refs_0_, ...), custom_call_target="tpu_custom_call" | custom-call | flops 80530636800 | bytes 40960000 | tf_op jit(solution)/shard_map/front/pallas_call | solution.py:1110
  158.5 0.0 copy-start.8
  158.5 0.0 copy-start.3
  158.5 0.0 copy-start.4
  158.5 147.8 %feed.1 = (f32[1024,384]{1,0:T(8,128)}, bf16[1024,384]{1,0:T(8,128)(2,1)}, bf16[1024,384]{1,0:T(8,128)(2,1)}, bf16[1024,384]{1,0:T(8,128)(2,1)}, f32[1024,384]{1...) custom-call(bf16[1024,384]{1,0:T(8,128)(2,1)} %get-tuple-element.76., ...), custom_call_target="tpu_custom_call" | custom-call | flops 86973087744 | bytes 41336832 | tf_op jit(solution)/shard_map/feed/pallas_call | solution.py:1426
  306.3 0.0 copy-done.8
  306.3 0.6 slice.33.refs_13_
  306.9 0.6 slice.32.refs_12_
  307.5 0.0 copy-done.3
  307.5 0.0 copy-done.4
  307.5 0.8 constant_dynamic-slice_fusion.2
  308.4 133.7 %back.1 = (bf16[1024,512]{1,0:T(8,128)(2,1)}, bf16[1024,512]{1,0:T(8,128)(2,1)}, f32[1024,384]{1,0:T(8,128)}, f32[8,384]{1,0:T(8,128)}, f32[8,512]{1,0:T(8,128)}...) custom-call(bf16[1024,384]{1,0:T(8,128)(2,1)} %get-tuple-element.88., ...), custom_call_target="tpu_custom_call" | custom-call | flops 103079215104 | bytes 31457280 | tf_op jit(solution)/shard_map/back/pallas_call | solution.py:1864
  442.0 59.5 %tail.1 = (bf16[384,1024]{1,0:T(8,128)(2,1)}, bf16[384,1024]{1,0:T(8,128)(2,1)}, f32[16,512]{1,0:T(8,128)}, f32[2,1024,192]{2,1,0:T(8,128)}, f32[2,1024,192]{2,1,0:T(8,128)}) custom-call(bf16[1024,1536]{1,0:T(8,128)(2,1)} %get-tuple-element.75.refs_0_, bf16[1024,512]{1,0:T(8,128)(2,1)} %get-tuple-element.109.refs_1_, ...), custom_call_target="tpu_custom_call" | custom-call | flops 48318382080 | bytes 5242880 | tf_op jit(solution)/shard_map/tail/pallas_call | solution.py:2117
  501.6 0.6 pad_add_fusion.place
  502.1 9.9 %arrange.1 = (f32[384,2304]{1,0:T(8,128)}, f32[384,2304]{1,0:T(8,128)}, f32[2304,384]{1,0:T(8,128)}, f32[384,1024]{1,0:T(8,128)}, f32[384,1024]{1,0:T(8,128)}, /*index=5*/f32[1024,384]{1,0:T(8,128)}) custom-call(s32[2]{0:T(128)} %pad_add_fusion.place, bf16[384,2304]{1,0:T(8,128)(2,1)} %get-tuple-element.122.mine_gu, ...), custom_call_target="tpu_custom_call" | custom-call | flops 1000000 | bytes 24000000 | tf_op jit(solution)/shard_map/arrange/pallas_call | solution.py:2185
  512.0 0.0 copy-start
  512.0 2.9 copy.43
  515.0 0.0 copy-done
  515.0 0.0 copy-start.5
  515.0 0.0 copy-start.7
  515.0 0.0 copy-start.1
  515.0 1.7 copy.44
  516.7 0.0 copy-done.5
  516.7 0.6 constant_dynamic-slice_fusion
  517.3 0.1 dynamic-slice_multiply_fusion
  517.3 0.0 copy-done.7
  517.3 0.6 divide_multiply_fusion
  517.9 0.6 fusion.2
  518.6 0.0 copy-done.1
  518.6 1.0 fusion.1
  (8 shorter events, 0.0 us)
Async XLA Ops:
  3.4 2.9 copy-start.2
  6.3 1.8 copy-start.6
  6.3 1.9 copy-start.9
  6.3 2.7 copy-start.10
  6.4 2.7 copy-start.11
  158.5 147.9 %copy-start.8 = (f32[8,512]{1,0:T(8,128)S(1)}, f32[8,512]{1,0:T(8,128)}, u32[]{:S(2)}) copy-start(f32[8,512]{1,0:T(8,128)} %get-tuple-element.99) | copy-start | bytes 49156
  158.5 149.0 %copy-start.3 = (f32[8,128,128]{2,1,0:T(8,128)S(1)}, f32[8,128,128]{2,1,0:T(8,128)}, u32[]{:S(2)}) copy-start(f32[8,128,128]{2,1,0:T(8,128)} %refs_10_.2) | copy-start | bytes 1572868
  158.5 149.0 %copy-start.4 = (f32[8,128,128]{2,1,0:T(8,128)S(1)}, f32[8,128,128]{2,1,0:T(8,128)}, u32[]{:S(2)}) copy-start(f32[8,128,128]{2,1,0:T(8,128)} %refs_11_.1) | copy-start | bytes 1572868
  512.0 2.9 copy-start
  515.0 1.7 copy-start.5
  515.0 2.4 copy-start.7
  515.0 3.6 copy-start.1

commit v6 on v5

--- a/solution.py
+++ b/solution.py
@@ -689,12 +689,12 @@
 def front_body(heads, blocks, count, *refs):
     (stream, cot, in_w, br_w, out_w, gate_w, up_w, down_w) = refs[:8]
     (gains_in, small_in, recall_gate, admit_gate, off) = refs[8:13]
-    (x, g, e_own, w_out, w_down, gains_out, small, s1, u, v, border_out, earlier_out, mid, own) = refs[13:27]
-    (n1, conv, recall, admit, states, mixed) = refs[27:33]
-    (mx, my, md, far_gu, sib_own, sib_far, w_in_out) = refs[33:40]
+    (e_own, w_down, gains_out, small, s1, border_out, earlier_out, mid, own) = refs[13:22]
+    (n1, conv, recall, admit, states, mixed) = refs[22:28]
+    (mx, my, md, far_gu, sib_own, sib_far, w_in_out, x_out, g_out, w_out_out, u_out, v_out) = refs[28:40]
     (x_own, x_recv, g_own, g_recv, gains_recv, small_recv, own_low, gx, gy, gd) = refs[40:50]
-    (w_in, gains, border, earlier) = refs[50:54]
-    (wo, wd, local, cum, ext, ends, q0, q1, q2, q3, r3, rx, ry, load, send, recv) = refs[54:]
+    (w_in, gains, border, earlier, x, g, w_out, u, v) = refs[50:59]
+    (wo, wd, local, cum, ext, ends, q0, q1, q2, q3, r3, rx, ry, load, send, recv) = refs[59:]
     i = pl.program_id(0)
     seq, row, col = lax.axis_index("seq"), lax.axis_index("row"), lax.axis_index("col")
     y = lax.div(col, 2)
@@ -774,6 +774,8 @@
     wd_own = copy(down_w.at[own_units, :], wd.at[0, 0])
     ahead = len(copies)
     w_in_store = copy(w_in, w_in_out)
+    x_store, g_store, w_out_store = copy(x, x_out), copy(g, g_out), copy(w_out, w_out_out)
+    u_store, v_store = copy(u, u_out), copy(v, v_out)
 
     gather_n = made.block(gather_messages_by_x, own_low, gx, gy, gd)
     scatter = made.block(scatter_messages, q1, q2, q3, r3, rx, ry)
@@ -786,7 +788,7 @@
 
         def one(n, carry):
             at = pl.ds(pl.multiple_of(n * step, step), step)
-            whole = jnp.concatenate([left[at, :], right[at, :]], axis=1)
+            whole = jnp.concatenate([left[:, at], right[:, at]], axis=0).T
             full[at, :] = whole
             low[at, :] = whole.astype(BF)
             return carry
@@ -807,6 +809,7 @@
         x_copy.wait()
         swap[0].wait_recv()
         put_together(x_own, x_recv, x, own_low)
+        x_store.start()
         for m in gather_n[:4]:
             m.start()
         for m in in_core:
@@ -852,6 +855,7 @@
         g_copy.wait()
         swap_g.wait_recv()
         put_together(g_own, g_recv, g, e_own)
+        g_store.start()
 
     @pl.when(i == blocks // 2)
     def _():
@@ -884,6 +888,11 @@
     @pl.when((i == blocks) & (seq > 0))
     def _():
         edge.wait_recv()
+
+    @pl.when(i == blocks)
+    def _():
+        u_store.start()
+        v_store.start()
 
     @pl.when(i == blocks - 1)
     def _():
@@ -967,6 +976,7 @@
         wo_core.wait_recv()
         wo_pass.wait_recv()
         columns_in_order(wo, w_out)
+        w_out_store.start()
 
     for n in range(1, count + 1):
 
@@ -1020,11 +1030,6 @@
         gains_out[...] = gains[...]
         border_out[...] = border[...]
         earlier_out[...] = earlier[...]
-        w_in_store.wait()
-        for m in ff_share:
-            m.wait_recv()
-        for m in ff_pass:
-            m.start()
         for base, first in ((0, 2), (half, 4)):
             scatter[first].wait_recv()
             scatter[first + 1].wait_recv()
@@ -1040,14 +1045,20 @@
             start = 0 if base == 0 else 2
             gather_m[start].start()
             gather_m[start + 1].start()
+        for m in ff_share:
+            m.wait_recv()
+        for m in ff_pass:
+            m.start()
+        gather_m[0].wait_recv()
+        gather_m[4].start()
+        gather_m[3].wait_recv()
+        gather_m[5].start()
         wd_own.wait()
         for m in ff_core + ff_pass:
             m.wait_recv()
         columns_in_order(wd, w_down)
-        gather_m[0].wait_recv()
-        gather_m[4].start()
-        gather_m[3].wait_recv()
-        gather_m[5].start()
+        for c in copies[ahead:]:
+            c.wait()
         for n in (1, 2, 4, 5):
             gather_m[n].wait_recv()
         sent = swap + [swap_g, gains_x, gains_y, gains_d] + in_far + in_core + in_pass
@@ -1067,7 +1078,7 @@
 
 
 def front(stream, cot, in_w, br_w, out_w, gate_w, up_w, down_w, gains, small, recall_gate, admit_gate, off, count):
-    rows, part = stream.shape[1:]
+    part, rows = stream.shape[1:]
     width = 2 * part
     channels = in_w.shape[1] // 2
     units = gate_w.shape[1] // 2
@@ -1087,16 +1098,11 @@
     chunk_low, chunk = sds((rows, width), BF), sds((rows, width), F32)
     wide = sds((rows, channels), F32)
     held = [
-        chunk,
-        chunk,
         chunk_low,
-        sds((channels, 4 * width), BF),
         sds((units, 4 * width), BF),
         sds((8, 4 * width), F32),
         sds((8, channels), F32),
         sds((rows, 1), F32),
-        wide,
-        wide,
         sds((8, channels), F32),
         sds((count, heads, 8, 128), F32),
         chunk,
@@ -1104,8 +1110,9 @@
     ]
     blocked = [sds((rows, 4 * width), BF), wide, wide, wide, wide, sds((rows, channels), BF)]
     away = [chunk_low] * 3 + [sds((width, 2 * units), BF)] * 3 + [sds((4 * width, 2 * channels), BF)]
+    away += [chunk, chunk, sds((channels, 4 * width), BF), wide, wide]
     piece = pltpu.VMEM((rows, width), BF)
-    side = pltpu.VMEM((rows, part), F32)
+    side = pltpu.VMEM((part, rows), F32)
     tall = pl.BlockSpec((rows, 128), head_at)
     return pl.pallas_call(
         functools.partial(front_body, heads, blocks, count),
@@ -1116,7 +1123,7 @@
         + [pl.BlockSpec((block, 4 * width), norm_at)]
         + [tall] * 3
         + [pl.BlockSpec((block, channels), mix_at)] * 2
-        + [any_spec()] * 7,
+        + [any_spec()] * len(away),
         out_shape=held + blocked + away,
         scratch_shapes=[side] * 4
         + [pltpu.VMEM(gains.shape, F32), pltpu.VMEM(small.shape, F32)]
@@ -1126,6 +1133,11 @@
             pltpu.VMEM((8, 4 * width), F32),
             pltpu.VMEM((8, channels), F32),
             pltpu.VMEM((count, heads, 8, 128), F32),
+            pltpu.VMEM((rows, width), F32),
+            pltpu.VMEM((rows, width), F32),
+            pltpu.VMEM((channels, 4 * width), BF),
+            pltpu.VMEM((rows, channels), F32),
+            pltpu.VMEM((rows, channels), F32),
             pltpu.VMEM((2, 2, channels, width), BF),
             pltpu.VMEM((2, 2, units, width), BF),
             pltpu.VMEM((heads, rows, 128), F32),
@@ -1135,7 +1147,7 @@
             pltpu.VMEM((rows, width), F32),
         ]
         + [piece] * 6
-        + [pltpu.SemaphoreType.DMA((9,))]
+        + [pltpu.SemaphoreType.DMA((14,))]
         + [pltpu.SemaphoreType.DMA((FRONT_MESSAGES,))] * 2,
         compiler_params=comm_params(1),
         cost_estimate=cost(200 * rows * in_w.size, rows * 40000),
@@ -1179,8 +1191,8 @@
         for lane in (width, 0)
         for n in range(2)
     ]
-    cut = 2 * width // 8
-    for n in range(FEED_CUTS // 2):
+    cut = width // 8
+    for n in range(FEED_CUTS):
         at = pl.ds(n * cut, cut)
         pieces.append([s_gu.at[pl.ds(width + n * cut, cut), :], a_gu.at[at, :], b_gu.at[at, :]])
     total = SeqSum(pieces, (send, recv), made.used)
@@ -1425,7 +1437,7 @@
     landing = pltpu.VMEM((units, 2 * width), BF)
     return pl.pallas_call(
         functools.partial(feed_body, blocks),
-        grid=(2 * blocks + tiles + 7 + FEED_CUTS // 2,),
+        grid=(2 * blocks + tiles + 7 + FEED_CUTS,),
         in_specs=[held(width)] * 4
         + [whole_spec(err_own.shape), whole_spec(mid.shape), any_spec(), whole_spec(gain.shape)]
         + [any_spec()] * 6,
@@ -1474,12 +1486,12 @@
     (w_out, states, branch, recall, conv, admit, u_head, off, soft) = refs[4:13]
     (taps, recall_w, admit_w, border, earlier, u, v, w_hbm, scale, x_hbm, dx_hbm, gain) = refs[13:25]
     (sum_gu, sum_down, mixed) = refs[25:28]
-    (ev, eu, grad, gain_grad, grad_small) = refs[28:33]
-    (mine_gu, far_gu, far_down, mine_out, far_out, gates) = refs[33:39]
-    (w, x, dx, paired, part, reach, ext, st, uext, dc, ends, later, edge, from_later, load) = refs[39:54]
-    (q0, q1, q2, q3, r3, rx, ry, dots, dots_x, dots_y) = refs[54:64]
-    (s_gu, a_gu, b_gu, s_out, p_out, c_out, a_out, b_out) = refs[64:72]
-    (s_gt, p_gt, c_gt, a_gt, b_gt, store, send, recv) = refs[72:]
+    (euv, grad, gain_grad, grad_small) = refs[28:32]
+    (mine_gu, far_gu, far_down, mine_out, far_out, gates) = refs[32:38]
+    (w, x, dx, paired, part, reach, ext, st, uext, dc, ends, later, edge, from_later, load) = refs[38:53]
+    (q0, q1, q2, q3, r3, rx, ry, dots, dots_x, dots_y) = refs[53:63]
+    (s_gu, a_gu, b_gu, s_out, p_out, c_out, a_out, b_out) = refs[63:71]
+    (s_gt, p_gt, c_gt, a_gt, b_gt, store, send, recv) = refs[71:]
     i = pl.program_id(0)
     sems = (send, recv)
     seq = lax.axis_index("seq")
@@ -1598,7 +1610,7 @@
 
     for t in range(len(pieces) + 2):
 
-        @pl.when(i == (2 * t + 2 if t <= heads else t + heads + 3))
+        @pl.when(i == (1 if t == 0 else 2 * t if t <= heads + 1 else t + heads + 2))
         def _():
             tick(t)
 
@@ -1613,7 +1625,7 @@
     def _():
         sp = soft[0:1, :]
         part_h, reach_h = part.at[i], reach.at[i]
-        lane = pl.ds(pl.multiple_of(i * 128, 128), 128)
+        lane = pl.ds(pl.multiple_of(channels + i * 128, 128), 128)
         for r in range(0, rows, step):
             at = slice(r, r + step)
             o = off[8 + r : 8 + r + step, :]
@@ -1623,7 +1635,7 @@
                 term = dot_nt(errs[j][at, :], w_out[:, j * width : (j + 1) * width])
                 dm = term if dm is None else dm + term
             act, slope = gelu_pair(branch[at, :])
-            ev[at, lane] = (dm * states[at, :] * slope).astype(BF)
+            euv[at, lane] = (dm * states[at, :] * slope).astype(BF)
             part_h[at, :] = dm * act
         ext[rows : rows + 8, :] = jnp.ones((8, 128), F32)
         for r in range(0, rows, step):
@@ -1755,8 +1767,8 @@
         extra = jnp.concatenate([jnp.zeros((block - 8, channels), F32), late], axis=0)
         d = d + jnp.where(i == third + blocks - 1, extra, 0.0)
         e = d.astype(BF)
-        eu[...] = e
-        b = ev[at, :]
+        euv[at, :channels] = e
+        b = euv[at, channels:]
         dots[:, at] = row_sums(e.astype(F32) * u[...] + b.astype(F32) * v[...])
         for j, q in ((3, q3), (1, q1), (2, q2), (0, q0)):
             rows_w = slice(j * width, (j + 1) * width)
@@ -1892,16 +1904,14 @@
             whole_spec(mixed.shape),
         ],
         out_specs=[
-            whole_spec((rows, channels)),
-            on((block, channels), third, 0),
+            whole_spec((rows, 2 * channels)),
             whole_spec((rows, width)),
             whole_spec((8, width)),
             on((8, 128), second, 1),
         ]
         + [any_spec()] * 6,
         out_shape=[
-            sds((rows, channels), BF),
-            sds((rows, channels), BF),
+            sds((rows, 2 * channels), BF),
             sds((rows, width), F32),
             sds((8, width), F32),
             sds((8, channels), F32),
@@ -1951,11 +1961,11 @@
 
 
 def tail_body(*refs):
-    (n1, eu, ev, grad_small, grad_mixer, grad_feed) = refs[:6]
-    (p0, p1, p2, p3, mid, grad_chunk) = refs[6:12]
-    (mine_in, far_in, tiny_out, out, grad) = refs[12:17]
-    (s_in, p_in, c_in, a_in, b_in, s_ty, p_ty, c_ty, a_ty, b_ty) = refs[17:27]
-    (q0, md, gc, q1, q2, q3, r3, rx, ry, own_a, other_a, own_b, other_b, load, send, recv) = refs[27:]
+    (n1, euv, grad_small, grad_mixer, grad_feed) = refs[:5]
+    (p0, p1, p2, p3, mid, grad_chunk) = refs[5:11]
+    (mine_in, far_in, tiny_out, out, grad) = refs[11:16]
+    (s_in, p_in, c_in, a_in, b_in, s_ty, p_ty, c_ty, a_ty, b_ty) = refs[16:26]
+    (q0, md, gc, q1, q2, q3, r3, rx, ry, own_a, other_a, own_b, other_b, load, send, recv) = refs[26:]
     made = Messages((send, recv))
     col = lax.axis_index("col")
     core = lax.rem(col, 2)
@@ -1963,7 +1973,6 @@
     rows, width = p0.shape
     part = width // 2
     half_tokens = rows // 2
-    channels = eu.shape[1]
     copies = []
 
     def copy(src, dst):
@@ -2006,9 +2015,7 @@
         def one(k, carry):
             at = pl.ds(pl.multiple_of(n * width + k * sub, sub), sub)
             where = pl.ds(pl.multiple_of(row + k * sub, sub), sub)
-            left = n1[:, at]
-            target[where, :channels] = dot_tn(left, eu[...]).astype(BF)
-            target[where, channels:] = dot_tn(left, ev[...]).astype(BF)
+            target[where, :] = dot_tn(n1[:, at], euv[...]).astype(BF)
             return carry
 
         lax.fori_loop(0, 3, one, 0)
@@ -2043,8 +2050,9 @@
         total.begin(n)
 
     def chunk_out(value, own, other, at):
-        own[at, :] = value[:, :part]
-        other[at, :] = pltpu.roll(value, part, 1)[:, :part]
+        turned = value.T
+        own[:, at] = turned[:part]
+        other[:, at] = turned[part:]
 
     def in_steps(start, size, body):
         def one(n, carry):
@@ -2103,20 +2111,20 @@
         c.wait()
 
 
-def tail(n1, eu, ev, grad_small, grad_mixer, grad_feed, parts, mid, grad_chunk):
-    rows, channels = eu.shape
+def tail(n1, euv, grad_small, grad_mixer, grad_feed, parts, mid, grad_chunk):
+    rows, channels = euv.shape[0], euv.shape[1] // 2
     width = mid.shape[1]
     part = width // 2
     big = pltpu.VMEM((2 * width, 2 * channels), BF)
     tiny = pltpu.VMEM((16, channels), F32)
     piece = pltpu.VMEM((rows, width), BF)
     full = pltpu.VMEM((rows, width), F32)
-    side = pltpu.VMEM((rows, part), F32)
+    side = pltpu.VMEM((part, rows), F32)
     quarter_in = (width, 2 * channels)
-    final = sds((2, rows, part), F32)
+    final = sds((2, part, rows), F32)
     return pl.pallas_call(
         tail_body,
-        in_specs=[pl.BlockSpec(memory_space=pltpu.VMEM)] * 6 + [any_spec()] * 6,
+        in_specs=[pl.BlockSpec(memory_space=pltpu.VMEM)] * 5 + [any_spec()] * 6,
         out_specs=[any_spec()] * 2 + [pl.BlockSpec(memory_space=pltpu.VMEM)] + [any_spec()] * 2,
         out_shape=[sds(quarter_in, BF)] * 2 + [sds((16, channels), F32), final, final],
         scratch_shapes=[big] * 5
@@ -2129,9 +2137,9 @@
         compiler_params=pltpu.CompilerParams(
             vmem_limit_bytes=VMEM_LIMIT, collective_id=6, has_side_effects=True
         ),
-        cost_estimate=cost(60 * rows * width * channels * 4, nbytes(n1, eu, ev)),
+        cost_estimate=cost(60 * rows * width * channels * 4, nbytes(n1, euv)),
         name="tail",
-    )(n1, eu, ev, grad_small, grad_mixer, grad_feed, *parts, mid, grad_chunk)
+    )(n1, euv, grad_small, grad_mixer, grad_feed, *parts, mid, grad_chunk)
 
 
 def arrange_body(place, mine_gu, far_gu, mine_dn, far_dn, mine_in, far_in, mine_out, far_out, *outs):
@@ -2161,22 +2169,23 @@
     width, units = far_dn.shape[1], far_dn.shape[0]
     inner = mine_out.shape[0]
     lanes_gu, lanes_in = mine_gu.shape[1], mine_in.shape[1]
-    quarter = width // 4
+    cuts = 2
+    piece = width // (2 * cuts)
 
     def rows_in(i, j, place):
-        return (2 * i + j, 0)
+        return (cuts * i + j, 0)
 
     def rows_to(i, j, place):
-        return (2 * (i + place[0] - 2 * i * place[0]) + j, 0)
+        return (cuts * (i + place[0] - 2 * i * place[0]) + j, 0)
 
     def near(i, j, place):
-        return (jnp.where(i == 0, j, 1), 0)
+        return (jnp.where(i == 0, j, cuts - 1), 0)
 
     def far(i, j, place):
         return (jnp.where(i == 0, 0, j), 0)
 
     def stack_to(i, j, place):
-        return (2 * (i + place[1] - 2 * i * place[1]) + j, 0)
+        return (cuts * (i + place[1] - 2 * i * place[1]) + j, 0)
 
     def spec(rows, lanes, at):
         return pl.BlockSpec((rows, lanes), at)
@@ -2186,21 +2195,21 @@
         arrange_body,
         grid_spec=pltpu.PrefetchScalarGridSpec(
             num_scalar_prefetch=1,
-            grid=(2, 2),
+            grid=(2, cuts),
             in_specs=[
-                spec(quarter, lanes_gu, rows_in),
-                spec(quarter, lanes_gu, rows_in),
-                spec(units // 2, width, near),
-                spec(units // 2, width, far),
-                spec(quarter, lanes_in, rows_in),
-                spec(quarter, lanes_in, rows_in),
-                spec(inner // 2, width, near),
-                spec(inner // 2, width, far),
+                spec(piece, lanes_gu, rows_in),
+                spec(piece, lanes_gu, rows_in),
+                spec(units // cuts, width, near),
+                spec(units // cuts, width, far),
+                spec(piece, lanes_in, rows_in),
+                spec(piece, lanes_in, rows_in),
+                spec(inner // cuts, width, near),
+                spec(inner // cuts, width, far),
             ],
-            out_specs=[spec(quarter, lanes_gu, rows_to)] * 2
-            + [spec(units // 2, width, stack_to)]
-            + [spec(quarter, lanes_in, rows_to)] * 2
-            + [spec(inner // 2, width, stack_to)],
+            out_specs=[spec(piece, lanes_gu, rows_to)] * 2
+            + [spec(units // cuts, width, stack_to)]
+            + [spec(piece, lanes_in, rows_to)] * 2
+            + [spec(inner // cuts, width, stack_to)],
         ),
         out_shape=[sds(s, F32) for s in shapes],
         compiler_params=pltpu.CompilerParams(vmem_limit_bytes=VMEM_LIMIT),
@@ -2248,10 +2257,11 @@
     off = jnp.concatenate([edge, offset, edge])[:, None]
 
     (
-        x, g, g_low, w_out, w_down, gains_all, small, s1, u, v, border, earlier, mid, mid_low,
+        g_low, w_down, gains_all, small, s1, border, earlier, mid, mid_low,
         n1, conv, recall, admit, states, mixed, mx, my, md, far_w, sib_own, sib_far, w_in,
+        x, g, w_out, u, v,
     ) = front(
-        stream_in, cotangent, input_weight, branch_weight, output_weight, gate_weight, up_weight, down_weight,
+        jnp.swapaxes(stream_in, 1, 2), jnp.swapaxes(cotangent, 1, 2), input_weight, branch_weight, output_weight, gate_weight, up_weight, down_weight,
         gains, small, recall_gate, admit_gate, off, count - 1,
     )
     taps, soft, decay = small[:KW], small[KW : KW + 1], small[KW + 1 : KW + 2]
@@ -2260,13 +2270,13 @@
         (gate_weight, up_weight, sib_own, far_w, sib_far),
     )
     (
-        ev, eu, grad_chunk, grad_mixer, grad_small, mine_gu, far_gu, far_down, mine_out, far_out, gates
+        euv, grad_chunk, grad_mixer, grad_small, mine_gu, far_gu, far_down, mine_out, far_out, gates
     ) = back(
         dx_all, w_out, states, v, recall, conv, admit, u, off, soft, taps, rw, aw, border, earlier,
         w_in, s1, x, dx2, gains_all, sum_gu, sum_down, mixed,
     )
     mine_in, far_in, tiny, out, grad = tail(
-        n1, eu, ev, grad_small, grad_mixer, grad_feed, (p0, p1, p2, p3), mid, grad_chunk
+        n1, euv, grad_small, grad_mixer, grad_feed, (p0, p1, p2, p3), mid, grad_chunk
     )
     place = jnp.stack([row, y]).astype(jnp.int32)
     grad_gate, grad_up, grad_down, grad_input, grad_branch, grad_output = arrange(
@@ -2277,8 +2287,8 @@
     mine = lax.dynamic_slice_in_dim(tiny[:8], core * own, own, 1)
     gain_grads = lax.dynamic_slice_in_dim(tiny[8:10, : 2 * part], core * part, part, 1)
     return (
-        out,
-        grad,
+        jnp.swapaxes(out, 1, 2),
+        jnp.swapaxes(grad, 1, 2),
         gain_grads[0],
         grad_input,
         grad_branch,

time: 520 us -> 503 us (0.967)
  Pallas kernels: 500 us -> 487 us
  local copies, waits for them, and re-layouts: 15.6 us -> 9.36 us
    pallas_call x1, Pallas kernels: 149 us -> 142 us  [front(): pl.pallas_call(functools.partial(front_body, heads, blocks, count), grid=...]
    unnamed x28 -> x18, local copies, waits for them, and re-layouts: 9.34 us -> 3.15 us
where the time goes in v6:
time: 503 us
  Pallas kernels  487 us (97%)
  local copies, waits for them, and re-layouts  9.36 us (2%)
  other arithmetic  5.64 us (1%)
    pallas_call x1, Pallas kernels, feed(): pl.pallas_call(functools.partial(feed_body, blocks), grid=(2 * blocks + t...  143 us
    pallas_call x1, Pallas kernels, front(): pl.pallas_call(functools.partial(front_body, heads, blocks, count), grid=...  142 us
    pallas_call x1, Pallas kernels, back(): pl.pallas_call(functools.partial(back_body, heads, blocks, count), grid=(...  133 us
    pallas_call x1, Pallas kernels, tail(): pl.pallas_call(tail_body, in_specs=[pl.BlockSpec(memory_space=pltpu.VMEM)...  58.5 us

profile of v6, /device:TPU:0, one launch (start us, length us, event | category | flops | bytes accessed | tf_op | source)
XLA Modules:
  0.0 502.9 jit_solution(9458968540647929953)
XLA Ops:
  0.7 0.7 constant_dynamic-slice_fusion.4
  1.4 0.2 reduce-window_clone.1
  1.5 0.7 subtract_bitcast_fusion
  2.2 0.1 select_reduce_fusion
  2.3 0.1 concatenate.11
  2.4 1.0 broadcast_in_dim.42.refs_12_.refs_11_
  3.4 0.7 compare_select_fusion
  4.1 0.1 pad.5.clone
  4.2 1.4 maximum_maximum_fusion.1.refs_9_
  5.6 0.1 pad.8.clone
  5.7 1.4 maximum_maximum_fusion.refs_8_
  7.0 142.0 %front.1 = (bf16[1024,384]{1,0:T(8,128)(2,1)}, bf16[1152,1536]{1,0:T(8,128)(2,1)}, f32[8,1536]{1,0:T(8,128)}, f32[8,512]{1,0:T(8,128)}, f32[1024,1]{1,0:T(8,128)...) custom-call(f32[2,192,1024]{2,1,0:T(8,128)} %bitcast.28, ...), custom_call_target="tpu_custom_call" | custom-call | flops 80530636800 | bytes 40960000 | tf_op jit(solution)/shard_map/front/pallas_call | solution.py:1117
  149.0 0.0 copy-start.7
  149.0 0.0 copy-start.3
  149.0 0.0 copy-start.4
  149.0 143.5 %feed.1 = (f32[1024,384]{1,0:T(8,128)}, bf16[1024,384]{1,0:T(8,128)(2,1)}, bf16[1024,384]{1,0:T(8,128)(2,1)}, bf16[1024,384]{1,0:T(8,128)(2,1)}, f32[1024,384]{1...) custom-call(bf16[1024,384]{1,0:T(8,128)(2,1)} %get-tuple-element.75., ...), custom_call_target="tpu_custom_call" | custom-call | flops 86973087744 | bytes 41336832 | tf_op jit(solution)/shard_map/feed/pallas_call | solution.py:1438
  292.5 0.0 copy-done.7
  292.5 0.6 slice.33.refs_13_
  293.1 0.6 slice.32.refs_12_
  293.7 0.0 copy-done.3
  293.7 0.0 copy-done.4
  293.7 0.8 constant_dynamic-slice_fusion.2
  294.5 133.1 %back.1 = (bf16[1024,1024]{1,0:T(8,128)(2,1)}, f32[1024,384]{1,0:T(8,128)}, f32[8,384]{1,0:T(8,128)}, f32[8,512]{1,0:T(8,128)}, bf16[384,2304]{1,0:T(8,128)(2,1)...) custom-call(bf16[1024,384]{1,0:T(8,128)(2,1)} %get-tuple-element.87., ...), custom_call_target="tpu_custom_call" | custom-call | flops 103079215104 | bytes 31457280 | tf_op jit(solution)/shard_map/back/pallas_call | solution.py:1876
  427.6 58.5 %tail.1 = (bf16[384,1024]{1,0:T(8,128)(2,1)}, bf16[384,1024]{1,0:T(8,128)(2,1)}, f32[16,512]{1,0:T(8,128)}, f32[2,192,1024]{2,1,0:T(8,128)}, f32[2,192,1024]{2,1,0:T(8,128)}) custom-call(bf16[1024,1536]{1,0:T(8,128)(2,1)} %get-tuple-element.74.refs_0_, bf16[1024,1024]{1,0:T(8,128)(2,1)} %get-tuple-element.108.refs_1_, f32[8,512]{1,0:T(8,128)} %get-tuple-element.109.refs_2_, ...), custom_call_target="tpu_custom_call" | custom-call | flops 48318382080 | bytes 5242880 | tf_op jit(solution)/shard_map/tail/pallas_call | solution.py:2125
  486.2 0.6 pad_add_fusion.place
  486.7 0.0 copy-start.5
  486.7 0.0 copy-start.6
  486.7 0.0 copy-start
  486.7 10.0 %arrange.1 = (f32[384,2304]{1,0:T(8,128)}, f32[384,2304]{1,0:T(8,128)}, f32[2304,384]{1,0:T(8,128)}, f32[384,1024]{1,0:T(8,128)}, f32[384,1024]{1,0:T(8,128)}, /*index=5*/f32[1024,384]{1,0:T(8,128)}) custom-call(s32[2]{0:T(128)} %pad_add_fusion.place, bf16[384,2304]{1,0:T(8,128)(2,1)} %get-tuple-element.120.mine_gu, ...), custom_call_target="tpu_custom_call" | custom-call | flops 1000000 | bytes 24000000 | tf_op jit(solution)/shard_map/arrange/pallas_call | solution.py:2194
  496.8 0.0 copy-done.5
  496.8 0.6 constant_dynamic-slice_fusion
  497.4 0.1 dynamic-slice_multiply_fusion
  497.5 0.0 copy-done.6
  497.5 0.6 divide_multiply_fusion
  498.1 0.0 copy-start.2
  498.1 0.6 fusion.2
  498.7 0.0 copy-done
  498.7 1.0 fusion.1
  499.7 0.0 copy-start.1
  499.7 0.0 copy-done.2
  499.7 1.1 copy.35
  500.9 0.8 copy-done.1
  501.7 1.1 copy.36
  (7 shorter events, 0.0 us)
Async XLA Ops:
  149.0 143.5 %copy-start.7 = (f32[8,512]{1,0:T(8,128)S(1)}, f32[8,512]{1,0:T(8,128)}, u32[]{:S(2)}) copy-start(f32[8,512]{1,0:T(8,128)} %get-tuple-element.98) | copy-start | bytes 49156
  149.0 144.7 %copy-start.3 = (f32[8,128,128]{2,1,0:T(8,128)S(1)}, f32[8,128,128]{2,1,0:T(8,128)}, u32[]{:S(2)}) copy-start(f32[8,128,128]{2,1,0:T(8,128)} %refs_10_.2) | copy-start | bytes 1572868
  149.0 144.7 %copy-start.4 = (f32[8,128,128]{2,1,0:T(8,128)S(1)}, f32[8,128,128]{2,1,0:T(8,128)}, u32[]{:S(2)}) copy-start(f32[8,128,128]{2,1,0:T(8,128)} %refs_11_.1) | copy-start | bytes 1572868
  486.7 10.0 %copy-start.5 = (f32[16,512]{1,0:T(8,128)S(1)}, f32[16,512]{1,0:T(8,128)}, u32[]{:S(2)}) copy-start(f32[16,512]{1,0:T(8,128)} %get-tuple-element.119) | copy-start | bytes 98308
  486.7 10.7 %copy-start.6 = (f32[256]{0:T(256)S(1)}, f32[256]{0:T(256)}, u32[]{:S(2)}) copy-start(f32[256]{0:T(256)} %param.24) | copy-start | bytes 3076
  486.7 12.0 %copy-start = (bf16[2048,128]{1,0:T(8,128)(2,1)S(1)}, bf16[2048,128]{1,0:T(8,128)(2,1)}, u32[]{:S(2)}) copy-start(bf16[2048,128]{1,0:T(8,128)(2,1)} %get-tuple-element.129) | copy-start | bytes 1572868
  498.1 1.7 copy-start.2
  499.7 2.0 copy-start.1

commit v7 on v6

--- a/solution.py
+++ b/solution.py
@@ -1192,9 +1192,11 @@
         for n in range(2)
     ]
     cut = width // 8
-    for n in range(FEED_CUTS):
-        at = pl.ds(n * cut, cut)
-        pieces.append([s_gu.at[pl.ds(width + n * cut, cut), :], a_gu.at[at, :], b_gu.at[at, :]])
+    spans = [(n * cut, cut) for n in range(FEED_CUTS - 1)]
+    spans += [((FEED_CUTS - 1) * cut, 2 * cut // 3), (FEED_CUTS * cut - cut // 3, cut // 3)]
+    for start, size in spans:
+        at = pl.ds(start, size)
+        pieces.append([s_gu.at[pl.ds(width + start, size), :], a_gu.at[at, :], b_gu.at[at, :]])
     total = SeqSum(pieces, (send, recv), made.used)
     made.used += 2 * len(pieces)
 
@@ -1437,7 +1439,7 @@
     landing = pltpu.VMEM((units, 2 * width), BF)
     return pl.pallas_call(
         functools.partial(feed_body, blocks),
-        grid=(2 * blocks + tiles + 7 + FEED_CUTS,),
+        grid=(2 * blocks + tiles + 8 + FEED_CUTS,),
         in_specs=[held(width)] * 4
         + [whole_spec(err_own.shape), whole_spec(mid.shape), any_spec(), whole_spec(gain.shape)]
         + [any_spec()] * 6,
@@ -1536,15 +1538,8 @@
             to_y[p] = [made.new(pieces[p][0], target, to_side)]
         else:
             to_out[p] = [store_copy(pieces[p][0], mine_gu.at[at, :])]
-    for lane in (width, 0):
-        for n in (0,):
-            p = len(pieces)
-            at = pl.ds(n * rows_out, rows_out)
-            pieces.append([r.at[at, pl.ds(lane, width)] for r in (s_out, a_out, b_out)])
-            if lane:
-                to_y[p] = [made.new(pieces[p][0], far_out.at[at, :], to_side)]
-            else:
-                to_out[p] = [store_copy(pieces[p][0], mine_out.at[at, :])]
+    pieces.append([r.at[:, pl.ds(width, width)] for r in (s_out, a_out, b_out)])
+    to_y[len(pieces) - 1] = [made.new(pieces[-1][0], far_out, to_side)]
     p = len(pieces)
     pieces.append([s_gt, a_gt, b_gt])
     to_y[p], to_out[p] = [], []
@@ -1553,6 +1548,10 @@
         target = gates.at[pl.ds(pl.multiple_of((2 * n + y) * size, size), size), :]
         to_y[p].append(made.new(source, target, to_side))
         to_out[p].append(store_copy(source, target))
+    for n in (0, 1):
+        at = pl.ds(n * (rows_out // 2), rows_out // 2)
+        pieces.append([r.at[at, pl.ds(0, width)] for r in (s_out, a_out, b_out)])
+        to_out[len(pieces) - 1] = [store_copy(pieces[-1][0], mine_out.at[at, :])]
     total = SeqSum(pieces, sems, made.used)
     made.used += 2 * len(pieces)
     core_out, core_gt = made.new(p_out, c_out, to_core), made.new(p_gt, c_gt, to_core)
@@ -1983,7 +1982,9 @@
     late = [copy(p0, q0), copy(mid, md), copy(grad_chunk, gc)]
     scatter = made.block(scatter_messages, q1, q2, q3, r3, rx, ry)
     cut = width // 4
-    order = [pl.ds(n * cut, cut) for n in (4, 5, 6, 7, 0, 1, 2, 3)]
+    spans = [(n * cut, cut) for n in (4, 5, 6, 7, 0, 1, 2)]
+    spans += [(3 * cut, cut // 2), (3 * cut + cut // 2, cut // 2)]
+    order = [pl.ds(*span) for span in spans]
     pieces = [[s_ty, a_ty, b_ty]] + [[r.at[at, :] for r in (s_in, a_in, b_in)] for at in order]
     count = len(pieces)
     total = SeqSum(pieces, (send, recv), made.used)
@@ -1996,7 +1997,7 @@
     }
     send_out, send_grad = made.new(other_a, out.at[core], to_core), made.new(other_b, grad.at[core], to_core)
     keep_out, keep_grad = copy(own_a, out.at[core]), copy(own_b, grad.at[core])
-    keep_in = {n + 1: copy(s_in.at[order[n], :], mine_in.at[pl.ds((n - 4) * cut, cut), :]) for n in range(4, 8)}
+    keep_in = {n + 1: copy(s_in.at[order[n], :], mine_in.at[order[n], :]) for n in range(4, len(order))}
 
     for m in outs_in:
         m.start()
@@ -2132,7 +2133,7 @@
         + [full] * 3
         + [piece] * 6
         + [side] * 4
-        + [pltpu.SemaphoreType.DMA((12,))]
+        + [pltpu.SemaphoreType.DMA((13,))]
         + [pltpu.SemaphoreType.DMA((TAIL_MESSAGES,))] * 2,
         compiler_params=pltpu.CompilerParams(
             vmem_limit_bytes=VMEM_LIMIT, collective_id=6, has_side_effects=True

time: 503 us -> 498 us (0.990)
  no operation moved by 1% of the time
where the time goes in v7:
time: 498 us
  Pallas kernels  482 us (97%)
  local copies, waits for them, and re-layouts  9.36 us (2%)
  other arithmetic  5.64 us (1%)
    pallas_call x1, Pallas kernels, feed(): pl.pallas_call(functools.partial(feed_body, blocks), grid=(2 * blocks + t...  143 us
    pallas_call x1, Pallas kernels, front(): pl.pallas_call(functools.partial(front_body, heads, blocks, count), grid=...  142 us
    pallas_call x1, Pallas kernels, back(): pl.pallas_call(functools.partial(back_body, heads, blocks, count), grid=(...  129 us
    pallas_call x1, Pallas kernels, tail(): pl.pallas_call(tail_body, in_specs=[pl.BlockSpec(memory_space=pltpu.VMEM)...  58.1 us
    pallas_call x1, Pallas kernels, arrange(): pl.pallas_call(arrange_body, grid_spec=pltpu.PrefetchScalarGridSpec(num_s...  10 us

profile of v7, /device:TPU:0, one launch (start us, length us, event | category | flops | bytes accessed | tf_op | source)
XLA Modules:
  0.0 498.0 jit_solution(2414825842129340317)
XLA Ops:
  0.7 0.7 constant_dynamic-slice_fusion.4
  1.4 0.2 reduce-window_clone.1
  1.5 0.7 subtract_bitcast_fusion
  2.2 0.1 select_reduce_fusion
  2.3 0.1 concatenate.11
  2.4 1.0 broadcast_in_dim.42.refs_12_.refs_11_
  3.4 0.7 compare_select_fusion
  4.1 0.1 pad.5.clone
  4.2 1.4 maximum_maximum_fusion.1.refs_9_
  5.6 0.1 pad.8.clone
  5.7 1.4 maximum_maximum_fusion.refs_8_
  7.0 142.0 %front.1 = (bf16[1024,384]{1,0:T(8,128)(2,1)}, bf16[1152,1536]{1,0:T(8,128)(2,1)}, f32[8,1536]{1,0:T(8,128)}, f32[8,512]{1,0:T(8,128)}, f32[1024,1]{1,0:T(8,128)...) custom-call(f32[2,192,1024]{2,1,0:T(8,128)} %bitcast.28, ...), custom_call_target="tpu_custom_call" | custom-call | flops 80530636800 | bytes 40960000 | tf_op jit(solution)/shard_map/front/pallas_call | solution.py:1117
  149.0 0.0 copy-start.7
  149.0 0.0 copy-start.3
  149.0 0.0 copy-start.4
  149.0 143.3 %feed.1 = (f32[1024,384]{1,0:T(8,128)}, bf16[1024,384]{1,0:T(8,128)(2,1)}, bf16[1024,384]{1,0:T(8,128)(2,1)}, bf16[1024,384]{1,0:T(8,128)(2,1)}, f32[1024,384]{1...) custom-call(bf16[1024,384]{1,0:T(8,128)(2,1)} %get-tuple-element.75., ...), custom_call_target="tpu_custom_call" | custom-call | flops 86973087744 | bytes 41336832 | tf_op jit(solution)/shard_map/feed/pallas_call | solution.py:1440
  292.4 0.0 copy-done.7
  292.4 0.6 slice.33.refs_13_
  293.0 0.6 slice.32.refs_12_
  293.6 0.0 copy-done.3
  293.6 0.0 copy-done.4
  293.6 0.8 constant_dynamic-slice_fusion.2
  294.4 128.7 %back.1 = (bf16[1024,1024]{1,0:T(8,128)(2,1)}, f32[1024,384]{1,0:T(8,128)}, f32[8,384]{1,0:T(8,128)}, f32[8,512]{1,0:T(8,128)}, bf16[384,2304]{1,0:T(8,128)(2,1)...) custom-call(bf16[1024,384]{1,0:T(8,128)(2,1)} %get-tuple-element.87., ...), custom_call_target="tpu_custom_call" | custom-call | flops 103079215104 | bytes 31457280 | tf_op jit(solution)/shard_map/back/pallas_call | solution.py:1875
  423.1 58.1 %tail.1 = (bf16[384,1024]{1,0:T(8,128)(2,1)}, bf16[384,1024]{1,0:T(8,128)(2,1)}, f32[16,512]{1,0:T(8,128)}, f32[2,192,1024]{2,1,0:T(8,128)}, f32[2,192,1024]{2,1,0:T(8,128)}) custom-call(bf16[1024,1536]{1,0:T(8,128)(2,1)} %get-tuple-element.74.refs_0_, bf16[1024,1024]{1,0:T(8,128)(2,1)} %get-tuple-element.108.refs_1_, f32[8,512]{1,0:T(8,128)} %get-tuple-element.109.refs_2_, ...), custom_call_target="tpu_custom_call" | custom-call | flops 48318382080 | bytes 5242880 | tf_op jit(solution)/shard_map/tail/pallas_call | solution.py:2126
  481.3 0.6 pad_add_fusion.place
  481.9 0.0 copy-start.5
  481.9 0.0 copy-start.6
  481.9 0.0 copy-start
  481.9 10.0 %arrange.1 = (f32[384,2304]{1,0:T(8,128)}, f32[384,2304]{1,0:T(8,128)}, f32[2304,384]{1,0:T(8,128)}, f32[384,1024]{1,0:T(8,128)}, f32[384,1024]{1,0:T(8,128)}, /*index=5*/f32[1024,384]{1,0:T(8,128)}) custom-call(s32[2]{0:T(128)} %pad_add_fusion.place, bf16[384,2304]{1,0:T(8,128)(2,1)} %get-tuple-element.120.mine_gu, ...), custom_call_target="tpu_custom_call" | custom-call | flops 1000000 | bytes 24000000 | tf_op jit(solution)/shard_map/arrange/pallas_call | solution.py:2195
  491.9 0.0 copy-done.5
  491.9 0.6 constant_dynamic-slice_fusion
  492.5 0.1 dynamic-slice_multiply_fusion
  492.6 0.0 copy-done.6
  492.6 0.6 divide_multiply_fusion
  493.2 0.0 copy-start.2
  493.2 0.6 fusion.2
  493.8 0.0 copy-done
  493.8 1.0 fusion.1
  494.9 0.0 copy-start.1
  494.9 0.0 copy-done.2
  494.9 1.1 copy.35
  496.0 0.8 copy-done.1
  496.8 1.1 copy.36
  (7 shorter events, 0.0 us)
Async XLA Ops:
  149.0 143.4 %copy-start.7 = (f32[8,512]{1,0:T(8,128)S(1)}, f32[8,512]{1,0:T(8,128)}, u32[]{:S(2)}) copy-start(f32[8,512]{1,0:T(8,128)} %get-tuple-element.98) | copy-start | bytes 49156
  149.0 144.6 %copy-start.3 = (f32[8,128,128]{2,1,0:T(8,128)S(1)}, f32[8,128,128]{2,1,0:T(8,128)}, u32[]{:S(2)}) copy-start(f32[8,128,128]{2,1,0:T(8,128)} %refs_10_.2) | copy-start | bytes 1572868
  149.0 144.6 %copy-start.4 = (f32[8,128,128]{2,1,0:T(8,128)S(1)}, f32[8,128,128]{2,1,0:T(8,128)}, u32[]{:S(2)}) copy-start(f32[8,128,128]{2,1,0:T(8,128)} %refs_11_.1) | copy-start | bytes 1572868
  481.9 10.0 %copy-start.5 = (f32[16,512]{1,0:T(8,128)S(1)}, f32[16,512]{1,0:T(8,128)}, u32[]{:S(2)}) copy-start(f32[16,512]{1,0:T(8,128)} %get-tuple-element.119) | copy-start | bytes 98308
  481.9 10.7 %copy-start.6 = (f32[256]{0:T(256)S(1)}, f32[256]{0:T(256)}, u32[]{:S(2)}) copy-start(f32[256]{0:T(256)} %param.24) | copy-start | bytes 3076
  481.9 12.0 %copy-start = (bf16[2048,128]{1,0:T(8,128)(2,1)S(1)}, bf16[2048,128]{1,0:T(8,128)(2,1)}, u32[]{:S(2)}) copy-start(bf16[2048,128]{1,0:T(8,128)(2,1)} %get-tuple-element.129) | copy-start | bytes 1572868
  493.2 1.7 copy-start.2
  494.9 2.0 copy-start.1
